TPU v7x, 32 devices: a whole 2x2x4 slice. The times are simulated.
32 devices in a mesh: tile: 4 (over z), sub: 8 (over y, x, core).
Axes of the slice: x: 2, y: 2, z: 4, core: 2. Of those that a mesh axis runs over, the one named last changes fastest.
Arguments:
- initial: float32 [64, 64, 2048], P(None, 'tile', 'sub'), may hold values from -6 to 6
- targets: float32 [64, 64, 2048], P(None, 'tile', 'sub'), may hold values from -6 to 6
- diffusivity: float32 [64, 2048], P('tile', 'sub'), may hold values from 0.02 to 0.24
- column_order: int32 [32, 4096], P(('tile', 'sub')), may hold values from 0 to 4095, each once within a row
- send_counts: int32 [32, 32], P(('tile', 'sub')), may hold values from 0 to 256, as said below
- w_first: bfloat16 [8, 64, 192], P('sub'), may hold values from -0.75 to 0.75
- w_inner: bfloat16 [8, 3, 192, 192], P('sub'), may hold values from -0.4375 to 0.4375
- w_last: bfloat16 [8, 192, 64], P('sub'), may hold values from -0.4375 to 0.4375
- b_inner: float32 [8, 4, 192], P('sub'), may hold values from -2 to 2
- b_last: float32 [8, 64], P('sub'), may hold values from -2 to 2
Outputs:
- grad_initial: float32 [64, 64, 2048], P(None, 'tile', 'sub')
- step_first: float32 [8, 64, 192], P('sub')
- step_inner: float32 [8, 3, 192, 192], P('sub')
- step_last: float32 [8, 192, 64], P('sub')
- step_bias_inner: float32 [8, 4, 192], P('sub')
- step_bias_last: float32 [8, 64], P('sub')
Inputs may be any that keep to these rules, and one draw needn't show every extreme that they name: `send_counts`: each row sums to 4096. For every pair of destinations d and d plus half of 32 (same sub index, tile indices half the tile axis apart) the two entries of a row sum to 256; some destination receives 256 from every device.
All inputs are finite; a program needn't handle non-finite values.
Results may differ from a plain program's by a relative error of at most 0.0095.
Values may be sent and summed in bfloat16 or wider, within the bound.
No kernel may reach another device: no remote copies, remote signals or barrier semaphores. Data moves between devices by JAX's collectives and lax.ppermute only.
A program may use at most 64 MiB of HBM per device.

v0:
```python
import functools
import jax
import jax.numpy as jnp
from jax import lax
from jax.experimental import pallas as pl
from jax.experimental.pallas import tpu as pltpu
from jax.sharding import PartitionSpec as P

LANES = 128
SUBLANES = 8
SECOND = 32
UNROLL = 16
VMEM = pl.BlockSpec(memory_space=pltpu.VMEM)
SMEM = pl.BlockSpec(memory_space=pltpu.SMEM)
PARAMS = pltpu.CompilerParams(vmem_limit_bytes=50 * 1024 * 1024)
F32 = jnp.float32
BF16 = jnp.bfloat16


def tile_rows(cells):
    levels, width_x, width_y = cells.shape
    split = cells.reshape(levels, width_x // SUBLANES, SUBLANES, width_y // LANES, LANES)
    return split.transpose(0, 1, 3, 2, 4).reshape(-1, LANES)


def untile_rows(rows, levels, width_x, width_y):
    split = rows.reshape(levels, width_x // SUBLANES, width_y // LANES, SUBLANES, LANES)
    return split.transpose(0, 1, 3, 2, 4).reshape(levels, width_x, width_y)


def row_offset(x, y_tile, y_tiles):
    return (x // SUBLANES * y_tiles + y_tile) * SUBLANES + x % SUBLANES


def load_row(ref, group, x, width_x, width_y):
    y_tiles = width_y // LANES
    stride = width_x * y_tiles
    base = group * (SUBLANES * stride)
    return jnp.concatenate(
        [
            ref[pl.ds(base + row_offset(x, y_tile, y_tiles), SUBLANES, stride=stride), :]
            for y_tile in range(y_tiles)
        ],
        axis=1,
    )


def load_wide(ref, x, width_y):
    y_tiles = width_y // LANES
    return jnp.concatenate(
        [
            jnp.broadcast_to(ref[pl.ds(row_offset(x, y_tile, y_tiles), 1), :], (SUBLANES, LANES))
            for y_tile in range(y_tiles)
        ],
        axis=1,
    )


def lane_ids(width):
    return lax.broadcasted_iota(jnp.int32, (SUBLANES, width), 1)


def compact_edges(row_of, width_x, width_y):
    lane = lane_ids(LANES)
    low = jnp.zeros((SUBLANES, LANES), F32)
    high = jnp.zeros((SUBLANES, LANES), F32)
    for x in range(width_x):
        row = row_of(x)
        low = jnp.where(lane == 1 + x, row[:, 0:1], low)
        low = jnp.where(lane == SECOND + 1 + x, row[:, 1:2], low)
        high = jnp.where(lane == 1 + x, row[:, width_y - 1 : width_y], high)
        high = jnp.where(lane == SECOND + 1 + x, row[:, width_y - 2 : width_y - 1], high)
    return low, high


def groups_at(group):
    return pl.ds(pl.multiple_of(group * SUBLANES, SUBLANES), SUBLANES)


def pack_body(levels, width_x, width_y, field, diff, top, bottom, low, high):
    def emit(where, row_of):
        for k in range(2):
            top[where, k * width_y : (k + 1) * width_y] = row_of(k)
            bottom[where, k * width_y : (k + 1) * width_y] = row_of(width_x - 2 + k)
        low_value, high_value = compact_edges(row_of, width_x, width_y)
        low[where, :] = low_value
        high[where, :] = high_value

    def step(group, carry):
        emit(groups_at(group), lambda x: load_row(field, group, x, width_x, width_y))
        return carry

    lax.fori_loop(0, levels // SUBLANES, step, 0)
    emit(pl.ds(levels, SUBLANES), lambda x: load_wide(diff, x, width_y))


def pack_edges(field_rows, diff_rows, levels, width_x, width_y):
    tall = levels + SUBLANES
    return pl.pallas_call(
        functools.partial(pack_body, levels, width_x, width_y),
        out_shape=[
            jax.ShapeDtypeStruct((tall, 2 * width_y), F32),
            jax.ShapeDtypeStruct((tall, 2 * width_y), F32),
            jax.ShapeDtypeStruct((tall, LANES), F32),
            jax.ShapeDtypeStruct((tall, LANES), F32),
        ],
        in_specs=[VMEM] * 2,
        out_specs=[VMEM] * 4,
        compiler_params=PARAMS,
        name="pack_edges",
    )(field_rows, diff_rows)


def shifted(array, shift_tile, shift_sub):
    tiles, subs = lax.axis_size("tile"), lax.axis_size("sub")
    if shift_tile == 0:
        return lax.ppermute(array, "sub", [(i, (i + shift_sub) % subs) for i in range(subs)])
    if shift_sub == 0:
        return lax.ppermute(array, "tile", [(i, (i + shift_tile) % tiles) for i in range(tiles)])
    pairs = []
    for t in range(tiles):
        for s in range(subs):
            target = (t + shift_tile) % tiles * subs + (s + shift_sub) % subs
            pairs.append((t * subs + s, target))
    return lax.ppermute(array, ("tile", "sub"), pairs)


def exchange(top, bottom, low, high):
    return (
        shifted(bottom, 1, 0),
        shifted(top, -1, 0),
        shifted(high, 0, 1),
        shifted(low, 0, -1),
        shifted(high, 1, 1),
        shifted(low, 1, -1),
        shifted(high, -1, 1),
        shifted(low, -1, -1),
    )


def with_corners(side, before, after, width_x):
    lane = lane_ids(LANES)
    value = jnp.where(lane == 0, pltpu.roll(before, LANES - width_x, 1), side)
    return jnp.where(lane == width_x + 1, pltpu.roll(after, width_x, 1), value)


def around(side):
    return pltpu.roll(side, 1, 1) + pltpu.roll(side, LANES - 1, 1)


def second(side):
    return pltpu.roll(side, LANES - SECOND, 1)


def beside(row, left, right, x):
    width = row.shape[1]
    lane = lane_ids(width)
    return jnp.where(lane == 0, left[:, x + 1 : x + 2], pltpu.roll(row, 1, 1)) + jnp.where(
        lane == width - 1, right[:, x + 1 : x + 2], pltpu.roll(row, width - 1, 1)
    )


def fill_starts(counts, starts, devices):
    def step(index, total):
        starts[index] = total
        return total + counts[index]

    lax.fori_loop(0, devices, step, jnp.int32(0))


def forward_body(
    levels, width_x, width_y, tiles, subs,
    counts, order, field, target, diff, own_low, own_high, up, down, left, right,
    up_left, up_right, down_left, down_right, out, e0, e1, wide, both, rows, picked, starts,
):
    cells = width_x * width_y
    devices = tiles * subs

    def at(x):
        return slice((x + 2) * width_y, (x + 3) * width_y)

    def sides(where):
        return (
            with_corners(left[where, :], up_left[where, :], down_left[where, :], width_x),
            with_corners(right[where, :], up_right[where, :], down_right[where, :], width_x),
        )

    last = pl.ds(levels, SUBLANES)
    for x in range(width_x):
        wide[:, at(x)] = load_wide(diff, x, width_y)
    wide[:, at(-1)] = up[last, width_y:]
    wide[:, at(width_x)] = down[last, :width_y]
    diff_left, diff_right = sides(last)

    def step(group, carry):
        where = groups_at(group)
        for x in range(width_x):
            e0[:, at(x)] = load_row(field, group, x, width_x, width_y)
        for k in range(2):
            e0[:, at(k - 2)] = up[where, k * width_y : (k + 1) * width_y]
            e0[:, at(width_x + k)] = down[where, k * width_y : (k + 1) * width_y]
        side_left, side_right = sides(where)

        def next_side(side, outer, own, coefficient):
            return side + coefficient * (around(side) + second(outer) + own - 4.0 * side)

        next_left = next_side(side_left, left[where, :], own_low[where, :], diff_left)
        next_right = next_side(side_right, right[where, :], own_high[where, :], diff_right)
        for x in range(-1, width_x + 1):
            row = e0[:, at(x)]
            near = e0[:, at(x - 1)] + e0[:, at(x + 1)] + beside(row, side_left, side_right, x)
            e1[:, at(x)] = row + wide[:, at(x)] * (near - 4.0 * row)
        for x in range(width_x):
            row = e1[:, at(x)]
            near = e1[:, at(x - 1)] + e1[:, at(x + 1)] + beside(row, next_left, next_right, x)
            value = row + wide[:, at(x)] * (near - 4.0 * row)
            both[where, x * width_y : (x + 1) * width_y] = value
            both[
                pl.ds(pl.multiple_of(levels + group * SUBLANES, SUBLANES), SUBLANES),
                x * width_y : (x + 1) * width_y,
            ] = value - load_row(target, group, x, width_x, width_y)
        return carry

    lax.fori_loop(0, levels // SUBLANES, step, 0)
    fill_starts(counts, starts, devices)

    def turn(tile, carry):
        span = pl.ds(pl.multiple_of(tile * LANES, LANES), LANES)
        rows[span, :] = both[:, span].T
        return carry

    lax.fori_loop(0, cells // LANES, turn, 0, unroll=2)

    def run(index, base):
        device = index % tiles * subs + index // tiles
        count = counts[device]
        start = starts[device]

        def copy(chunk, carry):
            offset = chunk * UNROLL
            taken = [rows[pl.ds(order[start + offset + u], 1), :] for u in range(UNROLL)]
            for u in range(UNROLL):
                picked[pl.ds(base + offset + u, 1), :] = taken[u]
            return carry

        lax.fori_loop(0, (count + UNROLL - 1) // UNROLL, copy, 0)
        return base + count

    lax.fori_loop(0, devices, run, jnp.int32(0))
    out[...] = picked[:cells, :].astype(BF16)


def forward(counts, order, field_rows, target_rows, diff_rows, own_low, own_high, halos, sizes):
    levels, width_x, width_y, tiles, subs = sizes
    cells = width_x * width_y
    return pl.pallas_call(
        functools.partial(forward_body, levels, width_x, width_y, tiles, subs),
        out_shape=jax.ShapeDtypeStruct((cells, 2 * levels), BF16),
        in_specs=[SMEM] * 2 + [VMEM] * 13,
        out_specs=VMEM,
        scratch_shapes=[
            pltpu.VMEM((SUBLANES, (width_x + 4) * width_y), F32),
            pltpu.VMEM((SUBLANES, (width_x + 4) * width_y), F32),
            pltpu.VMEM((SUBLANES, (width_x + 4) * width_y), F32),
            pltpu.VMEM((2 * levels, cells), F32),
            pltpu.VMEM((cells + SUBLANES, 2 * levels), F32),
            pltpu.VMEM((cells + UNROLL, 2 * levels), F32),
            pltpu.SMEM((tiles * subs,), jnp.int32),
        ],
        compiler_params=PARAMS,
        name="forward",
    )(counts, order, field_rows, target_rows, diff_rows, own_low, own_high, *halos)


def squeeze_lanes(wide_part, half):
    count = wide_part.shape[0] // 2
    lane = lax.broadcasted_iota(jnp.int32, (count, LANES), 1)
    low = wide_part[:count]
    high = wide_part[count:]
    if half == 0:
        high = pltpu.roll(high, LANES // 2, 1)
    else:
        low = pltpu.roll(low, LANES // 2, 1)
    return jnp.where(lane < LANES // 2, low, high)


def network_body(
    levels, width, packet, inputs, first_in, first_out, inner, last, bias, bias_last,
    out, grads, acc_first, acc_inner, acc_last, acc_bias, acc_bias_last,
):
    block = pl.program_id(0)
    cells = inputs.shape[0]
    lane = lax.broadcasted_iota(jnp.int32, (cells, LANES), 1)

    @pl.when(block == 0)
    def _():
        for ref in (acc_first, acc_inner, acc_last, acc_bias, acc_bias_last):
            ref[...] = jnp.zeros(ref.shape, ref.dtype)

    given = inputs[...]
    feeds = [given]
    slopes = []
    for k in range(4):
        weight = first_in[...] if k == 0 else inner[k - 1]
        preact = jnp.dot(feeds[-1], weight, preferred_element_type=F32) + bias[k : k + 1, :]
        gate = 0.5 * jnp.tanh(0.5 * preact) + 0.5
        active = preact * gate
        slopes.append(gate + active * (1.0 - gate))
        feeds.append(active.astype(BF16))
    output = jnp.dot(feeds[-1], last[...], preferred_element_type=F32) + bias_last[...]
    residue = jnp.where(lane >= levels, given.astype(F32) + output, 0.0)
    error = residue.astype(BF16)
    over_rows = (((0,), (0,)), ((), ()))
    over_lanes = (((1,), (1,)), ((), ()))

    def row_sum(value):
        return jnp.sum(value.reshape(cells // SUBLANES, SUBLANES, value.shape[1]), axis=0)

    acc_bias_last[...] += row_sum(error.astype(F32))
    acc_last[...] += lax.dot_general(feeds[4], error, over_rows, preferred_element_type=F32)
    carried = lax.dot_general(error, last[...], over_lanes, preferred_element_type=F32)
    for k in (3, 2, 1, 0):
        exact = carried * slopes[k]
        error = exact.astype(BF16)
        acc_bias[k] += row_sum(error.astype(F32))
        product = lax.dot_general(feeds[k], error, over_rows, preferred_element_type=F32)
        if k > 0:
            acc_inner[k - 1] += product
            carried = lax.dot_general(error, inner[k - 1], over_lanes, preferred_element_type=F32)
        else:
            acc_first[...] += product[:levels]
            carried = lax.dot_general(error, first_out[...], over_lanes, preferred_element_type=F32)
    back = residue + carried
    out[...] = squeeze_lanes(back, 1).astype(BF16)

    @pl.when(block == pl.num_programs(0) - 1)
    def _():
        row = 0

        def put(value):
            nonlocal row
            grads[row : row + value.shape[0], :] = value.astype(BF16)
            row += value.shape[0]

        for k in range(3):
            put(acc_inner[k][:, :LANES])
            put(squeeze_lanes(widen(acc_inner[k][:, LANES:]), 0))
        put(acc_first[...][:, :LANES])
        put(squeeze_lanes(widen(acc_first[...][:, LANES:]), 0))
        put(squeeze_lanes(acc_last[...], 1))
        pieces = [jnp.sum(acc_bias[k], axis=0, keepdims=True) for k in range(4)]
        tail = [piece[:, :LANES] for piece in pieces]
        tail += [widen(piece[:, LANES:]) for piece in pieces]
        tail.append(pltpu.roll(jnp.sum(acc_bias_last[...], axis=0, keepdims=True), LANES // 2, 1))
        tail.append(jnp.zeros((grads.shape[0] - row - len(tail), LANES), F32))
        put(jnp.concatenate(tail, axis=0))


def widen(value):
    missing = LANES - value.shape[1]
    return jnp.concatenate([value, jnp.zeros((value.shape[0], missing), value.dtype)], axis=1)


def grad_rows(levels, width, tiles):
    rows = 3 * (width + width // 2) + levels + levels // 2 + width // 2 + 16
    unit = 16 * tiles
    return (rows + unit - 1) // unit * unit


def network(received, w_first, w_inner, w_last, b_inner, b_last, tiles, subs):
    cells, doubled = received.shape
    levels = doubled // 2
    width = w_first.shape[1]
    block = cells // subs
    zeros = jnp.zeros_like(w_first)
    first_in = jnp.concatenate([w_first, zeros], axis=0)
    first_out = jnp.concatenate([zeros, w_first], axis=0)
    last = jnp.concatenate([jnp.zeros_like(w_last), w_last], axis=1)
    bias_last = jnp.concatenate([jnp.zeros_like(b_last), b_last])[None]
    rows = grad_rows(levels, width, tiles)

    def whole(*shape):
        return pl.BlockSpec(shape, lambda i: (0,) * len(shape))

    return pl.pallas_call(
        functools.partial(network_body, levels, width, block),
        grid=(subs,),
        out_shape=[
            jax.ShapeDtypeStruct((cells // 2, doubled), BF16),
            jax.ShapeDtypeStruct((rows, LANES), BF16),
        ],
        in_specs=[
            pl.BlockSpec((block, doubled), lambda i: (i, 0)),
            whole(doubled, width),
            whole(doubled, width),
            whole(3, width, width),
            whole(width, doubled),
            whole(4, width),
            whole(1, doubled),
        ],
        out_specs=[
            pl.BlockSpec((block // 2, doubled), lambda i: (i, 0)),
            whole(rows, LANES),
        ],
        scratch_shapes=[
            pltpu.VMEM((levels, width), F32),
            pltpu.VMEM((3, width, width), F32),
            pltpu.VMEM((width, doubled), F32),
            pltpu.VMEM((4, SUBLANES, width), F32),
            pltpu.VMEM((SUBLANES, doubled), F32),
        ],
        compiler_params=PARAMS,
        name="network",
    )(received, first_in, first_out, w_inner, last, b_inner, bias_last)


def sum_body(parts, out):
    total = parts[0].astype(F32)
    for index in range(1, parts.shape[0]):
        total = total + parts[index].astype(F32)
    total = total.astype(BF16)
    for index in range(parts.shape[0]):
        out[index] = total


def sum_parts(parts):
    return pl.pallas_call(
        sum_body,
        out_shape=jax.ShapeDtypeStruct(parts.shape, BF16),
        in_specs=[VMEM],
        out_specs=VMEM,
        compiler_params=PARAMS,
        name="sum_parts",
    )(parts)


def steps_body(levels, width, count, whole, first, inner, last, bias, bias_last):
    def squares(index, total):
        part = whole[pl.ds(pl.multiple_of(index * 16, 16), 16), :].astype(F32)
        return total + part * part

    total = lax.fori_loop(0, whole.shape[0] // 16, squares, jnp.zeros((16, LANES), F32), unroll=4)
    factor = 1.0 / jnp.sqrt(jnp.broadcast_to(jnp.sum(total), (1, LANES)) / count + 1e-06)
    row = 0

    def take(size):
        nonlocal row
        value = whole[row : row + size, :].astype(F32) * factor
        row += size
        return value

    half = LANES // 2

    def unpack(ref, size):
        low = take(size)
        narrow = take(size // 2)
        ref[:, :LANES] = low
        ref[: size // 2, LANES:] = narrow[:, :half]
        ref[size // 2 :, LANES:] = pltpu.roll(narrow, half, 1)[:, :half]

    for k in range(3):
        unpack(inner.at[k], width)
    unpack(first, levels)
    narrow = take(width // 2)
    last[: width // 2, :] = narrow[:, :half]
    last[width // 2 :, :] = pltpu.roll(narrow, half, 1)[:, :half]
    tail = take(16)
    bias[:, :LANES] = tail[0:4]
    bias[:, LANES:] = tail[4:8, :half]
    bias_last[...] = tail[8:9, :half]


def make_steps(whole, levels, width):
    count = 2 * levels * width + 3 * width * width + 4 * width + levels
    return pl.pallas_call(
        functools.partial(steps_body, levels, width, float(count)),
        out_shape=[
            jax.ShapeDtypeStruct((levels, width), F32),
            jax.ShapeDtypeStruct((3, width, width), F32),
            jax.ShapeDtypeStruct((width, levels), F32),
            jax.ShapeDtypeStruct((4, width), F32),
            jax.ShapeDtypeStruct((1, levels), F32),
        ],
        in_specs=[VMEM],
        out_specs=[VMEM] * 5,
        compiler_params=PARAMS,
        name="make_steps",
    )(whole)


def scatter_body(
    levels, width_x, width_y, tiles, subs,
    counts, order, answers, grid, top, bottom, low, high, slots, rows, bases, starts,
):
    cells = width_x * width_y
    devices = tiles * subs
    packet = cells // subs
    half = packet // 2
    fill_starts(counts, starts, devices)

    def place(index, base):
        device = index % tiles * subs + index // tiles
        bases[device] = base
        return base + counts[device]

    lax.fori_loop(0, devices, place, jnp.int32(0))
    for expert in range(subs):
        pair = answers[expert * half : (expert + 1) * half, :].astype(F32)
        slots[expert * packet : expert * packet + half, :] = pair
        slots[expert * packet + half : (expert + 1) * packet, :] = pltpu.roll(pair, levels, 1)

    def run(device, carry):
        count = counts[device]
        start = starts[device]
        base = bases[device]

        def copy(chunk, carry):
            offset = chunk * UNROLL
            taken = [slots[pl.ds(base + offset + u, 1), :] for u in range(UNROLL)]
            for u in range(UNROLL):
                rows[pl.ds(order[start + offset + u], 1), :] = taken[u]
            return carry

        lax.fori_loop(0, (count + UNROLL - 1) // UNROLL, copy, 0)
        return carry

    lax.fori_loop(0, devices, run, 0)

    def turn(tile, carry):
        span = pl.ds(pl.multiple_of(tile * LANES, LANES), LANES)
        grid[:, span] = rows[span, :].T[:levels]
        return carry

    lax.fori_loop(0, cells // LANES, turn, 0, unroll=2)

    lows, highs = [], []
    for group in range(levels // SUBLANES):
        where = slice(group * SUBLANES, (group + 1) * SUBLANES)
        low_value, high_value = compact_edges(
            lambda x: grid[where, x * width_y : (x + 1) * width_y], width_x, width_y
        )
        lows.append(low_value)
        highs.append(high_value)
    low[...] = jnp.concatenate(lows, axis=0).astype(BF16)
    high[...] = jnp.concatenate(highs, axis=0).astype(BF16)
    top[...] = grid[:, : 2 * width_y].astype(BF16)
    bottom[...] = grid[:, cells - 2 * width_y :].astype(BF16)


def scatter(counts, order, answers, sizes):
    levels, width_x, width_y, tiles, subs = sizes
    cells = width_x * width_y
    return pl.pallas_call(
        functools.partial(scatter_body, levels, width_x, width_y, tiles, subs),
        out_shape=[
            jax.ShapeDtypeStruct((levels, cells), F32),
            jax.ShapeDtypeStruct((levels, 2 * width_y), BF16),
            jax.ShapeDtypeStruct((levels, 2 * width_y), BF16),
            jax.ShapeDtypeStruct((levels, LANES), BF16),
            jax.ShapeDtypeStruct((levels, LANES), BF16),
        ],
        in_specs=[SMEM] * 2 + [VMEM],
        out_specs=[VMEM] * 5,
        scratch_shapes=[
            pltpu.VMEM((cells + UNROLL, 2 * levels), F32),
            pltpu.VMEM((cells + SUBLANES, 2 * levels), F32),
            pltpu.SMEM((tiles * subs,), jnp.int32),
            pltpu.SMEM((tiles * subs,), jnp.int32),
        ],
        compiler_params=PARAMS,
        name="scatter",
    )(counts, order, answers)


def adjoint_body(
    levels, width_x, width_y,
    grid, diff, own_low, own_high, diff_own_low, diff_own_high,
    up, down, left, right, up_left, up_right, down_left, down_right,
    diff_up, diff_down, diff_left, diff_right,
    diff_up_left, diff_up_right, diff_down_left, diff_down_right,
    out, wide, flow, e1,
):
    y_tiles = width_y // LANES
    stride = width_x * y_tiles

    def at(x):
        return slice((x + 2) * width_y, (x + 3) * width_y)

    last = pl.ds(levels, SUBLANES)
    for x in range(width_x):
        wide[:, at(x)] = load_wide(diff, x, width_y)
    for k in range(2):
        wide[:, at(k - 2)] = diff_up[last, k * width_y : (k + 1) * width_y]
        wide[:, at(width_x + k)] = diff_down[last, k * width_y : (k + 1) * width_y]
    rate_left = with_corners(
        diff_left[last, :], diff_up_left[last, :], diff_down_left[last, :], width_x
    )
    rate_right = with_corners(
        diff_right[last, :], diff_up_right[last, :], diff_down_right[last, :], width_x
    )

    def pair(value, which):
        return value.astype(F32)[which * SUBLANES : (which + 1) * SUBLANES]

    def step(double, carry):
        where = pl.ds(pl.multiple_of(double * 2 * SUBLANES, 2 * SUBLANES), 2 * SUBLANES)
        packed = [
            ref[where, :]
            for ref in (
                own_low, own_high, up, down, left, right,
                up_left, up_right, down_left, down_right,
            )
        ]
        for which in range(2):
            group = double * 2 + which
            own = groups_at(group)
            (
                own_l, own_h, above, below, at_left, at_right, at_ul, at_ur, at_dl, at_dr
            ) = [pair(value, which) for value in packed]
            side_left = with_corners(at_left, at_ul, at_dl, width_x)
            side_right = with_corners(at_right, at_ur, at_dr, width_x)

            def next_side(side, rate, outer, outer_rate, mine, mine_rate):
                product = side * rate
                return product, side + (
                    around(product)
                    + second(outer) * second(outer_rate)
                    + mine * mine_rate
                    - 4.0 * product
                )

            flow_left, next_left = next_side(
                side_left, rate_left, at_left, diff_left[last, :], own_l, diff_own_low[last, :]
            )
            flow_right, next_right = next_side(
                side_right, rate_right, at_right, diff_right[last, :], own_h, diff_own_high[last, :]
            )

            def value(x):
                if x < 0:
                    return above[:, (x + 2) * width_y : (x + 3) * width_y]
                if x >= width_x:
                    return below[:, (x - width_x) * width_y : (x - width_x + 1) * width_y]
                return grid[own, x * width_y : (x + 1) * width_y]

            for x in range(-2, width_x + 2):
                flow[:, at(x)] = value(x) * wide[:, at(x)]
            for x in range(-1, width_x + 1):
                row = flow[:, at(x)]
                near = flow[:, at(x - 1)] + flow[:, at(x + 1)]
                near = near + beside(row, flow_left, flow_right, x)
                e1[:, at(x)] = value(x) + near - 4.0 * row
            for x in range(-1, width_x + 1):
                flow[:, at(x)] = e1[:, at(x)] * wide[:, at(x)]
            flow_left = next_left * rate_left
            flow_right = next_right * rate_right
            for x in range(width_x):
                row = flow[:, at(x)]
                near = flow[:, at(x - 1)] + flow[:, at(x + 1)]
                near = near + beside(row, flow_left, flow_right, x)
                result = e1[:, at(x)] + near - 4.0 * row
                for y_tile in range(y_tiles):
                    offset = group * (SUBLANES * stride) + row_offset(x, y_tile, y_tiles)
                    out[pl.ds(offset, SUBLANES, stride=stride), :] = result[
                        :, y_tile * LANES : (y_tile + 1) * LANES
                    ]
        return carry

    lax.fori_loop(0, levels // (2 * SUBLANES), step, 0)


def adjoint(grid, diff_rows, own, diff_own, halos, diff_halos, sizes):
    levels, width_x, width_y, _, _ = sizes
    extended = (SUBLANES, (width_x + 4) * width_y)
    return pl.pallas_call(
        functools.partial(adjoint_body, levels, width_x, width_y),
        out_shape=jax.ShapeDtypeStruct((levels * width_x * width_y // LANES, LANES), F32),
        in_specs=[VMEM] * 22,
        out_specs=VMEM,
        scratch_shapes=[pltpu.VMEM(extended, F32)] * 3,
        compiler_params=PARAMS,
        name="adjoint",
    )(grid, diff_rows, *own, *diff_own, *halos, *diff_halos)


def per_device(
    initial, targets, diffusivity, column_order, send_counts,
    w_first, w_inner, w_last, b_inner, b_last,
):
    levels, width_x, width_y = initial.shape
    tiles, subs = lax.axis_size("tile"), lax.axis_size("sub")
    cells = width_x * width_y
    sizes = (levels, width_x, width_y, tiles, subs)
    field_rows = tile_rows(initial)
    target_rows = tile_rows(targets)
    diff_rows = tile_rows(diffusivity[None])
    counts = send_counts[0]
    order = jnp.pad(column_order[0], (0, LANES), constant_values=cells)
    top, bottom, low, high = pack_edges(field_rows, diff_rows, levels, width_x, width_y)
    halos = exchange(top, bottom, low, high)
    blocks = forward(counts, order, field_rows, target_rows, diff_rows, low, high, halos, sizes)
    received = lax.all_to_all(
        blocks.reshape(subs, cells // subs, 2 * levels), "sub", split_axis=0, concat_axis=0, tiled=True
    ).reshape(cells, 2 * levels)
    returning, gradients = network(
        received, w_first[0], w_inner[0], w_last[0], b_inner[0], b_last[0], tiles, subs
    )
    answers = lax.all_to_all(
        returning.reshape(subs, cells // subs // 2, 2 * levels),
        "sub", split_axis=0, concat_axis=0, tiled=True,
    ).reshape(cells // 2, 2 * levels)
    parts = lax.all_to_all(
        gradients.reshape(tiles, -1, LANES), "tile", split_axis=0, concat_axis=0, tiled=True
    )
    whole = lax.all_to_all(
        sum_parts(parts), "tile", split_axis=0, concat_axis=0, tiled=True
    ).reshape(-1, LANES)
    steps = make_steps(whole, levels, w_first.shape[2])
    grid, g_top, g_bottom, g_low, g_high = scatter(counts, order, answers, sizes)
    g_halos = exchange(g_top, g_bottom, g_low, g_high)
    result = adjoint(grid, diff_rows, (g_low, g_high), (low, high), g_halos, halos, sizes)
    return (
        untile_rows(result, levels, width_x, width_y),
        steps[0][None], steps[1][None], steps[2][None], steps[3][None], steps[4],
    )


def solution(mesh):
    placed = (
        P(None, "tile", "sub"),
        P(None, "tile", "sub"),
        P("tile", "sub"),
        P(("tile", "sub"), None),
        P(("tile", "sub"), None),
        P("sub", None, None),
        P("sub", None, None, None),
        P("sub", None, None),
        P("sub", None, None),
        P("sub", None),
    )
    return jax.shard_map(
        per_device,
        mesh=mesh,
        in_specs=placed,
        out_specs=(
            P(None, "tile", "sub"),
            P("sub", None, None),
            P("sub", None, None, None),
            P("sub", None, None),
            P("sub", None, None),
            P("sub", None),
        ),
        check_vma=False,
    )
```

profile of v0, /device:TPU:0, one launch (start us, length us, event | category | flops | bytes accessed | tf_op | source)
XLA Modules:
  0.0 139.0 jit_solution(7740235007553571622)
XLA Ops:
  0.6 0.0 copy-start
  0.6 1.2 copy-done
  1.9 0.7 copy-done.3
  2.6 1.6 %pack_edges.1 = (f32[72,512]{1,0:T(8,128)S(1)}, f32[72,512]{1,0:T(8,128)S(1)}, f32[72,128]{1,0:T(8,128)S(1)}, f32[72,128]{1,0:T(8,128)S(1)}) custom-call(f32[2048,128]{1,0:T(8,128)S(1)} %bitcast.39, f32[32,128]{1,0:T(8,128)S(1)} %bitcast.47), custom_call_target="tpu_custom_call" | custom-call | tf_op jit(solution)/shard_map/pack_edges/pallas_call | solution.py:99
  4.2 3.1 %collective-permute-start = (f32[72,512]{1,0:T(8,128)S(1)}, f32[72,512]{1,0:T(8,128)S(1)}, u32[]{:S(2)}, u32[]{:S(2)}) collective-permute-start(f32[72,512]{1,0:T(8,128)S(1)} %get-tuple-element.24), channel_id=1, source_target_pairs={{0,8},{8,16},{16,24},{24,0},{1,9},{9,17},{17,25},{25,1},{2,10},{10... | collective-permute-start | bytes 442376 | tf_op jit(solution)/shard_map/ppermute | solution.py:119
  7.3 2.1 %collective-permute-start.1 = (f32[72,512]{1,0:T(8,128)S(1)}, f32[72,512]{1,0:T(8,128)S(1)}, u32[]{:S(2)}, u32[]{:S(2)}) collective-permute-start(f32[72,512]{1,0:T(8,128)S(1)} %get-tuple-element.25), channel_id=1, source_target_pairs={{0,24},{8,0},{16,8},{24,16},{1,25},{9,1},{17,9},{25,17},{2,26},{10... | collective-permute-start | bytes 442376 | tf_op jit(solution)/shard_map/ppermute | solution.py:119
  9.4 0.0 collective-permute-start.2
  9.4 2.6 %collective-permute-start.3 = (f32[72,128]{1,0:T(8,128)S(1)}, f32[72,128]{1,0:T(8,128)S(1)}, u32[]{:S(2)}, u32[]{:S(2)}) collective-permute-start(f32[72,128]{1,0:T(8,128)S(1)} %get-tuple-element.22.own_low.diff_own_low), channel_id=1, source_target_pairs={{0,7},{1,0},{2,1},{3,2},{4,3},{5,4},{6,5},{7,6},{8,15},{9,8},{10,9... | collective-permute-start | bytes 110600 | tf_op jit(solution)/shard_map/ppermute | solution.py:117
  12.1 0.0 collective-permute-start.4
  12.1 1.6 %collective-permute-done.2.left.diff_left = f32[72,128]{1,0:T(8,128)S(1)} collective-permute-done((f32[72,128]{1,0:T(8,128)S(1)}, f32[72,128]{1,0:T(8,128)S(1)}, u32[]{:S(2)}, u32[]{:S(2)}) %collective-permute-start.2) | collective-permute-done | bytes 36896 | tf_op jit(solution)/shard_map/ppermute | solution.py:117
  13.7 1.4 %collective-permute-start.5 = (f32[72,128]{1,0:T(8,128)S(1)}, f32[72,128]{1,0:T(8,128)S(1)}, u32[]{:S(2)}, u32[]{:S(2)}) collective-permute-start(f32[72,128]{1,0:T(8,128)S(1)} %get-tuple-element.22.own_low.diff_own_low), channel_id=1, source_target_pairs={{0,15},{1,8},{2,9},{3,10},{4,11},{5,12},{6,13},{7,14},{8,23},{9,16... | collective-permute-start | bytes 110600 | tf_op jit(solution)/shard_map/ppermute | solution.py:125
  15.1 0.0 collective-permute-done.3.right.diff_right
  15.1 2.1 %collective-permute-start.6 = (f32[72,128]{1,0:T(8,128)S(1)}, f32[72,128]{1,0:T(8,128)S(1)}, u32[]{:S(2)}, u32[]{:S(2)}) collective-permute-start(f32[72,128]{1,0:T(8,128)S(1)} %get-tuple-element.23.own_high.diff_own_high), channel_id=1, source_target_pairs={{0,25},{1,26},{2,27},{3,28},{4,29},{5,30},{6,31},{7,24},{8,1},{9,2... | collective-permute-start | bytes 110600 | tf_op jit(solution)/shard_map/ppermute | solution.py:125
  17.3 1.8 %collective-permute-done.4.up_left.diff_up_left = f32[72,128]{1,0:T(8,128)S(1)} collective-permute-done((f32[72,128]{1,0:T(8,128)S(1)}, f32[72,128]{1,0:T(8,128)S(1)}, u32[]{:S(2)}, u32[]{:S(2)}) %collective-permute-start.4) | collective-permute-done | bytes 36896 | tf_op jit(solution)/shard_map/ppermute | solution.py:125
  19.1 1.9 %collective-permute-start.7 = (f32[72,128]{1,0:T(8,128)S(1)}, f32[72,128]{1,0:T(8,128)S(1)}, u32[]{:S(2)}, u32[]{:S(2)}) collective-permute-start(f32[72,128]{1,0:T(8,128)S(1)} %get-tuple-element.22.own_low.diff_own_low), channel_id=1, source_target_pairs={{0,31},{1,24},{2,25},{3,26},{4,27},{5,28},{6,29},{7,30},{8,7},{9,0... | collective-permute-start | bytes 110600 | tf_op jit(solution)/shard_map/ppermute | solution.py:125
  21.0 0.0 copy-done.9
  21.0 0.0 collective-permute-done.5.up_right.diff_up_right
  21.0 0.0 collective-permute-done.6.down_left.diff_down_left
  21.0 1.6 %collective-permute-done.7.down_right.diff_down_right = f32[72,128]{1,0:T(8,128)S(1)} collective-permute-done((f32[72,128]{1,0:T(8,128)S(1)}, f32[72,128]{1,0:T(8,128)S(1)}, u32[]{:S(2)}, u32[]{:S(2)}) %collective-permute-start.7) | collective-permute-done | bytes 36896 | tf_op jit(solution)/shard_map/ppermute | solution.py:125
  22.6 0.0 collective-permute-done.up.diff_up
  22.6 0.0 collective-permute-done.1.down.diff_down
  22.6 0.0 copy-done.1
  22.6 0.6 copy-done.6
  23.3 14.0 %forward.1 = bf16[4096,128]{1,0:T(8,128)(2,1)} custom-call(s32[32]{0:T(128)S(1)} %bitcast.52, s32[4224]{0:T(1024)S(1)} %pad.8.order, f32[2048,128]{1,0:T(8,128)S(1)} %bitcast.40, f32[2048,128]{1,0:T(8,128)S(1)} %bitcast.44, f32[32,128]{1,0:T(8,128)S(1)} %bitcast.48, f32[72,128]{1,0:T(8,128)S(1)} %get-tuple-element.22.own_low.diff_own_low, ...), custom_call_target="tpu_custom_call" | custom-call | tf_op jit(solution)/shard_map/forward/pallas_call | solution.py:256
  37.3 3.7 %all-to-all-start = ((bf16[8,512,128]{2,1,0:T(8,128)(2,1)}), bf16[8,512,128]{2,1,0:T(8,128)(2,1)S(1)}, u32[]{:S(2)}, u32[]{:S(2)}) async-start(bf16[8,512,128]{2,1,0:T(8,128)(2,1)} %bitcast.15), calls=%async_computation | async-start | bytes 2097152 | tf_op jit(solution)/shard_map/all_to_all | solution.py:702
  41.0 0.0 copy-done.8
  41.0 0.0 copy-start.2
  41.0 0.1 copy.16
  41.1 0.1 concatenate.14.last
  41.2 0.0 copy-done.10
  41.2 0.1 pad_bitcast_fusion.bias_last
  41.3 0.0 copy-done.7
  41.3 15.0 %all-to-all-done = bf16[8,512,128]{2,1,0:T(8,128)(2,1)S(1)} async-done(((bf16[8,512,128]{2,1,0:T(8,128)(2,1)}), bf16[8,512,128]{2,1,0:T(8,128)(2,1)S(1)}, u32[]{:S(2)}, u32[]{:S(2)}) %all-to-all-start) | async-done | bytes 1048608 | tf_op jit(solution)/shard_map/all_to_all | solution.py:702
  56.3 0.0 copy-done.2
  56.3 0.7 copy-done.5
  57.0 19.6 %network.1 = (bf16[2048,128]{1,0:T(8,128)(2,1)}, bf16[1088,128]{1,0:T(8,128)(2,1)S(1)}) custom-call(bf16[4096,128]{1,0:T(8,128)(2,1)S(1)} %bitcast.41, bf16[128,192]{1,0:T(8,128)(2,1)S(1)} %get-tuple-element.45.first_in, bf16[128,192]{1,0:T(8,128)(2,1)S(1)} %get-tuple-element.44.first_out, bf16[3,192,192]{2,1,0:T(8,128)(2,1)S(1)} %bitcast.45, ...), custom_call_target="tpu_custom_call" | custom-call | tf_op jit(solution)/shard_map/network/pallas_call | solution.py:385
  76.6 12.6 %all_to_all.20.parts = bf16[4,272,128]{2,1,0:T(8,128)(2,1)S(1)} all-to-all(bf16[4,272,128]{2,1,0:T(8,128)(2,1)S(1)} %bitcast.46), channel_id=1, replica_groups=mesh['tile'=4,'sub'=8] {'tile'}, dimensions={0} | all-to-all | bytes 557056 | tf_op jit(solution)/shard_map/all_to_all | solution.py:712
  89.2 3.5 %all-to-all-start.1 = ((bf16[8,256,128]{2,1,0:T(8,128)(2,1)}), bf16[8,256,128]{2,1,0:T(8,128)(2,1)S(1)}, u32[]{:S(2)}, u32[]{:S(2)}) async-start(bf16[8,256,128]{2,1,0:T(8,128)(2,1)} %bitcast.23), calls=%async_computation.1 | async-start | bytes 1048576 | tf_op jit(solution)/shard_map/all_to_all | solution.py:708
  92.7 0.7 sum_parts.1
  93.5 9.0 %all-to-all-done.1 = bf16[8,256,128]{2,1,0:T(8,128)(2,1)S(1)} async-done(((bf16[8,256,128]{2,1,0:T(8,128)(2,1)}), bf16[8,256,128]{2,1,0:T(8,128)(2,1)S(1)}, u32[]{:S(2)}, u32[]{:S(2)}) %all-to-all-start.1) | async-done | bytes 524320 | tf_op jit(solution)/shard_map/all_to_all | solution.py:708
  102.4 3.4 %all-to-all-start.3 = ((bf16[4,272,128]{2,1,0:T(8,128)(2,1)}), bf16[4,272,128]{2,1,0:T(8,128)(2,1)S(1)}, u32[]{:S(2)}, u32[]{:S(2)}) async-start(bf16[4,272,128]{2,1,0:T(8,128)(2,1)} %sum_parts.1), calls=%async_computation.3 | async-start | bytes 557056 | tf_op jit(solution)/shard_map/all_to_all | solution.py:715
  105.9 0.0 copy-start.4
  105.9 8.7 %scatter.1 = (f32[64,4096]{1,0:T(8,128)S(1)}, bf16[64,512]{1,0:T(8,128)(2,1)S(1)}, bf16[64,512]{1,0:T(8,128)(2,1)S(1)}, bf16[64,128]{1,0:T(8,128)(2,1)S(1)}, bf16[64,128]{1,0:T(8,128)(2,1)S(1)}) custom-call(s32[32]{0:T(128)S(1)} %bitcast.53, s32[4224]{0:T(1024)S(1)} %pad.8.order, bf16[2048,128]{1,0:T(8,128)(2,1)S(1)} %bitcast.42), custom_call_target="tpu_custom_call" | custom-call | tf_op jit(solution)/shard_map/scatter/pallas_call | solution.py:553
  114.6 2.1 %collective-permute-start.8 = (bf16[64,512]{1,0:T(8,128)(2,1)S(1)}, bf16[64,512]{1,0:T(8,128)(2,1)S(1)}, u32[]{:S(2)}, u32[]{:S(2)}) collective-permute-start(bf16[64,512]{1,0:T(8,128)(2,1)S(1)} %get-tuple-element.30), channel_id=1, source_target_pairs={{0,8},{8,16},{16,24},{24,0},{1,9},{9,17},{17,25},{25,1},{2,10},{10... | collective-permute-start | bytes 196616 | tf_op jit(solution)/shard_map/ppermute | solution.py:119
  116.7 1.9 %collective-permute-start.9 = (bf16[64,512]{1,0:T(8,128)(2,1)S(1)}, bf16[64,512]{1,0:T(8,128)(2,1)S(1)}, u32[]{:S(2)}, u32[]{:S(2)}) collective-permute-start(bf16[64,512]{1,0:T(8,128)(2,1)S(1)} %get-tuple-element.31), channel_id=1, source_target_pairs={{0,24},{8,0},{16,8},{24,16},{1,25},{9,1},{17,9},{25,17},{2,26},{10... | collective-permute-start | bytes 196616 | tf_op jit(solution)/shard_map/ppermute | solution.py:119
  118.5 0.0 collective-permute-start.10
  118.5 2.6 %collective-permute-start.11 = (bf16[64,128]{1,0:T(8,128)(2,1)S(1)}, bf16[64,128]{1,0:T(8,128)(2,1)S(1)}, u32[]{:S(2)}, u32[]{:S(2)}) collective-permute-start(bf16[64,128]{1,0:T(8,128)(2,1)S(1)} %get-tuple-element.28.own_low), channel_id=1, source_target_pairs={{0,7},{1,0},{2,1},{3,2},{4,3},{5,4},{6,5},{7,6},{8,15},{9,8},{10,9... | collective-permute-start | bytes 49160 | tf_op jit(solution)/shard_map/ppermute | solution.py:117
  121.2 0.0 collective-permute-start.12
  121.2 1.5 %collective-permute-done.10.left = bf16[64,128]{1,0:T(8,128)(2,1)S(1)} collective-permute-done((bf16[64,128]{1,0:T(8,128)(2,1)S(1)}, bf16[64,128]{1,0:T(8,128)(2,1)S(1)}, u32[]{:S(2)}, u32[]{:S(2)}) %collective-permute-start.10) | collective-permute-done | bytes 16416 | tf_op jit(solution)/shard_map/ppermute | solution.py:117
  122.7 1.6 %collective-permute-start.13 = (bf16[64,128]{1,0:T(8,128)(2,1)S(1)}, bf16[64,128]{1,0:T(8,128)(2,1)S(1)}, u32[]{:S(2)}, u32[]{:S(2)}) collective-permute-start(bf16[64,128]{1,0:T(8,128)(2,1)S(1)} %get-tuple-element.28.own_low), channel_id=1, source_target_pairs={{0,15},{1,8},{2,9},{3,10},{4,11},{5,12},{6,13},{7,14},{8,23},{9,16... | collective-permute-start | bytes 49160 | tf_op jit(solution)/shard_map/ppermute | solution.py:125
  124.3 0.0 collective-permute-done.11.right
  124.3 2.0 %collective-permute-start.14 = (bf16[64,128]{1,0:T(8,128)(2,1)S(1)}, bf16[64,128]{1,0:T(8,128)(2,1)S(1)}, u32[]{:S(2)}, u32[]{:S(2)}) collective-permute-start(bf16[64,128]{1,0:T(8,128)(2,1)S(1)} %get-tuple-element.29.own_high), channel_id=1, source_target_pairs={{0,25},{1,26},{2,27},{3,28},{4,29},{5,30},{6,31},{7,24},{8,1},{9,2... | collective-permute-start | bytes 49160 | tf_op jit(solution)/shard_map/ppermute | solution.py:125
  126.3 1.7 %collective-permute-done.12.up_left = bf16[64,128]{1,0:T(8,128)(2,1)S(1)} collective-permute-done((bf16[64,128]{1,0:T(8,128)(2,1)S(1)}, bf16[64,128]{1,0:T(8,128)(2,1)S(1)}, u32[]{:S(2)}, u32[]{:S(2)}) %collective-permute-start.12) | collective-permute-done | bytes 16416 | tf_op jit(solution)/shard_map/ppermute | solution.py:125
  127.9 2.1 %collective-permute-start.15 = (bf16[64,128]{1,0:T(8,128)(2,1)S(1)}, bf16[64,128]{1,0:T(8,128)(2,1)S(1)}, u32[]{:S(2)}, u32[]{:S(2)}) collective-permute-start(bf16[64,128]{1,0:T(8,128)(2,1)S(1)} %get-tuple-element.28.own_low), channel_id=1, source_target_pairs={{0,31},{1,24},{2,25},{3,26},{4,27},{5,28},{6,29},{7,30},{8,7},{9,0... | collective-permute-start | bytes 49160 | tf_op jit(solution)/shard_map/ppermute | solution.py:125
  130.1 0.0 collective-permute-done.13.up_right
  130.1 0.0 collective-permute-done.14.down_left
  130.1 1.4 %collective-permute-done.15.down_right = bf16[64,128]{1,0:T(8,128)(2,1)S(1)} collective-permute-done((bf16[64,128]{1,0:T(8,128)(2,1)S(1)}, bf16[64,128]{1,0:T(8,128)(2,1)S(1)}, u32[]{:S(2)}, u32[]{:S(2)}) %collective-permute-start.15) | collective-permute-done | bytes 16416 | tf_op jit(solution)/shard_map/ppermute | solution.py:125
  131.5 0.0 collective-permute-done.8.up
  131.5 0.0 collective-permute-done.9.down
  131.5 0.0 copy-done.4
  131.5 5.5 %adjoint.1 = f32[2048,128]{1,0:T(8,128)} custom-call(f32[64,4096]{1,0:T(8,128)S(1)} %get-tuple-element.27.grid, f32[32,128]{1,0:T(8,128)S(1)} %bitcast.49, bf16[64,128]{1,0:T(8,128)(2,1)S(1)} %get-tuple-element.28.own_low, bf16[64,128]{1,0:T(8,128)(2,1)S(1)} %get-tuple-element.29.own_high, f32[72,128]{1,0:T(8,128)S(1)} %get-tuple-element.22.own_low.diff_own_low, ...), custom_call_target="tpu_custom_call" | custom-call | tf_op jit(solution)/shard_map/adjoint/pallas_call | solution.py:675
  137.0 0.0 all-to-all-done.3
  137.0 1.2 make_steps.1
  138.3 0.7 copy.17
  (10 shorter events, 0.0 us)
Async XLA Ops:
  0.6 1.2 copy-start
  1.9 0.7 copy-start.3
  2.6 18.4 %copy-start.9 = (s32[1,4096]{1,0:T(1,128)S(1)}, s32[1,4096]{1,0:T(1,128)}, u32[]{:S(2)}) copy-start(s32[1,4096]{1,0:T(1,128)} %param.13) | copy-start | bytes 49156
  2.6 20.0 %copy-start.1 = (f32[64,16,256]{2,1,0:T(8,128)S(1)}, f32[64,16,256]{2,1,0:T(8,128)}, u32[]{:S(2)}) copy-start(f32[64,16,256]{2,1,0:T(8,128)} %param.11) | copy-start | bytes 3145732
  4.2 18.4 %collective-permute-start = (f32[72,512]{1,0:T(8,128)S(1)}, f32[72,512]{1,0:T(8,128)S(1)}, u32[]{:S(2)}, u32[]{:S(2)}) collective-permute-start(f32[72,512]{1,0:T(8,128)S(1)} %get-tuple-element.24), channel_id=1, source_target_pairs={{0,8},{8,16},{16,24},{24,0},{1,9},{9,17},{17,25},{25,1},{2,10},{10... | collective-permute-start | bytes 442376 | tf_op jit(solution)/shard_map/ppermute | solution.py:119
  7.3 15.3 %collective-permute-start.1 = (f32[72,512]{1,0:T(8,128)S(1)}, f32[72,512]{1,0:T(8,128)S(1)}, u32[]{:S(2)}, u32[]{:S(2)}) collective-permute-start(f32[72,512]{1,0:T(8,128)S(1)} %get-tuple-element.25), channel_id=1, source_target_pairs={{0,24},{8,0},{16,8},{24,16},{1,25},{9,1},{17,9},{25,17},{2,26},{10... | collective-permute-start | bytes 442376 | tf_op jit(solution)/shard_map/ppermute | solution.py:119
  9.4 4.3 %collective-permute-start.2 = (f32[72,128]{1,0:T(8,128)S(1)}, f32[72,128]{1,0:T(8,128)S(1)}, u32[]{:S(2)}, u32[]{:S(2)}) collective-permute-start(f32[72,128]{1,0:T(8,128)S(1)} %get-tuple-element.23.own_high.diff_own_high), channel_id=1, source_target_pairs={{0,1},{1,2},{2,3},{3,4},{4,5},{5,6},{6,7},{7,0},{8,9},{9,10},{10,1... | collective-permute-start | bytes 110600 | tf_op jit(solution)/shard_map/ppermute | solution.py:117
  9.4 5.7 %collective-permute-start.3 = (f32[72,128]{1,0:T(8,128)S(1)}, f32[72,128]{1,0:T(8,128)S(1)}, u32[]{:S(2)}, u32[]{:S(2)}) collective-permute-start(f32[72,128]{1,0:T(8,128)S(1)} %get-tuple-element.22.own_low.diff_own_low), channel_id=1, source_target_pairs={{0,7},{1,0},{2,1},{3,2},{4,3},{5,4},{6,5},{7,6},{8,15},{9,8},{10,9... | collective-permute-start | bytes 110600 | tf_op jit(solution)/shard_map/ppermute | solution.py:117
  12.1 7.0 %collective-permute-start.4 = (f32[72,128]{1,0:T(8,128)S(1)}, f32[72,128]{1,0:T(8,128)S(1)}, u32[]{:S(2)}, u32[]{:S(2)}) collective-permute-start(f32[72,128]{1,0:T(8,128)S(1)} %get-tuple-element.23.own_high.diff_own_high), channel_id=1, source_target_pairs={{0,9},{1,10},{2,11},{3,12},{4,13},{5,14},{6,15},{7,8},{8,17},{9,18... | collective-permute-start | bytes 110600 | tf_op jit(solution)/shard_map/ppermute | solution.py:125
  13.7 7.3 %collective-permute-start.5 = (f32[72,128]{1,0:T(8,128)S(1)}, f32[72,128]{1,0:T(8,128)S(1)}, u32[]{:S(2)}, u32[]{:S(2)}) collective-permute-start(f32[72,128]{1,0:T(8,128)S(1)} %get-tuple-element.22.own_low.diff_own_low), channel_id=1, source_target_pairs={{0,15},{1,8},{2,9},{3,10},{4,11},{5,12},{6,13},{7,14},{8,23},{9,16... | collective-permute-start | bytes 110600 | tf_op jit(solution)/shard_map/ppermute | solution.py:125
  15.1 5.9 %collective-permute-start.6 = (f32[72,128]{1,0:T(8,128)S(1)}, f32[72,128]{1,0:T(8,128)S(1)}, u32[]{:S(2)}, u32[]{:S(2)}) collective-permute-start(f32[72,128]{1,0:T(8,128)S(1)} %get-tuple-element.23.own_high.diff_own_high), channel_id=1, source_target_pairs={{0,25},{1,26},{2,27},{3,28},{4,29},{5,30},{6,31},{7,24},{8,1},{9,2... | collective-permute-start | bytes 110600 | tf_op jit(solution)/shard_map/ppermute | solution.py:125
  19.1 3.5 %collective-permute-start.7 = (f32[72,128]{1,0:T(8,128)S(1)}, f32[72,128]{1,0:T(8,128)S(1)}, u32[]{:S(2)}, u32[]{:S(2)}) collective-permute-start(f32[72,128]{1,0:T(8,128)S(1)} %get-tuple-element.22.own_low.diff_own_low), channel_id=1, source_target_pairs={{0,31},{1,24},{2,25},{3,26},{4,27},{5,28},{6,29},{7,30},{8,7},{9,0... | collective-permute-start | bytes 110600 | tf_op jit(solution)/shard_map/ppermute | solution.py:125
  22.6 0.7 copy-start.6
  37.2 3.7 %copy-start.8 = (bf16[1,192,64]{1,2,0:T(8,128)(2,1)S(1)}, bf16[1,192,64]{1,2,0:T(8,128)(2,1)}, u32[]{:S(2)}) copy-start(bf16[1,192,64]{1,2,0:T(8,128)(2,1)} %param.17) | copy-start | bytes 73732
  37.2 3.9 %copy-start.10 = (f32[1,64]{1,0:T(1,128)S(1)}, f32[1,64]{1,0:T(1,128)}, u32[]{:S(2)}) copy-start(f32[1,64]{1,0:T(1,128)} %param.19) | copy-start | bytes 772
  37.3 4.0 %copy-start.7 = (bf16[1,64,192]{2,1,0:T(8,128)(2,1)S(1)}, bf16[1,64,192]{2,1,0:T(8,128)(2,1)}, u32[]{:S(2)}) copy-start(bf16[1,64,192]{2,1,0:T(8,128)(2,1)} %param.15) | copy-start | bytes 73732
  37.3 19.1 %all-to-all-start = ((bf16[8,512,128]{2,1,0:T(8,128)(2,1)}), bf16[8,512,128]{2,1,0:T(8,128)(2,1)S(1)}, u32[]{:S(2)}, u32[]{:S(2)}) async-start(bf16[8,512,128]{2,1,0:T(8,128)(2,1)} %bitcast.15), calls=%async_computation | async-start | bytes 2097152 | tf_op jit(solution)/shard_map/all_to_all | solution.py:702
  41.0 15.4 %copy-start.2 = (bf16[1,3,192,192]{3,2,1,0:T(8,128)(2,1)S(1)}, bf16[1,3,192,192]{3,2,1,0:T(8,128)(2,1)}, u32[]{:S(2)}) copy-start(bf16[1,3,192,192]{3,2,1,0:T(8,128)(2,1)} %param.16) | copy-start | bytes 663556
  56.3 0.7 copy-start.5
  89.2 13.2 %all-to-all-start.1 = ((bf16[8,256,128]{2,1,0:T(8,128)(2,1)}), bf16[8,256,128]{2,1,0:T(8,128)(2,1)S(1)}, u32[]{:S(2)}, u32[]{:S(2)}) async-start(bf16[8,256,128]{2,1,0:T(8,128)(2,1)} %bitcast.23), calls=%async_computation.1 | async-start | bytes 1048576 | tf_op jit(solution)/shard_map/all_to_all | solution.py:708
  102.4 34.6 %all-to-all-start.3 = ((bf16[4,272,128]{2,1,0:T(8,128)(2,1)}), bf16[4,272,128]{2,1,0:T(8,128)(2,1)S(1)}, u32[]{:S(2)}, u32[]{:S(2)}) async-start(bf16[4,272,128]{2,1,0:T(8,128)(2,1)} %sum_parts.1), calls=%async_computation.3 | async-start | bytes 557056 | tf_op jit(solution)/shard_map/all_to_all | solution.py:715
  105.9 25.6 %copy-start.4 = (f32[16,256]{1,0:T(8,128)S(1)}, f32[16,256]{1,0:T(8,128)}, u32[]{:S(2)}) copy-start(f32[16,256]{1,0:T(8,128)} %param.12) | copy-start | bytes 49156
  114.6 16.9 %collective-permute-start.8 = (bf16[64,512]{1,0:T(8,128)(2,1)S(1)}, bf16[64,512]{1,0:T(8,128)(2,1)S(1)}, u32[]{:S(2)}, u32[]{:S(2)}) collective-permute-start(bf16[64,512]{1,0:T(8,128)(2,1)S(1)} %get-tuple-element.30), channel_id=1, source_target_pairs={{0,8},{8,16},{16,24},{24,0},{1,9},{9,17},{17,25},{25,1},{2,10},{10... | collective-permute-start | bytes 196616 | tf_op jit(solution)/shard_map/ppermute | solution.py:119
  116.7 14.9 %collective-permute-start.9 = (bf16[64,512]{1,0:T(8,128)(2,1)S(1)}, bf16[64,512]{1,0:T(8,128)(2,1)S(1)}, u32[]{:S(2)}, u32[]{:S(2)}) collective-permute-start(bf16[64,512]{1,0:T(8,128)(2,1)S(1)} %get-tuple-element.31), channel_id=1, source_target_pairs={{0,24},{8,0},{16,8},{24,16},{1,25},{9,1},{17,9},{25,17},{2,26},{10... | collective-permute-start | bytes 196616 | tf_op jit(solution)/shard_map/ppermute | solution.py:119
  118.5 4.2 %collective-permute-start.10 = (bf16[64,128]{1,0:T(8,128)(2,1)S(1)}, bf16[64,128]{1,0:T(8,128)(2,1)S(1)}, u32[]{:S(2)}, u32[]{:S(2)}) collective-permute-start(bf16[64,128]{1,0:T(8,128)(2,1)S(1)} %get-tuple-element.29.own_high), channel_id=1, source_target_pairs={{0,1},{1,2},{2,3},{3,4},{4,5},{5,6},{6,7},{7,0},{8,9},{9,10},{10,1... | collective-permute-start | bytes 49160 | tf_op jit(solution)/shard_map/ppermute | solution.py:117
  118.5 5.8 %collective-permute-start.11 = (bf16[64,128]{1,0:T(8,128)(2,1)S(1)}, bf16[64,128]{1,0:T(8,128)(2,1)S(1)}, u32[]{:S(2)}, u32[]{:S(2)}) collective-permute-start(bf16[64,128]{1,0:T(8,128)(2,1)S(1)} %get-tuple-element.28.own_low), channel_id=1, source_target_pairs={{0,7},{1,0},{2,1},{3,2},{4,3},{5,4},{6,5},{7,6},{8,15},{9,8},{10,9... | collective-permute-start | bytes 49160 | tf_op jit(solution)/shard_map/ppermute | solution.py:117
  121.2 6.8 %collective-permute-start.12 = (bf16[64,128]{1,0:T(8,128)(2,1)S(1)}, bf16[64,128]{1,0:T(8,128)(2,1)S(1)}, u32[]{:S(2)}, u32[]{:S(2)}) collective-permute-start(bf16[64,128]{1,0:T(8,128)(2,1)S(1)} %get-tuple-element.29.own_high), channel_id=1, source_target_pairs={{0,9},{1,10},{2,11},{3,12},{4,13},{5,14},{6,15},{7,8},{8,17},{9,18... | collective-permute-start | bytes 49160 | tf_op jit(solution)/shard_map/ppermute | solution.py:125
  122.7 7.4 %collective-permute-start.13 = (bf16[64,128]{1,0:T(8,128)(2,1)S(1)}, bf16[64,128]{1,0:T(8,128)(2,1)S(1)}, u32[]{:S(2)}, u32[]{:S(2)}) collective-permute-start(bf16[64,128]{1,0:T(8,128)(2,1)S(1)} %get-tuple-element.28.own_low), channel_id=1, source_target_pairs={{0,15},{1,8},{2,9},{3,10},{4,11},{5,12},{6,13},{7,14},{8,23},{9,16... | collective-permute-start | bytes 49160 | tf_op jit(solution)/shard_map/ppermute | solution.py:125
  124.3 5.8 %collective-permute-start.14 = (bf16[64,128]{1,0:T(8,128)(2,1)S(1)}, bf16[64,128]{1,0:T(8,128)(2,1)S(1)}, u32[]{:S(2)}, u32[]{:S(2)}) collective-permute-start(bf16[64,128]{1,0:T(8,128)(2,1)S(1)} %get-tuple-element.29.own_high), channel_id=1, source_target_pairs={{0,25},{1,26},{2,27},{3,28},{4,29},{5,30},{6,31},{7,24},{8,1},{9,2... | collective-permute-start | bytes 49160 | tf_op jit(solution)/shard_map/ppermute | solution.py:125
  127.9 3.6 %collective-permute-start.15 = (bf16[64,128]{1,0:T(8,128)(2,1)S(1)}, bf16[64,128]{1,0:T(8,128)(2,1)S(1)}, u32[]{:S(2)}, u32[]{:S(2)}) collective-permute-start(bf16[64,128]{1,0:T(8,128)(2,1)S(1)} %get-tuple-element.28.own_low), channel_id=1, source_target_pairs={{0,31},{1,24},{2,25},{3,26},{4,27},{5,28},{6,29},{7,30},{8,7},{9,0... | collective-permute-start | bytes 49160 | tf_op jit(solution)/shard_map/ppermute | solution.py:125
where the time goes:
time: 140 us; the launch traced here: 139 us
  Pallas kernels  51.3 us (37%)
  starting transfers between devices  36.2 us (26%)
  waiting for transfers between devices  33.7 us (24%)
  blocking collectives  12.6 us (9%)
  local copies, waits for them, and re-layouts  4.3 us (3%)
    pallas_call x1, Pallas kernels, network(): pl.pallas_call(functools.partial(network_body, levels, width, block), gri...  19.6 us
    all_to_all x1, waiting for transfers between devices, per_device(): lax.all_to_all(blocks.reshape(subs, cells // subs, 2 * levels), 'sub', sp...  15 us
    pallas_call x1, Pallas kernels, forward(): pl.pallas_call(functools.partial(forward_body, levels, width_x, width_y,...  14 us
    all_to_all x1, blocking collectives, per_device(): lax.all_to_all(gradients.reshape(tiles, -1, LANES), 'tile', split_axis=0,...  12.6 us
    ppermute x8, starting transfers between devices, shifted(): return lax.ppermute(array, ('tile', 'sub'), pairs)  11.1 us
    ppermute x4, starting transfers between devices, shifted(): lax.ppermute(array, 'tile', [(i, (i + shift_tile) % tiles) for i in range...  9.12 us
    all_to_all x1, waiting for transfers between devices, per_device(): lax.all_to_all(returning.reshape(subs, cells // subs // 2, 2 * levels), '...  8.97 us
    pallas_call x1, Pallas kernels, scatter(): pl.pallas_call(functools.partial(scatter_body, levels, width_x, width_y,...  8.69 us
  transfers between devices with their start and end apart: 19, of which 8 were waited for; matrix products, arithmetic and copies ran while one was open for 0% of the time, Pallas kernels for 11%

commit v1 on v0

--- a/solution.py
+++ b/solution.py
@@ -12,7 +12,7 @@
 UNROLL = 16
 VMEM = pl.BlockSpec(memory_space=pltpu.VMEM)
 SMEM = pl.BlockSpec(memory_space=pltpu.SMEM)
-PARAMS = pltpu.CompilerParams(vmem_limit_bytes=50 * 1024 * 1024)
+PARAMS = pltpu.CompilerParams(vmem_limit_bytes=32 * 1024 * 1024)
 F32 = jnp.float32
 BF16 = jnp.bfloat16
 
@@ -160,21 +160,12 @@
     )
 
 
-def fill_starts(counts, starts, devices):
-    def step(index, total):
-        starts[index] = total
-        return total + counts[index]
-
-    lax.fori_loop(0, devices, step, jnp.int32(0))
-
-
 def forward_body(
-    levels, width_x, width_y, tiles, subs,
-    counts, order, field, target, diff, own_low, own_high, up, down, left, right,
-    up_left, up_right, down_left, down_right, out, e0, e1, wide, both, rows, picked, starts,
+    levels, width_x, width_y,
+    field, target, diff, own_low, own_high, up, down, left, right,
+    up_left, up_right, down_left, down_right, rows, e0, e1, wide, both,
 ):
     cells = width_x * width_y
-    devices = tiles * subs
 
     def at(x):
         return slice((x + 2) * width_y, (x + 3) * width_y)
@@ -222,7 +213,6 @@
         return carry
 
     lax.fori_loop(0, levels // SUBLANES, step, 0)
-    fill_starts(counts, starts, devices)
 
     def turn(tile, carry):
         span = pl.ds(pl.multiple_of(tile * LANES, LANES), LANES)
@@ -231,202 +221,380 @@
 
     lax.fori_loop(0, cells // LANES, turn, 0, unroll=2)
 
-    def run(index, base):
-        device = index % tiles * subs + index // tiles
-        count = counts[device]
-        start = starts[device]
-
-        def copy(chunk, carry):
-            offset = chunk * UNROLL
-            taken = [rows[pl.ds(order[start + offset + u], 1), :] for u in range(UNROLL)]
-            for u in range(UNROLL):
-                picked[pl.ds(base + offset + u, 1), :] = taken[u]
-            return carry
-
-        lax.fori_loop(0, (count + UNROLL - 1) // UNROLL, copy, 0)
-        return base + count
-
-    lax.fori_loop(0, devices, run, jnp.int32(0))
-    out[...] = picked[:cells, :].astype(BF16)
-
-
-def forward(counts, order, field_rows, target_rows, diff_rows, own_low, own_high, halos, sizes):
-    levels, width_x, width_y, tiles, subs = sizes
+
+def forward(field_rows, target_rows, diff_rows, own_low, own_high, halos, sizes):
+    levels, width_x, width_y, _, _ = sizes
     cells = width_x * width_y
     return pl.pallas_call(
-        functools.partial(forward_body, levels, width_x, width_y, tiles, subs),
-        out_shape=jax.ShapeDtypeStruct((cells, 2 * levels), BF16),
-        in_specs=[SMEM] * 2 + [VMEM] * 13,
+        functools.partial(forward_body, levels, width_x, width_y),
+        out_shape=jax.ShapeDtypeStruct((cells, 2 * levels), F32),
+        in_specs=[VMEM] * 13,
         out_specs=VMEM,
         scratch_shapes=[
             pltpu.VMEM((SUBLANES, (width_x + 4) * width_y), F32),
             pltpu.VMEM((SUBLANES, (width_x + 4) * width_y), F32),
             pltpu.VMEM((SUBLANES, (width_x + 4) * width_y), F32),
             pltpu.VMEM((2 * levels, cells), F32),
-            pltpu.VMEM((cells + SUBLANES, 2 * levels), F32),
-            pltpu.VMEM((cells + UNROLL, 2 * levels), F32),
-            pltpu.SMEM((tiles * subs,), jnp.int32),
         ],
         compiler_params=PARAMS,
         name="forward",
-    )(counts, order, field_rows, target_rows, diff_rows, own_low, own_high, *halos)
-
-
-def squeeze_lanes(wide_part, half):
-    count = wide_part.shape[0] // 2
-    lane = lax.broadcasted_iota(jnp.int32, (count, LANES), 1)
-    low = wide_part[:count]
-    high = wide_part[count:]
-    if half == 0:
-        high = pltpu.roll(high, LANES // 2, 1)
-    else:
-        low = pltpu.roll(low, LANES // 2, 1)
-    return jnp.where(lane < LANES // 2, low, high)
+    )(field_rows, target_rows, diff_rows, own_low, own_high, *halos)
+
+
+def index_body(tiles, subs, lead, rows_each, parity, counts, order, out, starts):
+    devices = tiles * subs
+
+    def begin(index, total):
+        starts[index] = total
+        return total + counts[index]
+
+    lax.fori_loop(0, devices, begin, jnp.int32(0))
+    half = subs // 2
+    flip = parity[0]
+    lane = lax.broadcasted_iota(jnp.int32, (SUBLANES, LANES), 1)
+    slot = lax.broadcasted_iota(jnp.int32, (SUBLANES, LANES), 0) * LANES + lane
+
+    def expert(block, carry):
+        second_half = block // half
+        network_id = (block - second_half * half) * 2 + (1 - flip) * (1 - second_half) + flip * second_half
+        value = jnp.zeros((SUBLANES, LANES), jnp.int32)
+        base = jnp.int32(0)
+        for t in range(tiles):
+            device = t * subs + network_id
+            count = counts[device]
+            offset = starts[device] - base + lead
+            shift = lax.rem(offset, LANES)
+            window = order[pl.ds(lax.div(offset, LANES), SUBLANES), :]
+            turned = pltpu.roll(window, lax.rem(LANES - shift, LANES), 1)
+            following = jnp.concatenate([turned[1:], turned[:1]], axis=0)
+            moved = jnp.where(lane < LANES - shift, turned, following)
+            value = jnp.where((slot >= base) & (slot < base + count), moved, value)
+            base = base + count
+        out[pl.ds(block * rows_each, SUBLANES), :] = value
+        return carry
+
+    lax.fori_loop(0, subs, expert, 0)
+
+
+def slot_cells(parity, counts, column_order, sizes):
+    _, width_x, width_y, tiles, subs = sizes
+    cells = width_x * width_y
+    packet = cells // subs
+    rows_each = packet // LANES
+    lead = packet
+    order = jnp.pad(column_order, (lead, SUBLANES * LANES)).reshape(-1, LANES)
+    return pl.pallas_call(
+        functools.partial(index_body, tiles, subs, lead, rows_each),
+        out_shape=jax.ShapeDtypeStruct((cells // LANES + SUBLANES, LANES), jnp.int32),
+        in_specs=[SMEM] * 2 + [VMEM],
+        out_specs=VMEM,
+        scratch_shapes=[pltpu.SMEM((tiles * subs,), jnp.int32)],
+        compiler_params=PARAMS,
+        name="slot_cells",
+    )(parity, counts, order).reshape(-1)
+
+
+def widen(value):
+    missing = LANES - value.shape[1]
+    return jnp.concatenate([value, jnp.zeros((value.shape[0], missing), value.dtype)], axis=1)
+
+
+def lower_half(rows):
+    return lax.broadcasted_iota(jnp.int32, (rows, LANES), 1) < LANES // 2
+
+
+def swap_halves(value):
+    return pltpu.roll(value, LANES // 2, 1)
+
+
+def squeeze_rows(value):
+    count = value.shape[0] // 2
+    return jnp.where(lower_half(count), value[:count], swap_halves(value[count:]))
+
+
+def pack_rows(put, inner, first, last, biases):
+    width = first.shape[1]
+    for k in range(3):
+        put(inner[k][:, :LANES])
+    low = lower_half(width)
+    put(jnp.where(low, widen(inner[0][:, LANES:]), swap_halves(widen(inner[1][:, LANES:]))))
+    put(jnp.where(low, widen(inner[2][:, LANES:]), last))
+    put(first[:, :LANES])
+    put(squeeze_rows(widen(first[:, LANES:])))
+    tail = []
+    for bias, bias_last in biases:
+        tail += [piece[:, :LANES] for piece in bias]
+        tail += [
+            jnp.where(
+                lower_half(1), widen(bias[k][:, LANES:]), swap_halves(widen(bias[k + 1][:, LANES:]))
+            )
+            for k in (0, 2)
+        ]
+        tail.append(bias_last)
+    return tail
+
+
+def pack_size(levels, width, tiles):
+    rows = 5 * width + levels + levels // 2 + 16
+    unit = 16 * tiles
+    return (rows + unit - 1) // unit * unit
+
+
+def weights_body(w_first, w_inner, w_last, b_inner, b_last, out):
+    row = 0
+
+    def put(value):
+        nonlocal row
+        value = value.astype(BF16)
+        for copy in range(out.shape[0]):
+            out[copy, row : row + value.shape[0], :] = value
+        row += value.shape[0]
+
+    bias = b_inner[...]
+    bias_last = swap_halves(widen(b_last[...]))
+    bias_high = bias.astype(BF16).astype(F32)
+    last_high = bias_last.astype(BF16).astype(F32)
+    bias_low = bias - bias_high
+    last_low = bias_last - last_high
+    tail = pack_rows(
+        put,
+        [w_inner[k].astype(F32) for k in range(3)],
+        w_first[...].astype(F32),
+        swap_halves(widen(w_last[...].astype(F32))),
+        [
+            ([bias_high[k : k + 1] for k in range(4)], last_high),
+            ([bias_low[k : k + 1] for k in range(4)], last_low),
+        ],
+    )
+    tail.append(jnp.zeros((out.shape[1] - row - len(tail), LANES), F32))
+    put(jnp.concatenate(tail, axis=0))
+
+
+def pack_weights(w_first, w_inner, w_last, b_inner, b_last, tiles, copies):
+    levels, width = w_first.shape
+    return pl.pallas_call(
+        weights_body,
+        out_shape=jax.ShapeDtypeStruct((copies, pack_size(levels, width, tiles), LANES), BF16),
+        in_specs=[VMEM] * 5,
+        out_specs=VMEM,
+        compiler_params=PARAMS,
+        name="pack_weights",
+    )(w_first, w_inner, w_last, b_inner, b_last)
 
 
 def network_body(
-    levels, width, packet, inputs, first_in, first_out, inner, last, bias, bias_last,
-    out, grads, acc_first, acc_inner, acc_last, acc_bias, acc_bias_last,
+    levels, width, packet, shift_block,
+    cells_of, packs, rows, back_in, back, grads,
+    taken, given_back, first_in, first_out, inner, last, last_half, bias, bias_last,
 ):
     block = pl.program_id(0)
-    cells = inputs.shape[0]
-    lane = lax.broadcasted_iota(jnp.int32, (cells, LANES), 1)
+    blocks = pl.num_programs(0)
+    narrow = width - LANES
+    lane = lax.broadcasted_iota(jnp.int32, (packet, LANES), 1)
+
+    def fetch(base, first_slot, count):
+        for u in range(first_slot, first_slot + count):
+            taken[u : u + 1, :] = rows[pl.ds(cells_of[base + u], 1), :]
+
+    def deliver(base, first_slot, count):
+        for u in range(first_slot, first_slot + count):
+            back[pl.ds(cells_of[base + u], 1), :] = given_back[u : u + 1, :]
+
+    here = (block + shift_block) * packet
 
     @pl.when(block == 0)
     def _():
-        for ref in (acc_first, acc_inner, acc_last, acc_bias, acc_bias_last):
-            ref[...] = jnp.zeros(ref.shape, ref.dtype)
-
-    given = inputs[...]
+        def step(index, carry):
+            for u in range(UNROLL):
+                slot = index * UNROLL + u
+                taken[pl.ds(slot, 1), :] = rows[pl.ds(cells_of[here + slot], 1), :]
+            return carry
+
+        lax.fori_loop(0, packet // UNROLL, step, 0)
+
+    row = 0
+
+    def take(size):
+        nonlocal row
+        value = packs[0, row : row + size, :].astype(F32)
+        row += size
+        return value
+
+    def halves(value):
+        return value[:, :narrow], swap_halves(value)[:, :narrow]
+
+    for k in range(3):
+        inner[k, :, :LANES] = (0.5 * take(width)).astype(BF16)
+    narrow_a, narrow_b = halves(0.5 * take(width))
+    inner[0, :, LANES:] = narrow_a.astype(BF16)
+    inner[1, :, LANES:] = narrow_b.astype(BF16)
+    mixed = take(width)
+    inner[2, :, LANES:] = (0.5 * mixed[:, :narrow]).astype(BF16)
+    out_weight = jnp.where(lower_half(width), 0.0, mixed)
+    last[...] = out_weight.astype(BF16)
+    last_half[...] = (0.5 * out_weight).astype(BF16)
+    wide_first = take(levels)
+    narrow_a, narrow_b = halves(take(levels // 2))
+    first_in[levels:, :] = jnp.zeros((levels, width), BF16)
+    first_out[:levels, :] = jnp.zeros((levels, width), BF16)
+    first_in[:levels, :LANES] = (0.5 * wide_first).astype(BF16)
+    first_out[levels:, :LANES] = wide_first.astype(BF16)
+    half_levels = levels // 2
+    first_in[:half_levels, LANES:] = (0.5 * narrow_a).astype(BF16)
+    first_in[half_levels:levels, LANES:] = (0.5 * narrow_b).astype(BF16)
+    first_out[levels : levels + half_levels, LANES:] = narrow_a.astype(BF16)
+    first_out[levels + half_levels :, LANES:] = narrow_b.astype(BF16)
+    tail = take(16)
+    tail = tail[0:7] + tail[7:14]
+    bias[:, :LANES] = 0.5 * tail[0:4]
+    for k in (0, 2):
+        narrow_a, narrow_b = halves(0.5 * tail[4 + k // 2 : 5 + k // 2])
+        bias[k : k + 1, LANES:] = narrow_a
+        bias[k + 1 : k + 2, LANES:] = narrow_b
+    bias_last[...] = tail[6:7]
+
+    given = taken[...].astype(BF16)
+    ahead = (lax.rem(block + 1, blocks) + shift_block) * packet
+    behind = (jnp.maximum(block - 1, 0) + shift_block) * packet
+    pieces = 8
+    size = packet // pieces
+
+    def move(piece):
+        deliver(behind, piece * size, size)
+        fetch(ahead, piece * size, size)
+
+    over_rows = (((0,), (0,)), ((), ()))
+    over_lanes = (((1,), (1,)), ((), ()))
     feeds = [given]
     slopes = []
     for k in range(4):
         weight = first_in[...] if k == 0 else inner[k - 1]
-        preact = jnp.dot(feeds[-1], weight, preferred_element_type=F32) + bias[k : k + 1, :]
-        gate = 0.5 * jnp.tanh(0.5 * preact) + 0.5
-        active = preact * gate
-        slopes.append(gate + active * (1.0 - gate))
+        half_preact = jnp.dot(feeds[-1], weight, preferred_element_type=F32) + bias[k : k + 1, :]
+        turn = jnp.tanh(half_preact)
+        plus = 1.0 + turn
+        active = half_preact * plus
+        slopes.append(plus + active * (1.0 - turn))
         feeds.append(active.astype(BF16))
+        move(k)
     output = jnp.dot(feeds[-1], last[...], preferred_element_type=F32) + bias_last[...]
     residue = jnp.where(lane >= levels, given.astype(F32) + output, 0.0)
     error = residue.astype(BF16)
-    over_rows = (((0,), (0,)), ((), ()))
-    over_lanes = (((1,), (1,)), ((), ()))
 
     def row_sum(value):
-        return jnp.sum(value.reshape(cells // SUBLANES, SUBLANES, value.shape[1]), axis=0)
-
-    acc_bias_last[...] += row_sum(error.astype(F32))
-    acc_last[...] += lax.dot_general(feeds[4], error, over_rows, preferred_element_type=F32)
-    carried = lax.dot_general(error, last[...], over_lanes, preferred_element_type=F32)
+        return jnp.sum(value, axis=0, keepdims=True)
+
+    last_bias = row_sum(residue)
+    last_grad = lax.dot_general(feeds[4], error, over_rows, preferred_element_type=F32)
+    carried = lax.dot_general(error, last_half[...], over_lanes, preferred_element_type=F32)
+    weight_grads = [None] * 4
+    bias_grads = [None] * 4
     for k in (3, 2, 1, 0):
         exact = carried * slopes[k]
         error = exact.astype(BF16)
-        acc_bias[k] += row_sum(error.astype(F32))
-        product = lax.dot_general(feeds[k], error, over_rows, preferred_element_type=F32)
-        if k > 0:
-            acc_inner[k - 1] += product
-            carried = lax.dot_general(error, inner[k - 1], over_lanes, preferred_element_type=F32)
-        else:
-            acc_first[...] += product[:levels]
-            carried = lax.dot_general(error, first_out[...], over_lanes, preferred_element_type=F32)
-    back = residue + carried
-    out[...] = squeeze_lanes(back, 1).astype(BF16)
-
-    @pl.when(block == pl.num_programs(0) - 1)
+        bias_grads[k] = row_sum(exact)
+        weight_grads[k] = lax.dot_general(feeds[k], error, over_rows, preferred_element_type=F32)
+        weight = inner[k - 1] if k > 0 else first_out[...]
+        carried = lax.dot_general(error, weight, over_lanes, preferred_element_type=F32)
+        move(7 - k)
+    given_back[...] = residue + carried
+
+    filled = 0
+
+    def put(value):
+        nonlocal filled
+        grads[0, filled : filled + value.shape[0], :] = value.astype(BF16)
+        filled += value.shape[0]
+
+    tail = pack_rows(
+        put, weight_grads[1:], weight_grads[0][:levels], last_grad, [(bias_grads, last_bias)]
+    )
+    tail.append(jnp.zeros((grads.shape[1] - filled - len(tail), LANES), F32))
+    put(jnp.concatenate(tail, axis=0))
+
+    @pl.when(block == blocks - 1)
     def _():
-        row = 0
-
-        def put(value):
-            nonlocal row
-            grads[row : row + value.shape[0], :] = value.astype(BF16)
-            row += value.shape[0]
-
-        for k in range(3):
-            put(acc_inner[k][:, :LANES])
-            put(squeeze_lanes(widen(acc_inner[k][:, LANES:]), 0))
-        put(acc_first[...][:, :LANES])
-        put(squeeze_lanes(widen(acc_first[...][:, LANES:]), 0))
-        put(squeeze_lanes(acc_last[...], 1))
-        pieces = [jnp.sum(acc_bias[k], axis=0, keepdims=True) for k in range(4)]
-        tail = [piece[:, :LANES] for piece in pieces]
-        tail += [widen(piece[:, LANES:]) for piece in pieces]
-        tail.append(pltpu.roll(jnp.sum(acc_bias_last[...], axis=0, keepdims=True), LANES // 2, 1))
-        tail.append(jnp.zeros((grads.shape[0] - row - len(tail), LANES), F32))
-        put(jnp.concatenate(tail, axis=0))
-
-
-def widen(value):
-    missing = LANES - value.shape[1]
-    return jnp.concatenate([value, jnp.zeros((value.shape[0], missing), value.dtype)], axis=1)
-
-
-def grad_rows(levels, width, tiles):
-    rows = 3 * (width + width // 2) + levels + levels // 2 + width // 2 + 16
-    unit = 16 * tiles
-    return (rows + unit - 1) // unit * unit
-
-
-def network(received, w_first, w_inner, w_last, b_inner, b_last, tiles, subs):
-    cells, doubled = received.shape
-    levels = doubled // 2
-    width = w_first.shape[1]
-    block = cells // subs
-    zeros = jnp.zeros_like(w_first)
-    first_in = jnp.concatenate([w_first, zeros], axis=0)
-    first_out = jnp.concatenate([zeros, w_first], axis=0)
-    last = jnp.concatenate([jnp.zeros_like(w_last), w_last], axis=1)
-    bias_last = jnp.concatenate([jnp.zeros_like(b_last), b_last])[None]
-    rows = grad_rows(levels, width, tiles)
-
-    def whole(*shape):
-        return pl.BlockSpec(shape, lambda i: (0,) * len(shape))
-
-    return pl.pallas_call(
-        functools.partial(network_body, levels, width, block),
-        grid=(subs,),
+        def step(index, carry):
+            for u in range(UNROLL):
+                slot = index * UNROLL + u
+                back[pl.ds(cells_of[here + slot], 1), :] = given_back[pl.ds(slot, 1), :]
+            return carry
+
+        lax.fori_loop(0, packet // UNROLL, step, 0)
+
+
+def network(cells_of, packs, rows, back, shift_block, levels, width, subs):
+    cells, doubled = rows.shape
+    packet = cells // subs
+    blocks, pack_rows_count, _ = packs.shape
+    body = functools.partial(network_body, levels, width, packet, shift_block)
+    operands = [cells_of, packs, rows]
+    in_specs = [SMEM, pl.BlockSpec((1, pack_rows_count, LANES), lambda i: (i, 0, 0)), VMEM]
+    aliases = {}
+    if back is None:
+        body = lambda a, b, c, *rest: network_body(
+            levels, width, packet, shift_block, a, b, c, None, *rest
+        )
+    else:
+        operands.append(back)
+        in_specs.append(VMEM)
+        aliases = {3: 0}
+    return pl.pallas_call(
+        body,
+        grid=(blocks,),
         out_shape=[
-            jax.ShapeDtypeStruct((cells // 2, doubled), BF16),
-            jax.ShapeDtypeStruct((rows, LANES), BF16),
+            jax.ShapeDtypeStruct((cells, doubled), F32),
+            jax.ShapeDtypeStruct(packs.shape, BF16),
         ],
-        in_specs=[
-            pl.BlockSpec((block, doubled), lambda i: (i, 0)),
-            whole(doubled, width),
-            whole(doubled, width),
-            whole(3, width, width),
-            whole(width, doubled),
-            whole(4, width),
-            whole(1, doubled),
+        in_specs=in_specs,
+        out_specs=[VMEM, pl.BlockSpec((1, pack_rows_count, LANES), lambda i: (i, 0, 0))],
+        scratch_shapes=[
+            pltpu.VMEM((packet, doubled), F32),
+            pltpu.VMEM((packet, doubled), F32),
+            pltpu.VMEM((doubled, width), BF16),
+            pltpu.VMEM((doubled, width), BF16),
+            pltpu.VMEM((3, width, width), BF16),
+            pltpu.VMEM((width, doubled), BF16),
+            pltpu.VMEM((width, doubled), BF16),
+            pltpu.VMEM((4, width), F32),
+            pltpu.VMEM((1, doubled), F32),
         ],
-        out_specs=[
-            pl.BlockSpec((block // 2, doubled), lambda i: (i, 0)),
-            whole(rows, LANES),
-        ],
-        scratch_shapes=[
-            pltpu.VMEM((levels, width), F32),
-            pltpu.VMEM((3, width, width), F32),
-            pltpu.VMEM((width, doubled), F32),
-            pltpu.VMEM((4, SUBLANES, width), F32),
-            pltpu.VMEM((SUBLANES, doubled), F32),
-        ],
+        input_output_aliases=aliases,
         compiler_params=PARAMS,
         name="network",
-    )(received, first_in, first_out, w_inner, last, b_inner, bias_last)
-
-
-def sum_body(parts, out):
+    )(*operands)
+
+
+def add_body(first, other, out):
+    out[...] = (first[...].astype(F32) + other[...].astype(F32)).astype(BF16)
+
+
+def add_pair(first, other):
+    return pl.pallas_call(
+        add_body,
+        out_shape=jax.ShapeDtypeStruct(first.shape, BF16),
+        in_specs=[VMEM] * 2,
+        out_specs=VMEM,
+        compiler_params=PARAMS,
+        name="add_pair",
+    )(first, other)
+
+
+def sum_body(copies, parts, out):
     total = parts[0].astype(F32)
     for index in range(1, parts.shape[0]):
         total = total + parts[index].astype(F32)
     total = total.astype(BF16)
-    for index in range(parts.shape[0]):
+    if copies == 0:
+        out[...] = total
+    for index in range(copies):
         out[index] = total
 
 
-def sum_parts(parts):
-    return pl.pallas_call(
-        sum_body,
-        out_shape=jax.ShapeDtypeStruct(parts.shape, BF16),
+def sum_parts(parts, copies):
+    shape = ((copies,) if copies else ()) + parts.shape[1:]
+    return pl.pallas_call(
+        functools.partial(sum_body, copies),
+        out_shape=jax.ShapeDtypeStruct(shape, BF16),
         in_specs=[VMEM],
         out_specs=VMEM,
         compiler_params=PARAMS,
@@ -450,24 +618,25 @@
         return value
 
     half = LANES // 2
-
-    def unpack(ref, size):
-        low = take(size)
-        narrow = take(size // 2)
-        ref[:, :LANES] = low
-        ref[: size // 2, LANES:] = narrow[:, :half]
-        ref[size // 2 :, LANES:] = pltpu.roll(narrow, half, 1)[:, :half]
-
     for k in range(3):
-        unpack(inner.at[k], width)
-    unpack(first, levels)
-    narrow = take(width // 2)
-    last[: width // 2, :] = narrow[:, :half]
-    last[width // 2 :, :] = pltpu.roll(narrow, half, 1)[:, :half]
+        inner[k, :, :LANES] = take(width)
+    narrow = take(width)
+    inner[0, :, LANES:] = narrow[:, :half]
+    inner[1, :, LANES:] = swap_halves(narrow)[:, :half]
+    narrow = take(width)
+    inner[2, :, LANES:] = narrow[:, :half]
+    last[...] = swap_halves(narrow)[:, :half]
+    first[:, :LANES] = take(levels)
+    narrow = take(levels // 2)
+    first[: levels // 2, LANES:] = narrow[:, :half]
+    first[levels // 2 :, LANES:] = swap_halves(narrow)[:, :half]
     tail = take(16)
     bias[:, :LANES] = tail[0:4]
-    bias[:, LANES:] = tail[4:8, :half]
-    bias_last[...] = tail[8:9, :half]
+    for k in (0, 2):
+        pair = tail[4 + k // 2 : 5 + k // 2]
+        bias[k : k + 1, LANES:] = pair[:, :half]
+        bias[k + 1 : k + 2, LANES:] = swap_halves(pair)[:, :half]
+    bias_last[...] = swap_halves(tail[6:7])[:, :half]
 
 
 def make_steps(whole, levels, width):
@@ -488,47 +657,12 @@
     )(whole)
 
 
-def scatter_body(
-    levels, width_x, width_y, tiles, subs,
-    counts, order, answers, grid, top, bottom, low, high, slots, rows, bases, starts,
-):
+def collect_body(levels, width_x, width_y, rows, grid, top, bottom, low, high):
     cells = width_x * width_y
-    devices = tiles * subs
-    packet = cells // subs
-    half = packet // 2
-    fill_starts(counts, starts, devices)
-
-    def place(index, base):
-        device = index % tiles * subs + index // tiles
-        bases[device] = base
-        return base + counts[device]
-
-    lax.fori_loop(0, devices, place, jnp.int32(0))
-    for expert in range(subs):
-        pair = answers[expert * half : (expert + 1) * half, :].astype(F32)
-        slots[expert * packet : expert * packet + half, :] = pair
-        slots[expert * packet + half : (expert + 1) * packet, :] = pltpu.roll(pair, levels, 1)
-
-    def run(device, carry):
-        count = counts[device]
-        start = starts[device]
-        base = bases[device]
-
-        def copy(chunk, carry):
-            offset = chunk * UNROLL
-            taken = [slots[pl.ds(base + offset + u, 1), :] for u in range(UNROLL)]
-            for u in range(UNROLL):
-                rows[pl.ds(order[start + offset + u], 1), :] = taken[u]
-            return carry
-
-        lax.fori_loop(0, (count + UNROLL - 1) // UNROLL, copy, 0)
-        return carry
-
-    lax.fori_loop(0, devices, run, 0)
 
     def turn(tile, carry):
         span = pl.ds(pl.multiple_of(tile * LANES, LANES), LANES)
-        grid[:, span] = rows[span, :].T[:levels]
+        grid[:, span] = rows[span, :].T[levels:].astype(BF16).astype(F32)
         return carry
 
     lax.fori_loop(0, cells // LANES, turn, 0, unroll=2)
@@ -547,11 +681,11 @@
     bottom[...] = grid[:, cells - 2 * width_y :].astype(BF16)
 
 
-def scatter(counts, order, answers, sizes):
-    levels, width_x, width_y, tiles, subs = sizes
+def collect(rows, sizes):
+    levels, width_x, width_y, _, _ = sizes
     cells = width_x * width_y
     return pl.pallas_call(
-        functools.partial(scatter_body, levels, width_x, width_y, tiles, subs),
+        functools.partial(collect_body, levels, width_x, width_y),
         out_shape=[
             jax.ShapeDtypeStruct((levels, cells), F32),
             jax.ShapeDtypeStruct((levels, 2 * width_y), BF16),
@@ -559,17 +693,11 @@
             jax.ShapeDtypeStruct((levels, LANES), BF16),
             jax.ShapeDtypeStruct((levels, LANES), BF16),
         ],
-        in_specs=[SMEM] * 2 + [VMEM],
+        in_specs=[VMEM],
         out_specs=[VMEM] * 5,
-        scratch_shapes=[
-            pltpu.VMEM((cells + UNROLL, 2 * levels), F32),
-            pltpu.VMEM((cells + SUBLANES, 2 * levels), F32),
-            pltpu.SMEM((tiles * subs,), jnp.int32),
-            pltpu.SMEM((tiles * subs,), jnp.int32),
-        ],
-        compiler_params=PARAMS,
-        name="scatter",
-    )(counts, order, answers)
+        compiler_params=PARAMS,
+        name="collect",
+    )(rows)
 
 
 def adjoint_body(
@@ -694,29 +822,38 @@
     field_rows = tile_rows(initial)
     target_rows = tile_rows(targets)
     diff_rows = tile_rows(diffusivity[None])
-    counts = send_counts[0]
-    order = jnp.pad(column_order[0], (0, LANES), constant_values=cells)
+    width = w_first.shape[2]
+    half = subs // 2
+    parity = lax.rem(lax.axis_index("sub"), 2).reshape(1)
+    same_core = [list(range(core, subs, 2)) for core in range(2)]
+    partner = [(i, i ^ 1) for i in range(subs)]
+
+    def spread(packs):
+        return lax.all_to_all(
+            packs, "sub", split_axis=0, concat_axis=0, tiled=True, axis_index_groups=same_core
+        )
+
     top, bottom, low, high = pack_edges(field_rows, diff_rows, levels, width_x, width_y)
+    weights = pack_weights(
+        w_first[0], w_inner[0], w_last[0], b_inner[0], b_last, tiles, half
+    )
     halos = exchange(top, bottom, low, high)
-    blocks = forward(counts, order, field_rows, target_rows, diff_rows, low, high, halos, sizes)
-    received = lax.all_to_all(
-        blocks.reshape(subs, cells // subs, 2 * levels), "sub", split_axis=0, concat_axis=0, tiled=True
-    ).reshape(cells, 2 * levels)
-    returning, gradients = network(
-        received, w_first[0], w_inner[0], w_last[0], b_inner[0], b_last[0], tiles, subs
-    )
-    answers = lax.all_to_all(
-        returning.reshape(subs, cells // subs // 2, 2 * levels),
-        "sub", split_axis=0, concat_axis=0, tiled=True,
-    ).reshape(cells // 2, 2 * levels)
+    own_weights = spread(weights)
+    other_weights = lax.ppermute(own_weights, "sub", partner)
+    cells_of = slot_cells(parity, send_counts[0], column_order[0], sizes)
+    rows = forward(field_rows, target_rows, diff_rows, low, high, halos, sizes)
+    back, other_grads = network(cells_of, other_weights, rows, None, 0, levels, width, subs)
+    partner_grads = lax.ppermute(other_grads, "sub", partner)
+    back, own_grads = network(cells_of, own_weights, rows, back, half, levels, width, subs)
+    mine = sum_parts(spread(add_pair(own_grads, partner_grads)), 0)
     parts = lax.all_to_all(
-        gradients.reshape(tiles, -1, LANES), "tile", split_axis=0, concat_axis=0, tiled=True
+        mine.reshape(tiles, -1, LANES), "tile", split_axis=0, concat_axis=0, tiled=True
     )
     whole = lax.all_to_all(
-        sum_parts(parts), "tile", split_axis=0, concat_axis=0, tiled=True
+        sum_parts(parts, tiles), "tile", split_axis=0, concat_axis=0, tiled=True
     ).reshape(-1, LANES)
-    steps = make_steps(whole, levels, w_first.shape[2])
-    grid, g_top, g_bottom, g_low, g_high = scatter(counts, order, answers, sizes)
+    steps = make_steps(whole, levels, width)
+    grid, g_top, g_bottom, g_low, g_high = collect(back, sizes)
     g_halos = exchange(g_top, g_bottom, g_low, g_high)
     result = adjoint(grid, diff_rows, (g_low, g_high), (low, high), g_halos, halos, sizes)
     return (

time: 140 us -> 152 us (1.086)
  blocking collectives: 12.6 us -> 49.7 us
  waiting for transfers between devices: 33.7 us -> 12.4 us
  starting transfers between devices: 36.2 us -> 25.5 us
  local copies, waits for them, and re-layouts: 4.3 us -> 11.6 us
    all_to_all x1 -> x3, blocking collectives: 12.6 us -> 49.7 us  [the longest x2 38.5 us: spread(): lax.all_to_all(packs, 'sub', split_axis=0, concat_axis=0, tiled=True, axi...]
    all_to_all x3 -> x1, waiting for transfers between devices: 24 us -> 0.01 us  [per_device(): lax.all_to_all(sum_parts(parts, tiles), 'tile', split_axis=0, concat_axis...]
    unnamed x24 -> x50, local copies, waits for them, and re-layouts: 4.12 us -> 11.6 us
    all_to_all x3 -> x1, starting transfers between devices: 10.7 us -> 3.45 us  [per_device(): lax.all_to_all(sum_parts(parts, tiles), 'tile', split_axis=0, concat_axis...]
    ppermute x8, waiting for transfers between devices: 6.53 us -> 12.4 us  [shifted(): return lax.ppermute(array, ('tile', 'sub'), pairs)]
    ppermute x4, waiting for transfers between devices: 3.17 us -> 0.01 us  [shifted(): lax.ppermute(array, 'sub', [(i, (i + shift_sub) % subs) for i in range(su...]
    pallas_call x4 -> x9, Pallas kernels: 43 us -> 40.8 us  [the longest x2 28.5 us: network(): pl.pallas_call(body, grid=(blocks,), out_shape=[jax.ShapeDtypeStruct((cel...]
    ppermute x4, starting transfers between devices: 9.12 us -> 7.02 us  [shifted(): lax.ppermute(array, 'tile', [(i, (i + shift_tile) % tiles) for i in range...]
  transfers between devices with their start and end apart: 19 -> 19, of which waited for: 8 -> 5; matrix products, arithmetic and copies ran while one was open for 0% -> 0% of each run, Pallas kernels for 11% -> 22%
where the time goes in v1:
time: 152 us; the launch traced here: 151 us
  Pallas kernels  50.6 us (33%)
  blocking collectives  49.7 us (33%)
  starting transfers between devices  25.5 us (17%)
  waiting for transfers between devices  12.4 us (8%)
  local copies, waits for them, and re-layouts  11.6 us (8%)
    all_to_all x2, blocking collectives, spread(): lax.all_to_all(packs, 'sub', split_axis=0, concat_axis=0, tiled=True, axi...  38.5 us
    pallas_call x2, Pallas kernels, network(): pl.pallas_call(body, grid=(blocks,), out_shape=[jax.ShapeDtypeStruct((cel...  28.5 us
    ppermute x8, waiting for transfers between devices, shifted(): return lax.ppermute(array, ('tile', 'sub'), pairs)  12.4 us
    unnamed x50, local copies, waits for them, and re-layouts  11.6 us
    ppermute x8, starting transfers between devices, shifted(): return lax.ppermute(array, ('tile', 'sub'), pairs)  11.5 us
    all_to_all x1, blocking collectives, per_device(): lax.all_to_all(mine.reshape(tiles, -1, LANES), 'tile', split_axis=0, conc...  11.2 us
    pallas_call x1, Pallas kernels, forward(): pl.pallas_call(functools.partial(forward_body, levels, width_x, width_y),...  7.24 us
    ppermute x4, starting transfers between devices, shifted(): lax.ppermute(array, 'tile', [(i, (i + shift_tile) % tiles) for i in range...  7.02 us
  transfers between devices with their start and end apart: 19, of which 5 were waited for; matrix products, arithmetic and copies ran while one was open for 0% of the time, Pallas kernels for 22%

profile of v1, /device:TPU:0, one launch (start us, length us, event | category | flops | bytes accessed | tf_op | source)
XLA Modules:
  0.0 150.7 jit_solution(15868612466359760635)
XLA Ops:
  0.6 0.9 copy.17
  1.5 0.0 copy-start.2
  1.5 1.0 copy-done.2
  2.5 0.8 copy-done.19
  3.2 0.7 copy-done.20
  3.9 0.7 copy-done.21
  4.6 0.1 pack_weights.1
  4.7 0.0 copy-start
  4.7 0.0 copy-start.3
  4.7 0.0 copy-start.23
  4.7 20.1 %all_to_all.20.packs = bf16[4,1088,128]{2,1,0:T(8,128)(2,1)S(1)} all-to-all(bf16[4,1088,128]{2,1,0:T(8,128)(2,1)S(1)} %pack_weights.1), channel_id=1, replica_groups={{0,2,4,6},{1,3,5,7},{8,10,12,14},{9,11,13,15},{16,18,20,22},{17,19,21,2..., dimensions={0} | all-to-all | bytes 2228224 | tf_op jit(solution)/shard_map/all_to_all | solution.py:832
  24.9 2.3 %pack_edges.1 = (f32[72,512]{1,0:T(8,128)}, f32[72,512]{1,0:T(8,128)}, f32[72,128]{1,0:T(8,128)S(1)}, f32[72,128]{1,0:T(8,128)}) custom-call(f32[2048,128]{1,0:T(8,128)S(1)} %bitcast.36, f32[32,128]{1,0:T(8,128)S(1)} %bitcast.45), custom_call_target="tpu_custom_call" | custom-call | tf_op jit(solution)/shard_map/pack_edges/pallas_call | solution.py:99
  27.2 3.9 %collective-permute-start.7 = (f32[72,128]{1,0:T(8,128)S(1)}, f32[72,128]{1,0:T(8,128)S(1)}, u32[]{:S(2)}, u32[]{:S(2)}) collective-permute-start(f32[72,128]{1,0:T(8,128)S(1)} %get-tuple-element.24.own_low.diff_own_low), channel_id=1, source_target_pairs={{0,31},{1,24},{2,25},{3,26},{4,27},{5,28},{6,29},{7,30},{8,7},{9,0... | collective-permute-start | bytes 110600 | tf_op jit(solution)/shard_map/ppermute | solution.py:125
  31.1 0.0 collective-permute-start.5
  31.1 0.2 collective-permute-start.3
  31.2 0.6 copy-done.4
  31.9 3.4 %collective-permute-start.6 = (f32[72,128]{1,0:T(8,128)}, f32[72,128]{1,0:T(8,128)S(1)}, u32[]{:S(2)}, u32[]{:S(2)}) collective-permute-start(f32[72,128]{1,0:T(8,128)} %get-tuple-element.25.own_high.diff_own_high), channel_id=1, source_target_pairs={{0,25},{1,26},{2,27},{3,28},{4,29},{5,30},{6,31},{7,24},{8,1},{9,2... | collective-permute-start | bytes 110600 | tf_op jit(solution)/shard_map/ppermute | solution.py:125
  35.2 0.6 copy-done.7
  35.9 0.7 collective-permute-done.5.up_right.diff_up_right
  36.5 0.6 copy-done.10
  37.1 3.1 %collective-permute-start.1 = (f32[72,512]{1,0:T(8,128)}, f32[72,512]{1,0:T(8,128)S(1)}, u32[]{:S(2)}, u32[]{:S(2)}) collective-permute-start(f32[72,512]{1,0:T(8,128)} %get-tuple-element.27), channel_id=1, source_target_pairs={{0,24},{8,0},{16,8},{24,16},{1,25},{9,1},{17,9},{25,17},{2,26},{10... | collective-permute-start | bytes 442376 | tf_op jit(solution)/shard_map/ppermute | solution.py:119
  40.3 0.0 collective-permute-done.3.right.diff_right
  40.3 0.6 copy-done.13
  40.9 0.0 collective-permute-start.4
  40.9 0.0 collective-permute-done.6.down_left.diff_down_left
  40.9 0.6 copy-done.16
  41.5 1.0 collective-permute-start.2
  42.5 1.5 slot_cells.1
  44.0 5.4 %collective-permute-done.4.up_left.diff_up_left = f32[72,128]{1,0:T(8,128)} collective-permute-done((f32[72,128]{1,0:T(8,128)}, f32[72,128]{1,0:T(8,128)}, u32[]{:S(2)}, u32[]{:S(2)}) %collective-permute-start.4) | collective-permute-done | bytes 36896 | tf_op jit(solution)/shard_map/ppermute | solution.py:125
  49.4 0.0 collective-permute-done.2.left.diff_left
  49.4 0.0 collective-permute-done.up.diff_up
  49.4 0.0 collective-permute-done.1.down.diff_down
  49.4 0.0 copy-start.5
  49.4 0.8 copy-done.5
  50.2 0.8 copy-done.8
  51.0 0.8 copy-done.11
  51.7 0.8 copy-done.14
  52.5 0.8 copy-done.17
  53.3 7.2 %forward.1.c.rows = f32[4096,128]{1,0:T(8,128)S(1)} custom-call(f32[2048,128]{1,0:T(8,128)S(1)} %bitcast.37, f32[2048,128]{1,0:T(8,128)S(1)} %bitcast.40, f32[32,128]{1,0:T(8,128)S(1)} %bitcast.46, f32[72,128]{1,0:T(8,128)S(1)} %copy-done.5, f32[72,128]{1,0:T(8,128)} %get-tuple-element.25.own_high.diff_own_high, ...), custom_call_target="tpu_custom_call" | custom-call | tf_op jit(solution)/shard_map/forward/pallas_call | solution.py:228
  60.5 0.0 collective-permute-done.8.b
  60.5 14.3 %network.2 = (f32[4096,128]{1,0:T(8,128)S(1)}, bf16[4,1088,128]{2,1,0:T(8,128)(2,1)S(1)}) custom-call(s32[5120]{0:T(1024)S(1)} %bitcast.43, bf16[4,1088,128]{2,1,0:T(8,128)(2,1)} %collective-permute-done.8.b, f32[4096,128]{1,0:T(8,128)S(1)} %forward.1.c.rows), custom_call_target="tpu_custom_call" | custom-call | tf_op jit(solution)/shard_map/network/pallas_call | solution.py:541
  74.8 0.1 collective-permute-start.17
  74.9 14.2 %network.3 = (f32[4096,128]{1,0:T(8,128)S(1)}, bf16[4,1088,128]{2,1,0:T(8,128)(2,1)S(1)}) custom-call(s32[5120]{0:T(1024)S(1)} %bitcast.44, bf16[4,1088,128]{2,1,0:T(8,128)(2,1)S(1)} %all_to_all.20.packs, f32[4096,128]{1,0:T(8,128)S(1)} %forward.1.c.rows, f32[4096,128]{1,0:T(8,128)S(1)} %get-tuple-element.28.back_in), custom_call_target="tpu_custom_call", output_to_operand_aliasing={{0}: (3, {})} | custom-call | tf_op jit(solution)/shard_map/network/pallas_call | solution.py:541
  89.1 0.0 collective-permute-done.17.other
  89.2 0.3 add_pair.1
  89.4 18.4 %all_to_all.21.parts = bf16[4,1088,128]{2,1,0:T(8,128)(2,1)S(1)} all-to-all(bf16[4,1088,128]{2,1,0:T(8,128)(2,1)S(1)} %add_pair.1), channel_id=1, replica_groups={{0,2,4,6},{1,3,5,7},{8,10,12,14},{9,11,13,15},{16,18,20,22},{17,19,21,2..., dimensions={0} | all-to-all | bytes 2228224 | tf_op jit(solution)/shard_map/all_to_all | solution.py:832
  107.8 0.1 sum_parts.2
  108.0 11.2 %all_to_all.22.parts = bf16[4,272,128]{2,1,0:T(8,128)(2,1)S(1)} all-to-all(bf16[4,272,128]{2,1,0:T(8,128)(2,1)S(1)} %bitcast.39), channel_id=1, replica_groups=mesh['tile'=4,'sub'=8] {'tile'}, dimensions={0} | all-to-all | bytes 557056 | tf_op jit(solution)/shard_map/all_to_all | solution.py:849
  119.1 0.7 sum_parts.3
  119.9 3.5 %all-to-all-start.3 = ((bf16[4,272,128]{2,1,0:T(8,128)(2,1)}), bf16[4,272,128]{2,1,0:T(8,128)(2,1)S(1)}, u32[]{:S(2)}, u32[]{:S(2)}) async-start(bf16[4,272,128]{2,1,0:T(8,128)(2,1)} %sum_parts.3), calls=%async_computation.3 | async-start | bytes 557056 | tf_op jit(solution)/shard_map/all_to_all | solution.py:852
  123.3 0.0 copy-start.6
  123.4 2.2 %collect.1 = (f32[64,4096]{1,0:T(8,128)S(1)}, bf16[64,512]{1,0:T(8,128)(2,1)S(1)}, bf16[64,512]{1,0:T(8,128)(2,1)S(1)}, bf16[64,128]{1,0:T(8,128)(2,1)S(1)}, bf16[64,128]{1,0:T(8,128)(2,1)S(1)}) custom-call(f32[4096,128]{1,0:T(8,128)S(1)} %get-tuple-element.29.rows), custom_call_target="tpu_custom_call" | custom-call | tf_op jit(solution)/shard_map/collect/pallas_call | solution.py:687
  125.6 2.0 %collective-permute-start.9 = (bf16[64,512]{1,0:T(8,128)(2,1)S(1)}, bf16[64,512]{1,0:T(8,128)(2,1)S(1)}, u32[]{:S(2)}, u32[]{:S(2)}) collective-permute-start(bf16[64,512]{1,0:T(8,128)(2,1)S(1)} %get-tuple-element.33), channel_id=1, source_target_pairs={{0,8},{8,16},{16,24},{24,0},{1,9},{9,17},{17,25},{25,1},{2,10},{10... | collective-permute-start | bytes 196616 | tf_op jit(solution)/shard_map/ppermute | solution.py:119
  127.6 1.9 %collective-permute-start.10 = (bf16[64,512]{1,0:T(8,128)(2,1)S(1)}, bf16[64,512]{1,0:T(8,128)(2,1)S(1)}, u32[]{:S(2)}, u32[]{:S(2)}) collective-permute-start(bf16[64,512]{1,0:T(8,128)(2,1)S(1)} %get-tuple-element.34), channel_id=1, source_target_pairs={{0,24},{8,0},{16,8},{24,16},{1,25},{9,1},{17,9},{25,17},{2,26},{10... | collective-permute-start | bytes 196616 | tf_op jit(solution)/shard_map/ppermute | solution.py:119
  129.5 2.3 %collective-permute-start.14 = (bf16[64,128]{1,0:T(8,128)(2,1)S(1)}, bf16[64,128]{1,0:T(8,128)(2,1)S(1)}, u32[]{:S(2)}, u32[]{:S(2)}) collective-permute-start(bf16[64,128]{1,0:T(8,128)(2,1)S(1)} %get-tuple-element.31.own_low), channel_id=1, source_target_pairs={{0,15},{1,8},{2,9},{3,10},{4,11},{5,12},{6,13},{7,14},{8,23},{9,16... | collective-permute-start | bytes 49160 | tf_op jit(solution)/shard_map/ppermute | solution.py:125
  131.8 0.5 collective-permute-start.12
  132.3 1.4 collective-permute-done.16.down_right
  133.7 2.0 %collective-permute-start.15 = (bf16[64,128]{1,0:T(8,128)(2,1)S(1)}, bf16[64,128]{1,0:T(8,128)(2,1)S(1)}, u32[]{:S(2)}, u32[]{:S(2)}) collective-permute-start(bf16[64,128]{1,0:T(8,128)(2,1)S(1)} %get-tuple-element.32.own_high), channel_id=1, source_target_pairs={{0,25},{1,26},{2,27},{3,28},{4,29},{5,30},{6,31},{7,24},{8,1},{9,2... | collective-permute-start | bytes 49160 | tf_op jit(solution)/shard_map/ppermute | solution.py:125
  135.7 1.8 %collective-permute-start.11 = (bf16[64,128]{1,0:T(8,128)(2,1)S(1)}, bf16[64,128]{1,0:T(8,128)(2,1)S(1)}, u32[]{:S(2)}, u32[]{:S(2)}) collective-permute-start(bf16[64,128]{1,0:T(8,128)(2,1)S(1)} %get-tuple-element.32.own_high), channel_id=1, source_target_pairs={{0,1},{1,2},{2,3},{3,4},{4,5},{5,6},{6,7},{7,0},{8,9},{9,10},{10,1... | collective-permute-start | bytes 49160 | tf_op jit(solution)/shard_map/ppermute | solution.py:117
  137.5 1.2 collective-permute-done.15.down_left
  138.7 3.8 %collective-permute-done.13.up_left = bf16[64,128]{1,0:T(8,128)(2,1)S(1)} collective-permute-done((bf16[64,128]{1,0:T(8,128)(2,1)S(1)}, bf16[64,128]{1,0:T(8,128)(2,1)S(1)}, u32[]{:S(2)}, u32[]{:S(2)}) %collective-permute-start.13) | collective-permute-done | bytes 16416 | tf_op jit(solution)/shard_map/ppermute | solution.py:125
  142.5 6.3 %adjoint.1 = f32[2048,128]{1,0:T(8,128)} custom-call(f32[64,4096]{1,0:T(8,128)S(1)} %get-tuple-element.30.grid, f32[32,128]{1,0:T(8,128)S(1)} %bitcast.47, bf16[64,128]{1,0:T(8,128)(2,1)S(1)} %get-tuple-element.31.own_low, bf16[64,128]{1,0:T(8,128)(2,1)S(1)} %get-tuple-element.32.own_high, f32[72,128]{1,0:T(8,128)S(1)} %copy-done.6, ...), custom_call_target="tpu_custom_call" | custom-call | tf_op jit(solution)/shard_map/adjoint/pallas_call | solution.py:803
  148.8 1.2 make_steps.1
  150.0 0.7 copy.18
  (40 shorter events, 0.1 us)
Async XLA Ops:
  1.5 1.0 copy-start.2
  2.5 0.8 copy-start.19
  3.2 0.7 copy-start.20
  3.9 0.7 copy-start.21
  4.7 20.2 %copy-start = (f32[64,16,256]{2,1,0:T(8,128)S(1)}, f32[64,16,256]{2,1,0:T(8,128)}, u32[]{:S(2)}) copy-start(f32[64,16,256]{2,1,0:T(8,128)} %param.10) | copy-start | bytes 3145732
  4.7 20.2 %copy-start.3 = (f32[16,256]{1,0:T(8,128)S(1)}, f32[16,256]{1,0:T(8,128)}, u32[]{:S(2)}) copy-start(f32[16,256]{1,0:T(8,128)} %param.12) | copy-start | bytes 49156
  4.7 37.8 %copy-start.23 = (s32[1,4096]{1,0:T(1,128)S(1)}, s32[1,4096]{1,0:T(1,128)}, u32[]{:S(2)}) copy-start(s32[1,4096]{1,0:T(1,128)} %param.13) | copy-start | bytes 49156
  24.9 17.7 %copy-start.22 = (s32[1,32]{1,0:T(1,128)S(1)}, s32[1,32]{1,0:T(1,128)}, u32[]{:S(2)}) copy-start(s32[1,32]{1,0:T(1,128)} %param.14) | copy-start | bytes 388
  24.9 24.5 %copy-start.1 = (f32[64,16,256]{2,1,0:T(8,128)S(1)}, f32[64,16,256]{2,1,0:T(8,128)}, u32[]{:S(2)}) copy-start(f32[64,16,256]{2,1,0:T(8,128)} %param.11) | copy-start | bytes 3145732
  24.9 35.6 %collective-permute-start.8 = (bf16[4,1088,128]{2,1,0:T(8,128)(2,1)S(1)}, bf16[4,1088,128]{2,1,0:T(8,128)(2,1)}, u32[]{:S(2)}, u32[]{:S(2)}) collective-permute-start(bf16[4,1088,128]{2,1,0:T(8,128)(2,1)S(1)} %all_to_all.20.packs), channel_id=1, source_target_pairs={{0,1},{1,0},{2,3},{3,2},{4,5},{5,4},{6,7},{7,6},{8,9},{9,8},{10,11... | collective-permute-start | bytes 3342344 | tf_op jit(solution)/shard_map/ppermute | solution.py:842
  27.2 8.1 %collective-permute-start.7 = (f32[72,128]{1,0:T(8,128)S(1)}, f32[72,128]{1,0:T(8,128)S(1)}, u32[]{:S(2)}, u32[]{:S(2)}) collective-permute-start(f32[72,128]{1,0:T(8,128)S(1)} %get-tuple-element.24.own_low.diff_own_low), channel_id=1, source_target_pairs={{0,31},{1,24},{2,25},{3,26},{4,27},{5,28},{6,29},{7,30},{8,7},{9,0... | collective-permute-start | bytes 110600 | tf_op jit(solution)/shard_map/ppermute | solution.py:125
  31.1 5.5 %collective-permute-start.5 = (f32[72,128]{1,0:T(8,128)S(1)}, f32[72,128]{1,0:T(8,128)S(1)}, u32[]{:S(2)}, u32[]{:S(2)}) collective-permute-start(f32[72,128]{1,0:T(8,128)S(1)} %get-tuple-element.24.own_low.diff_own_low), channel_id=1, source_target_pairs={{0,15},{1,8},{2,9},{3,10},{4,11},{5,12},{6,13},{7,14},{8,23},{9,16... | collective-permute-start | bytes 110600 | tf_op jit(solution)/shard_map/ppermute | solution.py:125
  31.1 9.2 %collective-permute-start.3 = (f32[72,128]{1,0:T(8,128)S(1)}, f32[72,128]{1,0:T(8,128)S(1)}, u32[]{:S(2)}, u32[]{:S(2)}) collective-permute-start(f32[72,128]{1,0:T(8,128)S(1)} %get-tuple-element.24.own_low.diff_own_low), channel_id=1, source_target_pairs={{0,7},{1,0},{2,1},{3,2},{4,3},{5,4},{6,5},{7,6},{8,15},{9,8},{10,9... | collective-permute-start | bytes 110600 | tf_op jit(solution)/shard_map/ppermute | solution.py:117
  31.2 0.6 copy-start.4
  31.9 9.1 %collective-permute-start.6 = (f32[72,128]{1,0:T(8,128)}, f32[72,128]{1,0:T(8,128)S(1)}, u32[]{:S(2)}, u32[]{:S(2)}) collective-permute-start(f32[72,128]{1,0:T(8,128)} %get-tuple-element.25.own_high.diff_own_high), channel_id=1, source_target_pairs={{0,25},{1,26},{2,27},{3,28},{4,29},{5,30},{6,31},{7,24},{8,1},{9,2... | collective-permute-start | bytes 110600 | tf_op jit(solution)/shard_map/ppermute | solution.py:125
  35.2 0.6 copy-start.7
  35.9 13.5 %collective-permute-start = (f32[72,512]{1,0:T(8,128)}, f32[72,512]{1,0:T(8,128)S(1)}, u32[]{:S(2)}, u32[]{:S(2)}) collective-permute-start(f32[72,512]{1,0:T(8,128)} %get-tuple-element.26), channel_id=1, source_target_pairs={{0,8},{8,16},{16,24},{24,0},{1,9},{9,17},{17,25},{25,1},{2,10},{10... | collective-permute-start | bytes 442376 | tf_op jit(solution)/shard_map/ppermute | solution.py:119
  36.5 0.6 copy-start.10
  37.1 12.2 %collective-permute-start.1 = (f32[72,512]{1,0:T(8,128)}, f32[72,512]{1,0:T(8,128)S(1)}, u32[]{:S(2)}, u32[]{:S(2)}) collective-permute-start(f32[72,512]{1,0:T(8,128)} %get-tuple-element.27), channel_id=1, source_target_pairs={{0,24},{8,0},{16,8},{24,16},{1,25},{9,1},{17,9},{25,17},{2,26},{10... | collective-permute-start | bytes 442376 | tf_op jit(solution)/shard_map/ppermute | solution.py:119
  40.3 0.6 copy-start.13
  40.9 8.5 %collective-permute-start.4 = (f32[72,128]{1,0:T(8,128)}, f32[72,128]{1,0:T(8,128)}, u32[]{:S(2)}, u32[]{:S(2)}) collective-permute-start(f32[72,128]{1,0:T(8,128)} %get-tuple-element.25.own_high.diff_own_high), channel_id=1, source_target_pairs={{0,9},{1,10},{2,11},{3,12},{4,13},{5,14},{6,15},{7,8},{8,17},{9,18... | collective-permute-start | bytes 110600 | tf_op jit(solution)/shard_map/ppermute | solution.py:125
  40.9 0.6 copy-start.16
  41.5 7.9 %collective-permute-start.2 = (f32[72,128]{1,0:T(8,128)}, f32[72,128]{1,0:T(8,128)}, u32[]{:S(2)}, u32[]{:S(2)}) collective-permute-start(f32[72,128]{1,0:T(8,128)} %get-tuple-element.25.own_high.diff_own_high), channel_id=1, source_target_pairs={{0,1},{1,2},{2,3},{3,4},{4,5},{5,6},{6,7},{7,0},{8,9},{9,10},{10,1... | collective-permute-start | bytes 110600 | tf_op jit(solution)/shard_map/ppermute | solution.py:117
  49.4 0.8 copy-start.5
  50.2 0.8 copy-start.8
  50.9 0.8 copy-start.11
  51.7 0.8 copy-start.14
  52.5 0.8 copy-start.17
  74.8 14.3 %collective-permute-start.17 = (bf16[4,1088,128]{2,1,0:T(8,128)(2,1)S(1)}, bf16[4,1088,128]{2,1,0:T(8,128)(2,1)S(1)}, u32[]{:S(2)}, u32[]{:S(2)}) collective-permute-start(bf16[4,1088,128]{2,1,0:T(8,128)(2,1)S(1)} %get-tuple-element.36), channel_id=1, source_target_pairs={{0,1},{1,0},{2,3},{3,2},{4,5},{5,4},{6,7},{7,6},{8,9},{9,8},{10,11... | collective-permute-start | bytes 3342344 | tf_op jit(solution)/shard_map/ppermute | solution.py:846
  119.9 28.9 %all-to-all-start.3 = ((bf16[4,272,128]{2,1,0:T(8,128)(2,1)}), bf16[4,272,128]{2,1,0:T(8,128)(2,1)S(1)}, u32[]{:S(2)}, u32[]{:S(2)}) async-start(bf16[4,272,128]{2,1,0:T(8,128)(2,1)} %sum_parts.3), calls=%async_computation.3 | async-start | bytes 557056 | tf_op jit(solution)/shard_map/all_to_all | solution.py:852
  123.3 19.1 %copy-start.6 = (f32[72,128]{1,0:T(8,128)S(1)}, f32[72,128]{1,0:T(8,128)}, u32[]{:S(2)}) copy-start(f32[72,128]{1,0:T(8,128)} %copy-done.4) | copy-start | bytes 110596
  123.4 19.1 %copy-start.9 = (f32[72,128]{1,0:T(8,128)S(1)}, f32[72,128]{1,0:T(8,128)}, u32[]{:S(2)}) copy-start(f32[72,128]{1,0:T(8,128)} %copy-done.7) | copy-start | bytes 110596
  123.4 19.1 %copy-start.12 = (f32[72,128]{1,0:T(8,128)S(1)}, f32[72,128]{1,0:T(8,128)}, u32[]{:S(2)}) copy-start(f32[72,128]{1,0:T(8,128)} %copy-done.10) | copy-start | bytes 110596
  123.4 19.1 %copy-start.15 = (f32[72,128]{1,0:T(8,128)S(1)}, f32[72,128]{1,0:T(8,128)}, u32[]{:S(2)}) copy-start(f32[72,128]{1,0:T(8,128)} %copy-done.13) | copy-start | bytes 110596
  123.4 19.1 %copy-start.18 = (f32[72,128]{1,0:T(8,128)S(1)}, f32[72,128]{1,0:T(8,128)}, u32[]{:S(2)}) copy-start(f32[72,128]{1,0:T(8,128)} %copy-done.16) | copy-start | bytes 110596
  125.6 16.8 %collective-permute-start.9 = (bf16[64,512]{1,0:T(8,128)(2,1)S(1)}, bf16[64,512]{1,0:T(8,128)(2,1)S(1)}, u32[]{:S(2)}, u32[]{:S(2)}) collective-permute-start(bf16[64,512]{1,0:T(8,128)(2,1)S(1)} %get-tuple-element.33), channel_id=1, source_target_pairs={{0,8},{8,16},{16,24},{24,0},{1,9},{9,17},{17,25},{25,1},{2,10},{10... | collective-permute-start | bytes 196616 | tf_op jit(solution)/shard_map/ppermute | solution.py:119
  127.6 14.8 %collective-permute-start.10 = (bf16[64,512]{1,0:T(8,128)(2,1)S(1)}, bf16[64,512]{1,0:T(8,128)(2,1)S(1)}, u32[]{:S(2)}, u32[]{:S(2)}) collective-permute-start(bf16[64,512]{1,0:T(8,128)(2,1)S(1)} %get-tuple-element.34), channel_id=1, source_target_pairs={{0,24},{8,0},{16,8},{24,16},{1,25},{9,1},{17,9},{25,17},{2,26},{10... | collective-permute-start | bytes 196616 | tf_op jit(solution)/shard_map/ppermute | solution.py:119
  129.5 4.2 %collective-permute-start.16 = (bf16[64,128]{1,0:T(8,128)(2,1)S(1)}, bf16[64,128]{1,0:T(8,128)(2,1)S(1)}, u32[]{:S(2)}, u32[]{:S(2)}) collective-permute-start(bf16[64,128]{1,0:T(8,128)(2,1)S(1)} %get-tuple-element.31.own_low), channel_id=1, source_target_pairs={{0,31},{1,24},{2,25},{3,26},{4,27},{5,28},{6,29},{7,30},{8,7},{9,0... | collective-permute-start | bytes 49160 | tf_op jit(solution)/shard_map/ppermute | solution.py:125
  129.5 6.2 %collective-permute-start.14 = (bf16[64,128]{1,0:T(8,128)(2,1)S(1)}, bf16[64,128]{1,0:T(8,128)(2,1)S(1)}, u32[]{:S(2)}, u32[]{:S(2)}) collective-permute-start(bf16[64,128]{1,0:T(8,128)(2,1)S(1)} %get-tuple-element.31.own_low), channel_id=1, source_target_pairs={{0,15},{1,8},{2,9},{3,10},{4,11},{5,12},{6,13},{7,14},{8,23},{9,16... | collective-permute-start | bytes 49160 | tf_op jit(solution)/shard_map/ppermute | solution.py:125
  131.8 3.9 %collective-permute-start.12 = (bf16[64,128]{1,0:T(8,128)(2,1)S(1)}, bf16[64,128]{1,0:T(8,128)(2,1)S(1)}, u32[]{:S(2)}, u32[]{:S(2)}) collective-permute-start(bf16[64,128]{1,0:T(8,128)(2,1)S(1)} %get-tuple-element.31.own_low), channel_id=1, source_target_pairs={{0,7},{1,0},{2,1},{3,2},{4,3},{5,4},{6,5},{7,6},{8,15},{9,8},{10,9... | collective-permute-start | bytes 49160 | tf_op jit(solution)/shard_map/ppermute | solution.py:117
  133.7 5.0 %collective-permute-start.15 = (bf16[64,128]{1,0:T(8,128)(2,1)S(1)}, bf16[64,128]{1,0:T(8,128)(2,1)S(1)}, u32[]{:S(2)}, u32[]{:S(2)}) collective-permute-start(bf16[64,128]{1,0:T(8,128)(2,1)S(1)} %get-tuple-element.32.own_high), channel_id=1, source_target_pairs={{0,25},{1,26},{2,27},{3,28},{4,29},{5,30},{6,31},{7,24},{8,1},{9,2... | collective-permute-start | bytes 49160 | tf_op jit(solution)/shard_map/ppermute | solution.py:125
  135.7 6.8 %collective-permute-start.13 = (bf16[64,128]{1,0:T(8,128)(2,1)S(1)}, bf16[64,128]{1,0:T(8,128)(2,1)S(1)}, u32[]{:S(2)}, u32[]{:S(2)}) collective-permute-start(bf16[64,128]{1,0:T(8,128)(2,1)S(1)} %get-tuple-element.32.own_high), channel_id=1, source_target_pairs={{0,9},{1,10},{2,11},{3,12},{4,13},{5,14},{6,15},{7,8},{8,17},{9,18... | collective-permute-start | bytes 49160 | tf_op jit(solution)/shard_map/ppermute | solution.py:125
  135.7 6.8 %collective-permute-start.11 = (bf16[64,128]{1,0:T(8,128)(2,1)S(1)}, bf16[64,128]{1,0:T(8,128)(2,1)S(1)}, u32[]{:S(2)}, u32[]{:S(2)}) collective-permute-start(bf16[64,128]{1,0:T(8,128)(2,1)S(1)} %get-tuple-element.32.own_high), channel_id=1, source_target_pairs={{0,1},{1,2},{2,3},{3,4},{4,5},{5,6},{6,7},{7,0},{8,9},{9,10},{10,1... | collective-permute-start | bytes 49160 | tf_op jit(solution)/shard_map/ppermute | solution.py:117

commit v2 on v1

--- a/solution.py
+++ b/solution.py
@@ -9,12 +9,41 @@
 LANES = 128
 SUBLANES = 8
 SECOND = 32
-UNROLL = 16
 VMEM = pl.BlockSpec(memory_space=pltpu.VMEM)
+ANY = pl.BlockSpec(memory_space=pl.ANY)
 SMEM = pl.BlockSpec(memory_space=pltpu.SMEM)
-PARAMS = pltpu.CompilerParams(vmem_limit_bytes=32 * 1024 * 1024)
+
+
+def params(mebibytes):
+    return pltpu.CompilerParams(vmem_limit_bytes=mebibytes * 1024 * 1024)
+
+
+def cost(microseconds):
+    moved = int(microseconds * 3e6)
+    return pl.CostEstimate(flops=0, transcendentals=0, bytes_accessed=moved)
+
+
 F32 = jnp.float32
 BF16 = jnp.bfloat16
+
+
+def load_all(sources, targets, semaphores, first=0):
+    copies = [
+        pltpu.make_async_copy(source, target, semaphores.at[first + index])
+        for index, (source, target) in enumerate(zip(sources, targets))
+    ]
+    for copy in copies:
+        copy.start()
+    return copies
+
+
+def wait_all(copies):
+    for copy in copies:
+        copy.wait()
+
+
+def buffers(operands):
+    return [pltpu.VMEM(operand.shape, operand.dtype) for operand in operands]
 
 
 def tile_rows(cells):
@@ -106,7 +135,8 @@
         ],
         in_specs=[VMEM] * 2,
         out_specs=[VMEM] * 4,
-        compiler_params=PARAMS,
+        compiler_params=params(8),
+        cost_estimate=cost(2),
         name="pack_edges",
     )(field_rows, diff_rows)
 
@@ -126,16 +156,14 @@
 
 
 def exchange(top, bottom, low, high):
-    return (
-        shifted(bottom, 1, 0),
-        shifted(top, -1, 0),
-        shifted(high, 0, 1),
-        shifted(low, 0, -1),
-        shifted(high, 1, 1),
-        shifted(low, 1, -1),
-        shifted(high, -1, 1),
-        shifted(low, -1, -1),
+    moves = (
+        (bottom, 1, 0), (top, -1, 0), (high, 0, 1), (low, 0, -1),
+        (high, 1, 1), (low, 1, -1), (high, -1, 1), (low, -1, -1),
     )
+    result = []
+    for move in moves:
+        result.append(shifted(*move))
+    return tuple(result)
 
 
 def with_corners(side, before, after, width_x):
@@ -160,12 +188,18 @@
     )
 
 
-def forward_body(
-    levels, width_x, width_y,
-    field, target, diff, own_low, own_high, up, down, left, right,
-    up_left, up_right, down_left, down_right, rows, e0, e1, wide, both,
-):
+def forward_body(levels, width_x, width_y, *refs):
     cells = width_x * width_y
+    sources, refs = refs[:13], refs[13:]
+    rows, rates, rate_sides = refs[:3]
+    targets = refs[3:16]
+    semaphores, e0, e1, wide, both = refs[16:]
+    copies = load_all(sources, targets, semaphores)
+    (
+        field, target, diff, own_low, own_high, up, down, left, right,
+        up_left, up_right, down_left, down_right,
+    ) = targets
+    wait_all(copies[:1] + copies[2:])
 
     def at(x):
         return slice((x + 2) * width_y, (x + 3) * width_y)
@@ -179,9 +213,19 @@
     last = pl.ds(levels, SUBLANES)
     for x in range(width_x):
         wide[:, at(x)] = load_wide(diff, x, width_y)
-    wide[:, at(-1)] = up[last, width_y:]
-    wide[:, at(width_x)] = down[last, :width_y]
+    for k in range(2):
+        wide[:, at(k - 2)] = up[last, k * width_y : (k + 1) * width_y]
+        wide[:, at(width_x + k)] = down[last, k * width_y : (k + 1) * width_y]
     diff_left, diff_right = sides(last)
+    rates[...] = wide[...]
+    for index, value in enumerate(
+        (
+            diff_left, diff_right, second(left[last, :]), second(right[last, :]),
+            own_low[last, :], own_high[last, :],
+        )
+    ):
+        rate_sides[index * SUBLANES : (index + 1) * SUBLANES, :] = value
+    wait_all(copies[1:2])
 
     def step(group, carry):
         where = groups_at(group)
@@ -225,20 +269,29 @@
 def forward(field_rows, target_rows, diff_rows, own_low, own_high, halos, sizes):
     levels, width_x, width_y, _, _ = sizes
     cells = width_x * width_y
+    operands = (field_rows, target_rows, diff_rows, own_low, own_high, *halos)
+    extended = (SUBLANES, (width_x + 4) * width_y)
     return pl.pallas_call(
         functools.partial(forward_body, levels, width_x, width_y),
-        out_shape=jax.ShapeDtypeStruct((cells, 2 * levels), F32),
-        in_specs=[VMEM] * 13,
-        out_specs=VMEM,
-        scratch_shapes=[
-            pltpu.VMEM((SUBLANES, (width_x + 4) * width_y), F32),
-            pltpu.VMEM((SUBLANES, (width_x + 4) * width_y), F32),
-            pltpu.VMEM((SUBLANES, (width_x + 4) * width_y), F32),
+        out_shape=[
+            jax.ShapeDtypeStruct((cells, 2 * levels), F32),
+            jax.ShapeDtypeStruct(extended, F32),
+            jax.ShapeDtypeStruct((6 * SUBLANES, LANES), F32),
+        ],
+        in_specs=[ANY] * 13,
+        out_specs=[VMEM] * 3,
+        scratch_shapes=buffers(operands)
+        + [
+            pltpu.SemaphoreType.DMA((13,)),
+            pltpu.VMEM(extended, F32),
+            pltpu.VMEM(extended, F32),
+            pltpu.VMEM(extended, F32),
             pltpu.VMEM((2 * levels, cells), F32),
         ],
-        compiler_params=PARAMS,
+        compiler_params=params(12),
+        cost_estimate=cost(8),
         name="forward",
-    )(field_rows, target_rows, diff_rows, own_low, own_high, *halos)
+    )(*operands)
 
 
 def index_body(tiles, subs, lead, rows_each, parity, counts, order, out, starts):
@@ -256,7 +309,7 @@
 
     def expert(block, carry):
         second_half = block // half
-        network_id = (block - second_half * half) * 2 + (1 - flip) * (1 - second_half) + flip * second_half
+        network_id = (block - second_half * half) * 2 + flip * (1 - second_half) + (1 - flip) * second_half
         value = jnp.zeros((SUBLANES, LANES), jnp.int32)
         base = jnp.int32(0)
         for t in range(tiles):
@@ -270,7 +323,7 @@
             moved = jnp.where(lane < LANES - shift, turned, following)
             value = jnp.where((slot >= base) & (slot < base + count), moved, value)
             base = base + count
-        out[pl.ds(block * rows_each, SUBLANES), :] = value
+        out[pl.ds(block * rows_each, rows_each), :] = value[:rows_each]
         return carry
 
     lax.fori_loop(0, subs, expert, 0)
@@ -285,13 +338,14 @@
     order = jnp.pad(column_order, (lead, SUBLANES * LANES)).reshape(-1, LANES)
     return pl.pallas_call(
         functools.partial(index_body, tiles, subs, lead, rows_each),
-        out_shape=jax.ShapeDtypeStruct((cells // LANES + SUBLANES, LANES), jnp.int32),
+        out_shape=jax.ShapeDtypeStruct((cells // LANES, LANES), jnp.int32),
         in_specs=[SMEM] * 2 + [VMEM],
         out_specs=VMEM,
         scratch_shapes=[pltpu.SMEM((tiles * subs,), jnp.int32)],
-        compiler_params=PARAMS,
+        compiler_params=params(4),
+        cost_estimate=cost(2),
         name="slot_cells",
-    )(parity, counts, order).reshape(-1)
+    )(parity, counts, order).reshape(subs, 1, packet)
 
 
 def widen(value):
@@ -340,7 +394,10 @@
     return (rows + unit - 1) // unit * unit
 
 
-def weights_body(w_first, w_inner, w_last, b_inner, b_last, out):
+def weights_body(*refs):
+    sources, out, targets, semaphores = refs[:5], refs[5], refs[6:11], refs[11]
+    wait_all(load_all(sources, targets, semaphores))
+    w_first, w_inner, w_last, b_inner, b_last = targets
     row = 0
 
     def put(value):
@@ -360,7 +417,7 @@
         put,
         [w_inner[k].astype(F32) for k in range(3)],
         w_first[...].astype(F32),
-        swap_halves(widen(w_last[...].astype(F32))),
+        swap_halves(widen(w_last[...].astype(F32).T)),
         [
             ([bias_high[k : k + 1] for k in range(4)], last_high),
             ([bias_low[k : k + 1] for k in range(4)], last_low),
@@ -372,45 +429,50 @@
 
 def pack_weights(w_first, w_inner, w_last, b_inner, b_last, tiles, copies):
     levels, width = w_first.shape
+    operands = (w_first, w_inner, w_last.T, b_inner, b_last)
     return pl.pallas_call(
         weights_body,
         out_shape=jax.ShapeDtypeStruct((copies, pack_size(levels, width, tiles), LANES), BF16),
-        in_specs=[VMEM] * 5,
+        in_specs=[ANY] * 5,
         out_specs=VMEM,
-        compiler_params=PARAMS,
+        scratch_shapes=buffers(operands) + [pltpu.SemaphoreType.DMA((5,))],
+        compiler_params=params(8),
+        cost_estimate=cost(1),
         name="pack_weights",
-    )(w_first, w_inner, w_last, b_inner, b_last)
+    )(*operands)
 
 
 def network_body(
-    levels, width, packet, shift_block,
-    cells_of, packs, rows, back_in, back, grads,
-    taken, given_back, first_in, first_out, inner, last, last_half, bias, bias_last,
+    levels, width, packet,
+    behind, ahead, packs, rows, back_in, back, grads,
+    taken, given_back, first_in, first_out, inner, last, last_half,
+    kept, feeds, slopes, residues,
 ):
+    certain = behind[0, 0, 0] >= 0
     block = pl.program_id(0)
     blocks = pl.num_programs(0)
     narrow = width - LANES
-    lane = lax.broadcasted_iota(jnp.int32, (packet, LANES), 1)
-
-    def fetch(base, first_slot, count):
+    wide = 2 * LANES
+    half = packet // 2
+
+    def fetch(cells_of, first_slot, count):
         for u in range(first_slot, first_slot + count):
-            taken[u : u + 1, :] = rows[pl.ds(cells_of[base + u], 1), :]
-
-    def deliver(base, first_slot, count):
+            taken[u : u + 1, :] = rows[pl.ds(cells_of[0, 0, u], 1), :]
+
+    def deliver(cells_of, first_slot, count):
         for u in range(first_slot, first_slot + count):
-            back[pl.ds(cells_of[base + u], 1), :] = given_back[u : u + 1, :]
-
-    here = (block + shift_block) * packet
+            back[pl.ds(cells_of[0, 0, u], 1), :] = given_back[u : u + 1, :]
 
     @pl.when(block == 0)
     def _():
-        def step(index, carry):
-            for u in range(UNROLL):
-                slot = index * UNROLL + u
-                taken[pl.ds(slot, 1), :] = rows[pl.ds(cells_of[here + slot], 1), :]
-            return carry
-
-        lax.fori_loop(0, packet // UNROLL, step, 0)
+        fetch(behind, 0, packet)
+        first_in[levels:, :] = jnp.zeros((wide - levels, wide), BF16)
+        first_out[...] = jnp.zeros((LANES, wide), BF16)
+        first_in[:levels, LANES:] = jnp.zeros((levels, LANES), BF16)
+        inner[:, :, LANES:] = jnp.zeros((3, wide, LANES), BF16)
+        inner[:, width:, :] = jnp.zeros((3, wide - width, wide), BF16)
+        last[...] = jnp.zeros((wide, LANES), BF16)
+        last_half[...] = jnp.zeros((wide, LANES), BF16)
 
     row = 0
 
@@ -424,120 +486,179 @@
         return value[:, :narrow], swap_halves(value)[:, :narrow]
 
     for k in range(3):
-        inner[k, :, :LANES] = (0.5 * take(width)).astype(BF16)
+        inner[k, :width, :LANES] = (0.5 * take(width)).astype(BF16)
     narrow_a, narrow_b = halves(0.5 * take(width))
-    inner[0, :, LANES:] = narrow_a.astype(BF16)
-    inner[1, :, LANES:] = narrow_b.astype(BF16)
+    inner[0, :width, LANES:width] = narrow_a.astype(BF16)
+    inner[1, :width, LANES:width] = narrow_b.astype(BF16)
     mixed = take(width)
-    inner[2, :, LANES:] = (0.5 * mixed[:, :narrow]).astype(BF16)
+    inner[2, :width, LANES:width] = (0.5 * mixed[:, :narrow]).astype(BF16)
     out_weight = jnp.where(lower_half(width), 0.0, mixed)
-    last[...] = out_weight.astype(BF16)
-    last_half[...] = (0.5 * out_weight).astype(BF16)
+    last[:width, :] = out_weight.astype(BF16)
+    last_half[:width, :] = (0.5 * out_weight).astype(BF16)
     wide_first = take(levels)
     narrow_a, narrow_b = halves(take(levels // 2))
-    first_in[levels:, :] = jnp.zeros((levels, width), BF16)
-    first_out[:levels, :] = jnp.zeros((levels, width), BF16)
+    half_levels = levels // 2
     first_in[:levels, :LANES] = (0.5 * wide_first).astype(BF16)
+    first_in[:half_levels, LANES:width] = (0.5 * narrow_a).astype(BF16)
+    first_in[half_levels:levels, LANES:width] = (0.5 * narrow_b).astype(BF16)
     first_out[levels:, :LANES] = wide_first.astype(BF16)
-    half_levels = levels // 2
-    first_in[:half_levels, LANES:] = (0.5 * narrow_a).astype(BF16)
-    first_in[half_levels:levels, LANES:] = (0.5 * narrow_b).astype(BF16)
-    first_out[levels : levels + half_levels, LANES:] = narrow_a.astype(BF16)
-    first_out[levels + half_levels :, LANES:] = narrow_b.astype(BF16)
+    first_out[levels : levels + half_levels, LANES:width] = narrow_a.astype(BF16)
+    first_out[levels + half_levels :, LANES:width] = narrow_b.astype(BF16)
     tail = take(16)
-    tail = tail[0:7] + tail[7:14]
-    bias[:, :LANES] = 0.5 * tail[0:4]
-    for k in (0, 2):
-        narrow_a, narrow_b = halves(0.5 * tail[4 + k // 2 : 5 + k // 2])
-        bias[k : k + 1, LANES:] = narrow_a
-        bias[k + 1 : k + 2, LANES:] = narrow_b
-    bias_last[...] = tail[6:7]
-
-    given = taken[...].astype(BF16)
-    ahead = (lax.rem(block + 1, blocks) + shift_block) * packet
-    behind = (jnp.maximum(block - 1, 0) + shift_block) * packet
-    pieces = 8
-    size = packet // pieces
-
-    def move(piece):
-        deliver(behind, piece * size, size)
-        fetch(ahead, piece * size, size)
+
+    def bias_rows(k):
+        parts = []
+        for base in (0, 7):
+            mixed = 0.5 * tail[base + 4 + k // 2 : base + 5 + k // 2]
+            side = mixed if k % 2 == 0 else swap_halves(mixed)
+            side = jnp.where(lower_half(1), side, 0.0)
+            parts.append(jnp.concatenate([0.5 * tail[base + k : base + k + 1], side], axis=1))
+        parts.append(jnp.zeros((14, wide), F32))
+        return jnp.concatenate(parts, axis=0).astype(BF16)
+
+    first_in[LANES : LANES + 16, :] = bias_rows(0)
+    for k in range(3):
+        inner[k, width : width + 16, :] = bias_rows(k + 1)
+    last[width : width + 16, :] = jnp.concatenate(
+        [tail[6:7], tail[13:14], jnp.zeros((14, LANES), F32)], axis=0
+    ).astype(BF16)
 
     over_rows = (((0,), (0,)), ((), ()))
     over_lanes = (((1,), (1,)), ((), ()))
-    feeds = [given]
-    slopes = []
-    for k in range(4):
-        weight = first_in[...] if k == 0 else inner[k - 1]
-        half_preact = jnp.dot(feeds[-1], weight, preferred_element_type=F32) + bias[k : k + 1, :]
-        turn = jnp.tanh(half_preact)
-        plus = 1.0 + turn
-        active = half_preact * plus
-        slopes.append(plus + active * (1.0 - turn))
-        feeds.append(active.astype(BF16))
-        move(k)
-    output = jnp.dot(feeds[-1], last[...], preferred_element_type=F32) + bias_last[...]
-    residue = jnp.where(lane >= levels, given.astype(F32) + output, 0.0)
-    error = residue.astype(BF16)
-
-    def row_sum(value):
-        return jnp.sum(value, axis=0, keepdims=True)
-
-    last_bias = row_sum(residue)
-    last_grad = lax.dot_general(feeds[4], error, over_rows, preferred_element_type=F32)
-    carried = lax.dot_general(error, last_half[...], over_lanes, preferred_element_type=F32)
-    weight_grads = [None] * 4
-    bias_grads = [None] * 4
-    for k in (3, 2, 1, 0):
-        exact = carried * slopes[k]
-        error = exact.astype(BF16)
-        bias_grads[k] = row_sum(exact)
-        weight_grads[k] = lax.dot_general(feeds[k], error, over_rows, preferred_element_type=F32)
-        weight = inner[k - 1] if k > 0 else first_out[...]
-        carried = lax.dot_general(error, weight, over_lanes, preferred_element_type=F32)
-        move(7 - k)
-    given_back[...] = residue + carried
-
-    filled = 0
-
-    def put(value):
-        nonlocal filled
-        grads[0, filled : filled + value.shape[0], :] = value.astype(BF16)
-        filled += value.shape[0]
-
-    tail = pack_rows(
-        put, weight_grads[1:], weight_grads[0][:levels], last_grad, [(bias_grads, last_bias)]
+    sides = (0, 1)
+    lower = lower_half(half)
+    ones = jnp.ones((half, LANES), BF16)
+
+    def span(side):
+        return slice(side * half, (side + 1) * half)
+
+    for side in sides:
+        kept[span(side), :] = taken[span(side), :].astype(BF16)
+
+    def layers(chosen, current, delivered, share):
+        for k in chosen:
+            for side in sides:
+                weight = first_in[...] if k == 0 else inner[k - 1]
+                u = jnp.dot(current[side], weight, preferred_element_type=F32)
+                turn = jnp.tanh(u)
+                plus = 1.0 + turn
+                active = u * plus
+                slopes[k, span(side), :] = plus + active * (1.0 - turn)
+                current[side] = jnp.concatenate(
+                    [active[:, :LANES], jnp.where(lower, active[:, LANES:], 1.0)], axis=1
+                ).astype(BF16)
+                feeds[k, span(side), :] = current[side]
+                deliver(behind, delivered, share)
+                delivered += share
+        return current
+
+    layers(
+        (0, 1), [jnp.concatenate([kept[span(side), :], ones], axis=1) for side in sides], 0, packet // 8
     )
-    tail.append(jnp.zeros((grads.shape[1] - filled - len(tail), LANES), F32))
-    put(jnp.concatenate(tail, axis=0))
+
+    @pl.when(certain)
+    def _():
+        current = layers((2, 3), [feeds[1, span(side), :] for side in sides], packet // 2, packet // 8)
+        for side in sides:
+            output = jnp.dot(current[side], last[...], preferred_element_type=F32)
+            residues[span(side), :] = jnp.where(
+                lower, 0.0, kept[span(side), :].astype(F32) + output
+            )
+
+    @pl.when(certain)
+    def _():
+        fetched = 0
+        share = packet // 10
+        errors = [residues[span(side), :].astype(BF16) for side in sides]
+
+        def weight_grad(k):
+            products = []
+            for side in sides:
+                if k == 0:
+                    feed = jnp.concatenate([kept[span(side), :], ones], axis=1)[:, : LANES + 16]
+                else:
+                    feed = feeds[k - 1, span(side), : width + 16]
+                products.append(
+                    lax.dot_general(feed, errors[side], over_rows, preferred_element_type=F32)
+                )
+            return products[0] + products[1]
+
+        grad_sums = [None] * 5
+        carried = [
+            lax.dot_general(errors[side], last_half[...], over_lanes, preferred_element_type=F32)
+            for side in sides
+        ]
+        grad_sums[4] = weight_grad(4)
+        for k in (3, 2, 1, 0):
+            for side in sides:
+                errors[side] = (carried[side] * slopes[k, span(side), :]).astype(BF16)
+                weight = inner[k - 1] if k > 0 else first_out[...]
+                carried[side] = lax.dot_general(
+                    errors[side], weight, over_lanes, preferred_element_type=F32
+                )
+                fetch(ahead, fetched, share)
+                fetched += share
+            grad_sums[k] = weight_grad(k)
+        fetch(ahead, fetched, packet - fetched)
+        for side in sides:
+            given_back[span(side), :] = residues[span(side), :] + carried[side]
+
+        filled = 0
+
+        def put(value):
+            nonlocal filled
+            grads[0, filled : filled + value.shape[0], :] = value.astype(BF16)
+            filled += value.shape[0]
+
+        tail = pack_rows(
+            put,
+            [grad_sums[k][:width, :width] for k in (1, 2, 3)],
+            grad_sums[0][:levels, :width],
+            grad_sums[4][:width],
+            [
+                (
+                    [grad_sums[0][LANES : LANES + 1, :width]]
+                    + [grad_sums[k][width : width + 1, :width] for k in (1, 2, 3)],
+                    grad_sums[4][width : width + 1],
+                )
+            ],
+        )
+        tail.append(jnp.zeros((grads.shape[1] - filled - len(tail), LANES), F32))
+        put(jnp.concatenate(tail, axis=0))
 
     @pl.when(block == blocks - 1)
     def _():
-        def step(index, carry):
-            for u in range(UNROLL):
-                slot = index * UNROLL + u
-                back[pl.ds(cells_of[here + slot], 1), :] = given_back[pl.ds(slot, 1), :]
-            return carry
-
-        lax.fori_loop(0, packet // UNROLL, step, 0)
-
-
-def network(cells_of, packs, rows, back, shift_block, levels, width, subs):
+        deliver(ahead, 0, packet)
+
+
+def network(cells_of, packs, rows, back, shift, levels, width, subs):
     cells, doubled = rows.shape
     packet = cells // subs
     blocks, pack_rows_count, _ = packs.shape
-    body = functools.partial(network_body, levels, width, packet, shift_block)
-    operands = [cells_of, packs, rows]
-    in_specs = [SMEM, pl.BlockSpec((1, pack_rows_count, LANES), lambda i: (i, 0, 0)), VMEM]
+    body = functools.partial(network_body, levels, width, packet)
+    operands = [cells_of, cells_of, packs, rows]
+    in_specs = [
+        pl.BlockSpec(
+            (1, 1, packet), lambda i: (jnp.maximum(i - 1, 0) + shift, 0, 0), memory_space=pltpu.SMEM
+        ),
+        pl.BlockSpec(
+            (1, 1, packet),
+            lambda i: (jnp.minimum(i + 1, blocks - 1) + shift, 0, 0),
+            memory_space=pltpu.SMEM,
+        ),
+        pl.BlockSpec((1, pack_rows_count, LANES), lambda i: (i, 0, 0)),
+        VMEM,
+    ]
     aliases = {}
     if back is None:
-        body = lambda a, b, c, *rest: network_body(
-            levels, width, packet, shift_block, a, b, c, None, *rest
+        body = lambda a, b, c, d, *rest: network_body(
+            levels, width, packet, a, b, c, d, None, *rest
         )
     else:
         operands.append(back)
         in_specs.append(VMEM)
-        aliases = {3: 0}
+        aliases = {4: 0}
+    wide = 2 * LANES
     return pl.pallas_call(
         body,
         grid=(blocks,),
@@ -550,16 +671,19 @@
         scratch_shapes=[
             pltpu.VMEM((packet, doubled), F32),
             pltpu.VMEM((packet, doubled), F32),
-            pltpu.VMEM((doubled, width), BF16),
-            pltpu.VMEM((doubled, width), BF16),
-            pltpu.VMEM((3, width, width), BF16),
-            pltpu.VMEM((width, doubled), BF16),
-            pltpu.VMEM((width, doubled), BF16),
-            pltpu.VMEM((4, width), F32),
-            pltpu.VMEM((1, doubled), F32),
+            pltpu.VMEM((wide, wide), BF16),
+            pltpu.VMEM((LANES, wide), BF16),
+            pltpu.VMEM((3, wide, wide), BF16),
+            pltpu.VMEM((wide, LANES), BF16),
+            pltpu.VMEM((wide, LANES), BF16),
+            pltpu.VMEM((packet, LANES), BF16),
+            pltpu.VMEM((4, packet, wide), BF16),
+            pltpu.VMEM((4, packet, wide), F32),
+            pltpu.VMEM((packet, LANES), F32),
         ],
         input_output_aliases=aliases,
-        compiler_params=PARAMS,
+        compiler_params=params(24),
+        cost_estimate=cost(12),
         name="network",
     )(*operands)
 
@@ -574,7 +698,8 @@
         out_shape=jax.ShapeDtypeStruct(first.shape, BF16),
         in_specs=[VMEM] * 2,
         out_specs=VMEM,
-        compiler_params=PARAMS,
+        compiler_params=params(8),
+        cost_estimate=cost(1),
         name="add_pair",
     )(first, other)
 
@@ -597,7 +722,8 @@
         out_shape=jax.ShapeDtypeStruct(shape, BF16),
         in_specs=[VMEM],
         out_specs=VMEM,
-        compiler_params=PARAMS,
+        compiler_params=params(8),
+        cost_estimate=cost(1),
         name="sum_parts",
     )(parts)
 
@@ -625,7 +751,7 @@
     inner[1, :, LANES:] = swap_halves(narrow)[:, :half]
     narrow = take(width)
     inner[2, :, LANES:] = narrow[:, :half]
-    last[...] = swap_halves(narrow)[:, :half]
+    last[...] = swap_halves(narrow).T[:half]
     first[:, :LANES] = take(levels)
     narrow = take(levels // 2)
     first[: levels // 2, LANES:] = narrow[:, :half]
@@ -646,13 +772,14 @@
         out_shape=[
             jax.ShapeDtypeStruct((levels, width), F32),
             jax.ShapeDtypeStruct((3, width, width), F32),
-            jax.ShapeDtypeStruct((width, levels), F32),
+            jax.ShapeDtypeStruct((levels, width), F32),
             jax.ShapeDtypeStruct((4, width), F32),
             jax.ShapeDtypeStruct((1, levels), F32),
         ],
         in_specs=[VMEM],
         out_specs=[VMEM] * 5,
-        compiler_params=PARAMS,
+        compiler_params=params(8),
+        cost_estimate=cost(2),
         name="make_steps",
     )(whole)
 
@@ -695,37 +822,29 @@
         ],
         in_specs=[VMEM],
         out_specs=[VMEM] * 5,
-        compiler_params=PARAMS,
+        compiler_params=params(8),
+        cost_estimate=cost(3),
         name="collect",
     )(rows)
 
 
-def adjoint_body(
-    levels, width_x, width_y,
-    grid, diff, own_low, own_high, diff_own_low, diff_own_high,
-    up, down, left, right, up_left, up_right, down_left, down_right,
-    diff_up, diff_down, diff_left, diff_right,
-    diff_up_left, diff_up_right, diff_down_left, diff_down_right,
-    out, wide, flow, e1,
-):
+def adjoint_body(levels, width_x, width_y, *refs):
+    sources, out, targets = refs[:13], refs[13], refs[14:27]
+    semaphores, flow, e1 = refs[27:]
+    wait_all(load_all(sources, targets, semaphores))
+    (
+        grid, wide, rate_sides, own_low, own_high, up, down, left, right,
+        up_left, up_right, down_left, down_right,
+    ) = targets
     y_tiles = width_y // LANES
     stride = width_x * y_tiles
 
     def at(x):
         return slice((x + 2) * width_y, (x + 3) * width_y)
 
-    last = pl.ds(levels, SUBLANES)
-    for x in range(width_x):
-        wide[:, at(x)] = load_wide(diff, x, width_y)
-    for k in range(2):
-        wide[:, at(k - 2)] = diff_up[last, k * width_y : (k + 1) * width_y]
-        wide[:, at(width_x + k)] = diff_down[last, k * width_y : (k + 1) * width_y]
-    rate_left = with_corners(
-        diff_left[last, :], diff_up_left[last, :], diff_down_left[last, :], width_x
-    )
-    rate_right = with_corners(
-        diff_right[last, :], diff_up_right[last, :], diff_down_right[last, :], width_x
-    )
+    rate_left, rate_right, outer_left, outer_right, mine_left, mine_right = [
+        rate_sides[index * SUBLANES : (index + 1) * SUBLANES, :] for index in range(6)
+    ]
 
     def pair(value, which):
         return value.astype(F32)[which * SUBLANES : (which + 1) * SUBLANES]
@@ -752,16 +871,16 @@
                 product = side * rate
                 return product, side + (
                     around(product)
-                    + second(outer) * second(outer_rate)
+                    + second(outer) * outer_rate
                     + mine * mine_rate
                     - 4.0 * product
                 )
 
             flow_left, next_left = next_side(
-                side_left, rate_left, at_left, diff_left[last, :], own_l, diff_own_low[last, :]
+                side_left, rate_left, at_left, outer_left, own_l, mine_left
             )
             flow_right, next_right = next_side(
-                side_right, rate_right, at_right, diff_right[last, :], own_h, diff_own_high[last, :]
+                side_right, rate_right, at_right, outer_right, own_h, mine_right
             )
 
             def value(x):
@@ -797,27 +916,29 @@
     lax.fori_loop(0, levels // (2 * SUBLANES), step, 0)
 
 
-def adjoint(grid, diff_rows, own, diff_own, halos, diff_halos, sizes):
+def adjoint(grid, rates, rate_sides, own, halos, sizes):
     levels, width_x, width_y, _, _ = sizes
+    operands = (grid, rates, rate_sides, *own, *halos)
     extended = (SUBLANES, (width_x + 4) * width_y)
     return pl.pallas_call(
         functools.partial(adjoint_body, levels, width_x, width_y),
         out_shape=jax.ShapeDtypeStruct((levels * width_x * width_y // LANES, LANES), F32),
-        in_specs=[VMEM] * 22,
+        in_specs=[ANY] * 13,
         out_specs=VMEM,
-        scratch_shapes=[pltpu.VMEM(extended, F32)] * 3,
-        compiler_params=PARAMS,
+        scratch_shapes=buffers(operands)
+        + [pltpu.SemaphoreType.DMA((13,)), pltpu.VMEM(extended, F32), pltpu.VMEM(extended, F32)],
+        compiler_params=params(8),
+        cost_estimate=cost(6),
         name="adjoint",
-    )(grid, diff_rows, *own, *diff_own, *halos, *diff_halos)
-
-
-def per_device(
+    )(*operands)
+
+
+def local_program(
     initial, targets, diffusivity, column_order, send_counts,
     w_first, w_inner, w_last, b_inner, b_last,
 ):
     levels, width_x, width_y = initial.shape
     tiles, subs = lax.axis_size("tile"), lax.axis_size("sub")
-    cells = width_x * width_y
     sizes = (levels, width_x, width_y, tiles, subs)
     field_rows = tile_rows(initial)
     target_rows = tile_rows(targets)
@@ -833,32 +954,39 @@
             packs, "sub", split_axis=0, concat_axis=0, tiled=True, axis_index_groups=same_core
         )
 
+    def across(parts):
+        return lax.all_to_all(parts, "tile", split_axis=0, concat_axis=0, tiled=True)
+
+    def swap(packs):
+        return lax.ppermute(packs, "sub", partner)
+
     top, bottom, low, high = pack_edges(field_rows, diff_rows, levels, width_x, width_y)
     weights = pack_weights(
         w_first[0], w_inner[0], w_last[0], b_inner[0], b_last, tiles, half
     )
     halos = exchange(top, bottom, low, high)
     own_weights = spread(weights)
-    other_weights = lax.ppermute(own_weights, "sub", partner)
+    other_weights = swap(own_weights)
     cells_of = slot_cells(parity, send_counts[0], column_order[0], sizes)
-    rows = forward(field_rows, target_rows, diff_rows, low, high, halos, sizes)
-    back, other_grads = network(cells_of, other_weights, rows, None, 0, levels, width, subs)
-    partner_grads = lax.ppermute(other_grads, "sub", partner)
-    back, own_grads = network(cells_of, own_weights, rows, back, half, levels, width, subs)
-    mine = sum_parts(spread(add_pair(own_grads, partner_grads)), 0)
-    parts = lax.all_to_all(
-        mine.reshape(tiles, -1, LANES), "tile", split_axis=0, concat_axis=0, tiled=True
+    rows, rates, rate_sides = forward(field_rows, target_rows, diff_rows, low, high, halos, sizes)
+    back, own_grads = network(cells_of, own_weights, rows, None, 0, levels, width, subs)
+    back, other_grads = network(
+        cells_of, other_weights, rows, back, half, levels, width, subs
     )
-    whole = lax.all_to_all(
-        sum_parts(parts, tiles), "tile", split_axis=0, concat_axis=0, tiled=True
-    ).reshape(-1, LANES)
+    partner_grads = swap(other_grads)
+    grid, g_top, g_bottom, g_low, g_high = collect(back, sizes)
+    both_grads = add_pair(own_grads, partner_grads)
+    spread_grads = spread(both_grads)
+    g_halos = exchange(g_top, g_bottom, g_low, g_high)
+    mine = sum_parts(spread_grads, 0)
+    parts = across(mine.reshape(tiles, -1, LANES))
+    result = adjoint(grid, rates, rate_sides, (g_low, g_high), g_halos, sizes)
+    summed = sum_parts(parts, tiles)
+    whole = across(summed).reshape(-1, LANES)
     steps = make_steps(whole, levels, width)
-    grid, g_top, g_bottom, g_low, g_high = collect(back, sizes)
-    g_halos = exchange(g_top, g_bottom, g_low, g_high)
-    result = adjoint(grid, diff_rows, (g_low, g_high), (low, high), g_halos, halos, sizes)
     return (
         untile_rows(result, levels, width_x, width_y),
-        steps[0][None], steps[1][None], steps[2][None], steps[3][None], steps[4],
+        steps[0][None], steps[1][None], steps[2].T[None], steps[3][None], steps[4],
     )
 
 
@@ -876,7 +1004,7 @@
         P("sub", None),
     )
     return jax.shard_map(
-        per_device,
+        local_program,
         mesh=mesh,
         in_specs=placed,
         out_specs=(

time: 152 us -> 150 us (0.987)
  Pallas kernels: 50.6 us -> 45 us
  waiting for transfers between devices: 12.4 us -> 15.2 us
    pallas_call x2, Pallas kernels: 28.5 us -> 22.1 us  [network(): pl.pallas_call(body, grid=(blocks,), out_shape=[jax.ShapeDtypeStruct((cel...]
    ppermute x2, waiting for transfers between devices: 0.01 us -> 2.74 us  [swap(): return lax.ppermute(packs, 'sub', partner)]
    unnamed x50 -> x46, local copies, waits for them, and re-layouts: 11.6 us -> 13 us
  transfers between devices with their start and end apart: 19 -> 19, of which waited for: 5 -> 6; matrix products, arithmetic and copies ran while one was open for 0% -> 0% of each run, Pallas kernels for 22% -> 21%
where the time goes in v2:
time: 150 us; the launch traced here: 149 us
  blocking collectives  48.8 us (33%)
  Pallas kernels  45 us (30%)
  starting transfers between devices  25.7 us (17%)
  waiting for transfers between devices  15.2 us (10%)
  local copies, waits for them, and re-layouts  13 us (9%)
    all_to_all x2, blocking collectives, spread(): lax.all_to_all(packs, 'sub', split_axis=0, concat_axis=0, tiled=True, axi...  38.2 us
    pallas_call x2, Pallas kernels, network(): pl.pallas_call(body, grid=(blocks,), out_shape=[jax.ShapeDtypeStruct((cel...  22.1 us
    unnamed x46, local copies, waits for them, and re-layouts  13 us
    ppermute x8, waiting for transfers between devices, shifted(): return lax.ppermute(array, ('tile', 'sub'), pairs)  12.4 us
    ppermute x8, starting transfers between devices, shifted(): return lax.ppermute(array, ('tile', 'sub'), pairs)  11.9 us
    all_to_all x1, blocking collectives, across(): lax.all_to_all(parts, 'tile', split_axis=0, concat_axis=0, tiled=True)  10.6 us
    pallas_call x1, Pallas kernels, forward(): pl.pallas_call(functools.partial(forward_body, levels, width_x, width_y),...  8 us
    ppermute x4, starting transfers between devices, shifted(): lax.ppermute(array, 'tile', [(i, (i + shift_tile) % tiles) for i in range...  7.05 us
  transfers between devices with their start and end apart: 19, of which 6 were waited for; matrix products, arithmetic and copies ran while one was open for 0% of the time, Pallas kernels for 21%

profile of v2, /device:TPU:0, one launch (start us, length us, event | category | flops | bytes accessed | tf_op | source)
XLA Modules:
  0.0 148.6 jit_solution(8623478297162231606)
XLA Ops:
  0.6 1.0 copy-done.2
  1.6 0.8 copy-done.17
  2.4 0.8 copy-done.18
  3.1 0.7 copy-done.19
  3.8 0.7 copy-done.20
  4.5 0.4 pack_weights.1
  4.8 0.0 copy-start
  4.8 0.0 copy-start.5
  4.8 0.0 copy-start.22
  4.9 20.1 %all_to_all.20.c = bf16[4,1088,128]{2,1,0:T(8,128)(2,1)S(1)} all-to-all(bf16[4,1088,128]{2,1,0:T(8,128)(2,1)S(1)} %pack_weights.1), channel_id=1, replica_groups={{0,2,4,6},{1,3,5,7},{8,10,12,14},{9,11,13,15},{16,18,20,22},{17,19,21,2..., dimensions={0} | all-to-all | bytes 2228224 | tf_op jit(solution)/shard_map/all_to_all | solution.py:953
  25.0 0.0 collective-permute-start
  25.0 2.3 %pack_edges.1 = (f32[72,512]{1,0:T(8,128)}, f32[72,512]{1,0:T(8,128)}, f32[72,128]{1,0:T(8,128)S(1)}, f32[72,128]{1,0:T(8,128)}) custom-call(f32[2048,128]{1,0:T(8,128)S(1)} %bitcast.40, f32[32,128]{1,0:T(8,128)S(1)} %bitcast.50), custom_call_target="tpu_custom_call" | custom-call | bytes 6000000 | tf_op jit(solution)/shard_map/pack_edges/pallas_call | solution.py:128
  27.3 3.9 %collective-permute-start.8 = (f32[72,128]{1,0:T(8,128)S(1)}, f32[72,128]{1,0:T(8,128)S(1)}, u32[]{:S(2)}, u32[]{:S(2)}) collective-permute-start(f32[72,128]{1,0:T(8,128)S(1)} %get-tuple-element.27.refs_3_), channel_id=1, source_target_pairs={{0,31},{1,24},{2,25},{3,26},{4,27},{5,28},{6,29},{7,30},{8,7},{9,0... | collective-permute-start | bytes 110600 | tf_op jit(solution)/shard_map/ppermute | solution.py:155
  31.2 0.0 collective-permute-start.6
  31.2 0.2 collective-permute-start.4
  31.4 0.6 copy-done.7
  32.0 3.4 %collective-permute-start.7 = (f32[72,128]{1,0:T(8,128)}, f32[72,128]{1,0:T(8,128)S(1)}, u32[]{:S(2)}, u32[]{:S(2)}) collective-permute-start(f32[72,128]{1,0:T(8,128)} %get-tuple-element.28.refs_4_), channel_id=1, source_target_pairs={{0,25},{1,26},{2,27},{3,28},{4,29},{5,30},{6,31},{7,24},{8,1},{9,2... | collective-permute-start | bytes 110600 | tf_op jit(solution)/shard_map/ppermute | solution.py:155
  35.3 0.0 collective-permute-done.8.refs_12_
  35.4 0.6 copy-done.9
  36.0 0.0 collective-permute-start.1
  36.0 0.7 collective-permute-done.6.refs_10_
  36.7 0.6 copy-done.11
  37.3 3.1 %collective-permute-start.2 = (f32[72,512]{1,0:T(8,128)}, f32[72,512]{1,0:T(8,128)S(1)}, u32[]{:S(2)}, u32[]{:S(2)}) collective-permute-start(f32[72,512]{1,0:T(8,128)} %get-tuple-element.30), channel_id=1, source_target_pairs={{0,24},{8,0},{16,8},{24,16},{1,25},{9,1},{17,9},{25,17},{2,26},{10... | collective-permute-start | bytes 442376 | tf_op jit(solution)/shard_map/ppermute | solution.py:149
  40.4 0.0 collective-permute-done.4.refs_8_
  40.4 0.6 copy-done.13
  41.0 0.6 copy-done.15
  41.6 1.0 collective-permute-start.3
  42.7 1.5 %slot_cells.1 = s32[32,128]{1,0:T(8,128)S(1)} custom-call(s32[1]{0:T(128)} %bitcast.parity, s32[32]{0:T(128)S(1)} %bitcast.55, s32[44,128]{1,0:T(8,128)S(1)} %pad_bitcast_fusion.order), custom_call_target="tpu_custom_call" | custom-call | bytes 6000000 | tf_op jit(solution)/shard_map/slot_cells/pallas_call | solution.py:339
  44.1 5.4 %collective-permute-done.5.refs_9_ = f32[72,128]{1,0:T(8,128)} collective-permute-done((f32[72,128]{1,0:T(8,128)}, f32[72,128]{1,0:T(8,128)}, u32[]{:S(2)}, u32[]{:S(2)}) %collective-permute-start.5) | collective-permute-done | bytes 36896 | tf_op jit(solution)/shard_map/ppermute | solution.py:155
  49.5 0.0 collective-permute-done.1.refs_5_
  49.5 0.0 collective-permute-done.2.refs_6_
  49.5 0.0 copy-start.3
  49.5 0.7 copy-done.3
  50.2 0.9 copy-done.4
  51.1 0.7 copy-done.6
  51.8 0.8 copy-done.8
  52.6 0.8 copy-done.10
  53.3 0.8 copy-done.12
  54.1 0.8 copy-done.14
  54.9 0.8 copy-done.16
  55.6 8.0 %forward.1 = (f32[4096,128]{1,0:T(8,128)S(1)}, f32[8,5120]{1,0:T(8,128)S(1)}, f32[48,128]{1,0:T(8,128)S(1)}) custom-call(f32[2048,128]{1,0:T(8,128)S(1)} %bitcast.41, f32[2048,128]{1,0:T(8,128)S(1)} %bitcast.44, f32[32,128]{1,0:T(8,128)S(1)} %bitcast.51, f32[72,128]{1,0:T(8,128)S(1)} %copy-done.8, f32[72,128]{1,0:T(8,128)} %get-tuple-element.28.refs_4_, ...), custom_call_target="tpu_custom_call" | custom-call | bytes 24000000 | tf_op jit(solution)/shard_map/forward/pallas_call | solution.py:274
  63.7 10.8 %network.2 = (f32[4096,128]{1,0:T(8,128)S(1)}, bf16[4,1088,128]{2,1,0:T(8,128)(2,1)S(1)}) custom-call(s32[8,1,512]{2,1,0:T(1,128)S(1)} %bitcast.45, s32[8,1,512]{2,1,0:T(1,128)S(1)} %bitcast.46, bf16[4,1088,128]{2,1,0:T(8,128)(2,1)S(1)} %all_to_all.20.c, f32[4096,128]{1,0:T(8,128)S(1)} %get-tuple-element.31.d.rows), custom_call_target="tpu_custom_call" | custom-call | bytes 36000000 | tf_op jit(solution)/shard_map/network/pallas_call | solution.py:662
  74.5 11.2 %network.3 = (f32[4096,128]{1,0:T(8,128)S(1)}, bf16[4,1088,128]{2,1,0:T(8,128)(2,1)S(1)}) custom-call(s32[8,1,512]{2,1,0:T(1,128)S(1)} %bitcast.47, s32[8,1,512]{2,1,0:T(1,128)S(1)} %bitcast.48, bf16[4,1088,128]{2,1,0:T(8,128)(2,1)} %collective-permute-done.packs, f32[4096,128]{1,0:T(8,128)S(1)} %get-tuple-element.31.d.rows, ...), custom_call_target="tpu_custom_call", output_to_operand_aliasing={{0}: (4, {})} | custom-call | bytes 36000000 | tf_op jit(solution)/shard_map/network/pallas_call | solution.py:662
  85.7 0.1 collective-permute-start.17
  85.8 2.7 %collective-permute-done.17.other = bf16[4,1088,128]{2,1,0:T(8,128)(2,1)S(1)} collective-permute-done((bf16[4,1088,128]{2,1,0:T(8,128)(2,1)S(1)}, bf16[4,1088,128]{2,1,0:T(8,128)(2,1)S(1)}, u32[]{:S(2)}, u32[]{:S(2)}) %collective-permute-start.17) | collective-permute-done | bytes 1114144 | tf_op jit(solution)/shard_map/ppermute | solution.py:961
  88.6 0.3 add_pair.1
  88.8 18.0 %all_to_all.21.parts = bf16[4,1088,128]{2,1,0:T(8,128)(2,1)S(1)} all-to-all(bf16[4,1088,128]{2,1,0:T(8,128)(2,1)S(1)} %add_pair.1), channel_id=1, replica_groups={{0,2,4,6},{1,3,5,7},{8,10,12,14},{9,11,13,15},{16,18,20,22},{17,19,21,2..., dimensions={0} | all-to-all | bytes 2228224 | tf_op jit(solution)/shard_map/all_to_all | solution.py:953
  106.9 0.1 sum_parts.2
  107.0 10.6 %all_to_all.22.parts = bf16[4,272,128]{2,1,0:T(8,128)(2,1)S(1)} all-to-all(bf16[4,272,128]{2,1,0:T(8,128)(2,1)S(1)} %bitcast.43), channel_id=1, replica_groups=mesh['tile'=4,'sub'=8] {'tile'}, dimensions={0} | all-to-all | bytes 557056 | tf_op jit(solution)/shard_map/all_to_all | solution.py:958
  117.6 0.7 sum_parts.3
  118.4 3.5 %all-to-all-start.3 = ((bf16[4,272,128]{2,1,0:T(8,128)(2,1)}), bf16[4,272,128]{2,1,0:T(8,128)(2,1)S(1)}, u32[]{:S(2)}, u32[]{:S(2)}) async-start(bf16[4,272,128]{2,1,0:T(8,128)(2,1)} %sum_parts.3), calls=%async_computation.3 | async-start | bytes 557056 | tf_op jit(solution)/shard_map/all_to_all | solution.py:958
  121.8 2.2 %collect.1 = (f32[64,4096]{1,0:T(8,128)S(1)}, bf16[64,512]{1,0:T(8,128)(2,1)S(1)}, bf16[64,512]{1,0:T(8,128)(2,1)S(1)}, bf16[64,128]{1,0:T(8,128)(2,1)S(1)}, bf16[64,128]{1,0:T(8,128)(2,1)S(1)}) custom-call(f32[4096,128]{1,0:T(8,128)S(1)} %get-tuple-element.33.rows), custom_call_target="tpu_custom_call" | custom-call | bytes 9000000 | tf_op jit(solution)/shard_map/collect/pallas_call | solution.py:814
  124.1 2.0 %collective-permute-start.9 = (bf16[64,512]{1,0:T(8,128)(2,1)S(1)}, bf16[64,512]{1,0:T(8,128)(2,1)S(1)}, u32[]{:S(2)}, u32[]{:S(2)}) collective-permute-start(bf16[64,512]{1,0:T(8,128)(2,1)S(1)} %get-tuple-element.39), channel_id=1, source_target_pairs={{0,8},{8,16},{16,24},{24,0},{1,9},{9,17},{17,25},{25,1},{2,10},{10... | collective-permute-start | bytes 196616 | tf_op jit(solution)/shard_map/ppermute | solution.py:149
  126.1 1.9 %collective-permute-start.10 = (bf16[64,512]{1,0:T(8,128)(2,1)S(1)}, bf16[64,512]{1,0:T(8,128)(2,1)S(1)}, u32[]{:S(2)}, u32[]{:S(2)}) collective-permute-start(bf16[64,512]{1,0:T(8,128)(2,1)S(1)} %get-tuple-element.40), channel_id=1, source_target_pairs={{0,24},{8,0},{16,8},{24,16},{1,25},{9,1},{17,9},{25,17},{2,26},{10... | collective-permute-start | bytes 196616 | tf_op jit(solution)/shard_map/ppermute | solution.py:149
  128.0 0.0 collective-permute-start.16
  128.0 2.1 %collective-permute-start.14 = (bf16[64,128]{1,0:T(8,128)(2,1)S(1)}, bf16[64,128]{1,0:T(8,128)(2,1)S(1)}, u32[]{:S(2)}, u32[]{:S(2)}) collective-permute-start(bf16[64,128]{1,0:T(8,128)(2,1)S(1)} %get-tuple-element.37.refs_3_), channel_id=1, source_target_pairs={{0,15},{1,8},{2,9},{3,10},{4,11},{5,12},{6,13},{7,14},{8,23},{9,16... | collective-permute-start | bytes 49160 | tf_op jit(solution)/shard_map/ppermute | solution.py:155
  130.0 0.5 collective-permute-start.12
  130.5 1.2 collective-permute-done.16.refs_12_
  131.7 2.6 %collective-permute-start.15 = (bf16[64,128]{1,0:T(8,128)(2,1)S(1)}, bf16[64,128]{1,0:T(8,128)(2,1)S(1)}, u32[]{:S(2)}, u32[]{:S(2)}) collective-permute-start(bf16[64,128]{1,0:T(8,128)(2,1)S(1)} %get-tuple-element.38.refs_4_), channel_id=1, source_target_pairs={{0,25},{1,26},{2,27},{3,28},{4,29},{5,30},{6,31},{7,24},{8,1},{9,2... | collective-permute-start | bytes 49160 | tf_op jit(solution)/shard_map/ppermute | solution.py:155
  134.3 1.6 %collective-permute-start.11 = (bf16[64,128]{1,0:T(8,128)(2,1)S(1)}, bf16[64,128]{1,0:T(8,128)(2,1)S(1)}, u32[]{:S(2)}, u32[]{:S(2)}) collective-permute-start(bf16[64,128]{1,0:T(8,128)(2,1)S(1)} %get-tuple-element.38.refs_4_), channel_id=1, source_target_pairs={{0,1},{1,2},{2,3},{3,4},{4,5},{5,6},{6,7},{7,0},{8,9},{9,10},{10,1... | collective-permute-start | bytes 49160 | tf_op jit(solution)/shard_map/ppermute | solution.py:147
  135.9 0.9 collective-permute-done.15.refs_11_
  136.8 4.3 %collective-permute-done.13.refs_9_ = bf16[64,128]{1,0:T(8,128)(2,1)S(1)} collective-permute-done((bf16[64,128]{1,0:T(8,128)(2,1)S(1)}, bf16[64,128]{1,0:T(8,128)(2,1)S(1)}, u32[]{:S(2)}, u32[]{:S(2)}) %collective-permute-start.13) | collective-permute-done | bytes 16416 | tf_op jit(solution)/shard_map/ppermute | solution.py:155
  141.1 6.2 %adjoint.1 = f32[2048,128]{1,0:T(8,128)} custom-call(f32[64,4096]{1,0:T(8,128)S(1)} %get-tuple-element.34.refs_0_, f32[8,5120]{1,0:T(8,128)S(1)} %get-tuple-element.35.refs_1_, f32[48,128]{1,0:T(8,128)S(1)} %get-tuple-element.36.refs_2_, bf16[64,128]{1,0:T(8,128)(2,1)S(1)} %get-tuple-element.37.refs_3_, bf16[64,128]{1,0:T(8,128)(2,1)S(1)} %get-tuple-element.38.refs_4_, ...), custom_call_target="tpu_custom_call" | custom-call | bytes 18000000 | tf_op jit(solution)/shard_map/adjoint/pallas_call | solution.py:923
  147.3 1.3 make_steps.1
  (36 shorter events, 0.1 us)
Async XLA Ops:
  0.6 1.0 copy-start.2
  1.6 0.8 copy-start.17
  2.4 0.8 copy-start.18
  3.1 0.7 copy-start.19
  3.8 0.7 copy-start.20
  4.8 20.2 %copy-start = (f32[64,16,256]{2,1,0:T(8,128)S(1)}, f32[64,16,256]{2,1,0:T(8,128)}, u32[]{:S(2)}) copy-start(f32[64,16,256]{2,1,0:T(8,128)} %param.10) | copy-start | bytes 3145732
  4.8 20.2 %copy-start.5 = (f32[16,256]{1,0:T(8,128)S(1)}, f32[16,256]{1,0:T(8,128)}, u32[]{:S(2)}) copy-start(f32[16,256]{1,0:T(8,128)} %param.12) | copy-start | bytes 49156
  4.8 37.8 %copy-start.22 = (s32[1,4096]{1,0:T(1,128)S(1)}, s32[1,4096]{1,0:T(1,128)}, u32[]{:S(2)}) copy-start(s32[1,4096]{1,0:T(1,128)} %param.13) | copy-start | bytes 49156
  25.0 17.7 %copy-start.21 = (s32[1,32]{1,0:T(1,128)S(1)}, s32[1,32]{1,0:T(1,128)}, u32[]{:S(2)}) copy-start(s32[1,32]{1,0:T(1,128)} %param.14) | copy-start | bytes 388
  25.0 25.2 %copy-start.1 = (f32[64,16,256]{2,1,0:T(8,128)S(1)}, f32[64,16,256]{2,1,0:T(8,128)}, u32[]{:S(2)}) copy-start(f32[64,16,256]{2,1,0:T(8,128)} %param.11) | copy-start | bytes 3145732
  25.0 49.5 %collective-permute-start = (bf16[4,1088,128]{2,1,0:T(8,128)(2,1)S(1)}, bf16[4,1088,128]{2,1,0:T(8,128)(2,1)}, u32[]{:S(2)}, u32[]{:S(2)}) collective-permute-start(bf16[4,1088,128]{2,1,0:T(8,128)(2,1)S(1)} %all_to_all.20.c), channel_id=1, source_target_pairs={{0,1},{1,0},{2,3},{3,2},{4,5},{5,4},{6,7},{7,6},{8,9},{9,8},{10,11... | collective-permute-start | bytes 3342344 | tf_op jit(solution)/shard_map/ppermute | solution.py:961
  27.3 8.1 %collective-permute-start.8 = (f32[72,128]{1,0:T(8,128)S(1)}, f32[72,128]{1,0:T(8,128)S(1)}, u32[]{:S(2)}, u32[]{:S(2)}) collective-permute-start(f32[72,128]{1,0:T(8,128)S(1)} %get-tuple-element.27.refs_3_), channel_id=1, source_target_pairs={{0,31},{1,24},{2,25},{3,26},{4,27},{5,28},{6,29},{7,30},{8,7},{9,0... | collective-permute-start | bytes 110600 | tf_op jit(solution)/shard_map/ppermute | solution.py:155
  31.2 5.5 %collective-permute-start.6 = (f32[72,128]{1,0:T(8,128)S(1)}, f32[72,128]{1,0:T(8,128)S(1)}, u32[]{:S(2)}, u32[]{:S(2)}) collective-permute-start(f32[72,128]{1,0:T(8,128)S(1)} %get-tuple-element.27.refs_3_), channel_id=1, source_target_pairs={{0,15},{1,8},{2,9},{3,10},{4,11},{5,12},{6,13},{7,14},{8,23},{9,16... | collective-permute-start | bytes 110600 | tf_op jit(solution)/shard_map/ppermute | solution.py:155
  31.2 9.2 %collective-permute-start.4 = (f32[72,128]{1,0:T(8,128)S(1)}, f32[72,128]{1,0:T(8,128)S(1)}, u32[]{:S(2)}, u32[]{:S(2)}) collective-permute-start(f32[72,128]{1,0:T(8,128)S(1)} %get-tuple-element.27.refs_3_), channel_id=1, source_target_pairs={{0,7},{1,0},{2,1},{3,2},{4,3},{5,4},{6,5},{7,6},{8,15},{9,8},{10,9... | collective-permute-start | bytes 110600 | tf_op jit(solution)/shard_map/ppermute | solution.py:147
  31.4 0.6 copy-start.7
  32.0 9.1 %collective-permute-start.7 = (f32[72,128]{1,0:T(8,128)}, f32[72,128]{1,0:T(8,128)S(1)}, u32[]{:S(2)}, u32[]{:S(2)}) collective-permute-start(f32[72,128]{1,0:T(8,128)} %get-tuple-element.28.refs_4_), channel_id=1, source_target_pairs={{0,25},{1,26},{2,27},{3,28},{4,29},{5,30},{6,31},{7,24},{8,1},{9,2... | collective-permute-start | bytes 110600 | tf_op jit(solution)/shard_map/ppermute | solution.py:155
  35.3 0.6 copy-start.9
  36.0 13.5 %collective-permute-start.1 = (f32[72,512]{1,0:T(8,128)}, f32[72,512]{1,0:T(8,128)S(1)}, u32[]{:S(2)}, u32[]{:S(2)}) collective-permute-start(f32[72,512]{1,0:T(8,128)} %get-tuple-element.29), channel_id=1, source_target_pairs={{0,8},{8,16},{16,24},{24,0},{1,9},{9,17},{17,25},{25,1},{2,10},{10... | collective-permute-start | bytes 442376 | tf_op jit(solution)/shard_map/ppermute | solution.py:149
  36.7 0.6 copy-start.11
  37.3 12.2 %collective-permute-start.2 = (f32[72,512]{1,0:T(8,128)}, f32[72,512]{1,0:T(8,128)S(1)}, u32[]{:S(2)}, u32[]{:S(2)}) collective-permute-start(f32[72,512]{1,0:T(8,128)} %get-tuple-element.30), channel_id=1, source_target_pairs={{0,24},{8,0},{16,8},{24,16},{1,25},{9,1},{17,9},{25,17},{2,26},{10... | collective-permute-start | bytes 442376 | tf_op jit(solution)/shard_map/ppermute | solution.py:149
  40.4 0.6 copy-start.13
  41.0 8.5 %collective-permute-start.5 = (f32[72,128]{1,0:T(8,128)}, f32[72,128]{1,0:T(8,128)}, u32[]{:S(2)}, u32[]{:S(2)}) collective-permute-start(f32[72,128]{1,0:T(8,128)} %get-tuple-element.28.refs_4_), channel_id=1, source_target_pairs={{0,9},{1,10},{2,11},{3,12},{4,13},{5,14},{6,15},{7,8},{8,17},{9,18... | collective-permute-start | bytes 110600 | tf_op jit(solution)/shard_map/ppermute | solution.py:155
  41.0 0.6 copy-start.15
  41.6 7.9 %collective-permute-start.3 = (f32[72,128]{1,0:T(8,128)}, f32[72,128]{1,0:T(8,128)}, u32[]{:S(2)}, u32[]{:S(2)}) collective-permute-start(f32[72,128]{1,0:T(8,128)} %get-tuple-element.28.refs_4_), channel_id=1, source_target_pairs={{0,1},{1,2},{2,3},{3,4},{4,5},{5,6},{6,7},{7,0},{8,9},{9,10},{10,1... | collective-permute-start | bytes 110600 | tf_op jit(solution)/shard_map/ppermute | solution.py:147
  49.5 0.7 copy-start.3
  50.2 0.9 copy-start.4
  51.1 0.7 copy-start.6
  51.8 0.8 copy-start.8
  52.6 0.8 copy-start.10
  53.3 0.8 copy-start.12
  54.1 0.8 copy-start.14
  54.9 0.8 copy-start.16
  85.7 2.8 %collective-permute-start.17 = (bf16[4,1088,128]{2,1,0:T(8,128)(2,1)S(1)}, bf16[4,1088,128]{2,1,0:T(8,128)(2,1)S(1)}, u32[]{:S(2)}, u32[]{:S(2)}) collective-permute-start(bf16[4,1088,128]{2,1,0:T(8,128)(2,1)S(1)} %get-tuple-element.42), channel_id=1, source_target_pairs={{0,1},{1,0},{2,3},{3,2},{4,5},{5,4},{6,7},{7,6},{8,9},{9,8},{10,11... | collective-permute-start | bytes 3342344 | tf_op jit(solution)/shard_map/ppermute | solution.py:961
  118.4 28.9 %all-to-all-start.3 = ((bf16[4,272,128]{2,1,0:T(8,128)(2,1)}), bf16[4,272,128]{2,1,0:T(8,128)(2,1)S(1)}, u32[]{:S(2)}, u32[]{:S(2)}) async-start(bf16[4,272,128]{2,1,0:T(8,128)(2,1)} %sum_parts.3), calls=%async_computation.3 | async-start | bytes 557056 | tf_op jit(solution)/shard_map/all_to_all | solution.py:958
  124.1 17.0 %collective-permute-start.9 = (bf16[64,512]{1,0:T(8,128)(2,1)S(1)}, bf16[64,512]{1,0:T(8,128)(2,1)S(1)}, u32[]{:S(2)}, u32[]{:S(2)}) collective-permute-start(bf16[64,512]{1,0:T(8,128)(2,1)S(1)} %get-tuple-element.39), channel_id=1, source_target_pairs={{0,8},{8,16},{16,24},{24,0},{1,9},{9,17},{17,25},{25,1},{2,10},{10... | collective-permute-start | bytes 196616 | tf_op jit(solution)/shard_map/ppermute | solution.py:149
  126.1 15.0 %collective-permute-start.10 = (bf16[64,512]{1,0:T(8,128)(2,1)S(1)}, bf16[64,512]{1,0:T(8,128)(2,1)S(1)}, u32[]{:S(2)}, u32[]{:S(2)}) collective-permute-start(bf16[64,512]{1,0:T(8,128)(2,1)S(1)} %get-tuple-element.40), channel_id=1, source_target_pairs={{0,24},{8,0},{16,8},{24,16},{1,25},{9,1},{17,9},{25,17},{2,26},{10... | collective-permute-start | bytes 196616 | tf_op jit(solution)/shard_map/ppermute | solution.py:149
  128.0 3.8 %collective-permute-start.16 = (bf16[64,128]{1,0:T(8,128)(2,1)S(1)}, bf16[64,128]{1,0:T(8,128)(2,1)S(1)}, u32[]{:S(2)}, u32[]{:S(2)}) collective-permute-start(bf16[64,128]{1,0:T(8,128)(2,1)S(1)} %get-tuple-element.37.refs_3_), channel_id=1, source_target_pairs={{0,31},{1,24},{2,25},{3,26},{4,27},{5,28},{6,29},{7,30},{8,7},{9,0... | collective-permute-start | bytes 49160 | tf_op jit(solution)/shard_map/ppermute | solution.py:155
  128.0 6.4 %collective-permute-start.14 = (bf16[64,128]{1,0:T(8,128)(2,1)S(1)}, bf16[64,128]{1,0:T(8,128)(2,1)S(1)}, u32[]{:S(2)}, u32[]{:S(2)}) collective-permute-start(bf16[64,128]{1,0:T(8,128)(2,1)S(1)} %get-tuple-element.37.refs_3_), channel_id=1, source_target_pairs={{0,15},{1,8},{2,9},{3,10},{4,11},{5,12},{6,13},{7,14},{8,23},{9,16... | collective-permute-start | bytes 49160 | tf_op jit(solution)/shard_map/ppermute | solution.py:155
  130.0 4.3 %collective-permute-start.12 = (bf16[64,128]{1,0:T(8,128)(2,1)S(1)}, bf16[64,128]{1,0:T(8,128)(2,1)S(1)}, u32[]{:S(2)}, u32[]{:S(2)}) collective-permute-start(bf16[64,128]{1,0:T(8,128)(2,1)S(1)} %get-tuple-element.37.refs_3_), channel_id=1, source_target_pairs={{0,7},{1,0},{2,1},{3,2},{4,3},{5,4},{6,5},{7,6},{8,15},{9,8},{10,9... | collective-permute-start | bytes 49160 | tf_op jit(solution)/shard_map/ppermute | solution.py:147
  131.7 5.1 %collective-permute-start.15 = (bf16[64,128]{1,0:T(8,128)(2,1)S(1)}, bf16[64,128]{1,0:T(8,128)(2,1)S(1)}, u32[]{:S(2)}, u32[]{:S(2)}) collective-permute-start(bf16[64,128]{1,0:T(8,128)(2,1)S(1)} %get-tuple-element.38.refs_4_), channel_id=1, source_target_pairs={{0,25},{1,26},{2,27},{3,28},{4,29},{5,30},{6,31},{7,24},{8,1},{9,2... | collective-permute-start | bytes 49160 | tf_op jit(solution)/shard_map/ppermute | solution.py:155
  134.3 6.8 %collective-permute-start.13 = (bf16[64,128]{1,0:T(8,128)(2,1)S(1)}, bf16[64,128]{1,0:T(8,128)(2,1)S(1)}, u32[]{:S(2)}, u32[]{:S(2)}) collective-permute-start(bf16[64,128]{1,0:T(8,128)(2,1)S(1)} %get-tuple-element.38.refs_4_), channel_id=1, source_target_pairs={{0,9},{1,10},{2,11},{3,12},{4,13},{5,14},{6,15},{7,8},{8,17},{9,18... | collective-permute-start | bytes 49160 | tf_op jit(solution)/shard_map/ppermute | solution.py:155
  134.3 6.8 %collective-permute-start.11 = (bf16[64,128]{1,0:T(8,128)(2,1)S(1)}, bf16[64,128]{1,0:T(8,128)(2,1)S(1)}, u32[]{:S(2)}, u32[]{:S(2)}) collective-permute-start(bf16[64,128]{1,0:T(8,128)(2,1)S(1)} %get-tuple-element.38.refs_4_), channel_id=1, source_target_pairs={{0,1},{1,2},{2,3},{3,4},{4,5},{5,6},{6,7},{7,0},{8,9},{9,10},{10,1... | collective-permute-start | bytes 49160 | tf_op jit(solution)/shard_map/ppermute | solution.py:147

commit v3 on v2

--- a/solution.py
+++ b/solution.py
@@ -89,87 +89,162 @@
     return lax.broadcasted_iota(jnp.int32, (SUBLANES, width), 1)
 
 
-def compact_edges(row_of, width_x, width_y):
-    lane = lane_ids(LANES)
-    low = jnp.zeros((SUBLANES, LANES), F32)
-    high = jnp.zeros((SUBLANES, LANES), F32)
-    for x in range(width_x):
-        row = row_of(x)
-        low = jnp.where(lane == 1 + x, row[:, 0:1], low)
-        low = jnp.where(lane == SECOND + 1 + x, row[:, 1:2], low)
-        high = jnp.where(lane == 1 + x, row[:, width_y - 1 : width_y], high)
-        high = jnp.where(lane == SECOND + 1 + x, row[:, width_y - 2 : width_y - 1], high)
-    return low, high
-
-
 def groups_at(group):
     return pl.ds(pl.multiple_of(group * SUBLANES, SUBLANES), SUBLANES)
 
 
-def pack_body(levels, width_x, width_y, field, diff, top, bottom, low, high):
-    def emit(where, row_of):
-        for k in range(2):
-            top[where, k * width_y : (k + 1) * width_y] = row_of(k)
-            bottom[where, k * width_y : (k + 1) * width_y] = row_of(width_x - 2 + k)
-        low_value, high_value = compact_edges(row_of, width_x, width_y)
-        low[where, :] = low_value
-        high[where, :] = high_value
-
-    def step(group, carry):
-        emit(groups_at(group), lambda x: load_row(field, group, x, width_x, width_y))
+def pairs_at(double):
+    return pl.ds(pl.multiple_of(double * 2 * SUBLANES, 2 * SUBLANES), 2 * SUBLANES)
+
+
+def two(parts):
+    return jnp.concatenate(parts, axis=0).astype(BF16)
+
+
+def store_rows(where, row_of, width_x, width_y, flag, first, other):
+    for k in range(2):
+        span = slice(k * width_y, (k + 1) * width_y)
+        top = two([row_of(which, k) for which in range(2)])
+        bottom = two([row_of(which, width_x - 2 + k) for which in range(2)])
+        first[where, span] = jnp.where(flag == 0, bottom.astype(F32), top.astype(F32)).astype(BF16)
+        other[where, span] = jnp.where(flag == 0, top.astype(F32), bottom.astype(F32)).astype(BF16)
+
+
+def store_columns(where, row_of, width_x, width_y, flag, first, other):
+    lane = lane_ids(LANES)
+    lows, highs = [], []
+    for which in range(2):
+        low = jnp.zeros((SUBLANES, LANES), F32)
+        high = jnp.zeros((SUBLANES, LANES), F32)
+        for x in range(-1, width_x + 1):
+            row = row_of(which, x)
+            low = jnp.where(lane == 1 + x, row[:, 0:1], low)
+            high = jnp.where(lane == 1 + x, row[:, width_y - 1 : width_y], high)
+            if 0 <= x < width_x:
+                low = jnp.where(lane == SECOND + 1 + x, row[:, 1:2], low)
+                high = jnp.where(
+                    lane == SECOND + 1 + x, row[:, width_y - 2 : width_y - 1], high
+                )
+        lows.append(low)
+        highs.append(high)
+    low = jnp.concatenate(lows, axis=0)
+    high = jnp.concatenate(highs, axis=0)
+    first[where, :] = jnp.where(flag == 0, high, low).astype(BF16)
+    other[where, :] = jnp.where(flag == 0, low, high).astype(BF16)
+
+
+def row_pack_body(levels, width_x, width_y, flags, field, diff, first, other):
+    def step(double, carry):
+        store_rows(
+            pairs_at(double),
+            lambda which, x: load_row(field, double * 2 + which, x, width_x, width_y),
+            width_x, width_y, flags[0], first, other,
+        )
         return carry
 
-    lax.fori_loop(0, levels // SUBLANES, step, 0)
-    emit(pl.ds(levels, SUBLANES), lambda x: load_wide(diff, x, width_y))
-
-
-def pack_edges(field_rows, diff_rows, levels, width_x, width_y):
-    tall = levels + SUBLANES
-    return pl.pallas_call(
-        functools.partial(pack_body, levels, width_x, width_y),
-        out_shape=[
-            jax.ShapeDtypeStruct((tall, 2 * width_y), F32),
-            jax.ShapeDtypeStruct((tall, 2 * width_y), F32),
-            jax.ShapeDtypeStruct((tall, LANES), F32),
-            jax.ShapeDtypeStruct((tall, LANES), F32),
-        ],
-        in_specs=[VMEM] * 2,
-        out_specs=[VMEM] * 4,
+    lax.fori_loop(0, levels // (2 * SUBLANES), step, 0)
+    store_rows(
+        pl.ds(levels, 2 * SUBLANES), lambda which, x: load_wide(diff, x, width_y),
+        width_x, width_y, flags[0], first, other,
+    )
+
+
+def pack_rows_out(flags, field_rows, diff_rows, levels, width_x, width_y):
+    shape = jax.ShapeDtypeStruct((levels + 2 * SUBLANES, 2 * width_y), BF16)
+    return pl.pallas_call(
+        functools.partial(row_pack_body, levels, width_x, width_y),
+        out_shape=[shape] * 2,
+        in_specs=[SMEM] + [VMEM] * 2,
+        out_specs=[VMEM] * 2,
         compiler_params=params(8),
-        cost_estimate=cost(2),
-        name="pack_edges",
-    )(field_rows, diff_rows)
-
-
-def shifted(array, shift_tile, shift_sub):
-    tiles, subs = lax.axis_size("tile"), lax.axis_size("sub")
-    if shift_tile == 0:
-        return lax.ppermute(array, "sub", [(i, (i + shift_sub) % subs) for i in range(subs)])
-    if shift_sub == 0:
-        return lax.ppermute(array, "tile", [(i, (i + shift_tile) % tiles) for i in range(tiles)])
-    pairs = []
-    for t in range(tiles):
-        for s in range(subs):
-            target = (t + shift_tile) % tiles * subs + (s + shift_sub) % subs
-            pairs.append((t * subs + s, target))
-    return lax.ppermute(array, ("tile", "sub"), pairs)
-
-
-def exchange(top, bottom, low, high):
-    moves = (
-        (bottom, 1, 0), (top, -1, 0), (high, 0, 1), (low, 0, -1),
-        (high, 1, 1), (low, 1, -1), (high, -1, 1), (low, -1, -1),
-    )
-    result = []
-    for move in moves:
-        result.append(shifted(*move))
-    return tuple(result)
-
-
-def with_corners(side, before, after, width_x):
-    lane = lane_ids(LANES)
-    value = jnp.where(lane == 0, pltpu.roll(before, LANES - width_x, 1), side)
-    return jnp.where(lane == width_x + 1, pltpu.roll(after, width_x, 1), value)
+        cost_estimate=cost(1),
+        name="pack_rows",
+    )(flags, field_rows, diff_rows)
+
+
+def outer_row(flag, first, other, where, which, x, width_x, width_y):
+    even, odd = (other, first) if x < 0 else (first, other)
+    start = (x + 2 if x < 0 else x - width_x) * width_y
+    span = slice(start, start + width_y)
+    value = jnp.where(flag == 0, even[where, span].astype(F32), odd[where, span].astype(F32))
+    return value[which * SUBLANES : (which + 1) * SUBLANES]
+
+
+def column_pack_body(levels, width_x, width_y, flags, field, diff, near, far, first, other):
+    def step(double, carry):
+        where = pairs_at(double)
+
+        def row_of(which, x):
+            if 0 <= x < width_x:
+                return load_row(field, double * 2 + which, x, width_x, width_y)
+            return outer_row(flags[0], near, far, where, which, x, width_x, width_y)
+
+        store_columns(where, row_of, width_x, width_y, flags[1], first, other)
+        return carry
+
+    lax.fori_loop(0, levels // (2 * SUBLANES), step, 0)
+    last = pl.ds(levels, 2 * SUBLANES)
+
+    def rate_of(which, x):
+        if 0 <= x < width_x:
+            return load_wide(diff, x, width_y)
+        return outer_row(flags[0], near, far, last, which, x, width_x, width_y)
+
+    store_columns(last, rate_of, width_x, width_y, flags[1], first, other)
+
+
+def pack_columns_out(flags, field_rows, diff_rows, near, far, levels, width_x, width_y):
+    shape = jax.ShapeDtypeStruct((levels + 2 * SUBLANES, LANES), BF16)
+    return pl.pallas_call(
+        functools.partial(column_pack_body, levels, width_x, width_y),
+        out_shape=[shape] * 2,
+        in_specs=[SMEM] + [VMEM] * 4,
+        out_specs=[VMEM] * 2,
+        compiler_params=params(8),
+        cost_estimate=cost(1),
+        name="pack_columns",
+    )(flags, field_rows, diff_rows, near, far)
+
+
+def back_pack_body(levels, width_x, width_y, flags, grid, near, far, first, other):
+    def step(double, carry):
+        where = pairs_at(double)
+
+        def row_of(which, x):
+            if 0 <= x < width_x:
+                return grid[groups_at(double * 2 + which), x * width_y : (x + 1) * width_y]
+            return outer_row(flags[0], near, far, where, which, x, width_x, width_y)
+
+        store_columns(where, row_of, width_x, width_y, flags[1], first, other)
+        return carry
+
+    lax.fori_loop(0, levels // (2 * SUBLANES), step, 0)
+
+
+def pack_columns_back(flags, grid, near, far, levels, width_x, width_y):
+    shape = jax.ShapeDtypeStruct((levels, LANES), BF16)
+    return pl.pallas_call(
+        functools.partial(back_pack_body, levels, width_x, width_y),
+        out_shape=[shape] * 2,
+        in_specs=[SMEM] + [VMEM] * 3,
+        out_specs=[VMEM] * 2,
+        compiler_params=params(8),
+        cost_estimate=cost(1),
+        name="pack_back",
+    )(flags, grid, near, far)
+
+
+def partners(size, offset):
+    return [(i, i ^ offset) for i in range(size)]
+
+
+def beyond(size):
+    return [(i, (i - 1) % size if i % 2 == 0 else (i + 1) % size) for i in range(size)]
+
+
+def trade_sides(first, other, axis):
+    size = lax.axis_size(axis)
+    return (lax.ppermute(first, axis, partners(size, 1)), lax.ppermute(other, axis, beyond(size)))
 
 
 def around(side):
@@ -188,75 +263,70 @@
     )
 
 
-def forward_body(levels, width_x, width_y, *refs):
+def split_sides(flag, first, other, where):
+    near = first[where, :].astype(F32)
+    far = other[where, :].astype(F32)
+    return jnp.where(flag == 0, far, near), jnp.where(flag == 0, near, far)
+
+
+def forward_body(
+    levels, width_x, width_y,
+    flags, field, target, diff, near, far, own_near, own_far, side_near, side_far,
+    rows, rates, rate_sides, e0, e1, wide, both,
+):
     cells = width_x * width_y
-    sources, refs = refs[:13], refs[13:]
-    rows, rates, rate_sides = refs[:3]
-    targets = refs[3:16]
-    semaphores, e0, e1, wide, both = refs[16:]
-    copies = load_all(sources, targets, semaphores)
-    (
-        field, target, diff, own_low, own_high, up, down, left, right,
-        up_left, up_right, down_left, down_right,
-    ) = targets
-    wait_all(copies[:1] + copies[2:])
 
     def at(x):
         return slice((x + 2) * width_y, (x + 3) * width_y)
 
-    def sides(where):
-        return (
-            with_corners(left[where, :], up_left[where, :], down_left[where, :], width_x),
-            with_corners(right[where, :], up_right[where, :], down_right[where, :], width_x),
-        )
-
-    last = pl.ds(levels, SUBLANES)
+    last = pl.ds(levels, 2 * SUBLANES)
     for x in range(width_x):
         wide[:, at(x)] = load_wide(diff, x, width_y)
-    for k in range(2):
-        wide[:, at(k - 2)] = up[last, k * width_y : (k + 1) * width_y]
-        wide[:, at(width_x + k)] = down[last, k * width_y : (k + 1) * width_y]
-    diff_left, diff_right = sides(last)
+    for x in (-2, -1, width_x, width_x + 1):
+        wide[:, at(x)] = outer_row(flags[0], near, far, last, 0, x, width_x, width_y)
     rates[...] = wide[...]
+
+    diff_left, diff_right = [v[:SUBLANES] for v in split_sides(flags[1], side_near, side_far, last)]
+    mine_low, mine_high = [v[:SUBLANES] for v in split_sides(flags[1], own_near, own_far, last)]
     for index, value in enumerate(
-        (
-            diff_left, diff_right, second(left[last, :]), second(right[last, :]),
-            own_low[last, :], own_high[last, :],
-        )
+        (diff_left, diff_right, second(diff_left), second(diff_right), mine_low, mine_high)
     ):
         rate_sides[index * SUBLANES : (index + 1) * SUBLANES, :] = value
-    wait_all(copies[1:2])
-
-    def step(group, carry):
-        where = groups_at(group)
-        for x in range(width_x):
-            e0[:, at(x)] = load_row(field, group, x, width_x, width_y)
-        for k in range(2):
-            e0[:, at(k - 2)] = up[where, k * width_y : (k + 1) * width_y]
-            e0[:, at(width_x + k)] = down[where, k * width_y : (k + 1) * width_y]
-        side_left, side_right = sides(where)
-
-        def next_side(side, outer, own, coefficient):
-            return side + coefficient * (around(side) + second(outer) + own - 4.0 * side)
-
-        next_left = next_side(side_left, left[where, :], own_low[where, :], diff_left)
-        next_right = next_side(side_right, right[where, :], own_high[where, :], diff_right)
-        for x in range(-1, width_x + 1):
-            row = e0[:, at(x)]
-            near = e0[:, at(x - 1)] + e0[:, at(x + 1)] + beside(row, side_left, side_right, x)
-            e1[:, at(x)] = row + wide[:, at(x)] * (near - 4.0 * row)
-        for x in range(width_x):
-            row = e1[:, at(x)]
-            near = e1[:, at(x - 1)] + e1[:, at(x + 1)] + beside(row, next_left, next_right, x)
-            value = row + wide[:, at(x)] * (near - 4.0 * row)
-            both[where, x * width_y : (x + 1) * width_y] = value
-            both[
-                pl.ds(pl.multiple_of(levels + group * SUBLANES, SUBLANES), SUBLANES),
-                x * width_y : (x + 1) * width_y,
-            ] = value - load_row(target, group, x, width_x, width_y)
+
+    def step(double, carry):
+        where = pairs_at(double)
+        sides = split_sides(flags[1], side_near, side_far, where)
+        own = split_sides(flags[1], own_near, own_far, where)
+        for which in range(2):
+            group = double * 2 + which
+            part = slice(which * SUBLANES, (which + 1) * SUBLANES)
+            for x in range(width_x):
+                e0[:, at(x)] = load_row(field, group, x, width_x, width_y)
+            for x in (-2, -1, width_x, width_x + 1):
+                e0[:, at(x)] = outer_row(flags[0], near, far, where, which, x, width_x, width_y)
+            side_left, side_right = sides[0][part], sides[1][part]
+
+            def next_side(side, mine, coefficient):
+                return side + coefficient * (around(side) + second(side) + mine - 4.0 * side)
+
+            next_left = next_side(side_left, own[0][part], diff_left)
+            next_right = next_side(side_right, own[1][part], diff_right)
+            for x in range(-1, width_x + 1):
+                row = e0[:, at(x)]
+                close = e0[:, at(x - 1)] + e0[:, at(x + 1)] + beside(row, side_left, side_right, x)
+                e1[:, at(x)] = row + wide[:, at(x)] * (close - 4.0 * row)
+            for x in range(width_x):
+                row = e1[:, at(x)]
+                close = e1[:, at(x - 1)] + e1[:, at(x + 1)] + beside(row, next_left, next_right, x)
+                value = row + wide[:, at(x)] * (close - 4.0 * row)
+                span = slice(x * width_y, (x + 1) * width_y)
+                both[groups_at(group), span] = value
+                both[
+                    pl.ds(pl.multiple_of(levels + group * SUBLANES, SUBLANES), SUBLANES), span
+                ] = value - load_row(target, group, x, width_x, width_y)
         return carry
 
-    lax.fori_loop(0, levels // SUBLANES, step, 0)
+    lax.fori_loop(0, levels // (2 * SUBLANES), step, 0)
 
     def turn(tile, carry):
         span = pl.ds(pl.multiple_of(tile * LANES, LANES), LANES)
@@ -266,10 +336,9 @@
     lax.fori_loop(0, cells // LANES, turn, 0, unroll=2)
 
 
-def forward(field_rows, target_rows, diff_rows, own_low, own_high, halos, sizes):
+def forward(flags, field_rows, target_rows, diff_rows, near, own, sides, sizes):
     levels, width_x, width_y, _, _ = sizes
     cells = width_x * width_y
-    operands = (field_rows, target_rows, diff_rows, own_low, own_high, *halos)
     extended = (SUBLANES, (width_x + 4) * width_y)
     return pl.pallas_call(
         functools.partial(forward_body, levels, width_x, width_y),
@@ -278,23 +347,21 @@
             jax.ShapeDtypeStruct(extended, F32),
             jax.ShapeDtypeStruct((6 * SUBLANES, LANES), F32),
         ],
-        in_specs=[ANY] * 13,
+        in_specs=[SMEM] + [VMEM] * 9,
         out_specs=[VMEM] * 3,
-        scratch_shapes=buffers(operands)
-        + [
-            pltpu.SemaphoreType.DMA((13,)),
+        scratch_shapes=[
             pltpu.VMEM(extended, F32),
             pltpu.VMEM(extended, F32),
             pltpu.VMEM(extended, F32),
             pltpu.VMEM((2 * levels, cells), F32),
         ],
-        compiler_params=params(12),
+        compiler_params=params(8),
         cost_estimate=cost(8),
         name="forward",
-    )(*operands)
-
-
-def index_body(tiles, subs, lead, rows_each, parity, counts, order, out, starts):
+    )(flags, field_rows, target_rows, diff_rows, *near, *own, *sides)
+
+
+def index_body(tiles, subs, lead, rows_each, flags, counts, order, out, starts):
     devices = tiles * subs
 
     def begin(index, total):
@@ -303,13 +370,13 @@
 
     lax.fori_loop(0, devices, begin, jnp.int32(0))
     half = subs // 2
-    flip = parity[0]
+    mine = flags[3]
     lane = lax.broadcasted_iota(jnp.int32, (SUBLANES, LANES), 1)
     slot = lax.broadcasted_iota(jnp.int32, (SUBLANES, LANES), 0) * LANES + lane
 
     def expert(block, carry):
         second_half = block // half
-        network_id = (block - second_half * half) * 2 + flip * (1 - second_half) + (1 - flip) * second_half
+        network_id = mine ^ ((block - second_half * half) * 2 + second_half)
         value = jnp.zeros((SUBLANES, LANES), jnp.int32)
         base = jnp.int32(0)
         for t in range(tiles):
@@ -329,7 +396,7 @@
     lax.fori_loop(0, subs, expert, 0)
 
 
-def slot_cells(parity, counts, column_order, sizes):
+def slot_cells(flags, counts, column_order, sizes):
     _, width_x, width_y, tiles, subs = sizes
     cells = width_x * width_y
     packet = cells // subs
@@ -345,7 +412,7 @@
         compiler_params=params(4),
         cost_estimate=cost(2),
         name="slot_cells",
-    )(parity, counts, order).reshape(subs, 1, packet)
+    )(flags, counts, order).reshape(subs, 1, packet)
 
 
 def widen(value):
@@ -402,9 +469,7 @@
 
     def put(value):
         nonlocal row
-        value = value.astype(BF16)
-        for copy in range(out.shape[0]):
-            out[copy, row : row + value.shape[0], :] = value
+        out[row : row + value.shape[0], :] = value.astype(BF16)
         row += value.shape[0]
 
     bias = b_inner[...]
@@ -423,17 +488,17 @@
             ([bias_low[k : k + 1] for k in range(4)], last_low),
         ],
     )
-    tail.append(jnp.zeros((out.shape[1] - row - len(tail), LANES), F32))
+    tail.append(jnp.zeros((out.shape[0] - row - len(tail), LANES), F32))
     put(jnp.concatenate(tail, axis=0))
 
 
-def pack_weights(w_first, w_inner, w_last, b_inner, b_last, tiles, copies):
+def pack_weights(w_first, w_inner, w_last, b_inner, b_last, tiles):
     levels, width = w_first.shape
     operands = (w_first, w_inner, w_last.T, b_inner, b_last)
     return pl.pallas_call(
         weights_body,
-        out_shape=jax.ShapeDtypeStruct((copies, pack_size(levels, width, tiles), LANES), BF16),
-        in_specs=[ANY] * 5,
+        out_shape=jax.ShapeDtypeStruct((pack_size(levels, width, tiles), LANES), BF16),
+        in_specs=[pl.BlockSpec(memory_space=pltpu.HBM)] * 5,
         out_specs=VMEM,
         scratch_shapes=buffers(operands) + [pltpu.SemaphoreType.DMA((5,))],
         compiler_params=params(8),
@@ -444,7 +509,7 @@
 
 def network_body(
     levels, width, packet,
-    behind, ahead, packs, rows, back_in, back, grads,
+    behind, ahead, pack_list, rows, back, grads, packs,
     taken, given_back, first_in, first_out, inner, last, last_half,
     kept, feeds, slopes, residues,
 ):
@@ -474,11 +539,17 @@
         last[...] = jnp.zeros((wide, LANES), BF16)
         last_half[...] = jnp.zeros((wide, LANES), BF16)
 
+    for index, source in enumerate(pack_list):
+
+        @pl.when(block == index)
+        def _():
+            packs[...] = source[...]
+
     row = 0
 
     def take(size):
         nonlocal row
-        value = packs[0, row : row + size, :].astype(F32)
+        value = packs[row : row + size, :].astype(F32)
         row += size
         return value
 
@@ -631,12 +702,18 @@
         deliver(ahead, 0, packet)
 
 
-def network(cells_of, packs, rows, back, shift, levels, width, subs):
+def network(cells_of, pack_list, rows, back, shift, levels, width, subs):
     cells, doubled = rows.shape
     packet = cells // subs
-    blocks, pack_rows_count, _ = packs.shape
-    body = functools.partial(network_body, levels, width, packet)
-    operands = [cells_of, cells_of, packs, rows]
+    blocks = len(pack_list)
+    pack_shape = pack_list[0].shape
+
+    def body(behind, ahead, *refs):
+        names = refs[:blocks]
+        rest = refs[blocks + 1 + (back is not None) :]
+        network_body(levels, width, packet, behind, ahead, names, refs[blocks], *rest)
+
+    operands = [cells_of, cells_of, *pack_list, rows]
     in_specs = [
         pl.BlockSpec(
             (1, 1, packet), lambda i: (jnp.maximum(i - 1, 0) + shift, 0, 0), memory_space=pltpu.SMEM
@@ -646,29 +723,24 @@
             lambda i: (jnp.minimum(i + 1, blocks - 1) + shift, 0, 0),
             memory_space=pltpu.SMEM,
         ),
-        pl.BlockSpec((1, pack_rows_count, LANES), lambda i: (i, 0, 0)),
-        VMEM,
-    ]
+    ] + [VMEM] * (blocks + 1)
     aliases = {}
-    if back is None:
-        body = lambda a, b, c, d, *rest: network_body(
-            levels, width, packet, a, b, c, d, None, *rest
-        )
-    else:
+    if back is not None:
+        aliases = {len(operands): 0}
         operands.append(back)
         in_specs.append(VMEM)
-        aliases = {4: 0}
     wide = 2 * LANES
     return pl.pallas_call(
         body,
         grid=(blocks,),
         out_shape=[
             jax.ShapeDtypeStruct((cells, doubled), F32),
-            jax.ShapeDtypeStruct(packs.shape, BF16),
+            jax.ShapeDtypeStruct((blocks, *pack_shape), BF16),
         ],
         in_specs=in_specs,
-        out_specs=[VMEM, pl.BlockSpec((1, pack_rows_count, LANES), lambda i: (i, 0, 0))],
+        out_specs=[VMEM, pl.BlockSpec((1, *pack_shape), lambda i: (i, 0, 0))],
         scratch_shapes=[
+            pltpu.VMEM(pack_shape, BF16),
             pltpu.VMEM((packet, doubled), F32),
             pltpu.VMEM((packet, doubled), F32),
             pltpu.VMEM((wide, wide), BF16),
@@ -688,47 +760,75 @@
     )(*operands)
 
 
-def add_body(first, other, out):
-    out[...] = (first[...].astype(F32) + other[...].astype(F32)).astype(BF16)
+def add_body(first, other, *outs):
+    for index, out in enumerate(outs):
+        out[...] = (first[index].astype(F32) + other[index].astype(F32)).astype(BF16)
 
 
 def add_pair(first, other):
     return pl.pallas_call(
         add_body,
-        out_shape=jax.ShapeDtypeStruct(first.shape, BF16),
+        out_shape=[jax.ShapeDtypeStruct(first.shape[1:], BF16)] * first.shape[0],
         in_specs=[VMEM] * 2,
-        out_specs=VMEM,
+        out_specs=[VMEM] * first.shape[0],
         compiler_params=params(8),
         cost_estimate=cost(1),
         name="add_pair",
     )(first, other)
 
 
-def sum_body(copies, parts, out):
-    total = parts[0].astype(F32)
-    for index in range(1, parts.shape[0]):
-        total = total + parts[index].astype(F32)
-    total = total.astype(BF16)
-    if copies == 0:
-        out[...] = total
-    for index in range(copies):
-        out[index] = total
-
-
-def sum_parts(parts, copies):
-    shape = ((copies,) if copies else ()) + parts.shape[1:]
-    return pl.pallas_call(
-        functools.partial(sum_body, copies),
-        out_shape=jax.ShapeDtypeStruct(shape, BF16),
-        in_specs=[VMEM],
+def total_of(parts):
+    total = parts[0][...].astype(F32)
+    for part in parts[1:]:
+        total = total + part[...].astype(F32)
+    return total.astype(BF16)
+
+
+def share_body(count, flags, *refs):
+    parts, outs, whole = refs[:count], refs[count:-1], refs[-1]
+    whole[...] = total_of(parts).astype(F32)
+    rows = outs[0].shape[0]
+    for offset, out in enumerate(outs):
+        start = pl.multiple_of((flags[2] ^ offset) * rows, 16)
+        out[...] = whole[pl.ds(start, rows), :].astype(BF16)
+
+
+def sum_and_share(flags, parts, tiles):
+    rows = parts[0].shape[0]
+    return pl.pallas_call(
+        functools.partial(share_body, len(parts)),
+        out_shape=[jax.ShapeDtypeStruct((rows // tiles, LANES), BF16)] * tiles,
+        in_specs=[SMEM] + [VMEM] * len(parts),
+        out_specs=[VMEM] * tiles,
+        scratch_shapes=[pltpu.VMEM((rows, LANES), F32)],
+        compiler_params=params(8),
+        cost_estimate=cost(1),
+        name="sum_and_share",
+    )(flags, *parts)
+
+
+def sum_body(*refs):
+    refs[-1][...] = total_of(refs[:-1])
+
+
+def sum_parts(parts):
+    return pl.pallas_call(
+        sum_body,
+        out_shape=jax.ShapeDtypeStruct(parts[0].shape, BF16),
+        in_specs=[VMEM] * len(parts),
         out_specs=VMEM,
         compiler_params=params(8),
         cost_estimate=cost(1),
         name="sum_parts",
-    )(parts)
-
-
-def steps_body(levels, width, count, whole, first, inner, last, bias, bias_last):
+    )(*parts)
+
+
+def steps_body(levels, width, count, tiles, flags, *refs):
+    parts, (first, inner, last, bias, bias_last, whole) = refs[:tiles], refs[tiles:]
+    share = parts[0].shape[0]
+    for offset, part in enumerate(parts):
+        whole[pl.ds(pl.multiple_of((flags[2] ^ offset) * share, 16), share), :] = part[...]
+
     def squares(index, total):
         part = whole[pl.ds(pl.multiple_of(index * 16, 16), 16), :].astype(F32)
         return total + part * part
@@ -765,10 +865,10 @@
     bias_last[...] = swap_halves(tail[6:7])[:, :half]
 
 
-def make_steps(whole, levels, width):
+def make_steps(flags, parts, levels, width):
     count = 2 * levels * width + 3 * width * width + 4 * width + levels
     return pl.pallas_call(
-        functools.partial(steps_body, levels, width, float(count)),
+        functools.partial(steps_body, levels, width, float(count), len(parts)),
         out_shape=[
             jax.ShapeDtypeStruct((levels, width), F32),
             jax.ShapeDtypeStruct((3, width, width), F32),
@@ -776,15 +876,16 @@
             jax.ShapeDtypeStruct((4, width), F32),
             jax.ShapeDtypeStruct((1, levels), F32),
         ],
-        in_specs=[VMEM],
+        in_specs=[SMEM] + [VMEM] * len(parts),
         out_specs=[VMEM] * 5,
+        scratch_shapes=[pltpu.VMEM((len(parts) * parts[0].shape[0], LANES), BF16)],
         compiler_params=params(8),
         cost_estimate=cost(2),
         name="make_steps",
-    )(whole)
-
-
-def collect_body(levels, width_x, width_y, rows, grid, top, bottom, low, high):
+    )(flags, *parts)
+
+
+def collect_body(levels, width_x, width_y, flags, rows, grid, first, other):
     cells = width_x * width_y
 
     def turn(tile, carry):
@@ -794,48 +895,36 @@
 
     lax.fori_loop(0, cells // LANES, turn, 0, unroll=2)
 
-    lows, highs = [], []
-    for group in range(levels // SUBLANES):
-        where = slice(group * SUBLANES, (group + 1) * SUBLANES)
-        low_value, high_value = compact_edges(
-            lambda x: grid[where, x * width_y : (x + 1) * width_y], width_x, width_y
+    def step(double, carry):
+        store_rows(
+            pairs_at(double),
+            lambda which, x: grid[groups_at(double * 2 + which), x * width_y : (x + 1) * width_y],
+            width_x, width_y, flags[0], first, other,
         )
-        lows.append(low_value)
-        highs.append(high_value)
-    low[...] = jnp.concatenate(lows, axis=0).astype(BF16)
-    high[...] = jnp.concatenate(highs, axis=0).astype(BF16)
-    top[...] = grid[:, : 2 * width_y].astype(BF16)
-    bottom[...] = grid[:, cells - 2 * width_y :].astype(BF16)
-
-
-def collect(rows, sizes):
+        return carry
+
+    lax.fori_loop(0, levels // (2 * SUBLANES), step, 0)
+
+
+def collect(flags, rows, sizes):
     levels, width_x, width_y, _, _ = sizes
     cells = width_x * width_y
+    shape = jax.ShapeDtypeStruct((levels, 2 * width_y), BF16)
     return pl.pallas_call(
         functools.partial(collect_body, levels, width_x, width_y),
-        out_shape=[
-            jax.ShapeDtypeStruct((levels, cells), F32),
-            jax.ShapeDtypeStruct((levels, 2 * width_y), BF16),
-            jax.ShapeDtypeStruct((levels, 2 * width_y), BF16),
-            jax.ShapeDtypeStruct((levels, LANES), BF16),
-            jax.ShapeDtypeStruct((levels, LANES), BF16),
-        ],
-        in_specs=[VMEM],
-        out_specs=[VMEM] * 5,
+        out_shape=[jax.ShapeDtypeStruct((levels, cells), F32), shape, shape],
+        in_specs=[SMEM, VMEM],
+        out_specs=[VMEM] * 3,
         compiler_params=params(8),
         cost_estimate=cost(3),
         name="collect",
-    )(rows)
-
-
-def adjoint_body(levels, width_x, width_y, *refs):
-    sources, out, targets = refs[:13], refs[13], refs[14:27]
-    semaphores, flow, e1 = refs[27:]
-    wait_all(load_all(sources, targets, semaphores))
-    (
-        grid, wide, rate_sides, own_low, own_high, up, down, left, right,
-        up_left, up_right, down_left, down_right,
-    ) = targets
+    )(flags, rows)
+
+
+def adjoint_body(
+    levels, width_x, width_y,
+    flags, grid, wide, rate_sides, near, far, own_near, own_far, side_near, side_far, out, flow, e1,
+):
     y_tiles = width_y // LANES
     stride = width_x * y_tiles
 
@@ -846,66 +935,49 @@
         rate_sides[index * SUBLANES : (index + 1) * SUBLANES, :] for index in range(6)
     ]
 
-    def pair(value, which):
-        return value.astype(F32)[which * SUBLANES : (which + 1) * SUBLANES]
-
     def step(double, carry):
-        where = pl.ds(pl.multiple_of(double * 2 * SUBLANES, 2 * SUBLANES), 2 * SUBLANES)
-        packed = [
-            ref[where, :]
-            for ref in (
-                own_low, own_high, up, down, left, right,
-                up_left, up_right, down_left, down_right,
-            )
-        ]
+        where = pairs_at(double)
+        sides = split_sides(flags[1], side_near, side_far, where)
+        owns = split_sides(flags[1], own_near, own_far, where)
         for which in range(2):
             group = double * 2 + which
             own = groups_at(group)
-            (
-                own_l, own_h, above, below, at_left, at_right, at_ul, at_ur, at_dl, at_dr
-            ) = [pair(value, which) for value in packed]
-            side_left = with_corners(at_left, at_ul, at_dl, width_x)
-            side_right = with_corners(at_right, at_ur, at_dr, width_x)
-
-            def next_side(side, rate, outer, outer_rate, mine, mine_rate):
+            part = slice(which * SUBLANES, (which + 1) * SUBLANES)
+
+            def next_side(side, rate, outer_rate, mine, mine_rate):
                 product = side * rate
                 return product, side + (
-                    around(product)
-                    + second(outer) * outer_rate
-                    + mine * mine_rate
-                    - 4.0 * product
+                    around(product) + second(side) * outer_rate + mine * mine_rate - 4.0 * product
                 )
 
             flow_left, next_left = next_side(
-                side_left, rate_left, at_left, outer_left, own_l, mine_left
+                sides[0][part], rate_left, outer_left, owns[0][part], mine_left
             )
             flow_right, next_right = next_side(
-                side_right, rate_right, at_right, outer_right, own_h, mine_right
+                sides[1][part], rate_right, outer_right, owns[1][part], mine_right
             )
 
             def value(x):
-                if x < 0:
-                    return above[:, (x + 2) * width_y : (x + 3) * width_y]
-                if x >= width_x:
-                    return below[:, (x - width_x) * width_y : (x - width_x + 1) * width_y]
-                return grid[own, x * width_y : (x + 1) * width_y]
+                if 0 <= x < width_x:
+                    return grid[own, x * width_y : (x + 1) * width_y]
+                return outer_row(flags[0], near, far, where, which, x, width_x, width_y)
 
             for x in range(-2, width_x + 2):
                 flow[:, at(x)] = value(x) * wide[:, at(x)]
             for x in range(-1, width_x + 1):
                 row = flow[:, at(x)]
-                near = flow[:, at(x - 1)] + flow[:, at(x + 1)]
-                near = near + beside(row, flow_left, flow_right, x)
-                e1[:, at(x)] = value(x) + near - 4.0 * row
+                close = flow[:, at(x - 1)] + flow[:, at(x + 1)]
+                close = close + beside(row, flow_left, flow_right, x)
+                e1[:, at(x)] = value(x) + close - 4.0 * row
             for x in range(-1, width_x + 1):
                 flow[:, at(x)] = e1[:, at(x)] * wide[:, at(x)]
             flow_left = next_left * rate_left
             flow_right = next_right * rate_right
             for x in range(width_x):
                 row = flow[:, at(x)]
-                near = flow[:, at(x - 1)] + flow[:, at(x + 1)]
-                near = near + beside(row, flow_left, flow_right, x)
-                result = e1[:, at(x)] + near - 4.0 * row
+                close = flow[:, at(x - 1)] + flow[:, at(x + 1)]
+                close = close + beside(row, flow_left, flow_right, x)
+                result = e1[:, at(x)] + close - 4.0 * row
                 for y_tile in range(y_tiles):
                     offset = group * (SUBLANES * stride) + row_offset(x, y_tile, y_tiles)
                     out[pl.ds(offset, SUBLANES, stride=stride), :] = result[
@@ -916,21 +988,19 @@
     lax.fori_loop(0, levels // (2 * SUBLANES), step, 0)
 
 
-def adjoint(grid, rates, rate_sides, own, halos, sizes):
+def adjoint(flags, grid, rates, rate_sides, near, own, sides, sizes):
     levels, width_x, width_y, _, _ = sizes
-    operands = (grid, rates, rate_sides, *own, *halos)
     extended = (SUBLANES, (width_x + 4) * width_y)
     return pl.pallas_call(
         functools.partial(adjoint_body, levels, width_x, width_y),
         out_shape=jax.ShapeDtypeStruct((levels * width_x * width_y // LANES, LANES), F32),
-        in_specs=[ANY] * 13,
+        in_specs=[SMEM] + [VMEM] * 9,
         out_specs=VMEM,
-        scratch_shapes=buffers(operands)
-        + [pltpu.SemaphoreType.DMA((13,)), pltpu.VMEM(extended, F32), pltpu.VMEM(extended, F32)],
+        scratch_shapes=[pltpu.VMEM(extended, F32), pltpu.VMEM(extended, F32)],
         compiler_params=params(8),
         cost_estimate=cost(6),
         name="adjoint",
-    )(*operands)
+    )(flags, grid, rates, rate_sides, *near, *own, *sides)
 
 
 def local_program(
@@ -945,45 +1015,42 @@
     diff_rows = tile_rows(diffusivity[None])
     width = w_first.shape[2]
     half = subs // 2
-    parity = lax.rem(lax.axis_index("sub"), 2).reshape(1)
-    same_core = [list(range(core, subs, 2)) for core in range(2)]
-    partner = [(i, i ^ 1) for i in range(subs)]
-
-    def spread(packs):
-        return lax.all_to_all(
-            packs, "sub", split_axis=0, concat_axis=0, tiled=True, axis_index_groups=same_core
-        )
-
-    def across(parts):
-        return lax.all_to_all(parts, "tile", split_axis=0, concat_axis=0, tiled=True)
-
-    def swap(packs):
-        return lax.ppermute(packs, "sub", partner)
-
-    top, bottom, low, high = pack_edges(field_rows, diff_rows, levels, width_x, width_y)
-    weights = pack_weights(
-        w_first[0], w_inner[0], w_last[0], b_inner[0], b_last, tiles, half
+    tile_id, sub_id = lax.axis_index("tile"), lax.axis_index("sub")
+    flags = jnp.stack([tile_id % 2, sub_id % 2, tile_id, sub_id]).astype(jnp.int32)
+    area = (levels, width_x, width_y)
+
+    first, other = pack_rows_out(flags, field_rows, diff_rows, *area)
+    near = trade_sides(first, other, "tile")
+    weights = pack_weights(w_first[0], w_inner[0], w_last[0], b_inner[0], b_last, tiles)
+    own_weights = [weights] + [
+        lax.ppermute(weights, "sub", partners(subs, 2 * c)) for c in range(1, half)
+    ]
+    own = pack_columns_out(flags, field_rows, diff_rows, *near, *area)
+    sides = trade_sides(*own, "sub")
+    cells_of = slot_cells(flags, send_counts[0], column_order[0], sizes)
+    rows, rates, rate_sides = forward(
+        flags, field_rows, target_rows, diff_rows, near, own, sides, sizes
     )
-    halos = exchange(top, bottom, low, high)
-    own_weights = spread(weights)
-    other_weights = swap(own_weights)
-    cells_of = slot_cells(parity, send_counts[0], column_order[0], sizes)
-    rows, rates, rate_sides = forward(field_rows, target_rows, diff_rows, low, high, halos, sizes)
+    other_weights = [lax.ppermute(pack, "sub", partners(subs, 1)) for pack in own_weights]
     back, own_grads = network(cells_of, own_weights, rows, None, 0, levels, width, subs)
-    back, other_grads = network(
-        cells_of, other_weights, rows, back, half, levels, width, subs
-    )
-    partner_grads = swap(other_grads)
-    grid, g_top, g_bottom, g_low, g_high = collect(back, sizes)
+    back, other_grads = network(cells_of, other_weights, rows, back, half, levels, width, subs)
+    partner_grads = lax.ppermute(other_grads, "sub", partners(subs, 1))
+    grid, g_first, g_other = collect(flags, back, sizes)
+    g_near = trade_sides(g_first, g_other, "tile")
     both_grads = add_pair(own_grads, partner_grads)
-    spread_grads = spread(both_grads)
-    g_halos = exchange(g_top, g_bottom, g_low, g_high)
-    mine = sum_parts(spread_grads, 0)
-    parts = across(mine.reshape(tiles, -1, LANES))
-    result = adjoint(grid, rates, rate_sides, (g_low, g_high), g_halos, sizes)
-    summed = sum_parts(parts, tiles)
-    whole = across(summed).reshape(-1, LANES)
-    steps = make_steps(whole, levels, width)
+    arrived = [both_grads[0]] + [
+        lax.ppermute(both_grads[c], "sub", partners(subs, 2 * c)) for c in range(1, half)
+    ]
+    g_own = pack_columns_back(flags, grid, *g_near, *area)
+    g_sides = trade_sides(*g_own, "sub")
+    result = adjoint(flags, grid, rates, rate_sides, g_near, g_own, g_sides, sizes)
+    shares = sum_and_share(flags, arrived, tiles)
+    mine = [shares[0]] + [
+        lax.ppermute(shares[d], "tile", partners(tiles, d)) for d in range(1, tiles)
+    ]
+    piece = sum_parts(mine)
+    pieces = [piece] + [lax.ppermute(piece, "tile", partners(tiles, d)) for d in range(1, tiles)]
+    steps = make_steps(flags, pieces, levels, width)
     return (
         untile_rows(result, levels, width_x, width_y),
         steps[0][None], steps[1][None], steps[2].T[None], steps[3][None], steps[4],

time: 150 us -> 113 us (0.75)
  blocking collectives: 48.8 us -> 0 us
  waiting for transfers between devices: 15.2 us -> 31.4 us
  local copies, waits for them, and re-layouts: 13 us -> 5.78 us
  starting transfers between devices: 25.7 us -> 29.8 us
    all_to_all x3 -> x0, blocking collectives: 48.8 us -> none  [the longest x2 38.2 us: spread(): lax.all_to_all(packs, 'sub', split_axis=0, concat_axis=0, tiled=True, axi...]
    ppermute x18 -> x25, waiting for transfers between devices: 15.2 us -> 31.4 us  [the longest x3 12.4 us: local_program(): lax.ppermute(both_grads[c], 'sub', partners(subs, 2 * c))]
    ppermute x18 -> x25, starting transfers between devices: 22.3 us -> 29.8 us  [the longest x4 9.67 us: trade_sides(): lax.ppermute(other, axis, beyond(size))]
    unnamed x46 -> x24, local copies, waits for them, and re-layouts: 13 us -> 5.78 us
    all_to_all x1 -> x0, starting transfers between devices: 3.45 us -> none  [across(): lax.all_to_all(parts, 'tile', split_axis=0, concat_axis=0, tiled=True)]
    pallas_call x6 -> x8, Pallas kernels: 5.07 us -> 7.02 us  [the longest x1 1.87 us: make_steps(): pl.pallas_call(functools.partial(steps_body, levels, width, float(count),...]
    pallas_call x1, Pallas kernels: 8 us -> 6.38 us  [forward(): pl.pallas_call(functools.partial(forward_body, levels, width_x, width_y),...]
  transfers between devices with their start and end apart: 19 -> 25, of which waited for: 6 -> 11; matrix products, arithmetic and copies ran while one was open for 0% -> 0% of each run, Pallas kernels for 21% -> 27%
where the time goes in v3:
time: 113 us; the launch traced here: 112 us
  Pallas kernels  44.5 us (39%)
  waiting for transfers between devices  31.4 us (28%)
  starting transfers between devices  29.8 us (26%)
  local copies, waits for them, and re-layouts  5.78 us (5%)
    pallas_call x2, Pallas kernels, network(): pl.pallas_call(body, grid=(blocks,), out_shape=[jax.ShapeDtypeStruct((cel...  21.8 us
    ppermute x3, waiting for transfers between devices, local_program(): lax.ppermute(both_grads[c], 'sub', partners(subs, 2 * c))  12.4 us
    ppermute x4, starting transfers between devices, trade_sides(): lax.ppermute(other, axis, beyond(size))  9.67 us
    ppermute x3, waiting for transfers between devices, local_program(): lax.ppermute(weights, 'sub', partners(subs, 2 * c))  7.46 us
    ppermute x4, waiting for transfers between devices, trade_sides(): lax.ppermute(other, axis, beyond(size))  6.85 us
    pallas_call x1, Pallas kernels, forward(): pl.pallas_call(functools.partial(forward_body, levels, width_x, width_y),...  6.38 us
    unnamed x24, local copies, waits for them, and re-layouts  5.78 us
    pallas_call x1, Pallas kernels, adjoint(): pl.pallas_call(functools.partial(adjoint_body, levels, width_x, width_y),...  5.55 us
  transfers between devices with their start and end apart: 25, of which 11 were waited for; matrix products, arithmetic and copies ran while one was open for 0% of the time, Pallas kernels for 27%

profile of v3, /device:TPU:0, one launch (start us, length us, event | category | flops | bytes accessed | tf_op | source)
XLA Modules:
  0.0 112.3 jit_solution(7637960504248749682)
XLA Ops:
  0.7 1.0 copy-done.3
  1.6 0.8 copy-done.6
  2.4 0.8 copy-done.7
  3.1 0.7 copy-done.8
  3.8 0.7 copy-done.10
  4.5 0.4 pack_weights.1.refs_0_
  4.9 4.0 %collective-permute-start.5 = (bf16[1088,128]{1,0:T(8,128)(2,1)S(1)}, bf16[1088,128]{1,0:T(8,128)(2,1)S(1)}, u32[]{:S(2)}, u32[]{:S(2)}) collective-permute-start(bf16[1088,128]{1,0:T(8,128)(2,1)S(1)} %pack_weights.1.refs_0_), channel_id=1, source_target_pairs={{0,6},{1,7},{2,4},{3,5},{4,2},{5,3},{6,0},{7,1},{8,14},{9,15},{10,... | collective-permute-start | bytes 835592 | tf_op jit(solution)/shard_map/ppermute | solution.py:1026
  8.8 0.5 collective-permute-start.3
  9.4 0.1 collective-permute-start.1
  9.5 0.1 pad_add_fusion.flags
  9.6 1.2 %copy-done = f32[64,16,256]{2,1,0:T(8,128)S(1)} copy-done((f32[64,16,256]{2,1,0:T(8,128)S(1)}, f32[64,16,256]{2,1,0:T(8,128)}, u32[]{:S(2)}) %copy-start) | copy-done | bytes 1048600
  10.8 0.7 copy-done.4
  11.5 0.7 pack_rows.1
  12.2 2.0 %collective-permute-start.7 = (bf16[80,512]{1,0:T(8,128)(2,1)S(1)}, bf16[80,512]{1,0:T(8,128)(2,1)S(1)}, u32[]{:S(2)}, u32[]{:S(2)}) collective-permute-start(bf16[80,512]{1,0:T(8,128)(2,1)S(1)} %get-tuple-element.35), channel_id=1, source_target_pairs={{0,8},{8,0},{16,24},{24,16},{1,9},{9,1},{17,25},{25,17},{2,10},{10... | collective-permute-start | bytes 245768 | tf_op jit(solution)/shard_map/ppermute | solution.py:247
  14.3 0.0 collective-permute-start
  14.3 2.1 %collective-permute-done.5.refs_3_ = bf16[1088,128]{1,0:T(8,128)(2,1)S(1)} collective-permute-done((bf16[1088,128]{1,0:T(8,128)(2,1)S(1)}, bf16[1088,128]{1,0:T(8,128)(2,1)S(1)}, u32[]{:S(2)}, u32[]{:S(2)}) %collective-permute-start.5) | collective-permute-done | bytes 278560 | tf_op jit(solution)/shard_map/ppermute | solution.py:1026
  16.4 0.0 collective-permute-start.6
  16.4 5.1 %collective-permute-done.3.refs_2_ = bf16[1088,128]{1,0:T(8,128)(2,1)S(1)} collective-permute-done((bf16[1088,128]{1,0:T(8,128)(2,1)S(1)}, bf16[1088,128]{1,0:T(8,128)(2,1)S(1)}, u32[]{:S(2)}, u32[]{:S(2)}) %collective-permute-start.3) | collective-permute-done | bytes 278560 | tf_op jit(solution)/shard_map/ppermute | solution.py:1026
  21.5 0.0 collective-permute-start.4
  21.5 0.3 collective-permute-done.1.refs_1_
  21.8 0.2 collective-permute-start.2
  22.0 0.0 collective-permute-done.7.near
  22.0 3.8 %collective-permute-start.8 = (bf16[80,512]{1,0:T(8,128)(2,1)S(1)}, bf16[80,512]{1,0:T(8,128)(2,1)S(1)}, u32[]{:S(2)}, u32[]{:S(2)}) collective-permute-start(bf16[80,512]{1,0:T(8,128)(2,1)S(1)} %get-tuple-element.36), channel_id=1, source_target_pairs={{0,24},{8,16},{16,8},{24,0},{1,25},{9,17},{17,9},{25,1},{2,26},{10... | collective-permute-start | bytes 245768 | tf_op jit(solution)/shard_map/ppermute | solution.py:247
  25.8 2.8 %collective-permute-done.8.far = bf16[80,512]{1,0:T(8,128)(2,1)S(1)} collective-permute-done((bf16[80,512]{1,0:T(8,128)(2,1)S(1)}, bf16[80,512]{1,0:T(8,128)(2,1)S(1)}, u32[]{:S(2)}, u32[]{:S(2)}) %collective-permute-start.8) | collective-permute-done | bytes 81952 | tf_op jit(solution)/shard_map/ppermute | solution.py:247
  28.6 1.6 %pack_columns.1 = (bf16[80,128]{1,0:T(8,128)(2,1)S(1)}, bf16[80,128]{1,0:T(8,128)(2,1)S(1)}) custom-call(s32[4]{0:T(128)S(1)} %pad_add_fusion.flags, f32[2048,128]{1,0:T(8,128)S(1)} %bitcast.42, f32[32,128]{1,0:T(8,128)S(1)} %bitcast.51, bf16[80,512]{1,0:T(8,128)(2,1)S(1)} %collective-permute-done.7.near, bf16[80,512]{1,0:T(8,128)(2,1)S(1)} %collective-permute-done.8.far), custom_call_target="tpu_custom_call" | custom-call | bytes 3000000 | tf_op jit(solution)/shard_map/pack_columns/pallas_call | solution.py:198
  30.2 0.1 collective-permute-start.9
  30.3 1.2 %collective-permute-done.9.side_near = bf16[80,128]{1,0:T(8,128)(2,1)S(1)} collective-permute-done((bf16[80,128]{1,0:T(8,128)(2,1)S(1)}, bf16[80,128]{1,0:T(8,128)(2,1)S(1)}, u32[]{:S(2)}, u32[]{:S(2)}) %collective-permute-start.9) | collective-permute-done | bytes 20512 | tf_op jit(solution)/shard_map/ppermute | solution.py:247
  31.5 1.5 %collective-permute-start.10 = (bf16[80,128]{1,0:T(8,128)(2,1)S(1)}, bf16[80,128]{1,0:T(8,128)(2,1)S(1)}, u32[]{:S(2)}, u32[]{:S(2)}) collective-permute-start(bf16[80,128]{1,0:T(8,128)(2,1)S(1)} %get-tuple-element.38.own_far), channel_id=1, source_target_pairs={{0,7},{1,2},{2,1},{3,4},{4,3},{5,6},{6,5},{7,0},{8,15},{9,10},{10,... | collective-permute-start | bytes 61448 | tf_op jit(solution)/shard_map/ppermute | solution.py:247
  33.0 1.5 %slot_cells.1 = s32[32,128]{1,0:T(8,128)S(1)} custom-call(s32[4]{0:T(128)S(1)} %pad_add_fusion.flags, s32[32]{0:T(128)S(1)} %bitcast.56, s32[44,128]{1,0:T(8,128)S(1)} %pad_bitcast_fusion.order), custom_call_target="tpu_custom_call" | custom-call | bytes 6000000 | tf_op jit(solution)/shard_map/slot_cells/pallas_call | solution.py:406
  34.5 1.1 collective-permute-done.10.side_far
  35.6 6.4 %forward.1 = (f32[4096,128]{1,0:T(8,128)S(1)}, f32[8,5120]{1,0:T(8,128)S(1)}, f32[48,128]{1,0:T(8,128)S(1)}) custom-call(s32[4]{0:T(128)S(1)} %pad_add_fusion.flags, f32[2048,128]{1,0:T(8,128)S(1)} %bitcast.43, f32[2048,128]{1,0:T(8,128)S(1)} %bitcast.44, f32[32,128]{1,0:T(8,128)S(1)} %bitcast.52, bf16[80,512]{1,0:T(8,128)(2,1)S(1)} %collective-permute-done.7.near, ...), custom_call_target="tpu_custom_call" | custom-call | bytes 24000000 | tf_op jit(solution)/shard_map/forward/pallas_call | solution.py:343
  42.0 10.9 %network.2 = (f32[4096,128]{1,0:T(8,128)S(1)}, bf16[4,1088,128]{2,1,0:T(8,128)(2,1)S(1)}) custom-call(s32[8,1,512]{2,1,0:T(1,128)S(1)} %bitcast.45, s32[8,1,512]{2,1,0:T(1,128)S(1)} %bitcast.46, bf16[1088,128]{1,0:T(8,128)(2,1)S(1)} %pack_weights.1.refs_0_, bf16[1088,128]{1,0:T(8,128)(2,1)S(1)} %collective-permute-done.1.refs_1_, ...), custom_call_target="tpu_custom_call" | custom-call | bytes 36000000 | tf_op jit(solution)/shard_map/network/pallas_call | solution.py:733
  52.9 0.0 collective-permute-done.4.refs_2_
  52.9 0.0 collective-permute-done.2.refs_1_
  52.9 10.9 %network.3 = (f32[4096,128]{1,0:T(8,128)S(1)}, bf16[4,1088,128]{2,1,0:T(8,128)(2,1)S(1)}) custom-call(s32[8,1,512]{2,1,0:T(1,128)S(1)} %bitcast.47, s32[8,1,512]{2,1,0:T(1,128)S(1)} %bitcast.48, bf16[1088,128]{1,0:T(8,128)(2,1)S(1)} %collective-permute-done.refs_0_, ...), custom_call_target="tpu_custom_call", output_to_operand_aliasing={{0}: (7, {})} | custom-call | bytes 36000000 | tf_op jit(solution)/shard_map/network/pallas_call | solution.py:733
  63.8 0.1 collective-permute-start.15
  63.9 2.7 %collective-permute-done.15.other = bf16[4,1088,128]{2,1,0:T(8,128)(2,1)S(1)} collective-permute-done((bf16[4,1088,128]{2,1,0:T(8,128)(2,1)S(1)}, bf16[4,1088,128]{2,1,0:T(8,128)(2,1)S(1)}, u32[]{:S(2)}, u32[]{:S(2)}) %collective-permute-start.15) | collective-permute-done | bytes 1114144 | tf_op jit(solution)/shard_map/ppermute | solution.py:1037
  66.6 0.3 add_pair.1
  66.9 1.3 %collective-permute-start.16 = (bf16[1088,128]{1,0:T(8,128)(2,1)S(1)}, bf16[1088,128]{1,0:T(8,128)(2,1)S(1)}, u32[]{:S(2)}, u32[]{:S(2)}) collective-permute-start(bf16[1088,128]{1,0:T(8,128)(2,1)S(1)} %get-tuple-element.52), channel_id=1, source_target_pairs={{0,2},{1,3},{2,0},{3,1},{4,6},{5,7},{6,4},{7,5},{8,10},{9,11},{10,... | collective-permute-start | bytes 835592 | tf_op jit(solution)/shard_map/ppermute | solution.py:1042
  68.2 0.8 collective-permute-start.17
  69.0 1.4 %collective-permute-start.18 = (bf16[1088,128]{1,0:T(8,128)(2,1)S(1)}, bf16[1088,128]{1,0:T(8,128)(2,1)S(1)}, u32[]{:S(2)}, u32[]{:S(2)}) collective-permute-start(bf16[1088,128]{1,0:T(8,128)(2,1)S(1)} %get-tuple-element.54), channel_id=1, source_target_pairs={{0,6},{1,7},{2,4},{3,5},{4,2},{5,3},{6,0},{7,1},{8,14},{9,15},{10,... | collective-permute-start | bytes 835592 | tf_op jit(solution)/shard_map/ppermute | solution.py:1042
  70.4 6.0 %collective-permute-done.16.refs_1_ = bf16[1088,128]{1,0:T(8,128)(2,1)S(1)} collective-permute-done((bf16[1088,128]{1,0:T(8,128)(2,1)S(1)}, bf16[1088,128]{1,0:T(8,128)(2,1)S(1)}, u32[]{:S(2)}, u32[]{:S(2)}) %collective-permute-start.16) | collective-permute-done | bytes 278560 | tf_op jit(solution)/shard_map/ppermute | solution.py:1042
  76.5 6.4 %collective-permute-done.17.refs_2_ = bf16[1088,128]{1,0:T(8,128)(2,1)S(1)} collective-permute-done((bf16[1088,128]{1,0:T(8,128)(2,1)S(1)}, bf16[1088,128]{1,0:T(8,128)(2,1)S(1)}, u32[]{:S(2)}, u32[]{:S(2)}) %collective-permute-start.17) | collective-permute-done | bytes 278560 | tf_op jit(solution)/shard_map/ppermute | solution.py:1042
  82.8 0.0 collective-permute-done.18.refs_3_
  82.8 0.8 sum_and_share.1
  83.7 1.4 %collective-permute-start.19 = (bf16[272,128]{1,0:T(8,128)(2,1)S(1)}, bf16[272,128]{1,0:T(8,128)(2,1)S(1)}, u32[]{:S(2)}, u32[]{:S(2)}) collective-permute-start(bf16[272,128]{1,0:T(8,128)(2,1)S(1)} %get-tuple-element.56), channel_id=1, source_target_pairs={{0,8},{8,0},{16,24},{24,16},{1,9},{9,1},{17,25},{25,17},{2,10},{10... | collective-permute-start | bytes 208904 | tf_op jit(solution)/shard_map/ppermute | solution.py:1049
  85.1 2.6 %collective-permute-start.20 = (bf16[272,128]{1,0:T(8,128)(2,1)S(1)}, bf16[272,128]{1,0:T(8,128)(2,1)S(1)}, u32[]{:S(2)}, u32[]{:S(2)}) collective-permute-start(bf16[272,128]{1,0:T(8,128)(2,1)S(1)} %get-tuple-element.57), channel_id=1, source_target_pairs={{0,16},{8,24},{16,0},{24,8},{1,17},{9,25},{17,1},{25,9},{2,18},{10... | collective-permute-start | bytes 208904 | tf_op jit(solution)/shard_map/ppermute | solution.py:1049
  87.8 0.4 collective-permute-start.21
  88.1 2.3 %collect.1 = (f32[64,4096]{1,0:T(8,128)S(1)}, bf16[64,512]{1,0:T(8,128)(2,1)S(1)}, bf16[64,512]{1,0:T(8,128)(2,1)S(1)}) custom-call(s32[4]{0:T(128)S(1)} %pad_add_fusion.flags, f32[4096,128]{1,0:T(8,128)S(1)} %get-tuple-element.41.rows), custom_call_target="tpu_custom_call" | custom-call | bytes 9000000 | tf_op jit(solution)/shard_map/collect/pallas_call | solution.py:913
  90.4 0.5 collective-permute-start.11
  91.0 3.1 %collective-permute-start.12 = (bf16[64,512]{1,0:T(8,128)(2,1)S(1)}, bf16[64,512]{1,0:T(8,128)(2,1)S(1)}, u32[]{:S(2)}, u32[]{:S(2)}) collective-permute-start(bf16[64,512]{1,0:T(8,128)(2,1)S(1)} %get-tuple-element.46), channel_id=1, source_target_pairs={{0,24},{8,16},{16,8},{24,0},{1,25},{9,17},{17,9},{25,1},{2,26},{10... | collective-permute-start | bytes 196616 | tf_op jit(solution)/shard_map/ppermute | solution.py:247
  94.0 0.0 collective-permute-done.19.refs_1_
  94.0 0.0 collective-permute-done.20.refs_2_
  94.0 0.7 collective-permute-done.21.refs_3_
  94.8 0.8 collective-permute-start.24
  95.5 1.1 %collective-permute-start.23 = (bf16[272,128]{1,0:T(8,128)(2,1)S(1)}, bf16[272,128]{1,0:T(8,128)(2,1)S(1)}, u32[]{:S(2)}, u32[]{:S(2)}) collective-permute-start(bf16[272,128]{1,0:T(8,128)(2,1)S(1)} %sum_parts.1.refs_0_), channel_id=1, source_target_pairs={{0,16},{8,24},{16,0},{24,8},{1,17},{9,25},{17,1},{25,9},{2,18},{10... | collective-permute-start | bytes 208904 | tf_op jit(solution)/shard_map/ppermute | solution.py:1052
  96.7 2.6 %collective-permute-start.22 = (bf16[272,128]{1,0:T(8,128)(2,1)S(1)}, bf16[272,128]{1,0:T(8,128)(2,1)S(1)}, u32[]{:S(2)}, u32[]{:S(2)}) collective-permute-start(bf16[272,128]{1,0:T(8,128)(2,1)S(1)} %sum_parts.1.refs_0_), channel_id=1, source_target_pairs={{0,8},{8,0},{16,24},{24,16},{1,9},{9,1},{17,25},{25,17},{2,10},{10... | collective-permute-start | bytes 208904 | tf_op jit(solution)/shard_map/ppermute | solution.py:1052
  99.2 1.3 %pack_back.1 = (bf16[64,128]{1,0:T(8,128)(2,1)S(1)}, bf16[64,128]{1,0:T(8,128)(2,1)S(1)}) custom-call(s32[4]{0:T(128)S(1)} %pad_add_fusion.flags, f32[64,4096]{1,0:T(8,128)S(1)} %get-tuple-element.42.grid, bf16[64,512]{1,0:T(8,128)(2,1)S(1)} %collective-permute-done.11.near, bf16[64,512]{1,0:T(8,128)(2,1)S(1)} %collective-permute-done.12.far), custom_call_target="tpu_custom_call" | custom-call | bytes 3000000 | tf_op jit(solution)/shard_map/pack_back/pallas_call | solution.py:226
  100.5 0.1 collective-permute-start.13
  100.6 1.3 %collective-permute-start.14 = (bf16[64,128]{1,0:T(8,128)(2,1)S(1)}, bf16[64,128]{1,0:T(8,128)(2,1)S(1)}, u32[]{:S(2)}, u32[]{:S(2)}) collective-permute-start(bf16[64,128]{1,0:T(8,128)(2,1)S(1)} %get-tuple-element.48.own_far), channel_id=1, source_target_pairs={{0,7},{1,2},{2,1},{3,4},{4,3},{5,6},{6,5},{7,0},{8,15},{9,10},{10,... | collective-permute-start | bytes 49160 | tf_op jit(solution)/shard_map/ppermute | solution.py:247
  101.9 2.9 %collective-permute-done.14.side_far = bf16[64,128]{1,0:T(8,128)(2,1)S(1)} collective-permute-done((bf16[64,128]{1,0:T(8,128)(2,1)S(1)}, bf16[64,128]{1,0:T(8,128)(2,1)S(1)}, u32[]{:S(2)}, u32[]{:S(2)}) %collective-permute-start.14) | collective-permute-done | bytes 16416 | tf_op jit(solution)/shard_map/ppermute | solution.py:247
  104.9 5.6 %adjoint.1 = f32[2048,128]{1,0:T(8,128)} custom-call(s32[4]{0:T(128)S(1)} %pad_add_fusion.flags, f32[64,4096]{1,0:T(8,128)S(1)} %get-tuple-element.42.grid, f32[8,5120]{1,0:T(8,128)S(1)} %get-tuple-element.43.wide, f32[48,128]{1,0:T(8,128)S(1)} %get-tuple-element.44.rate_sides, bf16[64,512]{1,0:T(8,128)(2,1)S(1)} %collective-permute-done.11.near, ...), custom_call_target="tpu_custom_call" | custom-call | bytes 18000000 | tf_op jit(solution)/shard_map/adjoint/pallas_call | solution.py:994
  110.4 0.0 collective-permute-done.24.refs_3_
  110.4 1.9 %make_steps.1 = (f32[64,192]{1,0:T(8,128)}, f32[3,192,192]{2,1,0:T(8,128)}, f32[64,192]{1,0:T(8,128)}, f32[4,192]{1,0:T(4,128)}, f32[1,64]{1,0:T(1,128)}) custom-call(s32[4]{0:T(128)S(1)} %pad_add_fusion.flags, bf16[272,128]{1,0:T(8,128)(2,1)S(1)} %sum_parts.1.refs_0_, bf16[272,128]{1,0:T(8,128)(2,1)S(1)} %collective-permute-done.22.refs_1_, ...), custom_call_target="tpu_custom_call" | custom-call | bytes 6000000 | tf_op jit(solution)/shard_map/make_steps/pallas_call | solution.py:870
  (26 shorter events, 0.1 us)
Async XLA Ops:
  0.6 32.3 %copy-start.9 = (s32[1,32]{1,0:T(1,128)S(1)}, s32[1,32]{1,0:T(1,128)}, u32[]{:S(2)}) copy-start(s32[1,32]{1,0:T(1,128)} %param.14) | copy-start | bytes 388
  0.6 1.0 copy-start.3
  1.6 0.8 copy-start.6
  2.4 0.8 copy-start.7
  3.1 0.7 copy-start.8
  3.8 0.7 copy-start.10
  4.5 28.5 %copy-start.11 = (s32[1,4096]{1,0:T(1,128)S(1)}, s32[1,4096]{1,0:T(1,128)}, u32[]{:S(2)}) copy-start(s32[1,4096]{1,0:T(1,128)} %param.13) | copy-start | bytes 49156
  4.5 31.1 %copy-start.5 = (f32[16,256]{1,0:T(8,128)S(1)}, f32[16,256]{1,0:T(8,128)}, u32[]{:S(2)}) copy-start(f32[16,256]{1,0:T(8,128)} %param.12) | copy-start | bytes 49156
  4.9 11.5 %collective-permute-start.5 = (bf16[1088,128]{1,0:T(8,128)(2,1)S(1)}, bf16[1088,128]{1,0:T(8,128)(2,1)S(1)}, u32[]{:S(2)}, u32[]{:S(2)}) collective-permute-start(bf16[1088,128]{1,0:T(8,128)(2,1)S(1)} %pack_weights.1.refs_0_), channel_id=1, source_target_pairs={{0,6},{1,7},{2,4},{3,5},{4,2},{5,3},{6,0},{7,1},{8,14},{9,15},{10,... | collective-permute-start | bytes 835592 | tf_op jit(solution)/shard_map/ppermute | solution.py:1026
  8.8 12.6 %collective-permute-start.3 = (bf16[1088,128]{1,0:T(8,128)(2,1)S(1)}, bf16[1088,128]{1,0:T(8,128)(2,1)S(1)}, u32[]{:S(2)}, u32[]{:S(2)}) collective-permute-start(bf16[1088,128]{1,0:T(8,128)(2,1)S(1)} %pack_weights.1.refs_0_), channel_id=1, source_target_pairs={{0,4},{1,5},{2,6},{3,7},{4,0},{5,1},{6,2},{7,3},{8,12},{9,13},{10,... | collective-permute-start | bytes 835592 | tf_op jit(solution)/shard_map/ppermute | solution.py:1026
  9.4 12.4 %collective-permute-start.1 = (bf16[1088,128]{1,0:T(8,128)(2,1)S(1)}, bf16[1088,128]{1,0:T(8,128)(2,1)S(1)}, u32[]{:S(2)}, u32[]{:S(2)}) collective-permute-start(bf16[1088,128]{1,0:T(8,128)(2,1)S(1)} %pack_weights.1.refs_0_), channel_id=1, source_target_pairs={{0,2},{1,3},{2,0},{3,1},{4,6},{5,7},{6,4},{7,5},{8,10},{9,11},{10,... | collective-permute-start | bytes 835592 | tf_op jit(solution)/shard_map/ppermute | solution.py:1026
  9.6 1.2 %copy-start = (f32[64,16,256]{2,1,0:T(8,128)S(1)}, f32[64,16,256]{2,1,0:T(8,128)}, u32[]{:S(2)}) copy-start(f32[64,16,256]{2,1,0:T(8,128)} %param.10) | copy-start | bytes 3145732
  10.8 0.7 copy-start.4
  11.5 24.1 %copy-start.1 = (f32[64,16,256]{2,1,0:T(8,128)S(1)}, f32[64,16,256]{2,1,0:T(8,128)}, u32[]{:S(2)}) copy-start(f32[64,16,256]{2,1,0:T(8,128)} %param.10) | copy-start | bytes 3145732
  11.5 24.1 %copy-start.2 = (f32[64,16,256]{2,1,0:T(8,128)S(1)}, f32[64,16,256]{2,1,0:T(8,128)}, u32[]{:S(2)}) copy-start(f32[64,16,256]{2,1,0:T(8,128)} %param.11) | copy-start | bytes 3145732
  12.2 9.8 %collective-permute-start.7 = (bf16[80,512]{1,0:T(8,128)(2,1)S(1)}, bf16[80,512]{1,0:T(8,128)(2,1)S(1)}, u32[]{:S(2)}, u32[]{:S(2)}) collective-permute-start(bf16[80,512]{1,0:T(8,128)(2,1)S(1)} %get-tuple-element.35), channel_id=1, source_target_pairs={{0,8},{8,0},{16,24},{24,16},{1,9},{9,1},{17,25},{25,17},{2,10},{10... | collective-permute-start | bytes 245768 | tf_op jit(solution)/shard_map/ppermute | solution.py:247
  14.3 38.6 %collective-permute-start = (bf16[1088,128]{1,0:T(8,128)(2,1)S(1)}, bf16[1088,128]{1,0:T(8,128)(2,1)S(1)}, u32[]{:S(2)}, u32[]{:S(2)}) collective-permute-start(bf16[1088,128]{1,0:T(8,128)(2,1)S(1)} %pack_weights.1.refs_0_), channel_id=1, source_target_pairs={{0,1},{1,0},{2,3},{3,2},{4,5},{5,4},{6,7},{7,6},{8,9},{9,8},{10,11... | collective-permute-start | bytes 835592 | tf_op jit(solution)/shard_map/ppermute | solution.py:1034
  16.4 36.5 %collective-permute-start.6 = (bf16[1088,128]{1,0:T(8,128)(2,1)S(1)}, bf16[1088,128]{1,0:T(8,128)(2,1)S(1)}, u32[]{:S(2)}, u32[]{:S(2)}) collective-permute-start(bf16[1088,128]{1,0:T(8,128)(2,1)S(1)} %collective-permute-done.5.refs_3_), channel_id=1, source_target_pairs={{0,1},{1,0},{2,3},{3,2},{4,5},{5,4},{6,7},{7,6},{8,9},{9,8},{10,11... | collective-permute-start | bytes 835592 | tf_op jit(solution)/shard_map/ppermute | solution.py:1034
  21.5 31.4 %collective-permute-start.4 = (bf16[1088,128]{1,0:T(8,128)(2,1)S(1)}, bf16[1088,128]{1,0:T(8,128)(2,1)S(1)}, u32[]{:S(2)}, u32[]{:S(2)}) collective-permute-start(bf16[1088,128]{1,0:T(8,128)(2,1)S(1)} %collective-permute-done.3.refs_2_), channel_id=1, source_target_pairs={{0,1},{1,0},{2,3},{3,2},{4,5},{5,4},{6,7},{7,6},{8,9},{9,8},{10,11... | collective-permute-start | bytes 835592 | tf_op jit(solution)/shard_map/ppermute | solution.py:1034
  21.8 31.1 %collective-permute-start.2 = (bf16[1088,128]{1,0:T(8,128)(2,1)S(1)}, bf16[1088,128]{1,0:T(8,128)(2,1)S(1)}, u32[]{:S(2)}, u32[]{:S(2)}) collective-permute-start(bf16[1088,128]{1,0:T(8,128)(2,1)S(1)} %collective-permute-done.1.refs_1_), channel_id=1, source_target_pairs={{0,1},{1,0},{2,3},{3,2},{4,5},{5,4},{6,7},{7,6},{8,9},{9,8},{10,11... | collective-permute-start | bytes 835592 | tf_op jit(solution)/shard_map/ppermute | solution.py:1034
  22.0 6.6 %collective-permute-start.8 = (bf16[80,512]{1,0:T(8,128)(2,1)S(1)}, bf16[80,512]{1,0:T(8,128)(2,1)S(1)}, u32[]{:S(2)}, u32[]{:S(2)}) collective-permute-start(bf16[80,512]{1,0:T(8,128)(2,1)S(1)} %get-tuple-element.36), channel_id=1, source_target_pairs={{0,24},{8,16},{16,8},{24,0},{1,25},{9,17},{17,9},{25,1},{2,26},{10... | collective-permute-start | bytes 245768 | tf_op jit(solution)/shard_map/ppermute | solution.py:247
  30.2 1.3 %collective-permute-start.9 = (bf16[80,128]{1,0:T(8,128)(2,1)S(1)}, bf16[80,128]{1,0:T(8,128)(2,1)S(1)}, u32[]{:S(2)}, u32[]{:S(2)}) collective-permute-start(bf16[80,128]{1,0:T(8,128)(2,1)S(1)} %get-tuple-element.37.own_near), channel_id=1, source_target_pairs={{0,1},{1,0},{2,3},{3,2},{4,5},{5,4},{6,7},{7,6},{8,9},{9,8},{10,11... | collective-permute-start | bytes 61448 | tf_op jit(solution)/shard_map/ppermute | solution.py:247
  31.5 4.1 %collective-permute-start.10 = (bf16[80,128]{1,0:T(8,128)(2,1)S(1)}, bf16[80,128]{1,0:T(8,128)(2,1)S(1)}, u32[]{:S(2)}, u32[]{:S(2)}) collective-permute-start(bf16[80,128]{1,0:T(8,128)(2,1)S(1)} %get-tuple-element.38.own_far), channel_id=1, source_target_pairs={{0,7},{1,2},{2,1},{3,4},{4,3},{5,6},{6,5},{7,0},{8,15},{9,10},{10,... | collective-permute-start | bytes 61448 | tf_op jit(solution)/shard_map/ppermute | solution.py:247
  63.8 2.8 %collective-permute-start.15 = (bf16[4,1088,128]{2,1,0:T(8,128)(2,1)S(1)}, bf16[4,1088,128]{2,1,0:T(8,128)(2,1)S(1)}, u32[]{:S(2)}, u32[]{:S(2)}) collective-permute-start(bf16[4,1088,128]{2,1,0:T(8,128)(2,1)S(1)} %get-tuple-element.50), channel_id=1, source_target_pairs={{0,1},{1,0},{2,3},{3,2},{4,5},{5,4},{6,7},{7,6},{8,9},{9,8},{10,11... | collective-permute-start | bytes 3342344 | tf_op jit(solution)/shard_map/ppermute | solution.py:1037
  66.9 9.6 %collective-permute-start.16 = (bf16[1088,128]{1,0:T(8,128)(2,1)S(1)}, bf16[1088,128]{1,0:T(8,128)(2,1)S(1)}, u32[]{:S(2)}, u32[]{:S(2)}) collective-permute-start(bf16[1088,128]{1,0:T(8,128)(2,1)S(1)} %get-tuple-element.52), channel_id=1, source_target_pairs={{0,2},{1,3},{2,0},{3,1},{4,6},{5,7},{6,4},{7,5},{8,10},{9,11},{10,... | collective-permute-start | bytes 835592 | tf_op jit(solution)/shard_map/ppermute | solution.py:1042
  68.2 14.6 %collective-permute-start.17 = (bf16[1088,128]{1,0:T(8,128)(2,1)S(1)}, bf16[1088,128]{1,0:T(8,128)(2,1)S(1)}, u32[]{:S(2)}, u32[]{:S(2)}) collective-permute-start(bf16[1088,128]{1,0:T(8,128)(2,1)S(1)} %get-tuple-element.53), channel_id=1, source_target_pairs={{0,4},{1,5},{2,6},{3,7},{4,0},{5,1},{6,2},{7,3},{8,12},{9,13},{10,... | collective-permute-start | bytes 835592 | tf_op jit(solution)/shard_map/ppermute | solution.py:1042
  69.0 13.9 %collective-permute-start.18 = (bf16[1088,128]{1,0:T(8,128)(2,1)S(1)}, bf16[1088,128]{1,0:T(8,128)(2,1)S(1)}, u32[]{:S(2)}, u32[]{:S(2)}) collective-permute-start(bf16[1088,128]{1,0:T(8,128)(2,1)S(1)} %get-tuple-element.54), channel_id=1, source_target_pairs={{0,6},{1,7},{2,4},{3,5},{4,2},{5,3},{6,0},{7,1},{8,14},{9,15},{10,... | collective-permute-start | bytes 835592 | tf_op jit(solution)/shard_map/ppermute | solution.py:1042
  83.7 10.3 %collective-permute-start.19 = (bf16[272,128]{1,0:T(8,128)(2,1)S(1)}, bf16[272,128]{1,0:T(8,128)(2,1)S(1)}, u32[]{:S(2)}, u32[]{:S(2)}) collective-permute-start(bf16[272,128]{1,0:T(8,128)(2,1)S(1)} %get-tuple-element.56), channel_id=1, source_target_pairs={{0,8},{8,0},{16,24},{24,16},{1,9},{9,1},{17,25},{25,17},{2,10},{10... | collective-permute-start | bytes 208904 | tf_op jit(solution)/shard_map/ppermute | solution.py:1049
  85.1 8.9 %collective-permute-start.20 = (bf16[272,128]{1,0:T(8,128)(2,1)S(1)}, bf16[272,128]{1,0:T(8,128)(2,1)S(1)}, u32[]{:S(2)}, u32[]{:S(2)}) collective-permute-start(bf16[272,128]{1,0:T(8,128)(2,1)S(1)} %get-tuple-element.57), channel_id=1, source_target_pairs={{0,16},{8,24},{16,0},{24,8},{1,17},{9,25},{17,1},{25,9},{2,18},{10... | collective-permute-start | bytes 208904 | tf_op jit(solution)/shard_map/ppermute | solution.py:1049
  87.8 7.0 %collective-permute-start.21 = (bf16[272,128]{1,0:T(8,128)(2,1)S(1)}, bf16[272,128]{1,0:T(8,128)(2,1)S(1)}, u32[]{:S(2)}, u32[]{:S(2)}) collective-permute-start(bf16[272,128]{1,0:T(8,128)(2,1)S(1)} %get-tuple-element.58), channel_id=1, source_target_pairs={{0,24},{8,16},{16,8},{24,0},{1,25},{9,17},{17,9},{25,1},{2,26},{10... | collective-permute-start | bytes 208904 | tf_op jit(solution)/shard_map/ppermute | solution.py:1049
  90.4 8.8 %collective-permute-start.11 = (bf16[64,512]{1,0:T(8,128)(2,1)S(1)}, bf16[64,512]{1,0:T(8,128)(2,1)S(1)}, u32[]{:S(2)}, u32[]{:S(2)}) collective-permute-start(bf16[64,512]{1,0:T(8,128)(2,1)S(1)} %get-tuple-element.45), channel_id=1, source_target_pairs={{0,8},{8,0},{16,24},{24,16},{1,9},{9,1},{17,25},{25,17},{2,10},{10... | collective-permute-start | bytes 196616 | tf_op jit(solution)/shard_map/ppermute | solution.py:247
  91.0 8.2 %collective-permute-start.12 = (bf16[64,512]{1,0:T(8,128)(2,1)S(1)}, bf16[64,512]{1,0:T(8,128)(2,1)S(1)}, u32[]{:S(2)}, u32[]{:S(2)}) collective-permute-start(bf16[64,512]{1,0:T(8,128)(2,1)S(1)} %get-tuple-element.46), channel_id=1, source_target_pairs={{0,24},{8,16},{16,8},{24,0},{1,25},{9,17},{17,9},{25,1},{2,26},{10... | collective-permute-start | bytes 196616 | tf_op jit(solution)/shard_map/ppermute | solution.py:247
  94.8 15.7 %collective-permute-start.24 = (bf16[272,128]{1,0:T(8,128)(2,1)S(1)}, bf16[272,128]{1,0:T(8,128)(2,1)S(1)}, u32[]{:S(2)}, u32[]{:S(2)}) collective-permute-start(bf16[272,128]{1,0:T(8,128)(2,1)S(1)} %sum_parts.1.refs_0_), channel_id=1, source_target_pairs={{0,24},{8,16},{16,8},{24,0},{1,25},{9,17},{17,9},{25,1},{2,26},{10... | collective-permute-start | bytes 208904 | tf_op jit(solution)/shard_map/ppermute | solution.py:1052
  95.5 14.9 %collective-permute-start.23 = (bf16[272,128]{1,0:T(8,128)(2,1)S(1)}, bf16[272,128]{1,0:T(8,128)(2,1)S(1)}, u32[]{:S(2)}, u32[]{:S(2)}) collective-permute-start(bf16[272,128]{1,0:T(8,128)(2,1)S(1)} %sum_parts.1.refs_0_), channel_id=1, source_target_pairs={{0,16},{8,24},{16,0},{24,8},{1,17},{9,25},{17,1},{25,9},{2,18},{10... | collective-permute-start | bytes 208904 | tf_op jit(solution)/shard_map/ppermute | solution.py:1052
  96.7 13.8 %collective-permute-start.22 = (bf16[272,128]{1,0:T(8,128)(2,1)S(1)}, bf16[272,128]{1,0:T(8,128)(2,1)S(1)}, u32[]{:S(2)}, u32[]{:S(2)}) collective-permute-start(bf16[272,128]{1,0:T(8,128)(2,1)S(1)} %sum_parts.1.refs_0_), channel_id=1, source_target_pairs={{0,8},{8,0},{16,24},{24,16},{1,9},{9,1},{17,25},{25,17},{2,10},{10... | collective-permute-start | bytes 208904 | tf_op jit(solution)/shard_map/ppermute | solution.py:1052
  100.5 1.4 %collective-permute-start.13 = (bf16[64,128]{1,0:T(8,128)(2,1)S(1)}, bf16[64,128]{1,0:T(8,128)(2,1)S(1)}, u32[]{:S(2)}, u32[]{:S(2)}) collective-permute-start(bf16[64,128]{1,0:T(8,128)(2,1)S(1)} %get-tuple-element.47.own_near), channel_id=1, source_target_pairs={{0,1},{1,0},{2,3},{3,2},{4,5},{5,4},{6,7},{7,6},{8,9},{9,8},{10,11... | collective-permute-start | bytes 49160 | tf_op jit(solution)/shard_map/ppermute | solution.py:247
  100.6 4.3 %collective-permute-start.14 = (bf16[64,128]{1,0:T(8,128)(2,1)S(1)}, bf16[64,128]{1,0:T(8,128)(2,1)S(1)}, u32[]{:S(2)}, u32[]{:S(2)}) collective-permute-start(bf16[64,128]{1,0:T(8,128)(2,1)S(1)} %get-tuple-element.48.own_far), channel_id=1, source_target_pairs={{0,7},{1,2},{2,1},{3,4},{4,3},{5,6},{6,5},{7,0},{8,15},{9,10},{10,... | collective-permute-start | bytes 49160 | tf_op jit(solution)/shard_map/ppermute | solution.py:247

commit v4 on v3

--- a/solution.py
+++ b/solution.py
@@ -116,15 +116,12 @@
     for which in range(2):
         low = jnp.zeros((SUBLANES, LANES), F32)
         high = jnp.zeros((SUBLANES, LANES), F32)
-        for x in range(-1, width_x + 1):
+        for x in range(width_x):
             row = row_of(which, x)
             low = jnp.where(lane == 1 + x, row[:, 0:1], low)
             high = jnp.where(lane == 1 + x, row[:, width_y - 1 : width_y], high)
-            if 0 <= x < width_x:
-                low = jnp.where(lane == SECOND + 1 + x, row[:, 1:2], low)
-                high = jnp.where(
-                    lane == SECOND + 1 + x, row[:, width_y - 2 : width_y - 1], high
-                )
+            low = jnp.where(lane == SECOND + 1 + x, row[:, 1:2], low)
+            high = jnp.where(lane == SECOND + 1 + x, row[:, width_y - 2 : width_y - 1], high)
         lows.append(low)
         highs.append(high)
     low = jnp.concatenate(lows, axis=0)
@@ -157,7 +154,7 @@
         in_specs=[SMEM] + [VMEM] * 2,
         out_specs=[VMEM] * 2,
         compiler_params=params(8),
-        cost_estimate=cost(1),
+        cost_estimate=cost(8),
         name="pack_rows",
     )(flags, field_rows, diff_rows)
 
@@ -170,68 +167,94 @@
     return value[which * SUBLANES : (which + 1) * SUBLANES]
 
 
-def column_pack_body(levels, width_x, width_y, flags, field, diff, near, far, first, other):
+def column_pack_body(levels, width_x, width_y, flags, field, diff, first, other):
     def step(double, carry):
-        where = pairs_at(double)
-
-        def row_of(which, x):
-            if 0 <= x < width_x:
-                return load_row(field, double * 2 + which, x, width_x, width_y)
-            return outer_row(flags[0], near, far, where, which, x, width_x, width_y)
-
-        store_columns(where, row_of, width_x, width_y, flags[1], first, other)
+        store_columns(
+            pairs_at(double),
+            lambda which, x: load_row(field, double * 2 + which, x, width_x, width_y),
+            width_x, width_y, flags[1], first, other,
+        )
         return carry
 
     lax.fori_loop(0, levels // (2 * SUBLANES), step, 0)
-    last = pl.ds(levels, 2 * SUBLANES)
-
-    def rate_of(which, x):
-        if 0 <= x < width_x:
-            return load_wide(diff, x, width_y)
-        return outer_row(flags[0], near, far, last, which, x, width_x, width_y)
-
-    store_columns(last, rate_of, width_x, width_y, flags[1], first, other)
-
-
-def pack_columns_out(flags, field_rows, diff_rows, near, far, levels, width_x, width_y):
+    store_columns(
+        pl.ds(levels, 2 * SUBLANES), lambda which, x: load_wide(diff, x, width_y),
+        width_x, width_y, flags[1], first, other,
+    )
+
+
+def pack_columns_out(flags, field_rows, diff_rows, levels, width_x, width_y):
     shape = jax.ShapeDtypeStruct((levels + 2 * SUBLANES, LANES), BF16)
     return pl.pallas_call(
         functools.partial(column_pack_body, levels, width_x, width_y),
+        out_shape=[shape] * 2,
+        in_specs=[SMEM] + [VMEM] * 2,
+        out_specs=[VMEM] * 2,
+        compiler_params=params(8),
+        cost_estimate=cost(2),
+        name="pack_columns",
+    )(flags, field_rows, diff_rows)
+
+
+def back_pack_body(levels, width_x, width_y, flags, grid, first, other):
+    def step(double, carry):
+        store_columns(
+            pairs_at(double),
+            lambda which, x: grid[groups_at(double * 2 + which), x * width_y : (x + 1) * width_y],
+            width_x, width_y, flags[1], first, other,
+        )
+        return carry
+
+    lax.fori_loop(0, levels // (2 * SUBLANES), step, 0)
+
+
+def pack_columns_back(flags, grid, levels, width_x, width_y):
+    shape = jax.ShapeDtypeStruct((levels, LANES), BF16)
+    return pl.pallas_call(
+        functools.partial(back_pack_body, levels, width_x, width_y),
+        out_shape=[shape] * 2,
+        in_specs=[SMEM] + [VMEM],
+        out_specs=[VMEM] * 2,
+        compiler_params=params(8),
+        cost_estimate=cost(2),
+        name="pack_back",
+    )(flags, grid)
+
+
+def corner_body(width_x, width_y, flags, near, far, first_in, other_in, first, other):
+    rows = near.shape[0]
+    lane = lax.broadcasted_iota(jnp.int32, (rows, LANES), 1)
+    near_value = near[...].astype(F32)
+    far_value = far[...].astype(F32)
+    above = jnp.where(flags[0] == 0, far_value[:, width_y:], near_value[:, width_y:])
+    below = jnp.where(flags[0] == 0, near_value[:, :width_y], far_value[:, :width_y])
+
+    def insert(given, edge_of):
+        value = given[...].astype(F32)
+        value = jnp.where(lane == 0, edge_of(above), value)
+        return jnp.where(lane == width_x + 1, edge_of(below), value).astype(BF16)
+
+    def low(row):
+        return row[:, 0:1]
+
+    def high(row):
+        return row[:, width_y - 1 : width_y]
+
+    first[...] = insert(first_in, lambda row: jnp.where(flags[1] == 0, high(row), low(row)))
+    other[...] = insert(other_in, lambda row: jnp.where(flags[1] == 0, low(row), high(row)))
+
+
+def add_corners(flags, near, far, first, other, width_x, width_y):
+    shape = jax.ShapeDtypeStruct(first.shape, BF16)
+    return pl.pallas_call(
+        functools.partial(corner_body, width_x, width_y),
         out_shape=[shape] * 2,
         in_specs=[SMEM] + [VMEM] * 4,
         out_specs=[VMEM] * 2,
         compiler_params=params(8),
         cost_estimate=cost(1),
-        name="pack_columns",
-    )(flags, field_rows, diff_rows, near, far)
-
-
-def back_pack_body(levels, width_x, width_y, flags, grid, near, far, first, other):
-    def step(double, carry):
-        where = pairs_at(double)
-
-        def row_of(which, x):
-            if 0 <= x < width_x:
-                return grid[groups_at(double * 2 + which), x * width_y : (x + 1) * width_y]
-            return outer_row(flags[0], near, far, where, which, x, width_x, width_y)
-
-        store_columns(where, row_of, width_x, width_y, flags[1], first, other)
-        return carry
-
-    lax.fori_loop(0, levels // (2 * SUBLANES), step, 0)
-
-
-def pack_columns_back(flags, grid, near, far, levels, width_x, width_y):
-    shape = jax.ShapeDtypeStruct((levels, LANES), BF16)
-    return pl.pallas_call(
-        functools.partial(back_pack_body, levels, width_x, width_y),
-        out_shape=[shape] * 2,
-        in_specs=[SMEM] + [VMEM] * 3,
-        out_specs=[VMEM] * 2,
-        compiler_params=params(8),
-        cost_estimate=cost(1),
-        name="pack_back",
-    )(flags, grid, near, far)
+        name="add_corners",
+    )(flags, near, far, first, other)
 
 
 def partners(size, offset):
@@ -376,7 +399,7 @@
 
     def expert(block, carry):
         second_half = block // half
-        network_id = mine ^ ((block - second_half * half) * 2 + second_half)
+        network_id = mine ^ ((block - second_half * half) * 2 + 1 - second_half)
         value = jnp.zeros((SUBLANES, LANES), jnp.int32)
         base = jnp.int32(0)
         for t in range(tiles):
@@ -501,16 +524,15 @@
         in_specs=[pl.BlockSpec(memory_space=pltpu.HBM)] * 5,
         out_specs=VMEM,
         scratch_shapes=buffers(operands) + [pltpu.SemaphoreType.DMA((5,))],
-        compiler_params=params(8),
+        compiler_params=params(62),
         cost_estimate=cost(1),
         name="pack_weights",
     )(*operands)
 
 
 def network_body(
-    levels, width, packet,
-    behind, ahead, pack_list, rows, back, grads, packs,
-    taken, given_back, first_in, first_out, inner, last, last_half,
+    levels, width, packet, carried_in,
+    behind, ahead, pack_list, rows, back, grads, taken, given_back, packs, first_in, first_out, inner, last, last_half,
     kept, feeds, slopes, residues,
 ):
     certain = behind[0, 0, 0] >= 0
@@ -530,7 +552,11 @@
 
     @pl.when(block == 0)
     def _():
-        fetch(behind, 0, packet)
+        if carried_in is None:
+            fetch(behind, 0, packet)
+        else:
+            taken[...] = carried_in[0][...]
+            given_back[...] = carried_in[1][...]
         first_in[levels:, :] = jnp.zeros((wide - levels, wide), BF16)
         first_out[...] = jnp.zeros((LANES, wide), BF16)
         first_in[:levels, LANES:] = jnp.zeros((levels, LANES), BF16)
@@ -697,52 +723,66 @@
         tail.append(jnp.zeros((grads.shape[1] - filled - len(tail), LANES), F32))
         put(jnp.concatenate(tail, axis=0))
 
-    @pl.when(block == blocks - 1)
-    def _():
-        deliver(ahead, 0, packet)
-
-
-def network(cells_of, pack_list, rows, back, shift, levels, width, subs):
+    if carried_in is not None:
+
+        @pl.when(block == blocks - 1)
+        def _():
+            deliver(ahead, 0, packet)
+
+
+def network(cells_of, pack_list, rows, before, shift, levels, width, subs):
     cells, doubled = rows.shape
     packet = cells // subs
     blocks = len(pack_list)
     pack_shape = pack_list[0].shape
+    final = before is not None
+    limit = blocks - 1 if final else blocks
+    wide = 2 * LANES
 
     def body(behind, ahead, *refs):
-        names = refs[:blocks]
-        rest = refs[blocks + 1 + (back is not None) :]
-        network_body(levels, width, packet, behind, ahead, names, refs[blocks], *rest)
+        names, rest = refs[:blocks], refs[blocks + 1 :]
+        carried_in = None
+        if final:
+            carried_in, rest = rest[1:3], rest[3:]
+        network_body(
+            levels, width, packet, carried_in, behind, ahead, names, refs[blocks], *rest
+        )
 
     operands = [cells_of, cells_of, *pack_list, rows]
     in_specs = [
         pl.BlockSpec(
-            (1, 1, packet), lambda i: (jnp.maximum(i - 1, 0) + shift, 0, 0), memory_space=pltpu.SMEM
+            (1, 1, packet),
+            lambda i: (jnp.maximum(i - 1 + shift, 0), 0, 0),
+            memory_space=pltpu.SMEM,
         ),
         pl.BlockSpec(
             (1, 1, packet),
-            lambda i: (jnp.minimum(i + 1, blocks - 1) + shift, 0, 0),
+            lambda i: (jnp.minimum(i + 1, limit) + shift, 0, 0),
             memory_space=pltpu.SMEM,
         ),
     ] + [VMEM] * (blocks + 1)
     aliases = {}
-    if back is not None:
+    held = [jax.ShapeDtypeStruct((packet, doubled), F32)] * 2
+    scratch = []
+    if final:
         aliases = {len(operands): 0}
-        operands.append(back)
-        in_specs.append(VMEM)
-    wide = 2 * LANES
+        operands += list(before)
+        in_specs += [VMEM] * 3
+        scratch = [pltpu.VMEM((packet, doubled), F32)] * 2
+        held = []
     return pl.pallas_call(
         body,
         grid=(blocks,),
         out_shape=[
             jax.ShapeDtypeStruct((cells, doubled), F32),
             jax.ShapeDtypeStruct((blocks, *pack_shape), BF16),
-        ],
+        ]
+        + held,
         in_specs=in_specs,
-        out_specs=[VMEM, pl.BlockSpec((1, *pack_shape), lambda i: (i, 0, 0))],
-        scratch_shapes=[
+        out_specs=[VMEM, pl.BlockSpec((1, *pack_shape), lambda i: (i, 0, 0))] + [VMEM] * len(held),
+        scratch_shapes=scratch
+        + [
             pltpu.VMEM(pack_shape, BF16),
-            pltpu.VMEM((packet, doubled), F32),
-            pltpu.VMEM((packet, doubled), F32),
             pltpu.VMEM((wide, wide), BF16),
             pltpu.VMEM((LANES, wide), BF16),
             pltpu.VMEM((3, wide, wide), BF16),
@@ -1020,34 +1060,41 @@
     area = (levels, width_x, width_y)
 
     first, other = pack_rows_out(flags, field_rows, diff_rows, *area)
-    near = trade_sides(first, other, "tile")
     weights = pack_weights(w_first[0], w_inner[0], w_last[0], b_inner[0], b_last, tiles)
     own_weights = [weights] + [
         lax.ppermute(weights, "sub", partners(subs, 2 * c)) for c in range(1, half)
     ]
-    own = pack_columns_out(flags, field_rows, diff_rows, *near, *area)
+    near = trade_sides(first, other, "tile")
+    cells_of = slot_cells(flags, send_counts[0], column_order[0], sizes)
+    own = pack_columns_out(flags, field_rows, diff_rows, *area)
+    own = add_corners(flags, *near, *own, width_x, width_y)
     sides = trade_sides(*own, "sub")
-    cells_of = slot_cells(flags, send_counts[0], column_order[0], sizes)
+    other_weights = [lax.ppermute(pack, "sub", partners(subs, 1)) for pack in own_weights]
     rows, rates, rate_sides = forward(
         flags, field_rows, target_rows, diff_rows, near, own, sides, sizes
     )
-    other_weights = [lax.ppermute(pack, "sub", partners(subs, 1)) for pack in own_weights]
-    back, own_grads = network(cells_of, own_weights, rows, None, 0, levels, width, subs)
-    back, other_grads = network(cells_of, other_weights, rows, back, half, levels, width, subs)
+    back, other_grads, taken, given_back = network(
+        cells_of, other_weights, rows, None, 0, levels, width, subs
+    )
     partner_grads = lax.ppermute(other_grads, "sub", partners(subs, 1))
-    grid, g_first, g_other = collect(flags, back, sizes)
-    g_near = trade_sides(g_first, g_other, "tile")
+    back, own_grads = network(
+        cells_of, own_weights, rows, (back, taken, given_back), half,
+        levels, width, subs,
+    )
     both_grads = add_pair(own_grads, partner_grads)
     arrived = [both_grads[0]] + [
         lax.ppermute(both_grads[c], "sub", partners(subs, 2 * c)) for c in range(1, half)
     ]
-    g_own = pack_columns_back(flags, grid, *g_near, *area)
+    grid, g_first, g_other = collect(flags, back, sizes)
+    g_near = trade_sides(g_first, g_other, "tile")
+    g_own = pack_columns_back(flags, grid, *area)
+    g_own = add_corners(flags, *g_near, *g_own, width_x, width_y)
     g_sides = trade_sides(*g_own, "sub")
-    result = adjoint(flags, grid, rates, rate_sides, g_near, g_own, g_sides, sizes)
     shares = sum_and_share(flags, arrived, tiles)
     mine = [shares[0]] + [
         lax.ppermute(shares[d], "tile", partners(tiles, d)) for d in range(1, tiles)
     ]
+    result = adjoint(flags, grid, rates, rate_sides, g_near, g_own, g_sides, sizes)
     piece = sum_parts(mine)
     pieces = [piece] + [lax.ppermute(piece, "tile", partners(tiles, d)) for d in range(1, tiles)]
     steps = make_steps(flags, pieces, levels, width)

time: 113 us -> 106 us (0.938)
  waiting for transfers between devices: 31.4 us -> 25.4 us
  local copies, waits for them, and re-layouts: 5.78 us -> 1.98 us
  Pallas kernels: 44.5 us -> 46.8 us
  starting transfers between devices: 29.8 us -> 31 us
    unnamed x24 -> x16, local copies, waits for them, and re-layouts: 5.78 us -> 1.97 us
    ppermute x4, waiting for transfers between devices: 6.85 us -> 3.99 us  [trade_sides(): lax.ppermute(other, axis, beyond(size))]
    ppermute x1, waiting for transfers between devices: 2.74 us -> 0.01 us  [local_program(): partner_grads = lax.ppermute(other_grads, 'sub', partners(subs, 1))]
    pallas_call x1, Pallas kernels: 0.37 us -> 1.94 us  [pack_weights(): pl.pallas_call(weights_body, out_shape=jax.ShapeDtypeStruct((pack_size(le...]
    pallas_call x0 -> x2, Pallas kernels: none -> 1.41 us  [add_corners(): pl.pallas_call(functools.partial(corner_body, width_x, width_y), out_shap...]
    ppermute x4, starting transfers between devices: 9.67 us -> 10.8 us  [trade_sides(): lax.ppermute(other, axis, beyond(size))]
  transfers between devices with their start and end apart: 25 -> 25, of which waited for: 11 -> 11; matrix products, arithmetic and copies ran while one was open for 0% -> 0% of each run, Pallas kernels for 27% -> 29%
where the time goes in v4:
time: 106 us
  Pallas kernels  46.8 us (44%)
  starting transfers between devices  31 us (29%)
  waiting for transfers between devices  25.4 us (24%)
  local copies, waits for them, and re-layouts  1.98 us (2%)
    pallas_call x2, Pallas kernels, network(): pl.pallas_call(body, grid=(blocks,), out_shape=[jax.ShapeDtypeStruct((cel...  21.2 us
    ppermute x3, waiting for transfers between devices, local_program(): lax.ppermute(both_grads[c], 'sub', partners(subs, 2 * c))  12.4 us
    ppermute x4, starting transfers between devices, trade_sides(): lax.ppermute(other, axis, beyond(size))  10.8 us
    ppermute x3, waiting for transfers between devices, local_program(): lax.ppermute(weights, 'sub', partners(subs, 2 * c))  7.67 us
    pallas_call x1, Pallas kernels, forward(): pl.pallas_call(functools.partial(forward_body, levels, width_x, width_y),...  6.38 us
    pallas_call x1, Pallas kernels, adjoint(): pl.pallas_call(functools.partial(adjoint_body, levels, width_x, width_y),...  5.51 us
    ppermute x3, starting transfers between devices, local_program(): lax.ppermute(weights, 'sub', partners(subs, 2 * c))  4.63 us
    ppermute x3, starting transfers between devices, local_program(): lax.ppermute(piece, 'tile', partners(tiles, d))  4.45 us
  transfers between devices with their start and end apart: 25, of which 11 were waited for; matrix products, arithmetic and copies ran while one was open for 0% of the time, Pallas kernels for 29%

profile of v4, /device:TPU:0, one launch (start us, length us, event | category | flops | bytes accessed | tf_op | source)
XLA Modules:
  0.0 106.1 jit_solution(10892460938502266187)
XLA Ops:
  0.6 0.0 copy-start.5
  0.7 1.9 %pack_weights.1.refs_0_ = bf16[1088,128]{1,0:T(8,128)(2,1)} custom-call(bf16[64,192]{1,0:T(8,128)(2,1)} %bitcast.55, bf16[3,192,192]{2,1,0:T(8,128)(2,1)} %bitcast.54, bf16[64,192]{1,0:T(8,128)(2,1)} %bitcast.56, f32[4,192]{1,0:T(4,128)} %bitcast.58, f32[1,64]{1,0:T(1,128)} %refs_4_.1), custom_call_target="tpu_custom_call" | custom-call | bytes 3000000 | tf_op jit(solution)/shard_map/pack_weights/pallas_call | solution.py:521
  2.6 4.0 %collective-permute-start.2 = (bf16[1088,128]{1,0:T(8,128)(2,1)}, bf16[1088,128]{1,0:T(8,128)(2,1)S(1)}, u32[]{:S(2)}, u32[]{:S(2)}) collective-permute-start(bf16[1088,128]{1,0:T(8,128)(2,1)} %pack_weights.1.refs_0_), channel_id=1, source_target_pairs={{0,6},{1,7},{2,4},{3,5},{4,2},{5,3},{6,0},{7,1},{8,14},{9,15},{10,... | collective-permute-start | bytes 835592 | tf_op jit(solution)/shard_map/ppermute | solution.py:1065
  6.6 0.5 collective-permute-start.1
  7.1 0.1 collective-permute-start
  7.2 0.1 pad_add_fusion.flags
  7.3 1.2 %copy-done = f32[64,16,256]{2,1,0:T(8,128)S(1)} copy-done((f32[64,16,256]{2,1,0:T(8,128)S(1)}, f32[64,16,256]{2,1,0:T(8,128)}, u32[]{:S(2)}) %copy-start) | copy-done | bytes 1048600
  8.6 0.7 copy-done.4
  9.3 0.7 pack_rows.1
  10.0 2.0 %collective-permute-start.3 = (bf16[80,512]{1,0:T(8,128)(2,1)S(1)}, bf16[80,512]{1,0:T(8,128)(2,1)S(1)}, u32[]{:S(2)}, u32[]{:S(2)}) collective-permute-start(bf16[80,512]{1,0:T(8,128)(2,1)S(1)} %get-tuple-element.41), channel_id=1, source_target_pairs={{0,8},{8,0},{16,24},{24,16},{1,9},{9,1},{17,25},{25,17},{2,10},{10... | collective-permute-start | bytes 245768 | tf_op jit(solution)/shard_map/ppermute | solution.py:270
  12.0 0.0 collective-permute-start.7
  12.0 2.3 %collective-permute-done.2.refs_3_ = bf16[1088,128]{1,0:T(8,128)(2,1)S(1)} collective-permute-done((bf16[1088,128]{1,0:T(8,128)(2,1)}, bf16[1088,128]{1,0:T(8,128)(2,1)S(1)}, u32[]{:S(2)}, u32[]{:S(2)}) %collective-permute-start.2) | collective-permute-done | bytes 278560 | tf_op jit(solution)/shard_map/ppermute | solution.py:1065
  14.4 0.0 collective-permute-start.10
  14.4 5.1 %collective-permute-done.1.refs_2_ = bf16[1088,128]{1,0:T(8,128)(2,1)S(1)} collective-permute-done((bf16[1088,128]{1,0:T(8,128)(2,1)}, bf16[1088,128]{1,0:T(8,128)(2,1)S(1)}, u32[]{:S(2)}, u32[]{:S(2)}) %collective-permute-start.1) | collective-permute-done | bytes 278560 | tf_op jit(solution)/shard_map/ppermute | solution.py:1065
  19.4 0.0 collective-permute-start.9
  19.5 0.3 collective-permute-done.refs_1_
  19.7 0.2 collective-permute-start.8
  20.0 0.0 collective-permute-done.3.near
  20.0 3.8 %collective-permute-start.4 = (bf16[80,512]{1,0:T(8,128)(2,1)S(1)}, bf16[80,512]{1,0:T(8,128)(2,1)S(1)}, u32[]{:S(2)}, u32[]{:S(2)}) collective-permute-start(bf16[80,512]{1,0:T(8,128)(2,1)S(1)} %get-tuple-element.42), channel_id=1, source_target_pairs={{0,24},{8,16},{16,8},{24,0},{1,25},{9,17},{17,9},{25,1},{2,26},{10... | collective-permute-start | bytes 245768 | tf_op jit(solution)/shard_map/ppermute | solution.py:270
  23.8 1.6 %pack_columns.1 = (bf16[80,128]{1,0:T(8,128)(2,1)S(1)}, bf16[80,128]{1,0:T(8,128)(2,1)S(1)}) custom-call(s32[4]{0:T(128)S(1)} %pad_add_fusion.flags, f32[2048,128]{1,0:T(8,128)S(1)} %bitcast.42, f32[32,128]{1,0:T(8,128)S(1)} %bitcast.50), custom_call_target="tpu_custom_call" | custom-call | bytes 6000000 | tf_op jit(solution)/shard_map/pack_columns/pallas_call | solution.py:188
  25.4 1.2 %collective-permute-done.4.far = bf16[80,512]{1,0:T(8,128)(2,1)S(1)} collective-permute-done((bf16[80,512]{1,0:T(8,128)(2,1)S(1)}, bf16[80,512]{1,0:T(8,128)(2,1)S(1)}, u32[]{:S(2)}, u32[]{:S(2)}) %collective-permute-start.4) | collective-permute-done | bytes 81952 | tf_op jit(solution)/shard_map/ppermute | solution.py:270
  26.6 0.7 add_corners.2
  27.3 0.1 collective-permute-start.5
  27.4 1.2 %collective-permute-done.5.side_near = bf16[80,128]{1,0:T(8,128)(2,1)S(1)} collective-permute-done((bf16[80,128]{1,0:T(8,128)(2,1)S(1)}, bf16[80,128]{1,0:T(8,128)(2,1)S(1)}, u32[]{:S(2)}, u32[]{:S(2)}) %collective-permute-start.5) | collective-permute-done | bytes 20512 | tf_op jit(solution)/shard_map/ppermute | solution.py:270
  28.5 1.5 %collective-permute-start.6 = (bf16[80,128]{1,0:T(8,128)(2,1)S(1)}, bf16[80,128]{1,0:T(8,128)(2,1)S(1)}, u32[]{:S(2)}, u32[]{:S(2)}) collective-permute-start(bf16[80,128]{1,0:T(8,128)(2,1)S(1)} %get-tuple-element.46.own_far), channel_id=1, source_target_pairs={{0,7},{1,2},{2,1},{3,4},{4,3},{5,6},{6,5},{7,0},{8,15},{9,10},{10,... | collective-permute-start | bytes 61448 | tf_op jit(solution)/shard_map/ppermute | solution.py:270
  30.0 1.5 %slot_cells.1 = s32[32,128]{1,0:T(8,128)S(1)} custom-call(s32[4]{0:T(128)S(1)} %pad_add_fusion.flags, s32[32]{0:T(128)S(1)} %bitcast.52, s32[44,128]{1,0:T(8,128)S(1)} %pad_bitcast_fusion.order), custom_call_target="tpu_custom_call" | custom-call | bytes 6000000 | tf_op jit(solution)/shard_map/slot_cells/pallas_call | solution.py:429
  31.5 1.1 %collective-permute-done.6.side_far = bf16[80,128]{1,0:T(8,128)(2,1)S(1)} collective-permute-done((bf16[80,128]{1,0:T(8,128)(2,1)S(1)}, bf16[80,128]{1,0:T(8,128)(2,1)S(1)}, u32[]{:S(2)}, u32[]{:S(2)}) %collective-permute-start.6) | collective-permute-done | bytes 20512 | tf_op jit(solution)/shard_map/ppermute | solution.py:270
  32.6 6.4 %forward.1 = (f32[4096,128]{1,0:T(8,128)S(1)}, f32[8,5120]{1,0:T(8,128)S(1)}, f32[48,128]{1,0:T(8,128)S(1)}) custom-call(s32[4]{0:T(128)S(1)} %pad_add_fusion.flags, f32[2048,128]{1,0:T(8,128)S(1)} %bitcast.43, f32[2048,128]{1,0:T(8,128)S(1)} %bitcast.44, f32[32,128]{1,0:T(8,128)S(1)} %bitcast.51, bf16[80,512]{1,0:T(8,128)(2,1)S(1)} %collective-permute-done.3.near, ...), custom_call_target="tpu_custom_call" | custom-call | bytes 24000000 | tf_op jit(solution)/shard_map/forward/pallas_call | solution.py:366
  39.0 0.0 copy-start.2
  39.1 0.0 collective-permute-done.10.refs_3_
  39.1 0.0 collective-permute-done.9.refs_2_
  39.1 10.6 %network.2 = (f32[4096,128]{1,0:T(8,128)S(1)}, bf16[4,1088,128]{2,1,0:T(8,128)(2,1)S(1)}, f32[512,128]{1,0:T(8,128)S(1)}, f32[512,128]{1,0:T(8,128)S(1)}) custom-call(s32[8,1,512]{2,1,0:T(1,128)S(1)} %bitcast.45, s32[8,1,512]{2,1,0:T(1,128)S(1)} %bitcast.46, bf16[1088,128]{1,0:T(8,128)(2,1)S(1)} %collective-permute-done.7.refs_0_, ...), custom_call_target="tpu_custom_call" | custom-call | bytes 36000000 | tf_op jit(solution)/shard_map/network/pallas_call | solution.py:773
  49.7 0.1 collective-permute-start.15
  49.8 10.6 %network.3 = (f32[4096,128]{1,0:T(8,128)S(1)}, bf16[4,1088,128]{2,1,0:T(8,128)(2,1)S(1)}) custom-call(s32[8,1,512]{2,1,0:T(1,128)S(1)} %bitcast.47, s32[8,1,512]{2,1,0:T(1,128)S(1)} %bitcast.48, bf16[1088,128]{1,0:T(8,128)(2,1)S(1)} %copy-done.2, bf16[1088,128]{1,0:T(8,128)(2,1)S(1)} %collective-permute-done.refs_1_, ...), custom_call_target="tpu_custom_call", output_to_operand_aliasing={{0}: (7, {})} | custom-call | bytes 36000000 | tf_op jit(solution)/shard_map/network/pallas_call | solution.py:773
  60.3 0.0 collective-permute-done.15.other
  60.4 0.3 add_pair.1
  60.6 1.6 %collective-permute-start.16 = (bf16[1088,128]{1,0:T(8,128)(2,1)S(1)}, bf16[1088,128]{1,0:T(8,128)(2,1)S(1)}, u32[]{:S(2)}, u32[]{:S(2)}) collective-permute-start(bf16[1088,128]{1,0:T(8,128)(2,1)S(1)} %get-tuple-element.64), channel_id=1, source_target_pairs={{0,2},{1,3},{2,0},{3,1},{4,6},{5,7},{6,4},{7,5},{8,10},{9,11},{10,... | collective-permute-start | bytes 835592 | tf_op jit(solution)/shard_map/ppermute | solution.py:1086
  62.3 0.8 collective-permute-start.17
  63.1 1.1 %collective-permute-start.18 = (bf16[1088,128]{1,0:T(8,128)(2,1)S(1)}, bf16[1088,128]{1,0:T(8,128)(2,1)S(1)}, u32[]{:S(2)}, u32[]{:S(2)}) collective-permute-start(bf16[1088,128]{1,0:T(8,128)(2,1)S(1)} %get-tuple-element.66), channel_id=1, source_target_pairs={{0,6},{1,7},{2,4},{3,5},{4,2},{5,3},{6,0},{7,1},{8,14},{9,15},{10,... | collective-permute-start | bytes 835592 | tf_op jit(solution)/shard_map/ppermute | solution.py:1086
  64.2 6.0 %collective-permute-done.16.refs_1_ = bf16[1088,128]{1,0:T(8,128)(2,1)S(1)} collective-permute-done((bf16[1088,128]{1,0:T(8,128)(2,1)S(1)}, bf16[1088,128]{1,0:T(8,128)(2,1)S(1)}, u32[]{:S(2)}, u32[]{:S(2)}) %collective-permute-start.16) | collective-permute-done | bytes 278560 | tf_op jit(solution)/shard_map/ppermute | solution.py:1086
  70.2 0.8 collective-permute-done.17.refs_2_
  71.0 5.6 %collective-permute-done.18.refs_3_ = bf16[1088,128]{1,0:T(8,128)(2,1)S(1)} collective-permute-done((bf16[1088,128]{1,0:T(8,128)(2,1)S(1)}, bf16[1088,128]{1,0:T(8,128)(2,1)S(1)}, u32[]{:S(2)}, u32[]{:S(2)}) %collective-permute-start.18) | collective-permute-done | bytes 278560 | tf_op jit(solution)/shard_map/ppermute | solution.py:1086
  76.6 0.8 sum_and_share.1
  77.5 1.4 %collective-permute-start.19 = (bf16[272,128]{1,0:T(8,128)(2,1)S(1)}, bf16[272,128]{1,0:T(8,128)(2,1)S(1)}, u32[]{:S(2)}, u32[]{:S(2)}) collective-permute-start(bf16[272,128]{1,0:T(8,128)(2,1)S(1)} %get-tuple-element.68), channel_id=1, source_target_pairs={{0,8},{8,0},{16,24},{24,16},{1,9},{9,1},{17,25},{25,17},{2,10},{10... | collective-permute-start | bytes 208904 | tf_op jit(solution)/shard_map/ppermute | solution.py:1095
  78.9 2.7 %collective-permute-start.20 = (bf16[272,128]{1,0:T(8,128)(2,1)S(1)}, bf16[272,128]{1,0:T(8,128)(2,1)S(1)}, u32[]{:S(2)}, u32[]{:S(2)}) collective-permute-start(bf16[272,128]{1,0:T(8,128)(2,1)S(1)} %get-tuple-element.69), channel_id=1, source_target_pairs={{0,16},{8,24},{16,0},{24,8},{1,17},{9,25},{17,1},{25,9},{2,18},{10... | collective-permute-start | bytes 208904 | tf_op jit(solution)/shard_map/ppermute | solution.py:1095
  81.5 0.4 collective-permute-start.21
  81.9 2.3 %collect.1 = (f32[64,4096]{1,0:T(8,128)S(1)}, bf16[64,512]{1,0:T(8,128)(2,1)S(1)}, bf16[64,512]{1,0:T(8,128)(2,1)S(1)}) custom-call(s32[4]{0:T(128)S(1)} %pad_add_fusion.flags, f32[4096,128]{1,0:T(8,128)S(1)} %get-tuple-element.51.rows), custom_call_target="tpu_custom_call" | custom-call | bytes 9000000 | tf_op jit(solution)/shard_map/collect/pallas_call | solution.py:953
  84.2 0.5 collective-permute-start.11
  84.7 3.1 %collective-permute-start.12 = (bf16[64,512]{1,0:T(8,128)(2,1)S(1)}, bf16[64,512]{1,0:T(8,128)(2,1)S(1)}, u32[]{:S(2)}, u32[]{:S(2)}) collective-permute-start(bf16[64,512]{1,0:T(8,128)(2,1)S(1)} %get-tuple-element.56), channel_id=1, source_target_pairs={{0,24},{8,16},{16,8},{24,0},{1,25},{9,17},{17,9},{25,1},{2,26},{10... | collective-permute-start | bytes 196616 | tf_op jit(solution)/shard_map/ppermute | solution.py:270
  87.8 0.0 collective-permute-done.19.refs_1_
  87.8 0.0 collective-permute-done.20.refs_2_
  87.8 0.1 collective-permute-done.21.refs_3_
  88.0 1.5 %collective-permute-start.24 = (bf16[272,128]{1,0:T(8,128)(2,1)S(1)}, bf16[272,128]{1,0:T(8,128)(2,1)S(1)}, u32[]{:S(2)}, u32[]{:S(2)}) collective-permute-start(bf16[272,128]{1,0:T(8,128)(2,1)S(1)} %sum_parts.1.refs_0_), channel_id=1, source_target_pairs={{0,24},{8,16},{16,8},{24,0},{1,25},{9,17},{17,9},{25,1},{2,26},{10... | collective-permute-start | bytes 208904 | tf_op jit(solution)/shard_map/ppermute | solution.py:1099
  89.5 0.9 collective-permute-start.23
  90.4 2.0 %collective-permute-start.22 = (bf16[272,128]{1,0:T(8,128)(2,1)S(1)}, bf16[272,128]{1,0:T(8,128)(2,1)S(1)}, u32[]{:S(2)}, u32[]{:S(2)}) collective-permute-start(bf16[272,128]{1,0:T(8,128)(2,1)S(1)} %sum_parts.1.refs_0_), channel_id=1, source_target_pairs={{0,8},{8,0},{16,24},{24,16},{1,9},{9,1},{17,25},{25,17},{2,10},{10... | collective-permute-start | bytes 208904 | tf_op jit(solution)/shard_map/ppermute | solution.py:1099
  92.4 1.3 %pack_back.1 = (bf16[64,128]{1,0:T(8,128)(2,1)S(1)}, bf16[64,128]{1,0:T(8,128)(2,1)S(1)}) custom-call(s32[4]{0:T(128)S(1)} %pad_add_fusion.flags, f32[64,4096]{1,0:T(8,128)S(1)} %get-tuple-element.52.grid), custom_call_target="tpu_custom_call" | custom-call | bytes 6000000 | tf_op jit(solution)/shard_map/pack_back/pallas_call | solution.py:213
  93.7 0.0 collective-permute-done.12.far
  93.7 0.7 add_corners.3
  94.4 0.1 collective-permute-start.13
  94.5 2.5 %collective-permute-start.14 = (bf16[64,128]{1,0:T(8,128)(2,1)S(1)}, bf16[64,128]{1,0:T(8,128)(2,1)S(1)}, u32[]{:S(2)}, u32[]{:S(2)}) collective-permute-start(bf16[64,128]{1,0:T(8,128)(2,1)S(1)} %get-tuple-element.60.own_far), channel_id=1, source_target_pairs={{0,7},{1,2},{2,1},{3,4},{4,3},{5,6},{6,5},{7,0},{8,15},{9,10},{10,... | collective-permute-start | bytes 49160 | tf_op jit(solution)/shard_map/ppermute | solution.py:270
  97.0 1.7 %collective-permute-done.14.side_far = bf16[64,128]{1,0:T(8,128)(2,1)S(1)} collective-permute-done((bf16[64,128]{1,0:T(8,128)(2,1)S(1)}, bf16[64,128]{1,0:T(8,128)(2,1)S(1)}, u32[]{:S(2)}, u32[]{:S(2)}) %collective-permute-start.14) | collective-permute-done | bytes 16416 | tf_op jit(solution)/shard_map/ppermute | solution.py:270
  98.7 5.5 %adjoint.1 = f32[2048,128]{1,0:T(8,128)} custom-call(s32[4]{0:T(128)S(1)} %pad_add_fusion.flags, f32[64,4096]{1,0:T(8,128)S(1)} %get-tuple-element.52.grid, f32[8,5120]{1,0:T(8,128)S(1)} %get-tuple-element.53.wide, f32[48,128]{1,0:T(8,128)S(1)} %get-tuple-element.54.rate_sides, bf16[64,512]{1,0:T(8,128)(2,1)S(1)} %collective-permute-done.11.near, ...), custom_call_target="tpu_custom_call" | custom-call | bytes 18000000 | tf_op jit(solution)/shard_map/adjoint/pallas_call | solution.py:1034
  104.2 0.0 collective-permute-done.24.refs_3_
  104.2 1.9 %make_steps.1 = (f32[64,192]{1,0:T(8,128)}, f32[3,192,192]{2,1,0:T(8,128)}, f32[64,192]{1,0:T(8,128)}, f32[4,192]{1,0:T(4,128)}, f32[1,64]{1,0:T(1,128)}) custom-call(s32[4]{0:T(128)S(1)} %pad_add_fusion.flags, bf16[272,128]{1,0:T(8,128)(2,1)S(1)} %sum_parts.1.refs_0_, bf16[272,128]{1,0:T(8,128)(2,1)S(1)} %collective-permute-done.22.refs_1_, ...), custom_call_target="tpu_custom_call" | custom-call | bytes 6000000 | tf_op jit(solution)/shard_map/make_steps/pallas_call | solution.py:910
  (20 shorter events, 0.1 us)
Async XLA Ops:
  0.6 32.0 %copy-start.5 = (f32[16,256]{1,0:T(8,128)S(1)}, f32[16,256]{1,0:T(8,128)}, u32[]{:S(2)}) copy-start(f32[16,256]{1,0:T(8,128)} %param.12) | copy-start | bytes 49156
  0.6 29.4 %copy-start.7 = (s32[1,4096]{1,0:T(1,128)S(1)}, s32[1,4096]{1,0:T(1,128)}, u32[]{:S(2)}) copy-start(s32[1,4096]{1,0:T(1,128)} %param.13) | copy-start | bytes 49156
  0.7 29.4 %copy-start.6 = (s32[1,32]{1,0:T(1,128)S(1)}, s32[1,32]{1,0:T(1,128)}, u32[]{:S(2)}) copy-start(s32[1,32]{1,0:T(1,128)} %param.14) | copy-start | bytes 388
  2.6 11.7 %collective-permute-start.2 = (bf16[1088,128]{1,0:T(8,128)(2,1)}, bf16[1088,128]{1,0:T(8,128)(2,1)S(1)}, u32[]{:S(2)}, u32[]{:S(2)}) collective-permute-start(bf16[1088,128]{1,0:T(8,128)(2,1)} %pack_weights.1.refs_0_), channel_id=1, source_target_pairs={{0,6},{1,7},{2,4},{3,5},{4,2},{5,3},{6,0},{7,1},{8,14},{9,15},{10,... | collective-permute-start | bytes 835592 | tf_op jit(solution)/shard_map/ppermute | solution.py:1065
  6.6 12.8 %collective-permute-start.1 = (bf16[1088,128]{1,0:T(8,128)(2,1)}, bf16[1088,128]{1,0:T(8,128)(2,1)S(1)}, u32[]{:S(2)}, u32[]{:S(2)}) collective-permute-start(bf16[1088,128]{1,0:T(8,128)(2,1)} %pack_weights.1.refs_0_), channel_id=1, source_target_pairs={{0,4},{1,5},{2,6},{3,7},{4,0},{5,1},{6,2},{7,3},{8,12},{9,13},{10,... | collective-permute-start | bytes 835592 | tf_op jit(solution)/shard_map/ppermute | solution.py:1065
  7.1 12.6 %collective-permute-start = (bf16[1088,128]{1,0:T(8,128)(2,1)}, bf16[1088,128]{1,0:T(8,128)(2,1)S(1)}, u32[]{:S(2)}, u32[]{:S(2)}) collective-permute-start(bf16[1088,128]{1,0:T(8,128)(2,1)} %pack_weights.1.refs_0_), channel_id=1, source_target_pairs={{0,2},{1,3},{2,0},{3,1},{4,6},{5,7},{6,4},{7,5},{8,10},{9,11},{10,... | collective-permute-start | bytes 835592 | tf_op jit(solution)/shard_map/ppermute | solution.py:1065
  7.3 1.2 %copy-start = (f32[64,16,256]{2,1,0:T(8,128)S(1)}, f32[64,16,256]{2,1,0:T(8,128)}, u32[]{:S(2)}) copy-start(f32[64,16,256]{2,1,0:T(8,128)} %param.10) | copy-start | bytes 3145732
  8.6 0.7 copy-start.4
  9.3 23.4 %copy-start.1 = (f32[64,16,256]{2,1,0:T(8,128)S(1)}, f32[64,16,256]{2,1,0:T(8,128)}, u32[]{:S(2)}) copy-start(f32[64,16,256]{2,1,0:T(8,128)} %param.10) | copy-start | bytes 3145732
  9.3 23.4 %copy-start.3 = (f32[64,16,256]{2,1,0:T(8,128)S(1)}, f32[64,16,256]{2,1,0:T(8,128)}, u32[]{:S(2)}) copy-start(f32[64,16,256]{2,1,0:T(8,128)} %param.11) | copy-start | bytes 3145732
  10.0 10.0 %collective-permute-start.3 = (bf16[80,512]{1,0:T(8,128)(2,1)S(1)}, bf16[80,512]{1,0:T(8,128)(2,1)S(1)}, u32[]{:S(2)}, u32[]{:S(2)}) collective-permute-start(bf16[80,512]{1,0:T(8,128)(2,1)S(1)} %get-tuple-element.41), channel_id=1, source_target_pairs={{0,8},{8,0},{16,24},{24,16},{1,9},{9,1},{17,25},{25,17},{2,10},{10... | collective-permute-start | bytes 245768 | tf_op jit(solution)/shard_map/ppermute | solution.py:270
  12.0 27.0 %collective-permute-start.7 = (bf16[1088,128]{1,0:T(8,128)(2,1)}, bf16[1088,128]{1,0:T(8,128)(2,1)S(1)}, u32[]{:S(2)}, u32[]{:S(2)}) collective-permute-start(bf16[1088,128]{1,0:T(8,128)(2,1)} %pack_weights.1.refs_0_), channel_id=1, source_target_pairs={{0,1},{1,0},{2,3},{3,2},{4,5},{5,4},{6,7},{7,6},{8,9},{9,8},{10,11... | collective-permute-start | bytes 835592 | tf_op jit(solution)/shard_map/ppermute | solution.py:1072
  14.4 24.7 %collective-permute-start.10 = (bf16[1088,128]{1,0:T(8,128)(2,1)S(1)}, bf16[1088,128]{1,0:T(8,128)(2,1)S(1)}, u32[]{:S(2)}, u32[]{:S(2)}) collective-permute-start(bf16[1088,128]{1,0:T(8,128)(2,1)S(1)} %collective-permute-done.2.refs_3_), channel_id=1, source_target_pairs={{0,1},{1,0},{2,3},{3,2},{4,5},{5,4},{6,7},{7,6},{8,9},{9,8},{10,11... | collective-permute-start | bytes 835592 | tf_op jit(solution)/shard_map/ppermute | solution.py:1072
  19.4 19.6 %collective-permute-start.9 = (bf16[1088,128]{1,0:T(8,128)(2,1)S(1)}, bf16[1088,128]{1,0:T(8,128)(2,1)S(1)}, u32[]{:S(2)}, u32[]{:S(2)}) collective-permute-start(bf16[1088,128]{1,0:T(8,128)(2,1)S(1)} %collective-permute-done.1.refs_2_), channel_id=1, source_target_pairs={{0,1},{1,0},{2,3},{3,2},{4,5},{5,4},{6,7},{7,6},{8,9},{9,8},{10,11... | collective-permute-start | bytes 835592 | tf_op jit(solution)/shard_map/ppermute | solution.py:1072
  19.7 19.4 %collective-permute-start.8 = (bf16[1088,128]{1,0:T(8,128)(2,1)S(1)}, bf16[1088,128]{1,0:T(8,128)(2,1)S(1)}, u32[]{:S(2)}, u32[]{:S(2)}) collective-permute-start(bf16[1088,128]{1,0:T(8,128)(2,1)S(1)} %collective-permute-done.refs_1_), channel_id=1, source_target_pairs={{0,1},{1,0},{2,3},{3,2},{4,5},{5,4},{6,7},{7,6},{8,9},{9,8},{10,11... | collective-permute-start | bytes 835592 | tf_op jit(solution)/shard_map/ppermute | solution.py:1072
  20.0 6.6 %collective-permute-start.4 = (bf16[80,512]{1,0:T(8,128)(2,1)S(1)}, bf16[80,512]{1,0:T(8,128)(2,1)S(1)}, u32[]{:S(2)}, u32[]{:S(2)}) collective-permute-start(bf16[80,512]{1,0:T(8,128)(2,1)S(1)} %get-tuple-element.42), channel_id=1, source_target_pairs={{0,24},{8,16},{16,8},{24,0},{1,25},{9,17},{17,9},{25,1},{2,26},{10... | collective-permute-start | bytes 245768 | tf_op jit(solution)/shard_map/ppermute | solution.py:270
  27.3 1.3 %collective-permute-start.5 = (bf16[80,128]{1,0:T(8,128)(2,1)S(1)}, bf16[80,128]{1,0:T(8,128)(2,1)S(1)}, u32[]{:S(2)}, u32[]{:S(2)}) collective-permute-start(bf16[80,128]{1,0:T(8,128)(2,1)S(1)} %get-tuple-element.45.own_near), channel_id=1, source_target_pairs={{0,1},{1,0},{2,3},{3,2},{4,5},{5,4},{6,7},{7,6},{8,9},{9,8},{10,11... | collective-permute-start | bytes 61448 | tf_op jit(solution)/shard_map/ppermute | solution.py:270
  28.5 4.1 %collective-permute-start.6 = (bf16[80,128]{1,0:T(8,128)(2,1)S(1)}, bf16[80,128]{1,0:T(8,128)(2,1)S(1)}, u32[]{:S(2)}, u32[]{:S(2)}) collective-permute-start(bf16[80,128]{1,0:T(8,128)(2,1)S(1)} %get-tuple-element.46.own_far), channel_id=1, source_target_pairs={{0,7},{1,2},{2,1},{3,4},{4,3},{5,6},{6,5},{7,0},{8,15},{9,10},{10,... | collective-permute-start | bytes 61448 | tf_op jit(solution)/shard_map/ppermute | solution.py:270
  39.0 10.7 %copy-start.2 = (bf16[1088,128]{1,0:T(8,128)(2,1)S(1)}, bf16[1088,128]{1,0:T(8,128)(2,1)}, u32[]{:S(2)}) copy-start(bf16[1088,128]{1,0:T(8,128)(2,1)} %pack_weights.1.refs_0_) | copy-start | bytes 835588
  49.7 10.7 %collective-permute-start.15 = (bf16[4,1088,128]{2,1,0:T(8,128)(2,1)S(1)}, bf16[4,1088,128]{2,1,0:T(8,128)(2,1)S(1)}, u32[]{:S(2)}, u32[]{:S(2)}) collective-permute-start(bf16[4,1088,128]{2,1,0:T(8,128)(2,1)S(1)} %get-tuple-element.62), channel_id=1, source_target_pairs={{0,1},{1,0},{2,3},{3,2},{4,5},{5,4},{6,7},{7,6},{8,9},{9,8},{10,11... | collective-permute-start | bytes 3342344 | tf_op jit(solution)/shard_map/ppermute | solution.py:1079
  60.6 9.6 %collective-permute-start.16 = (bf16[1088,128]{1,0:T(8,128)(2,1)S(1)}, bf16[1088,128]{1,0:T(8,128)(2,1)S(1)}, u32[]{:S(2)}, u32[]{:S(2)}) collective-permute-start(bf16[1088,128]{1,0:T(8,128)(2,1)S(1)} %get-tuple-element.64), channel_id=1, source_target_pairs={{0,2},{1,3},{2,0},{3,1},{4,6},{5,7},{6,4},{7,5},{8,10},{9,11},{10,... | collective-permute-start | bytes 835592 | tf_op jit(solution)/shard_map/ppermute | solution.py:1086
  62.3 8.7 %collective-permute-start.17 = (bf16[1088,128]{1,0:T(8,128)(2,1)S(1)}, bf16[1088,128]{1,0:T(8,128)(2,1)S(1)}, u32[]{:S(2)}, u32[]{:S(2)}) collective-permute-start(bf16[1088,128]{1,0:T(8,128)(2,1)S(1)} %get-tuple-element.65), channel_id=1, source_target_pairs={{0,4},{1,5},{2,6},{3,7},{4,0},{5,1},{6,2},{7,3},{8,12},{9,13},{10,... | collective-permute-start | bytes 835592 | tf_op jit(solution)/shard_map/ppermute | solution.py:1086
  63.1 13.5 %collective-permute-start.18 = (bf16[1088,128]{1,0:T(8,128)(2,1)S(1)}, bf16[1088,128]{1,0:T(8,128)(2,1)S(1)}, u32[]{:S(2)}, u32[]{:S(2)}) collective-permute-start(bf16[1088,128]{1,0:T(8,128)(2,1)S(1)} %get-tuple-element.66), channel_id=1, source_target_pairs={{0,6},{1,7},{2,4},{3,5},{4,2},{5,3},{6,0},{7,1},{8,14},{9,15},{10,... | collective-permute-start | bytes 835592 | tf_op jit(solution)/shard_map/ppermute | solution.py:1086
  77.5 10.4 %collective-permute-start.19 = (bf16[272,128]{1,0:T(8,128)(2,1)S(1)}, bf16[272,128]{1,0:T(8,128)(2,1)S(1)}, u32[]{:S(2)}, u32[]{:S(2)}) collective-permute-start(bf16[272,128]{1,0:T(8,128)(2,1)S(1)} %get-tuple-element.68), channel_id=1, source_target_pairs={{0,8},{8,0},{16,24},{24,16},{1,9},{9,1},{17,25},{25,17},{2,10},{10... | collective-permute-start | bytes 208904 | tf_op jit(solution)/shard_map/ppermute | solution.py:1095
  78.9 8.9 %collective-permute-start.20 = (bf16[272,128]{1,0:T(8,128)(2,1)S(1)}, bf16[272,128]{1,0:T(8,128)(2,1)S(1)}, u32[]{:S(2)}, u32[]{:S(2)}) collective-permute-start(bf16[272,128]{1,0:T(8,128)(2,1)S(1)} %get-tuple-element.69), channel_id=1, source_target_pairs={{0,16},{8,24},{16,0},{24,8},{1,17},{9,25},{17,1},{25,9},{2,18},{10... | collective-permute-start | bytes 208904 | tf_op jit(solution)/shard_map/ppermute | solution.py:1095
  81.5 6.4 %collective-permute-start.21 = (bf16[272,128]{1,0:T(8,128)(2,1)S(1)}, bf16[272,128]{1,0:T(8,128)(2,1)S(1)}, u32[]{:S(2)}, u32[]{:S(2)}) collective-permute-start(bf16[272,128]{1,0:T(8,128)(2,1)S(1)} %get-tuple-element.70), channel_id=1, source_target_pairs={{0,24},{8,16},{16,8},{24,0},{1,25},{9,17},{17,9},{25,1},{2,26},{10... | collective-permute-start | bytes 208904 | tf_op jit(solution)/shard_map/ppermute | solution.py:1095
  84.2 9.5 %collective-permute-start.11 = (bf16[64,512]{1,0:T(8,128)(2,1)S(1)}, bf16[64,512]{1,0:T(8,128)(2,1)S(1)}, u32[]{:S(2)}, u32[]{:S(2)}) collective-permute-start(bf16[64,512]{1,0:T(8,128)(2,1)S(1)} %get-tuple-element.55), channel_id=1, source_target_pairs={{0,8},{8,0},{16,24},{24,16},{1,9},{9,1},{17,25},{25,17},{2,10},{10... | collective-permute-start | bytes 196616 | tf_op jit(solution)/shard_map/ppermute | solution.py:270
  84.7 9.0 %collective-permute-start.12 = (bf16[64,512]{1,0:T(8,128)(2,1)S(1)}, bf16[64,512]{1,0:T(8,128)(2,1)S(1)}, u32[]{:S(2)}, u32[]{:S(2)}) collective-permute-start(bf16[64,512]{1,0:T(8,128)(2,1)S(1)} %get-tuple-element.56), channel_id=1, source_target_pairs={{0,24},{8,16},{16,8},{24,0},{1,25},{9,17},{17,9},{25,1},{2,26},{10... | collective-permute-start | bytes 196616 | tf_op jit(solution)/shard_map/ppermute | solution.py:270
  88.0 16.2 %collective-permute-start.24 = (bf16[272,128]{1,0:T(8,128)(2,1)S(1)}, bf16[272,128]{1,0:T(8,128)(2,1)S(1)}, u32[]{:S(2)}, u32[]{:S(2)}) collective-permute-start(bf16[272,128]{1,0:T(8,128)(2,1)S(1)} %sum_parts.1.refs_0_), channel_id=1, source_target_pairs={{0,24},{8,16},{16,8},{24,0},{1,25},{9,17},{17,9},{25,1},{2,26},{10... | collective-permute-start | bytes 208904 | tf_op jit(solution)/shard_map/ppermute | solution.py:1099
  89.5 14.7 %collective-permute-start.23 = (bf16[272,128]{1,0:T(8,128)(2,1)S(1)}, bf16[272,128]{1,0:T(8,128)(2,1)S(1)}, u32[]{:S(2)}, u32[]{:S(2)}) collective-permute-start(bf16[272,128]{1,0:T(8,128)(2,1)S(1)} %sum_parts.1.refs_0_), channel_id=1, source_target_pairs={{0,16},{8,24},{16,0},{24,8},{1,17},{9,25},{17,1},{25,9},{2,18},{10... | collective-permute-start | bytes 208904 | tf_op jit(solution)/shard_map/ppermute | solution.py:1099
  90.4 13.8 %collective-permute-start.22 = (bf16[272,128]{1,0:T(8,128)(2,1)S(1)}, bf16[272,128]{1,0:T(8,128)(2,1)S(1)}, u32[]{:S(2)}, u32[]{:S(2)}) collective-permute-start(bf16[272,128]{1,0:T(8,128)(2,1)S(1)} %sum_parts.1.refs_0_), channel_id=1, source_target_pairs={{0,8},{8,0},{16,24},{24,16},{1,9},{9,1},{17,25},{25,17},{2,10},{10... | collective-permute-start | bytes 208904 | tf_op jit(solution)/shard_map/ppermute | solution.py:1099
  94.4 2.6 %collective-permute-start.13 = (bf16[64,128]{1,0:T(8,128)(2,1)S(1)}, bf16[64,128]{1,0:T(8,128)(2,1)S(1)}, u32[]{:S(2)}, u32[]{:S(2)}) collective-permute-start(bf16[64,128]{1,0:T(8,128)(2,1)S(1)} %get-tuple-element.59.own_near), channel_id=1, source_target_pairs={{0,1},{1,0},{2,3},{3,2},{4,5},{5,4},{6,7},{7,6},{8,9},{9,8},{10,11... | collective-permute-start | bytes 49160 | tf_op jit(solution)/shard_map/ppermute | solution.py:270
  94.5 4.2 %collective-permute-start.14 = (bf16[64,128]{1,0:T(8,128)(2,1)S(1)}, bf16[64,128]{1,0:T(8,128)(2,1)S(1)}, u32[]{:S(2)}, u32[]{:S(2)}) collective-permute-start(bf16[64,128]{1,0:T(8,128)(2,1)S(1)} %get-tuple-element.60.own_far), channel_id=1, source_target_pairs={{0,7},{1,2},{2,1},{3,4},{4,3},{5,6},{6,5},{7,0},{8,15},{9,10},{10,... | collective-permute-start | bytes 49160 | tf_op jit(solution)/shard_map/ppermute | solution.py:270

commit v5 on v4

--- a/solution.py
+++ b/solution.py
@@ -9,6 +9,7 @@
 LANES = 128
 SUBLANES = 8
 SECOND = 32
+UNIT_INPUT = (0.640625, -0.00139273)
 VMEM = pl.BlockSpec(memory_space=pltpu.VMEM)
 ANY = pl.BlockSpec(memory_space=pl.ANY)
 SMEM = pl.BlockSpec(memory_space=pltpu.SMEM)
@@ -535,7 +536,6 @@
     behind, ahead, pack_list, rows, back, grads, taken, given_back, packs, first_in, first_out, inner, last, last_half,
     kept, feeds, slopes, residues,
 ):
-    certain = behind[0, 0, 0] >= 0
     block = pl.program_id(0)
     blocks = pl.num_programs(0)
     narrow = width - LANES
@@ -603,12 +603,16 @@
     first_out[levels + half_levels :, LANES:width] = narrow_b.astype(BF16)
     tail = take(16)
 
+    spare_lane = lax.broadcasted_iota(jnp.int32, (1, LANES), 1) - narrow
+    spare = (spare_lane == 0) | (spare_lane == 1)
+
     def bias_rows(k):
         parts = []
         for base in (0, 7):
             mixed = 0.5 * tail[base + 4 + k // 2 : base + 5 + k // 2]
             side = mixed if k % 2 == 0 else swap_halves(mixed)
             side = jnp.where(lower_half(1), side, 0.0)
+            side = jnp.where(spare, UNIT_INPUT[0] if base == 0 else UNIT_INPUT[1], side)
             parts.append(jnp.concatenate([0.5 * tail[base + k : base + k + 1], side], axis=1))
         parts.append(jnp.zeros((14, wide), F32))
         return jnp.concatenate(parts, axis=0).astype(BF16)
@@ -640,10 +644,8 @@
                 turn = jnp.tanh(u)
                 plus = 1.0 + turn
                 active = u * plus
-                slopes[k, span(side), :] = plus + active * (1.0 - turn)
-                current[side] = jnp.concatenate(
-                    [active[:, :LANES], jnp.where(lower, active[:, LANES:], 1.0)], axis=1
-                ).astype(BF16)
+                slopes[k, span(side), :] = plus
+                current[side] = active.astype(BF16)
                 feeds[k, span(side), :] = current[side]
                 deliver(behind, delivered, share)
                 delivered += share
@@ -653,8 +655,7 @@
         (0, 1), [jnp.concatenate([kept[span(side), :], ones], axis=1) for side in sides], 0, packet // 8
     )
 
-    @pl.when(certain)
-    def _():
+    def second_part():
         current = layers((2, 3), [feeds[1, span(side), :] for side in sides], packet // 2, packet // 8)
         for side in sides:
             output = jnp.dot(current[side], last[...], preferred_element_type=F32)
@@ -662,8 +663,9 @@
                 lower, 0.0, kept[span(side), :].astype(F32) + output
             )
 
-    @pl.when(certain)
-    def _():
+    second_part()
+
+    def third_part():
         fetched = 0
         share = packet // 10
         errors = [residues[span(side), :].astype(BF16) for side in sides]
@@ -688,7 +690,9 @@
         grad_sums[4] = weight_grad(4)
         for k in (3, 2, 1, 0):
             for side in sides:
-                errors[side] = (carried[side] * slopes[k, span(side), :]).astype(BF16)
+                plus = slopes[k, span(side), :]
+                slope = plus + feeds[k, span(side), :].astype(F32) * (2.0 - plus)
+                errors[side] = (carried[side] * slope).astype(BF16)
                 weight = inner[k - 1] if k > 0 else first_out[...]
                 carried[side] = lax.dot_general(
                     errors[side], weight, over_lanes, preferred_element_type=F32
@@ -723,6 +727,7 @@
         tail.append(jnp.zeros((grads.shape[1] - filled - len(tail), LANES), F32))
         put(jnp.concatenate(tail, axis=0))
 
+    third_part()
     if carried_in is not None:
 
         @pl.when(block == blocks - 1)

time: 106 us -> 104 us (0.981)
  Pallas kernels: 46.8 us -> 44.5 us
    pallas_call x2, Pallas kernels: 21.2 us -> 18.9 us  [network(): pl.pallas_call(body, grid=(blocks,), out_shape=[jax.ShapeDtypeStruct((cel...]
where the time goes in v5:
time: 104 us
  Pallas kernels  44.5 us (43%)
  starting transfers between devices  30.9 us (30%)
  waiting for transfers between devices  25.5 us (25%)
  local copies, waits for them, and re-layouts  1.98 us (2%)
    pallas_call x2, Pallas kernels, network(): pl.pallas_call(body, grid=(blocks,), out_shape=[jax.ShapeDtypeStruct((cel...  18.9 us
    ppermute x3, waiting for transfers between devices, local_program(): lax.ppermute(both_grads[c], 'sub', partners(subs, 2 * c))  12.4 us
    ppermute x4, starting transfers between devices, trade_sides(): lax.ppermute(other, axis, beyond(size))  10.8 us
    ppermute x3, waiting for transfers between devices, local_program(): lax.ppermute(weights, 'sub', partners(subs, 2 * c))  7.67 us
    pallas_call x1, Pallas kernels, forward(): pl.pallas_call(functools.partial(forward_body, levels, width_x, width_y),...  6.38 us
    pallas_call x1, Pallas kernels, adjoint(): pl.pallas_call(functools.partial(adjoint_body, levels, width_x, width_y),...  5.51 us
    ppermute x3, starting transfers between devices, local_program(): lax.ppermute(weights, 'sub', partners(subs, 2 * c))  4.63 us
    ppermute x3, starting transfers between devices, local_program(): lax.ppermute(piece, 'tile', partners(tiles, d))  4.45 us
  transfers between devices with their start and end apart: 25, of which 11 were waited for; matrix products, arithmetic and copies ran while one was open for 0% of the time, Pallas kernels for 29%

profile of v5, /device:TPU:0, one launch (start us, length us, event | category | flops | bytes accessed | tf_op | source)
XLA Modules:
  0.0 103.8 jit_solution(11123069654104152691)
XLA Ops:
  0.6 0.0 copy-start.5
  0.7 1.9 %pack_weights.1.refs_0_ = bf16[1088,128]{1,0:T(8,128)(2,1)} custom-call(bf16[64,192]{1,0:T(8,128)(2,1)} %bitcast.55, bf16[3,192,192]{2,1,0:T(8,128)(2,1)} %bitcast.54, bf16[64,192]{1,0:T(8,128)(2,1)} %bitcast.56, f32[4,192]{1,0:T(4,128)} %bitcast.58, f32[1,64]{1,0:T(1,128)} %refs_4_.1), custom_call_target="tpu_custom_call" | custom-call | bytes 3000000 | tf_op jit(solution)/shard_map/pack_weights/pallas_call | solution.py:522
  2.6 4.0 %collective-permute-start.2 = (bf16[1088,128]{1,0:T(8,128)(2,1)}, bf16[1088,128]{1,0:T(8,128)(2,1)S(1)}, u32[]{:S(2)}, u32[]{:S(2)}) collective-permute-start(bf16[1088,128]{1,0:T(8,128)(2,1)} %pack_weights.1.refs_0_), channel_id=1, source_target_pairs={{0,6},{1,7},{2,4},{3,5},{4,2},{5,3},{6,0},{7,1},{8,14},{9,15},{10,... | collective-permute-start | bytes 835592 | tf_op jit(solution)/shard_map/ppermute | solution.py:1070
  6.6 0.5 collective-permute-start.1
  7.1 0.1 collective-permute-start
  7.2 0.1 pad_add_fusion.flags
  7.3 1.2 %copy-done = f32[64,16,256]{2,1,0:T(8,128)S(1)} copy-done((f32[64,16,256]{2,1,0:T(8,128)S(1)}, f32[64,16,256]{2,1,0:T(8,128)}, u32[]{:S(2)}) %copy-start) | copy-done | bytes 1048600
  8.6 0.7 copy-done.4
  9.3 0.7 pack_rows.1
  10.0 2.0 %collective-permute-start.3 = (bf16[80,512]{1,0:T(8,128)(2,1)S(1)}, bf16[80,512]{1,0:T(8,128)(2,1)S(1)}, u32[]{:S(2)}, u32[]{:S(2)}) collective-permute-start(bf16[80,512]{1,0:T(8,128)(2,1)S(1)} %get-tuple-element.41), channel_id=1, source_target_pairs={{0,8},{8,0},{16,24},{24,16},{1,9},{9,1},{17,25},{25,17},{2,10},{10... | collective-permute-start | bytes 245768 | tf_op jit(solution)/shard_map/ppermute | solution.py:271
  12.0 0.0 collective-permute-start.7
  12.0 2.3 %collective-permute-done.2.refs_3_ = bf16[1088,128]{1,0:T(8,128)(2,1)S(1)} collective-permute-done((bf16[1088,128]{1,0:T(8,128)(2,1)}, bf16[1088,128]{1,0:T(8,128)(2,1)S(1)}, u32[]{:S(2)}, u32[]{:S(2)}) %collective-permute-start.2) | collective-permute-done | bytes 278560 | tf_op jit(solution)/shard_map/ppermute | solution.py:1070
  14.4 0.0 collective-permute-start.10
  14.4 5.1 %collective-permute-done.1.refs_2_ = bf16[1088,128]{1,0:T(8,128)(2,1)S(1)} collective-permute-done((bf16[1088,128]{1,0:T(8,128)(2,1)}, bf16[1088,128]{1,0:T(8,128)(2,1)S(1)}, u32[]{:S(2)}, u32[]{:S(2)}) %collective-permute-start.1) | collective-permute-done | bytes 278560 | tf_op jit(solution)/shard_map/ppermute | solution.py:1070
  19.4 0.0 collective-permute-start.9
  19.5 0.3 collective-permute-done.refs_1_
  19.7 0.2 collective-permute-start.8
  20.0 0.0 collective-permute-done.3.near
  20.0 3.8 %collective-permute-start.4 = (bf16[80,512]{1,0:T(8,128)(2,1)S(1)}, bf16[80,512]{1,0:T(8,128)(2,1)S(1)}, u32[]{:S(2)}, u32[]{:S(2)}) collective-permute-start(bf16[80,512]{1,0:T(8,128)(2,1)S(1)} %get-tuple-element.42), channel_id=1, source_target_pairs={{0,24},{8,16},{16,8},{24,0},{1,25},{9,17},{17,9},{25,1},{2,26},{10... | collective-permute-start | bytes 245768 | tf_op jit(solution)/shard_map/ppermute | solution.py:271
  23.8 1.6 %pack_columns.1 = (bf16[80,128]{1,0:T(8,128)(2,1)S(1)}, bf16[80,128]{1,0:T(8,128)(2,1)S(1)}) custom-call(s32[4]{0:T(128)S(1)} %pad_add_fusion.flags, f32[2048,128]{1,0:T(8,128)S(1)} %bitcast.42, f32[32,128]{1,0:T(8,128)S(1)} %bitcast.50), custom_call_target="tpu_custom_call" | custom-call | bytes 6000000 | tf_op jit(solution)/shard_map/pack_columns/pallas_call | solution.py:189
  25.4 1.2 %collective-permute-done.4.far = bf16[80,512]{1,0:T(8,128)(2,1)S(1)} collective-permute-done((bf16[80,512]{1,0:T(8,128)(2,1)S(1)}, bf16[80,512]{1,0:T(8,128)(2,1)S(1)}, u32[]{:S(2)}, u32[]{:S(2)}) %collective-permute-start.4) | collective-permute-done | bytes 81952 | tf_op jit(solution)/shard_map/ppermute | solution.py:271
  26.6 0.7 add_corners.2
  27.3 0.1 collective-permute-start.5
  27.4 1.2 %collective-permute-done.5.side_near = bf16[80,128]{1,0:T(8,128)(2,1)S(1)} collective-permute-done((bf16[80,128]{1,0:T(8,128)(2,1)S(1)}, bf16[80,128]{1,0:T(8,128)(2,1)S(1)}, u32[]{:S(2)}, u32[]{:S(2)}) %collective-permute-start.5) | collective-permute-done | bytes 20512 | tf_op jit(solution)/shard_map/ppermute | solution.py:271
  28.5 1.5 %collective-permute-start.6 = (bf16[80,128]{1,0:T(8,128)(2,1)S(1)}, bf16[80,128]{1,0:T(8,128)(2,1)S(1)}, u32[]{:S(2)}, u32[]{:S(2)}) collective-permute-start(bf16[80,128]{1,0:T(8,128)(2,1)S(1)} %get-tuple-element.46.own_far), channel_id=1, source_target_pairs={{0,7},{1,2},{2,1},{3,4},{4,3},{5,6},{6,5},{7,0},{8,15},{9,10},{10,... | collective-permute-start | bytes 61448 | tf_op jit(solution)/shard_map/ppermute | solution.py:271
  30.0 1.5 %slot_cells.1 = s32[32,128]{1,0:T(8,128)S(1)} custom-call(s32[4]{0:T(128)S(1)} %pad_add_fusion.flags, s32[32]{0:T(128)S(1)} %bitcast.52, s32[44,128]{1,0:T(8,128)S(1)} %pad_bitcast_fusion.order), custom_call_target="tpu_custom_call" | custom-call | bytes 6000000 | tf_op jit(solution)/shard_map/slot_cells/pallas_call | solution.py:430
  31.5 1.1 %collective-permute-done.6.side_far = bf16[80,128]{1,0:T(8,128)(2,1)S(1)} collective-permute-done((bf16[80,128]{1,0:T(8,128)(2,1)S(1)}, bf16[80,128]{1,0:T(8,128)(2,1)S(1)}, u32[]{:S(2)}, u32[]{:S(2)}) %collective-permute-start.6) | collective-permute-done | bytes 20512 | tf_op jit(solution)/shard_map/ppermute | solution.py:271
  32.6 6.4 %forward.1 = (f32[4096,128]{1,0:T(8,128)S(1)}, f32[8,5120]{1,0:T(8,128)S(1)}, f32[48,128]{1,0:T(8,128)S(1)}) custom-call(s32[4]{0:T(128)S(1)} %pad_add_fusion.flags, f32[2048,128]{1,0:T(8,128)S(1)} %bitcast.43, f32[2048,128]{1,0:T(8,128)S(1)} %bitcast.44, f32[32,128]{1,0:T(8,128)S(1)} %bitcast.51, bf16[80,512]{1,0:T(8,128)(2,1)S(1)} %collective-permute-done.3.near, ...), custom_call_target="tpu_custom_call" | custom-call | bytes 24000000 | tf_op jit(solution)/shard_map/forward/pallas_call | solution.py:367
  39.0 0.0 copy-start.2
  39.1 0.0 collective-permute-done.10.refs_3_
  39.1 0.0 collective-permute-done.9.refs_2_
  39.1 9.4 %network.2 = (f32[4096,128]{1,0:T(8,128)S(1)}, bf16[4,1088,128]{2,1,0:T(8,128)(2,1)S(1)}, f32[512,128]{1,0:T(8,128)S(1)}, f32[512,128]{1,0:T(8,128)S(1)}) custom-call(s32[8,1,512]{2,1,0:T(1,128)S(1)} %bitcast.45, s32[8,1,512]{2,1,0:T(1,128)S(1)} %bitcast.46, bf16[1088,128]{1,0:T(8,128)(2,1)S(1)} %collective-permute-done.7.refs_0_, ...), custom_call_target="tpu_custom_call" | custom-call | bytes 36000000 | tf_op jit(solution)/shard_map/network/pallas_call | solution.py:778
  48.5 0.1 collective-permute-start.15
  48.6 9.5 %network.3 = (f32[4096,128]{1,0:T(8,128)S(1)}, bf16[4,1088,128]{2,1,0:T(8,128)(2,1)S(1)}) custom-call(s32[8,1,512]{2,1,0:T(1,128)S(1)} %bitcast.47, s32[8,1,512]{2,1,0:T(1,128)S(1)} %bitcast.48, bf16[1088,128]{1,0:T(8,128)(2,1)S(1)} %copy-done.2, bf16[1088,128]{1,0:T(8,128)(2,1)S(1)} %collective-permute-done.refs_1_, ...), custom_call_target="tpu_custom_call", output_to_operand_aliasing={{0}: (7, {})} | custom-call | bytes 36000000 | tf_op jit(solution)/shard_map/network/pallas_call | solution.py:778
  58.1 0.0 collective-permute-done.15.other
  58.1 0.3 add_pair.1
  58.3 1.7 %collective-permute-start.16 = (bf16[1088,128]{1,0:T(8,128)(2,1)S(1)}, bf16[1088,128]{1,0:T(8,128)(2,1)S(1)}, u32[]{:S(2)}, u32[]{:S(2)}) collective-permute-start(bf16[1088,128]{1,0:T(8,128)(2,1)S(1)} %get-tuple-element.64), channel_id=1, source_target_pairs={{0,2},{1,3},{2,0},{3,1},{4,6},{5,7},{6,4},{7,5},{8,10},{9,11},{10,... | collective-permute-start | bytes 835592 | tf_op jit(solution)/shard_map/ppermute | solution.py:1091
  60.0 0.8 collective-permute-start.17
  60.8 1.1 %collective-permute-start.18 = (bf16[1088,128]{1,0:T(8,128)(2,1)S(1)}, bf16[1088,128]{1,0:T(8,128)(2,1)S(1)}, u32[]{:S(2)}, u32[]{:S(2)}) collective-permute-start(bf16[1088,128]{1,0:T(8,128)(2,1)S(1)} %get-tuple-element.66), channel_id=1, source_target_pairs={{0,6},{1,7},{2,4},{3,5},{4,2},{5,3},{6,0},{7,1},{8,14},{9,15},{10,... | collective-permute-start | bytes 835592 | tf_op jit(solution)/shard_map/ppermute | solution.py:1091
  61.9 6.0 %collective-permute-done.16.refs_1_ = bf16[1088,128]{1,0:T(8,128)(2,1)S(1)} collective-permute-done((bf16[1088,128]{1,0:T(8,128)(2,1)S(1)}, bf16[1088,128]{1,0:T(8,128)(2,1)S(1)}, u32[]{:S(2)}, u32[]{:S(2)}) %collective-permute-start.16) | collective-permute-done | bytes 278560 | tf_op jit(solution)/shard_map/ppermute | solution.py:1091
  67.9 0.9 collective-permute-done.17.refs_2_
  68.8 5.5 %collective-permute-done.18.refs_3_ = bf16[1088,128]{1,0:T(8,128)(2,1)S(1)} collective-permute-done((bf16[1088,128]{1,0:T(8,128)(2,1)S(1)}, bf16[1088,128]{1,0:T(8,128)(2,1)S(1)}, u32[]{:S(2)}, u32[]{:S(2)}) %collective-permute-start.18) | collective-permute-done | bytes 278560 | tf_op jit(solution)/shard_map/ppermute | solution.py:1091
  74.3 0.8 sum_and_share.1
  75.2 1.4 %collective-permute-start.19 = (bf16[272,128]{1,0:T(8,128)(2,1)S(1)}, bf16[272,128]{1,0:T(8,128)(2,1)S(1)}, u32[]{:S(2)}, u32[]{:S(2)}) collective-permute-start(bf16[272,128]{1,0:T(8,128)(2,1)S(1)} %get-tuple-element.68), channel_id=1, source_target_pairs={{0,8},{8,0},{16,24},{24,16},{1,9},{9,1},{17,25},{25,17},{2,10},{10... | collective-permute-start | bytes 208904 | tf_op jit(solution)/shard_map/ppermute | solution.py:1100
  76.6 2.6 %collective-permute-start.20 = (bf16[272,128]{1,0:T(8,128)(2,1)S(1)}, bf16[272,128]{1,0:T(8,128)(2,1)S(1)}, u32[]{:S(2)}, u32[]{:S(2)}) collective-permute-start(bf16[272,128]{1,0:T(8,128)(2,1)S(1)} %get-tuple-element.69), channel_id=1, source_target_pairs={{0,16},{8,24},{16,0},{24,8},{1,17},{9,25},{17,1},{25,9},{2,18},{10... | collective-permute-start | bytes 208904 | tf_op jit(solution)/shard_map/ppermute | solution.py:1100
  79.2 0.4 collective-permute-start.21
  79.6 2.3 %collect.1 = (f32[64,4096]{1,0:T(8,128)S(1)}, bf16[64,512]{1,0:T(8,128)(2,1)S(1)}, bf16[64,512]{1,0:T(8,128)(2,1)S(1)}) custom-call(s32[4]{0:T(128)S(1)} %pad_add_fusion.flags, f32[4096,128]{1,0:T(8,128)S(1)} %get-tuple-element.51.rows), custom_call_target="tpu_custom_call" | custom-call | bytes 9000000 | tf_op jit(solution)/shard_map/collect/pallas_call | solution.py:958
  81.9 0.5 collective-permute-start.11
  82.5 3.1 %collective-permute-start.12 = (bf16[64,512]{1,0:T(8,128)(2,1)S(1)}, bf16[64,512]{1,0:T(8,128)(2,1)S(1)}, u32[]{:S(2)}, u32[]{:S(2)}) collective-permute-start(bf16[64,512]{1,0:T(8,128)(2,1)S(1)} %get-tuple-element.56), channel_id=1, source_target_pairs={{0,24},{8,16},{16,8},{24,0},{1,25},{9,17},{17,9},{25,1},{2,26},{10... | collective-permute-start | bytes 196616 | tf_op jit(solution)/shard_map/ppermute | solution.py:271
  85.5 0.0 collective-permute-done.19.refs_1_
  85.5 0.1 collective-permute-done.21.refs_3_
  85.7 1.5 %collective-permute-start.24 = (bf16[272,128]{1,0:T(8,128)(2,1)S(1)}, bf16[272,128]{1,0:T(8,128)(2,1)S(1)}, u32[]{:S(2)}, u32[]{:S(2)}) collective-permute-start(bf16[272,128]{1,0:T(8,128)(2,1)S(1)} %sum_parts.1.refs_0_), channel_id=1, source_target_pairs={{0,24},{8,16},{16,8},{24,0},{1,25},{9,17},{17,9},{25,1},{2,26},{10... | collective-permute-start | bytes 208904 | tf_op jit(solution)/shard_map/ppermute | solution.py:1104
  87.2 0.9 collective-permute-start.23
  88.1 2.0 %collective-permute-start.22 = (bf16[272,128]{1,0:T(8,128)(2,1)S(1)}, bf16[272,128]{1,0:T(8,128)(2,1)S(1)}, u32[]{:S(2)}, u32[]{:S(2)}) collective-permute-start(bf16[272,128]{1,0:T(8,128)(2,1)S(1)} %sum_parts.1.refs_0_), channel_id=1, source_target_pairs={{0,8},{8,0},{16,24},{24,16},{1,9},{9,1},{17,25},{25,17},{2,10},{10... | collective-permute-start | bytes 208904 | tf_op jit(solution)/shard_map/ppermute | solution.py:1104
  90.2 1.3 %pack_back.1 = (bf16[64,128]{1,0:T(8,128)(2,1)S(1)}, bf16[64,128]{1,0:T(8,128)(2,1)S(1)}) custom-call(s32[4]{0:T(128)S(1)} %pad_add_fusion.flags, f32[64,4096]{1,0:T(8,128)S(1)} %get-tuple-element.52.grid), custom_call_target="tpu_custom_call" | custom-call | bytes 6000000 | tf_op jit(solution)/shard_map/pack_back/pallas_call | solution.py:214
  91.4 0.0 collective-permute-done.11.near
  91.4 0.7 add_corners.3
  92.2 0.1 collective-permute-start.13
  92.2 2.5 %collective-permute-start.14 = (bf16[64,128]{1,0:T(8,128)(2,1)S(1)}, bf16[64,128]{1,0:T(8,128)(2,1)S(1)}, u32[]{:S(2)}, u32[]{:S(2)}) collective-permute-start(bf16[64,128]{1,0:T(8,128)(2,1)S(1)} %get-tuple-element.60.own_far), channel_id=1, source_target_pairs={{0,7},{1,2},{2,1},{3,4},{4,3},{5,6},{6,5},{7,0},{8,15},{9,10},{10,... | collective-permute-start | bytes 49160 | tf_op jit(solution)/shard_map/ppermute | solution.py:271
  94.7 1.7 %collective-permute-done.14.side_far = bf16[64,128]{1,0:T(8,128)(2,1)S(1)} collective-permute-done((bf16[64,128]{1,0:T(8,128)(2,1)S(1)}, bf16[64,128]{1,0:T(8,128)(2,1)S(1)}, u32[]{:S(2)}, u32[]{:S(2)}) %collective-permute-start.14) | collective-permute-done | bytes 16416 | tf_op jit(solution)/shard_map/ppermute | solution.py:271
  96.4 5.5 %adjoint.1 = f32[2048,128]{1,0:T(8,128)} custom-call(s32[4]{0:T(128)S(1)} %pad_add_fusion.flags, f32[64,4096]{1,0:T(8,128)S(1)} %get-tuple-element.52.grid, f32[8,5120]{1,0:T(8,128)S(1)} %get-tuple-element.53.wide, f32[48,128]{1,0:T(8,128)S(1)} %get-tuple-element.54.rate_sides, bf16[64,512]{1,0:T(8,128)(2,1)S(1)} %collective-permute-done.11.near, ...), custom_call_target="tpu_custom_call" | custom-call | bytes 18000000 | tf_op jit(solution)/shard_map/adjoint/pallas_call | solution.py:1039
  101.9 0.0 collective-permute-done.23.refs_2_
  101.9 0.0 collective-permute-done.22.refs_1_
  101.9 1.9 %make_steps.1 = (f32[64,192]{1,0:T(8,128)}, f32[3,192,192]{2,1,0:T(8,128)}, f32[64,192]{1,0:T(8,128)}, f32[4,192]{1,0:T(4,128)}, f32[1,64]{1,0:T(1,128)}) custom-call(s32[4]{0:T(128)S(1)} %pad_add_fusion.flags, bf16[272,128]{1,0:T(8,128)(2,1)S(1)} %sum_parts.1.refs_0_, bf16[272,128]{1,0:T(8,128)(2,1)S(1)} %collective-permute-done.22.refs_1_, ...), custom_call_target="tpu_custom_call" | custom-call | bytes 6000000 | tf_op jit(solution)/shard_map/make_steps/pallas_call | solution.py:915
  (20 shorter events, 0.1 us)
Async XLA Ops:
  0.6 32.0 %copy-start.5 = (f32[16,256]{1,0:T(8,128)S(1)}, f32[16,256]{1,0:T(8,128)}, u32[]{:S(2)}) copy-start(f32[16,256]{1,0:T(8,128)} %param.12) | copy-start | bytes 49156
  0.6 29.4 %copy-start.7 = (s32[1,4096]{1,0:T(1,128)S(1)}, s32[1,4096]{1,0:T(1,128)}, u32[]{:S(2)}) copy-start(s32[1,4096]{1,0:T(1,128)} %param.13) | copy-start | bytes 49156
  0.7 29.4 %copy-start.6 = (s32[1,32]{1,0:T(1,128)S(1)}, s32[1,32]{1,0:T(1,128)}, u32[]{:S(2)}) copy-start(s32[1,32]{1,0:T(1,128)} %param.14) | copy-start | bytes 388
  2.6 11.7 %collective-permute-start.2 = (bf16[1088,128]{1,0:T(8,128)(2,1)}, bf16[1088,128]{1,0:T(8,128)(2,1)S(1)}, u32[]{:S(2)}, u32[]{:S(2)}) collective-permute-start(bf16[1088,128]{1,0:T(8,128)(2,1)} %pack_weights.1.refs_0_), channel_id=1, source_target_pairs={{0,6},{1,7},{2,4},{3,5},{4,2},{5,3},{6,0},{7,1},{8,14},{9,15},{10,... | collective-permute-start | bytes 835592 | tf_op jit(solution)/shard_map/ppermute | solution.py:1070
  6.6 12.8 %collective-permute-start.1 = (bf16[1088,128]{1,0:T(8,128)(2,1)}, bf16[1088,128]{1,0:T(8,128)(2,1)S(1)}, u32[]{:S(2)}, u32[]{:S(2)}) collective-permute-start(bf16[1088,128]{1,0:T(8,128)(2,1)} %pack_weights.1.refs_0_), channel_id=1, source_target_pairs={{0,4},{1,5},{2,6},{3,7},{4,0},{5,1},{6,2},{7,3},{8,12},{9,13},{10,... | collective-permute-start | bytes 835592 | tf_op jit(solution)/shard_map/ppermute | solution.py:1070
  7.1 12.6 %collective-permute-start = (bf16[1088,128]{1,0:T(8,128)(2,1)}, bf16[1088,128]{1,0:T(8,128)(2,1)S(1)}, u32[]{:S(2)}, u32[]{:S(2)}) collective-permute-start(bf16[1088,128]{1,0:T(8,128)(2,1)} %pack_weights.1.refs_0_), channel_id=1, source_target_pairs={{0,2},{1,3},{2,0},{3,1},{4,6},{5,7},{6,4},{7,5},{8,10},{9,11},{10,... | collective-permute-start | bytes 835592 | tf_op jit(solution)/shard_map/ppermute | solution.py:1070
  7.3 1.2 %copy-start = (f32[64,16,256]{2,1,0:T(8,128)S(1)}, f32[64,16,256]{2,1,0:T(8,128)}, u32[]{:S(2)}) copy-start(f32[64,16,256]{2,1,0:T(8,128)} %param.10) | copy-start | bytes 3145732
  8.6 0.7 copy-start.4
  9.3 23.4 %copy-start.1 = (f32[64,16,256]{2,1,0:T(8,128)S(1)}, f32[64,16,256]{2,1,0:T(8,128)}, u32[]{:S(2)}) copy-start(f32[64,16,256]{2,1,0:T(8,128)} %param.10) | copy-start | bytes 3145732
  9.3 23.4 %copy-start.3 = (f32[64,16,256]{2,1,0:T(8,128)S(1)}, f32[64,16,256]{2,1,0:T(8,128)}, u32[]{:S(2)}) copy-start(f32[64,16,256]{2,1,0:T(8,128)} %param.11) | copy-start | bytes 3145732
  10.0 10.0 %collective-permute-start.3 = (bf16[80,512]{1,0:T(8,128)(2,1)S(1)}, bf16[80,512]{1,0:T(8,128)(2,1)S(1)}, u32[]{:S(2)}, u32[]{:S(2)}) collective-permute-start(bf16[80,512]{1,0:T(8,128)(2,1)S(1)} %get-tuple-element.41), channel_id=1, source_target_pairs={{0,8},{8,0},{16,24},{24,16},{1,9},{9,1},{17,25},{25,17},{2,10},{10... | collective-permute-start | bytes 245768 | tf_op jit(solution)/shard_map/ppermute | solution.py:271
  12.0 27.0 %collective-permute-start.7 = (bf16[1088,128]{1,0:T(8,128)(2,1)}, bf16[1088,128]{1,0:T(8,128)(2,1)S(1)}, u32[]{:S(2)}, u32[]{:S(2)}) collective-permute-start(bf16[1088,128]{1,0:T(8,128)(2,1)} %pack_weights.1.refs_0_), channel_id=1, source_target_pairs={{0,1},{1,0},{2,3},{3,2},{4,5},{5,4},{6,7},{7,6},{8,9},{9,8},{10,11... | collective-permute-start | bytes 835592 | tf_op jit(solution)/shard_map/ppermute | solution.py:1077
  14.4 24.7 %collective-permute-start.10 = (bf16[1088,128]{1,0:T(8,128)(2,1)S(1)}, bf16[1088,128]{1,0:T(8,128)(2,1)S(1)}, u32[]{:S(2)}, u32[]{:S(2)}) collective-permute-start(bf16[1088,128]{1,0:T(8,128)(2,1)S(1)} %collective-permute-done.2.refs_3_), channel_id=1, source_target_pairs={{0,1},{1,0},{2,3},{3,2},{4,5},{5,4},{6,7},{7,6},{8,9},{9,8},{10,11... | collective-permute-start | bytes 835592 | tf_op jit(solution)/shard_map/ppermute | solution.py:1077
  19.4 19.6 %collective-permute-start.9 = (bf16[1088,128]{1,0:T(8,128)(2,1)S(1)}, bf16[1088,128]{1,0:T(8,128)(2,1)S(1)}, u32[]{:S(2)}, u32[]{:S(2)}) collective-permute-start(bf16[1088,128]{1,0:T(8,128)(2,1)S(1)} %collective-permute-done.1.refs_2_), channel_id=1, source_target_pairs={{0,1},{1,0},{2,3},{3,2},{4,5},{5,4},{6,7},{7,6},{8,9},{9,8},{10,11... | collective-permute-start | bytes 835592 | tf_op jit(solution)/shard_map/ppermute | solution.py:1077
  19.7 19.4 %collective-permute-start.8 = (bf16[1088,128]{1,0:T(8,128)(2,1)S(1)}, bf16[1088,128]{1,0:T(8,128)(2,1)S(1)}, u32[]{:S(2)}, u32[]{:S(2)}) collective-permute-start(bf16[1088,128]{1,0:T(8,128)(2,1)S(1)} %collective-permute-done.refs_1_), channel_id=1, source_target_pairs={{0,1},{1,0},{2,3},{3,2},{4,5},{5,4},{6,7},{7,6},{8,9},{9,8},{10,11... | collective-permute-start | bytes 835592 | tf_op jit(solution)/shard_map/ppermute | solution.py:1077
  20.0 6.6 %collective-permute-start.4 = (bf16[80,512]{1,0:T(8,128)(2,1)S(1)}, bf16[80,512]{1,0:T(8,128)(2,1)S(1)}, u32[]{:S(2)}, u32[]{:S(2)}) collective-permute-start(bf16[80,512]{1,0:T(8,128)(2,1)S(1)} %get-tuple-element.42), channel_id=1, source_target_pairs={{0,24},{8,16},{16,8},{24,0},{1,25},{9,17},{17,9},{25,1},{2,26},{10... | collective-permute-start | bytes 245768 | tf_op jit(solution)/shard_map/ppermute | solution.py:271
  27.3 1.3 %collective-permute-start.5 = (bf16[80,128]{1,0:T(8,128)(2,1)S(1)}, bf16[80,128]{1,0:T(8,128)(2,1)S(1)}, u32[]{:S(2)}, u32[]{:S(2)}) collective-permute-start(bf16[80,128]{1,0:T(8,128)(2,1)S(1)} %get-tuple-element.45.own_near), channel_id=1, source_target_pairs={{0,1},{1,0},{2,3},{3,2},{4,5},{5,4},{6,7},{7,6},{8,9},{9,8},{10,11... | collective-permute-start | bytes 61448 | tf_op jit(solution)/shard_map/ppermute | solution.py:271
  28.5 4.1 %collective-permute-start.6 = (bf16[80,128]{1,0:T(8,128)(2,1)S(1)}, bf16[80,128]{1,0:T(8,128)(2,1)S(1)}, u32[]{:S(2)}, u32[]{:S(2)}) collective-permute-start(bf16[80,128]{1,0:T(8,128)(2,1)S(1)} %get-tuple-element.46.own_far), channel_id=1, source_target_pairs={{0,7},{1,2},{2,1},{3,4},{4,3},{5,6},{6,5},{7,0},{8,15},{9,10},{10,... | collective-permute-start | bytes 61448 | tf_op jit(solution)/shard_map/ppermute | solution.py:271
  39.0 9.5 %copy-start.2 = (bf16[1088,128]{1,0:T(8,128)(2,1)S(1)}, bf16[1088,128]{1,0:T(8,128)(2,1)}, u32[]{:S(2)}) copy-start(bf16[1088,128]{1,0:T(8,128)(2,1)} %pack_weights.1.refs_0_) | copy-start | bytes 835588
  48.5 9.6 %collective-permute-start.15 = (bf16[4,1088,128]{2,1,0:T(8,128)(2,1)S(1)}, bf16[4,1088,128]{2,1,0:T(8,128)(2,1)S(1)}, u32[]{:S(2)}, u32[]{:S(2)}) collective-permute-start(bf16[4,1088,128]{2,1,0:T(8,128)(2,1)S(1)} %get-tuple-element.62), channel_id=1, source_target_pairs={{0,1},{1,0},{2,3},{3,2},{4,5},{5,4},{6,7},{7,6},{8,9},{9,8},{10,11... | collective-permute-start | bytes 3342344 | tf_op jit(solution)/shard_map/ppermute | solution.py:1084
  58.3 9.6 %collective-permute-start.16 = (bf16[1088,128]{1,0:T(8,128)(2,1)S(1)}, bf16[1088,128]{1,0:T(8,128)(2,1)S(1)}, u32[]{:S(2)}, u32[]{:S(2)}) collective-permute-start(bf16[1088,128]{1,0:T(8,128)(2,1)S(1)} %get-tuple-element.64), channel_id=1, source_target_pairs={{0,2},{1,3},{2,0},{3,1},{4,6},{5,7},{6,4},{7,5},{8,10},{9,11},{10,... | collective-permute-start | bytes 835592 | tf_op jit(solution)/shard_map/ppermute | solution.py:1091
  60.0 8.8 %collective-permute-start.17 = (bf16[1088,128]{1,0:T(8,128)(2,1)S(1)}, bf16[1088,128]{1,0:T(8,128)(2,1)S(1)}, u32[]{:S(2)}, u32[]{:S(2)}) collective-permute-start(bf16[1088,128]{1,0:T(8,128)(2,1)S(1)} %get-tuple-element.65), channel_id=1, source_target_pairs={{0,4},{1,5},{2,6},{3,7},{4,0},{5,1},{6,2},{7,3},{8,12},{9,13},{10,... | collective-permute-start | bytes 835592 | tf_op jit(solution)/shard_map/ppermute | solution.py:1091
  60.8 13.5 %collective-permute-start.18 = (bf16[1088,128]{1,0:T(8,128)(2,1)S(1)}, bf16[1088,128]{1,0:T(8,128)(2,1)S(1)}, u32[]{:S(2)}, u32[]{:S(2)}) collective-permute-start(bf16[1088,128]{1,0:T(8,128)(2,1)S(1)} %get-tuple-element.66), channel_id=1, source_target_pairs={{0,6},{1,7},{2,4},{3,5},{4,2},{5,3},{6,0},{7,1},{8,14},{9,15},{10,... | collective-permute-start | bytes 835592 | tf_op jit(solution)/shard_map/ppermute | solution.py:1091
  75.2 10.3 %collective-permute-start.19 = (bf16[272,128]{1,0:T(8,128)(2,1)S(1)}, bf16[272,128]{1,0:T(8,128)(2,1)S(1)}, u32[]{:S(2)}, u32[]{:S(2)}) collective-permute-start(bf16[272,128]{1,0:T(8,128)(2,1)S(1)} %get-tuple-element.68), channel_id=1, source_target_pairs={{0,8},{8,0},{16,24},{24,16},{1,9},{9,1},{17,25},{25,17},{2,10},{10... | collective-permute-start | bytes 208904 | tf_op jit(solution)/shard_map/ppermute | solution.py:1100
  76.6 8.9 %collective-permute-start.20 = (bf16[272,128]{1,0:T(8,128)(2,1)S(1)}, bf16[272,128]{1,0:T(8,128)(2,1)S(1)}, u32[]{:S(2)}, u32[]{:S(2)}) collective-permute-start(bf16[272,128]{1,0:T(8,128)(2,1)S(1)} %get-tuple-element.69), channel_id=1, source_target_pairs={{0,16},{8,24},{16,0},{24,8},{1,17},{9,25},{17,1},{25,9},{2,18},{10... | collective-permute-start | bytes 208904 | tf_op jit(solution)/shard_map/ppermute | solution.py:1100
  79.2 6.4 %collective-permute-start.21 = (bf16[272,128]{1,0:T(8,128)(2,1)S(1)}, bf16[272,128]{1,0:T(8,128)(2,1)S(1)}, u32[]{:S(2)}, u32[]{:S(2)}) collective-permute-start(bf16[272,128]{1,0:T(8,128)(2,1)S(1)} %get-tuple-element.70), channel_id=1, source_target_pairs={{0,24},{8,16},{16,8},{24,0},{1,25},{9,17},{17,9},{25,1},{2,26},{10... | collective-permute-start | bytes 208904 | tf_op jit(solution)/shard_map/ppermute | solution.py:1100
  81.9 9.5 %collective-permute-start.11 = (bf16[64,512]{1,0:T(8,128)(2,1)S(1)}, bf16[64,512]{1,0:T(8,128)(2,1)S(1)}, u32[]{:S(2)}, u32[]{:S(2)}) collective-permute-start(bf16[64,512]{1,0:T(8,128)(2,1)S(1)} %get-tuple-element.55), channel_id=1, source_target_pairs={{0,8},{8,0},{16,24},{24,16},{1,9},{9,1},{17,25},{25,17},{2,10},{10... | collective-permute-start | bytes 196616 | tf_op jit(solution)/shard_map/ppermute | solution.py:271
  82.5 9.0 %collective-permute-start.12 = (bf16[64,512]{1,0:T(8,128)(2,1)S(1)}, bf16[64,512]{1,0:T(8,128)(2,1)S(1)}, u32[]{:S(2)}, u32[]{:S(2)}) collective-permute-start(bf16[64,512]{1,0:T(8,128)(2,1)S(1)} %get-tuple-element.56), channel_id=1, source_target_pairs={{0,24},{8,16},{16,8},{24,0},{1,25},{9,17},{17,9},{25,1},{2,26},{10... | collective-permute-start | bytes 196616 | tf_op jit(solution)/shard_map/ppermute | solution.py:271
  85.7 16.2 %collective-permute-start.24 = (bf16[272,128]{1,0:T(8,128)(2,1)S(1)}, bf16[272,128]{1,0:T(8,128)(2,1)S(1)}, u32[]{:S(2)}, u32[]{:S(2)}) collective-permute-start(bf16[272,128]{1,0:T(8,128)(2,1)S(1)} %sum_parts.1.refs_0_), channel_id=1, source_target_pairs={{0,24},{8,16},{16,8},{24,0},{1,25},{9,17},{17,9},{25,1},{2,26},{10... | collective-permute-start | bytes 208904 | tf_op jit(solution)/shard_map/ppermute | solution.py:1104
  87.2 14.7 %collective-permute-start.23 = (bf16[272,128]{1,0:T(8,128)(2,1)S(1)}, bf16[272,128]{1,0:T(8,128)(2,1)S(1)}, u32[]{:S(2)}, u32[]{:S(2)}) collective-permute-start(bf16[272,128]{1,0:T(8,128)(2,1)S(1)} %sum_parts.1.refs_0_), channel_id=1, source_target_pairs={{0,16},{8,24},{16,0},{24,8},{1,17},{9,25},{17,1},{25,9},{2,18},{10... | collective-permute-start | bytes 208904 | tf_op jit(solution)/shard_map/ppermute | solution.py:1104
  88.1 13.8 %collective-permute-start.22 = (bf16[272,128]{1,0:T(8,128)(2,1)S(1)}, bf16[272,128]{1,0:T(8,128)(2,1)S(1)}, u32[]{:S(2)}, u32[]{:S(2)}) collective-permute-start(bf16[272,128]{1,0:T(8,128)(2,1)S(1)} %sum_parts.1.refs_0_), channel_id=1, source_target_pairs={{0,8},{8,0},{16,24},{24,16},{1,9},{9,1},{17,25},{25,17},{2,10},{10... | collective-permute-start | bytes 208904 | tf_op jit(solution)/shard_map/ppermute | solution.py:1104
  92.2 2.5 %collective-permute-start.13 = (bf16[64,128]{1,0:T(8,128)(2,1)S(1)}, bf16[64,128]{1,0:T(8,128)(2,1)S(1)}, u32[]{:S(2)}, u32[]{:S(2)}) collective-permute-start(bf16[64,128]{1,0:T(8,128)(2,1)S(1)} %get-tuple-element.59.own_near), channel_id=1, source_target_pairs={{0,1},{1,0},{2,3},{3,2},{4,5},{5,4},{6,7},{7,6},{8,9},{9,8},{10,11... | collective-permute-start | bytes 49160 | tf_op jit(solution)/shard_map/ppermute | solution.py:271
  92.2 4.2 %collective-permute-start.14 = (bf16[64,128]{1,0:T(8,128)(2,1)S(1)}, bf16[64,128]{1,0:T(8,128)(2,1)S(1)}, u32[]{:S(2)}, u32[]{:S(2)}) collective-permute-start(bf16[64,128]{1,0:T(8,128)(2,1)S(1)} %get-tuple-element.60.own_far), channel_id=1, source_target_pairs={{0,7},{1,2},{2,1},{3,4},{4,3},{5,6},{6,5},{7,0},{8,15},{9,10},{10,... | collective-permute-start | bytes 49160 | tf_op jit(solution)/shard_map/ppermute | solution.py:271

commit v6 on v5

--- a/solution.py
+++ b/solution.py
@@ -26,6 +26,14 @@
 
 F32 = jnp.float32
 BF16 = jnp.bfloat16
+
+
+def with_flags(body):
+    def inner(*refs):
+        tile, sub = lax.axis_index("tile"), lax.axis_index("sub")
+        return body((tile & 1, sub & 1, tile, sub), *refs)
+
+    return inner
 
 
 def load_all(sources, targets, semaphores, first=0):
@@ -147,17 +155,17 @@
     )
 
 
-def pack_rows_out(flags, field_rows, diff_rows, levels, width_x, width_y):
+def pack_rows_out(field_rows, diff_rows, levels, width_x, width_y):
     shape = jax.ShapeDtypeStruct((levels + 2 * SUBLANES, 2 * width_y), BF16)
     return pl.pallas_call(
-        functools.partial(row_pack_body, levels, width_x, width_y),
+        with_flags(functools.partial(row_pack_body, levels, width_x, width_y)),
         out_shape=[shape] * 2,
-        in_specs=[SMEM] + [VMEM] * 2,
+        in_specs=[VMEM] * 2,
         out_specs=[VMEM] * 2,
         compiler_params=params(8),
         cost_estimate=cost(8),
         name="pack_rows",
-    )(flags, field_rows, diff_rows)
+    )(field_rows, diff_rows)
 
 
 def outer_row(flag, first, other, where, which, x, width_x, width_y):
@@ -184,17 +192,17 @@
     )
 
 
-def pack_columns_out(flags, field_rows, diff_rows, levels, width_x, width_y):
+def pack_columns_out(field_rows, diff_rows, levels, width_x, width_y):
     shape = jax.ShapeDtypeStruct((levels + 2 * SUBLANES, LANES), BF16)
     return pl.pallas_call(
-        functools.partial(column_pack_body, levels, width_x, width_y),
+        with_flags(functools.partial(column_pack_body, levels, width_x, width_y)),
         out_shape=[shape] * 2,
-        in_specs=[SMEM] + [VMEM] * 2,
+        in_specs=[VMEM] * 2,
         out_specs=[VMEM] * 2,
         compiler_params=params(8),
         cost_estimate=cost(2),
         name="pack_columns",
-    )(flags, field_rows, diff_rows)
+    )(field_rows, diff_rows)
 
 
 def back_pack_body(levels, width_x, width_y, flags, grid, first, other):
@@ -209,17 +217,17 @@
     lax.fori_loop(0, levels // (2 * SUBLANES), step, 0)
 
 
-def pack_columns_back(flags, grid, levels, width_x, width_y):
+def pack_columns_back(grid, levels, width_x, width_y):
     shape = jax.ShapeDtypeStruct((levels, LANES), BF16)
     return pl.pallas_call(
-        functools.partial(back_pack_body, levels, width_x, width_y),
+        with_flags(functools.partial(back_pack_body, levels, width_x, width_y)),
         out_shape=[shape] * 2,
-        in_specs=[SMEM] + [VMEM],
+        in_specs=[VMEM],
         out_specs=[VMEM] * 2,
         compiler_params=params(8),
         cost_estimate=cost(2),
         name="pack_back",
-    )(flags, grid)
+    )(grid)
 
 
 def corner_body(width_x, width_y, flags, near, far, first_in, other_in, first, other):
@@ -245,17 +253,17 @@
     other[...] = insert(other_in, lambda row: jnp.where(flags[1] == 0, low(row), high(row)))
 
 
-def add_corners(flags, near, far, first, other, width_x, width_y):
+def add_corners(near, far, first, other, width_x, width_y):
     shape = jax.ShapeDtypeStruct(first.shape, BF16)
     return pl.pallas_call(
-        functools.partial(corner_body, width_x, width_y),
+        with_flags(functools.partial(corner_body, width_x, width_y)),
         out_shape=[shape] * 2,
-        in_specs=[SMEM] + [VMEM] * 4,
+        in_specs=[VMEM] * 4,
         out_specs=[VMEM] * 2,
         compiler_params=params(8),
         cost_estimate=cost(1),
         name="add_corners",
-    )(flags, near, far, first, other)
+    )(near, far, first, other)
 
 
 def partners(size, offset):
@@ -360,18 +368,18 @@
     lax.fori_loop(0, cells // LANES, turn, 0, unroll=2)
 
 
-def forward(flags, field_rows, target_rows, diff_rows, near, own, sides, sizes):
+def forward(field_rows, target_rows, diff_rows, near, own, sides, sizes):
     levels, width_x, width_y, _, _ = sizes
     cells = width_x * width_y
     extended = (SUBLANES, (width_x + 4) * width_y)
     return pl.pallas_call(
-        functools.partial(forward_body, levels, width_x, width_y),
+        with_flags(functools.partial(forward_body, levels, width_x, width_y)),
         out_shape=[
             jax.ShapeDtypeStruct((cells, 2 * levels), F32),
             jax.ShapeDtypeStruct(extended, F32),
             jax.ShapeDtypeStruct((6 * SUBLANES, LANES), F32),
         ],
-        in_specs=[SMEM] + [VMEM] * 9,
+        in_specs=[VMEM] * 9,
         out_specs=[VMEM] * 3,
         scratch_shapes=[
             pltpu.VMEM(extended, F32),
@@ -382,7 +390,7 @@
         compiler_params=params(8),
         cost_estimate=cost(8),
         name="forward",
-    )(flags, field_rows, target_rows, diff_rows, *near, *own, *sides)
+    )(field_rows, target_rows, diff_rows, *near, *own, *sides)
 
 
 def index_body(tiles, subs, lead, rows_each, flags, counts, order, out, starts):
@@ -420,7 +428,7 @@
     lax.fori_loop(0, subs, expert, 0)
 
 
-def slot_cells(flags, counts, column_order, sizes):
+def slot_cells(counts, column_order, sizes):
     _, width_x, width_y, tiles, subs = sizes
     cells = width_x * width_y
     packet = cells // subs
@@ -428,15 +436,15 @@
     lead = packet
     order = jnp.pad(column_order, (lead, SUBLANES * LANES)).reshape(-1, LANES)
     return pl.pallas_call(
-        functools.partial(index_body, tiles, subs, lead, rows_each),
+        with_flags(functools.partial(index_body, tiles, subs, lead, rows_each)),
         out_shape=jax.ShapeDtypeStruct((cells // LANES, LANES), jnp.int32),
-        in_specs=[SMEM] * 2 + [VMEM],
+        in_specs=[SMEM] + [VMEM],
         out_specs=VMEM,
         scratch_shapes=[pltpu.SMEM((tiles * subs,), jnp.int32)],
         compiler_params=params(4),
         cost_estimate=cost(2),
         name="slot_cells",
-    )(flags, counts, order).reshape(subs, 1, packet)
+    )(counts, order).reshape(subs, 1, packet)
 
 
 def widen(value):
@@ -838,18 +846,18 @@
         out[...] = whole[pl.ds(start, rows), :].astype(BF16)
 
 
-def sum_and_share(flags, parts, tiles):
+def sum_and_share(parts, tiles):
     rows = parts[0].shape[0]
     return pl.pallas_call(
-        functools.partial(share_body, len(parts)),
+        with_flags(functools.partial(share_body, len(parts))),
         out_shape=[jax.ShapeDtypeStruct((rows // tiles, LANES), BF16)] * tiles,
-        in_specs=[SMEM] + [VMEM] * len(parts),
+        in_specs=[VMEM] * len(parts),
         out_specs=[VMEM] * tiles,
         scratch_shapes=[pltpu.VMEM((rows, LANES), F32)],
         compiler_params=params(8),
         cost_estimate=cost(1),
         name="sum_and_share",
-    )(flags, *parts)
+    )(*parts)
 
 
 def sum_body(*refs):
@@ -910,10 +918,10 @@
     bias_last[...] = swap_halves(tail[6:7])[:, :half]
 
 
-def make_steps(flags, parts, levels, width):
+def make_steps(parts, levels, width):
     count = 2 * levels * width + 3 * width * width + 4 * width + levels
     return pl.pallas_call(
-        functools.partial(steps_body, levels, width, float(count), len(parts)),
+        with_flags(functools.partial(steps_body, levels, width, float(count), len(parts))),
         out_shape=[
             jax.ShapeDtypeStruct((levels, width), F32),
             jax.ShapeDtypeStruct((3, width, width), F32),
@@ -921,13 +929,13 @@
             jax.ShapeDtypeStruct((4, width), F32),
             jax.ShapeDtypeStruct((1, levels), F32),
         ],
-        in_specs=[SMEM] + [VMEM] * len(parts),
+        in_specs=[VMEM] * len(parts),
         out_specs=[VMEM] * 5,
         scratch_shapes=[pltpu.VMEM((len(parts) * parts[0].shape[0], LANES), BF16)],
         compiler_params=params(8),
         cost_estimate=cost(2),
         name="make_steps",
-    )(flags, *parts)
+    )(*parts)
 
 
 def collect_body(levels, width_x, width_y, flags, rows, grid, first, other):
@@ -951,19 +959,19 @@
     lax.fori_loop(0, levels // (2 * SUBLANES), step, 0)
 
 
-def collect(flags, rows, sizes):
+def collect(rows, sizes):
     levels, width_x, width_y, _, _ = sizes
     cells = width_x * width_y
     shape = jax.ShapeDtypeStruct((levels, 2 * width_y), BF16)
     return pl.pallas_call(
-        functools.partial(collect_body, levels, width_x, width_y),
+        with_flags(functools.partial(collect_body, levels, width_x, width_y)),
         out_shape=[jax.ShapeDtypeStruct((levels, cells), F32), shape, shape],
-        in_specs=[SMEM, VMEM],
+        in_specs=[VMEM],
         out_specs=[VMEM] * 3,
         compiler_params=params(8),
         cost_estimate=cost(3),
         name="collect",
-    )(flags, rows)
+    )(rows)
 
 
 def adjoint_body(
@@ -1033,19 +1041,19 @@
     lax.fori_loop(0, levels // (2 * SUBLANES), step, 0)
 
 
-def adjoint(flags, grid, rates, rate_sides, near, own, sides, sizes):
+def adjoint(grid, rates, rate_sides, near, own, sides, sizes):
     levels, width_x, width_y, _, _ = sizes
     extended = (SUBLANES, (width_x + 4) * width_y)
     return pl.pallas_call(
-        functools.partial(adjoint_body, levels, width_x, width_y),
+        with_flags(functools.partial(adjoint_body, levels, width_x, width_y)),
         out_shape=jax.ShapeDtypeStruct((levels * width_x * width_y // LANES, LANES), F32),
-        in_specs=[SMEM] + [VMEM] * 9,
+        in_specs=[VMEM] * 9,
         out_specs=VMEM,
         scratch_shapes=[pltpu.VMEM(extended, F32), pltpu.VMEM(extended, F32)],
         compiler_params=params(8),
         cost_estimate=cost(6),
         name="adjoint",
-    )(flags, grid, rates, rate_sides, *near, *own, *sides)
+    )(grid, rates, rate_sides, *near, *own, *sides)
 
 
 def local_program(
@@ -1060,24 +1068,20 @@
     diff_rows = tile_rows(diffusivity[None])
     width = w_first.shape[2]
     half = subs // 2
-    tile_id, sub_id = lax.axis_index("tile"), lax.axis_index("sub")
-    flags = jnp.stack([tile_id % 2, sub_id % 2, tile_id, sub_id]).astype(jnp.int32)
     area = (levels, width_x, width_y)
 
-    first, other = pack_rows_out(flags, field_rows, diff_rows, *area)
+    first, other = pack_rows_out(field_rows, diff_rows, *area)
     weights = pack_weights(w_first[0], w_inner[0], w_last[0], b_inner[0], b_last, tiles)
     own_weights = [weights] + [
         lax.ppermute(weights, "sub", partners(subs, 2 * c)) for c in range(1, half)
     ]
     near = trade_sides(first, other, "tile")
-    cells_of = slot_cells(flags, send_counts[0], column_order[0], sizes)
-    own = pack_columns_out(flags, field_rows, diff_rows, *area)
-    own = add_corners(flags, *near, *own, width_x, width_y)
+    cells_of = slot_cells(send_counts[0], column_order[0], sizes)
+    own = pack_columns_out(field_rows, diff_rows, *area)
+    own = add_corners(*near, *own, width_x, width_y)
     sides = trade_sides(*own, "sub")
     other_weights = [lax.ppermute(pack, "sub", partners(subs, 1)) for pack in own_weights]
-    rows, rates, rate_sides = forward(
-        flags, field_rows, target_rows, diff_rows, near, own, sides, sizes
-    )
+    rows, rates, rate_sides = forward(field_rows, target_rows, diff_rows, near, own, sides, sizes)
     back, other_grads, taken, given_back = network(
         cells_of, other_weights, rows, None, 0, levels, width, subs
     )
@@ -1090,19 +1094,19 @@
     arrived = [both_grads[0]] + [
         lax.ppermute(both_grads[c], "sub", partners(subs, 2 * c)) for c in range(1, half)
     ]
-    grid, g_first, g_other = collect(flags, back, sizes)
+    grid, g_first, g_other = collect(back, sizes)
     g_near = trade_sides(g_first, g_other, "tile")
-    g_own = pack_columns_back(flags, grid, *area)
-    g_own = add_corners(flags, *g_near, *g_own, width_x, width_y)
+    g_own = pack_columns_back(grid, *area)
+    g_own = add_corners(*g_near, *g_own, width_x, width_y)
     g_sides = trade_sides(*g_own, "sub")
-    shares = sum_and_share(flags, arrived, tiles)
+    shares = sum_and_share(arrived, tiles)
     mine = [shares[0]] + [
         lax.ppermute(shares[d], "tile", partners(tiles, d)) for d in range(1, tiles)
     ]
-    result = adjoint(flags, grid, rates, rate_sides, g_near, g_own, g_sides, sizes)
+    result = adjoint(grid, rates, rate_sides, g_near, g_own, g_sides, sizes)
     piece = sum_parts(mine)
     pieces = [piece] + [lax.ppermute(piece, "tile", partners(tiles, d)) for d in range(1, tiles)]
-    steps = make_steps(flags, pieces, levels, width)
+    steps = make_steps(pieces, levels, width)
     return (
         untile_rows(result, levels, width_x, width_y),
         steps[0][None], steps[1][None], steps[2].T[None], steps[3][None], steps[4],

time: 104 us -> 101 us (0.971)
  Pallas kernels: 44.5 us -> 39 us
  waiting for transfers between devices: 25.5 us -> 28.8 us
    pallas_call x11, Pallas kernels: 23.4 us -> 18 us  [the longest x1 5.79 us: forward(): pl.pallas_call(with_flags(functools.partial(forward_body, levels, width_x...]
    ppermute x4, waiting for transfers between devices: 4.01 us -> 5.59 us  [trade_sides(): lax.ppermute(other, axis, beyond(size))]
    ppermute x3, waiting for transfers between devices: 0.15 us -> 1.23 us  [local_program(): lax.ppermute(shares[d], 'tile', partners(tiles, d))]
  transfers between devices with their start and end apart: 25 -> 25, of which waited for: 11 -> 11; matrix products, arithmetic and copies ran while one was open for 0% -> 0% of each run, Pallas kernels for 29% -> 26%
where the time goes in v6:
time: 101 us
  Pallas kernels  39 us (39%)
  starting transfers between devices  29.9 us (30%)
  waiting for transfers between devices  28.8 us (29%)
  local copies, waits for them, and re-layouts  1.97 us (2%)
    pallas_call x2, Pallas kernels, network(): pl.pallas_call(body, grid=(blocks,), out_shape=[jax.ShapeDtypeStruct((cel...  18.8 us
    ppermute x3, waiting for transfers between devices, local_program(): lax.ppermute(both_grads[c], 'sub', partners(subs, 2 * c))  12.5 us
    ppermute x4, starting transfers between devices, trade_sides(): lax.ppermute(other, axis, beyond(size))  9.84 us
    ppermute x3, waiting for transfers between devices, local_program(): lax.ppermute(weights, 'sub', partners(subs, 2 * c))  8.3 us
    pallas_call x1, Pallas kernels, forward(): pl.pallas_call(with_flags(functools.partial(forward_body, levels, width_x...  5.79 us
    ppermute x4, waiting for transfers between devices, trade_sides(): lax.ppermute(other, axis, beyond(size))  5.59 us
    pallas_call x1, Pallas kernels, adjoint(): pl.pallas_call(with_flags(functools.partial(adjoint_body, levels, width_x...  4.99 us
    ppermute x3, starting transfers between devices, local_program(): lax.ppermute(weights, 'sub', partners(subs, 2 * c))  4.63 us
  transfers between devices with their start and end apart: 25, of which 11 were waited for; matrix products, arithmetic and copies ran while one was open for 0% of the time, Pallas kernels for 26%

profile of v6, /device:TPU:0, one launch (start us, length us, event | category | flops | bytes accessed | tf_op | source)
XLA Modules:
  0.0 100.6 jit_solution(10859965344105830092)
XLA Ops:
  0.6 0.0 copy-start.5
  0.7 1.9 %pack_weights.1.refs_0_ = bf16[1088,128]{1,0:T(8,128)(2,1)} custom-call(bf16[64,192]{1,0:T(8,128)(2,1)} %bitcast.51, bf16[3,192,192]{2,1,0:T(8,128)(2,1)} %bitcast.50, bf16[64,192]{1,0:T(8,128)(2,1)} %bitcast.52, f32[4,192]{1,0:T(4,128)} %bitcast.54, f32[1,64]{1,0:T(1,128)} %refs_4_.1), custom_call_target="tpu_custom_call" | custom-call | bytes 3000000 | tf_op jit(solution)/shard_map/pack_weights/pallas_call | solution.py:530
  2.6 4.0 %collective-permute-start.2 = (bf16[1088,128]{1,0:T(8,128)(2,1)}, bf16[1088,128]{1,0:T(8,128)(2,1)S(1)}, u32[]{:S(2)}, u32[]{:S(2)}) collective-permute-start(bf16[1088,128]{1,0:T(8,128)(2,1)} %pack_weights.1.refs_0_), channel_id=1, source_target_pairs={{0,6},{1,7},{2,4},{3,5},{4,2},{5,3},{6,0},{7,1},{8,14},{9,15},{10,... | collective-permute-start | bytes 835592 | tf_op jit(solution)/shard_map/ppermute | solution.py:1076
  6.6 0.5 collective-permute-start.1
  7.1 0.1 collective-permute-start
  7.3 1.2 %copy-done = f32[64,16,256]{2,1,0:T(8,128)S(1)} copy-done((f32[64,16,256]{2,1,0:T(8,128)S(1)}, f32[64,16,256]{2,1,0:T(8,128)}, u32[]{:S(2)}) %copy-start) | copy-done | bytes 1048600
  8.5 0.7 copy-done.4
  9.2 0.2 pack_rows.1
  9.4 2.0 %collective-permute-start.3 = (bf16[80,512]{1,0:T(8,128)(2,1)S(1)}, bf16[80,512]{1,0:T(8,128)(2,1)S(1)}, u32[]{:S(2)}, u32[]{:S(2)}) collective-permute-start(bf16[80,512]{1,0:T(8,128)(2,1)S(1)} %get-tuple-element.41), channel_id=1, source_target_pairs={{0,8},{8,0},{16,24},{24,16},{1,9},{9,1},{17,25},{25,17},{2,10},{10... | collective-permute-start | bytes 245768 | tf_op jit(solution)/shard_map/ppermute | solution.py:279
  11.4 0.0 collective-permute-start.7
  11.4 3.0 %collective-permute-done.2.refs_3_ = bf16[1088,128]{1,0:T(8,128)(2,1)S(1)} collective-permute-done((bf16[1088,128]{1,0:T(8,128)(2,1)}, bf16[1088,128]{1,0:T(8,128)(2,1)S(1)}, u32[]{:S(2)}, u32[]{:S(2)}) %collective-permute-start.2) | collective-permute-done | bytes 278560 | tf_op jit(solution)/shard_map/ppermute | solution.py:1076
  14.4 0.0 collective-permute-start.10
  14.4 5.1 %collective-permute-done.1.refs_2_ = bf16[1088,128]{1,0:T(8,128)(2,1)S(1)} collective-permute-done((bf16[1088,128]{1,0:T(8,128)(2,1)}, bf16[1088,128]{1,0:T(8,128)(2,1)S(1)}, u32[]{:S(2)}, u32[]{:S(2)}) %collective-permute-start.1) | collective-permute-done | bytes 278560 | tf_op jit(solution)/shard_map/ppermute | solution.py:1076
  19.4 0.0 collective-permute-start.9
  19.5 0.3 collective-permute-done.refs_1_
  19.7 0.2 collective-permute-start.8
  20.0 0.0 collective-permute-done.3.refs_0_.refs_3_
  20.0 3.8 %collective-permute-start.4 = (bf16[80,512]{1,0:T(8,128)(2,1)S(1)}, bf16[80,512]{1,0:T(8,128)(2,1)S(1)}, u32[]{:S(2)}, u32[]{:S(2)}) collective-permute-start(bf16[80,512]{1,0:T(8,128)(2,1)S(1)} %get-tuple-element.42), channel_id=1, source_target_pairs={{0,24},{8,16},{16,8},{24,0},{1,25},{9,17},{17,9},{25,1},{2,26},{10... | collective-permute-start | bytes 245768 | tf_op jit(solution)/shard_map/ppermute | solution.py:279
  23.8 1.1 %pack_columns.1 = (bf16[80,128]{1,0:T(8,128)(2,1)S(1)}, bf16[80,128]{1,0:T(8,128)(2,1)S(1)}) custom-call(f32[2048,128]{1,0:T(8,128)S(1)} %bitcast.38, f32[32,128]{1,0:T(8,128)S(1)} %bitcast.46), custom_call_target="tpu_custom_call" | custom-call | bytes 6000000 | tf_op jit(solution)/shard_map/pack_columns/pallas_call | solution.py:197
  24.8 1.7 %collective-permute-done.4.refs_1_.refs_4_ = bf16[80,512]{1,0:T(8,128)(2,1)S(1)} collective-permute-done((bf16[80,512]{1,0:T(8,128)(2,1)S(1)}, bf16[80,512]{1,0:T(8,128)(2,1)S(1)}, u32[]{:S(2)}, u32[]{:S(2)}) %collective-permute-start.4) | collective-permute-done | bytes 81952 | tf_op jit(solution)/shard_map/ppermute | solution.py:279
  26.6 0.2 add_corners.2
  26.7 0.1 collective-permute-start.5
  26.8 1.2 %collective-permute-done.5.refs_7_ = bf16[80,128]{1,0:T(8,128)(2,1)S(1)} collective-permute-done((bf16[80,128]{1,0:T(8,128)(2,1)S(1)}, bf16[80,128]{1,0:T(8,128)(2,1)S(1)}, u32[]{:S(2)}, u32[]{:S(2)}) %collective-permute-start.5) | collective-permute-done | bytes 20512 | tf_op jit(solution)/shard_map/ppermute | solution.py:279
  28.0 1.5 %collective-permute-start.6 = (bf16[80,128]{1,0:T(8,128)(2,1)S(1)}, bf16[80,128]{1,0:T(8,128)(2,1)S(1)}, u32[]{:S(2)}, u32[]{:S(2)}) collective-permute-start(bf16[80,128]{1,0:T(8,128)(2,1)S(1)} %get-tuple-element.46.refs_6_), channel_id=1, source_target_pairs={{0,7},{1,2},{2,1},{3,4},{4,3},{5,6},{6,5},{7,0},{8,15},{9,10},{10,... | collective-permute-start | bytes 61448 | tf_op jit(solution)/shard_map/ppermute | solution.py:279
  29.5 1.5 %slot_cells.1 = s32[32,128]{1,0:T(8,128)S(1)} custom-call(s32[32]{0:T(128)S(1)} %bitcast.48, s32[44,128]{1,0:T(8,128)S(1)} %pad_bitcast_fusion.refs_1_), custom_call_target="tpu_custom_call" | custom-call | bytes 6000000 | tf_op jit(solution)/shard_map/slot_cells/pallas_call | solution.py:438
  31.0 1.1 %collective-permute-done.6.refs_8_ = bf16[80,128]{1,0:T(8,128)(2,1)S(1)} collective-permute-done((bf16[80,128]{1,0:T(8,128)(2,1)S(1)}, bf16[80,128]{1,0:T(8,128)(2,1)S(1)}, u32[]{:S(2)}, u32[]{:S(2)}) %collective-permute-start.6) | collective-permute-done | bytes 20512 | tf_op jit(solution)/shard_map/ppermute | solution.py:279
  32.1 5.8 %forward.1 = (f32[4096,128]{1,0:T(8,128)S(1)}, f32[8,5120]{1,0:T(8,128)S(1)}, f32[48,128]{1,0:T(8,128)S(1)}) custom-call(f32[2048,128]{1,0:T(8,128)S(1)} %bitcast.39, f32[2048,128]{1,0:T(8,128)S(1)} %bitcast.40, f32[32,128]{1,0:T(8,128)S(1)} %bitcast.47, bf16[80,512]{1,0:T(8,128)(2,1)S(1)} %collective-permute-done.3.refs_0_.refs_3_, ...), custom_call_target="tpu_custom_call" | custom-call | bytes 24000000 | tf_op jit(solution)/shard_map/forward/pallas_call | solution.py:375
  37.9 0.0 copy-start.2
  37.9 0.0 collective-permute-done.7.refs_0_
  37.9 0.0 collective-permute-done.10.refs_3_
  37.9 0.0 collective-permute-done.9.refs_2_
  37.9 0.0 collective-permute-done.8.refs_1_
  38.0 9.4 %network.2 = (f32[4096,128]{1,0:T(8,128)S(1)}, bf16[4,1088,128]{2,1,0:T(8,128)(2,1)S(1)}, f32[512,128]{1,0:T(8,128)S(1)}, f32[512,128]{1,0:T(8,128)S(1)}) custom-call(s32[8,1,512]{2,1,0:T(1,128)S(1)} %bitcast.41, s32[8,1,512]{2,1,0:T(1,128)S(1)} %bitcast.42, bf16[1088,128]{1,0:T(8,128)(2,1)S(1)} %collective-permute-done.7.refs_0_, ...), custom_call_target="tpu_custom_call" | custom-call | bytes 36000000 | tf_op jit(solution)/shard_map/network/pallas_call | solution.py:786
  47.3 0.1 collective-permute-start.15
  47.4 9.5 %network.3 = (f32[4096,128]{1,0:T(8,128)S(1)}, bf16[4,1088,128]{2,1,0:T(8,128)(2,1)S(1)}) custom-call(s32[8,1,512]{2,1,0:T(1,128)S(1)} %bitcast.43, s32[8,1,512]{2,1,0:T(1,128)S(1)} %bitcast.44, bf16[1088,128]{1,0:T(8,128)(2,1)S(1)} %copy-done.2, bf16[1088,128]{1,0:T(8,128)(2,1)S(1)} %collective-permute-done.refs_1_, ...), custom_call_target="tpu_custom_call", output_to_operand_aliasing={{0}: (7, {})} | custom-call | bytes 36000000 | tf_op jit(solution)/shard_map/network/pallas_call | solution.py:786
  56.9 0.3 add_pair.1
  57.2 1.7 %collective-permute-start.16 = (bf16[1088,128]{1,0:T(8,128)(2,1)S(1)}, bf16[1088,128]{1,0:T(8,128)(2,1)S(1)}, u32[]{:S(2)}, u32[]{:S(2)}) collective-permute-start(bf16[1088,128]{1,0:T(8,128)(2,1)S(1)} %get-tuple-element.64), channel_id=1, source_target_pairs={{0,2},{1,3},{2,0},{3,1},{4,6},{5,7},{6,4},{7,5},{8,10},{9,11},{10,... | collective-permute-start | bytes 835592 | tf_op jit(solution)/shard_map/ppermute | solution.py:1095
  58.8 0.8 collective-permute-start.17
  59.7 1.1 %collective-permute-start.18 = (bf16[1088,128]{1,0:T(8,128)(2,1)S(1)}, bf16[1088,128]{1,0:T(8,128)(2,1)S(1)}, u32[]{:S(2)}, u32[]{:S(2)}) collective-permute-start(bf16[1088,128]{1,0:T(8,128)(2,1)S(1)} %get-tuple-element.66), channel_id=1, source_target_pairs={{0,6},{1,7},{2,4},{3,5},{4,2},{5,3},{6,0},{7,1},{8,14},{9,15},{10,... | collective-permute-start | bytes 835592 | tf_op jit(solution)/shard_map/ppermute | solution.py:1095
  60.7 6.0 %collective-permute-done.16.refs_1_ = bf16[1088,128]{1,0:T(8,128)(2,1)S(1)} collective-permute-done((bf16[1088,128]{1,0:T(8,128)(2,1)S(1)}, bf16[1088,128]{1,0:T(8,128)(2,1)S(1)}, u32[]{:S(2)}, u32[]{:S(2)}) %collective-permute-start.16) | collective-permute-done | bytes 278560 | tf_op jit(solution)/shard_map/ppermute | solution.py:1095
  66.8 0.8 collective-permute-done.17.refs_2_
  67.6 5.6 %collective-permute-done.18.refs_3_ = bf16[1088,128]{1,0:T(8,128)(2,1)S(1)} collective-permute-done((bf16[1088,128]{1,0:T(8,128)(2,1)S(1)}, bf16[1088,128]{1,0:T(8,128)(2,1)S(1)}, u32[]{:S(2)}, u32[]{:S(2)}) %collective-permute-start.18) | collective-permute-done | bytes 278560 | tf_op jit(solution)/shard_map/ppermute | solution.py:1095
  73.2 0.3 sum_and_share.1
  73.5 1.4 %collective-permute-start.19 = (bf16[272,128]{1,0:T(8,128)(2,1)S(1)}, bf16[272,128]{1,0:T(8,128)(2,1)S(1)}, u32[]{:S(2)}, u32[]{:S(2)}) collective-permute-start(bf16[272,128]{1,0:T(8,128)(2,1)S(1)} %get-tuple-element.68), channel_id=1, source_target_pairs={{0,8},{8,0},{16,24},{24,16},{1,9},{9,1},{17,25},{25,17},{2,10},{10... | collective-permute-start | bytes 208904 | tf_op jit(solution)/shard_map/ppermute | solution.py:1104
  74.9 2.6 %collective-permute-start.20 = (bf16[272,128]{1,0:T(8,128)(2,1)S(1)}, bf16[272,128]{1,0:T(8,128)(2,1)S(1)}, u32[]{:S(2)}, u32[]{:S(2)}) collective-permute-start(bf16[272,128]{1,0:T(8,128)(2,1)S(1)} %get-tuple-element.69), channel_id=1, source_target_pairs={{0,16},{8,24},{16,0},{24,8},{1,17},{9,25},{17,1},{25,9},{2,18},{10... | collective-permute-start | bytes 208904 | tf_op jit(solution)/shard_map/ppermute | solution.py:1104
  77.6 0.4 collective-permute-start.21
  78.0 1.7 %collect.1 = (f32[64,4096]{1,0:T(8,128)S(1)}, bf16[64,512]{1,0:T(8,128)(2,1)S(1)}, bf16[64,512]{1,0:T(8,128)(2,1)S(1)}) custom-call(f32[4096,128]{1,0:T(8,128)S(1)} %get-tuple-element.51.refs_0_), custom_call_target="tpu_custom_call" | custom-call | bytes 9000000 | tf_op jit(solution)/shard_map/collect/pallas_call | solution.py:966
  79.7 0.5 collective-permute-start.11
  80.2 3.1 %collective-permute-start.12 = (bf16[64,512]{1,0:T(8,128)(2,1)S(1)}, bf16[64,512]{1,0:T(8,128)(2,1)S(1)}, u32[]{:S(2)}, u32[]{:S(2)}) collective-permute-start(bf16[64,512]{1,0:T(8,128)(2,1)S(1)} %get-tuple-element.56), channel_id=1, source_target_pairs={{0,24},{8,16},{16,8},{24,0},{1,25},{9,17},{17,9},{25,1},{2,26},{10... | collective-permute-start | bytes 196616 | tf_op jit(solution)/shard_map/ppermute | solution.py:279
  83.3 0.0 collective-permute-done.19.refs_1_
  83.3 1.2 %collective-permute-done.21.refs_3_ = bf16[272,128]{1,0:T(8,128)(2,1)S(1)} collective-permute-done((bf16[272,128]{1,0:T(8,128)(2,1)S(1)}, bf16[272,128]{1,0:T(8,128)(2,1)S(1)}, u32[]{:S(2)}, u32[]{:S(2)}) %collective-permute-start.21) | collective-permute-done | bytes 69664 | tf_op jit(solution)/shard_map/ppermute | solution.py:1104
  84.5 1.0 %collective-permute-start.24 = (bf16[272,128]{1,0:T(8,128)(2,1)S(1)}, bf16[272,128]{1,0:T(8,128)(2,1)S(1)}, u32[]{:S(2)}, u32[]{:S(2)}) collective-permute-start(bf16[272,128]{1,0:T(8,128)(2,1)S(1)} %sum_parts.1.refs_0_), channel_id=1, source_target_pairs={{0,24},{8,16},{16,8},{24,0},{1,25},{9,17},{17,9},{25,1},{2,26},{10... | collective-permute-start | bytes 208904 | tf_op jit(solution)/shard_map/ppermute | solution.py:1108
  85.6 0.3 collective-permute-start.23
  85.9 3.1 %collective-permute-start.22 = (bf16[272,128]{1,0:T(8,128)(2,1)S(1)}, bf16[272,128]{1,0:T(8,128)(2,1)S(1)}, u32[]{:S(2)}, u32[]{:S(2)}) collective-permute-start(bf16[272,128]{1,0:T(8,128)(2,1)S(1)} %sum_parts.1.refs_0_), channel_id=1, source_target_pairs={{0,8},{8,0},{16,24},{24,16},{1,9},{9,1},{17,25},{25,17},{2,10},{10... | collective-permute-start | bytes 208904 | tf_op jit(solution)/shard_map/ppermute | solution.py:1108
  89.0 0.7 pack_back.1
  89.8 0.2 add_corners.3
  89.9 0.1 collective-permute-start.13
  90.0 1.5 %collective-permute-start.14 = (bf16[64,128]{1,0:T(8,128)(2,1)S(1)}, bf16[64,128]{1,0:T(8,128)(2,1)S(1)}, u32[]{:S(2)}, u32[]{:S(2)}) collective-permute-start(bf16[64,128]{1,0:T(8,128)(2,1)S(1)} %get-tuple-element.60.refs_6_), channel_id=1, source_target_pairs={{0,7},{1,2},{2,1},{3,4},{4,3},{5,6},{6,5},{7,0},{8,15},{9,10},{10,... | collective-permute-start | bytes 49160 | tf_op jit(solution)/shard_map/ppermute | solution.py:279
  91.5 2.7 %collective-permute-done.14.refs_8_ = bf16[64,128]{1,0:T(8,128)(2,1)S(1)} collective-permute-done((bf16[64,128]{1,0:T(8,128)(2,1)S(1)}, bf16[64,128]{1,0:T(8,128)(2,1)S(1)}, u32[]{:S(2)}, u32[]{:S(2)}) %collective-permute-start.14) | collective-permute-done | bytes 16416 | tf_op jit(solution)/shard_map/ppermute | solution.py:279
  94.3 5.0 %adjoint.1 = f32[2048,128]{1,0:T(8,128)} custom-call(f32[64,4096]{1,0:T(8,128)S(1)} %get-tuple-element.52.refs_0_, f32[8,5120]{1,0:T(8,128)S(1)} %get-tuple-element.53.refs_1_, f32[48,128]{1,0:T(8,128)S(1)} %get-tuple-element.54.refs_2_, bf16[64,512]{1,0:T(8,128)(2,1)S(1)} %collective-permute-done.11.refs_0_.refs_3_, ...), custom_call_target="tpu_custom_call" | custom-call | bytes 18000000 | tf_op jit(solution)/shard_map/adjoint/pallas_call | solution.py:1047
  99.3 0.0 collective-permute-done.24.refs_3_
  99.3 0.0 collective-permute-done.23.refs_2_
  99.3 0.0 collective-permute-done.22.refs_1_
  99.3 1.3 %make_steps.1 = (f32[64,192]{1,0:T(8,128)}, f32[3,192,192]{2,1,0:T(8,128)}, f32[64,192]{1,0:T(8,128)}, f32[4,192]{1,0:T(4,128)}, f32[1,64]{1,0:T(1,128)}) custom-call(bf16[272,128]{1,0:T(8,128)(2,1)S(1)} %sum_parts.1.refs_0_, bf16[272,128]{1,0:T(8,128)(2,1)S(1)} %collective-permute-done.22.refs_1_, bf16[272,128]{1,0:T(8,128)(2,1)S(1)} %collective-permute-done.23.refs_2_, ...), custom_call_target="tpu_custom_call" | custom-call | bytes 6000000 | tf_op jit(solution)/shard_map/make_steps/pallas_call | solution.py:923
  (19 shorter events, 0.1 us)
Async XLA Ops:
  0.6 31.5 %copy-start.5 = (f32[16,256]{1,0:T(8,128)S(1)}, f32[16,256]{1,0:T(8,128)}, u32[]{:S(2)}) copy-start(f32[16,256]{1,0:T(8,128)} %param.12) | copy-start | bytes 49156
  0.6 28.8 %copy-start.7 = (s32[1,4096]{1,0:T(1,128)S(1)}, s32[1,4096]{1,0:T(1,128)}, u32[]{:S(2)}) copy-start(s32[1,4096]{1,0:T(1,128)} %param.13) | copy-start | bytes 49156
  0.7 28.8 %copy-start.6 = (s32[1,32]{1,0:T(1,128)S(1)}, s32[1,32]{1,0:T(1,128)}, u32[]{:S(2)}) copy-start(s32[1,32]{1,0:T(1,128)} %param.14) | copy-start | bytes 388
  2.6 11.7 %collective-permute-start.2 = (bf16[1088,128]{1,0:T(8,128)(2,1)}, bf16[1088,128]{1,0:T(8,128)(2,1)S(1)}, u32[]{:S(2)}, u32[]{:S(2)}) collective-permute-start(bf16[1088,128]{1,0:T(8,128)(2,1)} %pack_weights.1.refs_0_), channel_id=1, source_target_pairs={{0,6},{1,7},{2,4},{3,5},{4,2},{5,3},{6,0},{7,1},{8,14},{9,15},{10,... | collective-permute-start | bytes 835592 | tf_op jit(solution)/shard_map/ppermute | solution.py:1076
  6.6 12.8 %collective-permute-start.1 = (bf16[1088,128]{1,0:T(8,128)(2,1)}, bf16[1088,128]{1,0:T(8,128)(2,1)S(1)}, u32[]{:S(2)}, u32[]{:S(2)}) collective-permute-start(bf16[1088,128]{1,0:T(8,128)(2,1)} %pack_weights.1.refs_0_), channel_id=1, source_target_pairs={{0,4},{1,5},{2,6},{3,7},{4,0},{5,1},{6,2},{7,3},{8,12},{9,13},{10,... | collective-permute-start | bytes 835592 | tf_op jit(solution)/shard_map/ppermute | solution.py:1076
  7.1 12.6 %collective-permute-start = (bf16[1088,128]{1,0:T(8,128)(2,1)}, bf16[1088,128]{1,0:T(8,128)(2,1)S(1)}, u32[]{:S(2)}, u32[]{:S(2)}) collective-permute-start(bf16[1088,128]{1,0:T(8,128)(2,1)} %pack_weights.1.refs_0_), channel_id=1, source_target_pairs={{0,2},{1,3},{2,0},{3,1},{4,6},{5,7},{6,4},{7,5},{8,10},{9,11},{10,... | collective-permute-start | bytes 835592 | tf_op jit(solution)/shard_map/ppermute | solution.py:1076
  7.2 1.2 %copy-start = (f32[64,16,256]{2,1,0:T(8,128)S(1)}, f32[64,16,256]{2,1,0:T(8,128)}, u32[]{:S(2)}) copy-start(f32[64,16,256]{2,1,0:T(8,128)} %param.10) | copy-start | bytes 3145732
  8.5 0.7 copy-start.4
  9.2 22.9 %copy-start.1 = (f32[64,16,256]{2,1,0:T(8,128)S(1)}, f32[64,16,256]{2,1,0:T(8,128)}, u32[]{:S(2)}) copy-start(f32[64,16,256]{2,1,0:T(8,128)} %param.10) | copy-start | bytes 3145732
  9.2 22.9 %copy-start.3 = (f32[64,16,256]{2,1,0:T(8,128)S(1)}, f32[64,16,256]{2,1,0:T(8,128)}, u32[]{:S(2)}) copy-start(f32[64,16,256]{2,1,0:T(8,128)} %param.11) | copy-start | bytes 3145732
  9.4 10.6 %collective-permute-start.3 = (bf16[80,512]{1,0:T(8,128)(2,1)S(1)}, bf16[80,512]{1,0:T(8,128)(2,1)S(1)}, u32[]{:S(2)}, u32[]{:S(2)}) collective-permute-start(bf16[80,512]{1,0:T(8,128)(2,1)S(1)} %get-tuple-element.41), channel_id=1, source_target_pairs={{0,8},{8,0},{16,24},{24,16},{1,9},{9,1},{17,25},{25,17},{2,10},{10... | collective-permute-start | bytes 245768 | tf_op jit(solution)/shard_map/ppermute | solution.py:279
  11.4 26.5 %collective-permute-start.7 = (bf16[1088,128]{1,0:T(8,128)(2,1)}, bf16[1088,128]{1,0:T(8,128)(2,1)S(1)}, u32[]{:S(2)}, u32[]{:S(2)}) collective-permute-start(bf16[1088,128]{1,0:T(8,128)(2,1)} %pack_weights.1.refs_0_), channel_id=1, source_target_pairs={{0,1},{1,0},{2,3},{3,2},{4,5},{5,4},{6,7},{7,6},{8,9},{9,8},{10,11... | collective-permute-start | bytes 835592 | tf_op jit(solution)/shard_map/ppermute | solution.py:1083
  14.4 23.6 %collective-permute-start.10 = (bf16[1088,128]{1,0:T(8,128)(2,1)S(1)}, bf16[1088,128]{1,0:T(8,128)(2,1)S(1)}, u32[]{:S(2)}, u32[]{:S(2)}) collective-permute-start(bf16[1088,128]{1,0:T(8,128)(2,1)S(1)} %collective-permute-done.2.refs_3_), channel_id=1, source_target_pairs={{0,1},{1,0},{2,3},{3,2},{4,5},{5,4},{6,7},{7,6},{8,9},{9,8},{10,11... | collective-permute-start | bytes 835592 | tf_op jit(solution)/shard_map/ppermute | solution.py:1083
  19.4 18.5 %collective-permute-start.9 = (bf16[1088,128]{1,0:T(8,128)(2,1)S(1)}, bf16[1088,128]{1,0:T(8,128)(2,1)S(1)}, u32[]{:S(2)}, u32[]{:S(2)}) collective-permute-start(bf16[1088,128]{1,0:T(8,128)(2,1)S(1)} %collective-permute-done.1.refs_2_), channel_id=1, source_target_pairs={{0,1},{1,0},{2,3},{3,2},{4,5},{5,4},{6,7},{7,6},{8,9},{9,8},{10,11... | collective-permute-start | bytes 835592 | tf_op jit(solution)/shard_map/ppermute | solution.py:1083
  19.7 18.2 %collective-permute-start.8 = (bf16[1088,128]{1,0:T(8,128)(2,1)S(1)}, bf16[1088,128]{1,0:T(8,128)(2,1)S(1)}, u32[]{:S(2)}, u32[]{:S(2)}) collective-permute-start(bf16[1088,128]{1,0:T(8,128)(2,1)S(1)} %collective-permute-done.refs_1_), channel_id=1, source_target_pairs={{0,1},{1,0},{2,3},{3,2},{4,5},{5,4},{6,7},{7,6},{8,9},{9,8},{10,11... | collective-permute-start | bytes 835592 | tf_op jit(solution)/shard_map/ppermute | solution.py:1083
  20.0 6.6 %collective-permute-start.4 = (bf16[80,512]{1,0:T(8,128)(2,1)S(1)}, bf16[80,512]{1,0:T(8,128)(2,1)S(1)}, u32[]{:S(2)}, u32[]{:S(2)}) collective-permute-start(bf16[80,512]{1,0:T(8,128)(2,1)S(1)} %get-tuple-element.42), channel_id=1, source_target_pairs={{0,24},{8,16},{16,8},{24,0},{1,25},{9,17},{17,9},{25,1},{2,26},{10... | collective-permute-start | bytes 245768 | tf_op jit(solution)/shard_map/ppermute | solution.py:279
  26.7 1.3 %collective-permute-start.5 = (bf16[80,128]{1,0:T(8,128)(2,1)S(1)}, bf16[80,128]{1,0:T(8,128)(2,1)S(1)}, u32[]{:S(2)}, u32[]{:S(2)}) collective-permute-start(bf16[80,128]{1,0:T(8,128)(2,1)S(1)} %get-tuple-element.45.refs_5_), channel_id=1, source_target_pairs={{0,1},{1,0},{2,3},{3,2},{4,5},{5,4},{6,7},{7,6},{8,9},{9,8},{10,11... | collective-permute-start | bytes 61448 | tf_op jit(solution)/shard_map/ppermute | solution.py:279
  28.0 4.1 %collective-permute-start.6 = (bf16[80,128]{1,0:T(8,128)(2,1)S(1)}, bf16[80,128]{1,0:T(8,128)(2,1)S(1)}, u32[]{:S(2)}, u32[]{:S(2)}) collective-permute-start(bf16[80,128]{1,0:T(8,128)(2,1)S(1)} %get-tuple-element.46.refs_6_), channel_id=1, source_target_pairs={{0,7},{1,2},{2,1},{3,4},{4,3},{5,6},{6,5},{7,0},{8,15},{9,10},{10,... | collective-permute-start | bytes 61448 | tf_op jit(solution)/shard_map/ppermute | solution.py:279
  37.9 9.5 %copy-start.2 = (bf16[1088,128]{1,0:T(8,128)(2,1)S(1)}, bf16[1088,128]{1,0:T(8,128)(2,1)}, u32[]{:S(2)}) copy-start(bf16[1088,128]{1,0:T(8,128)(2,1)} %pack_weights.1.refs_0_) | copy-start | bytes 835588
  47.3 9.6 %collective-permute-start.15 = (bf16[4,1088,128]{2,1,0:T(8,128)(2,1)S(1)}, bf16[4,1088,128]{2,1,0:T(8,128)(2,1)S(1)}, u32[]{:S(2)}, u32[]{:S(2)}) collective-permute-start(bf16[4,1088,128]{2,1,0:T(8,128)(2,1)S(1)} %get-tuple-element.62), channel_id=1, source_target_pairs={{0,1},{1,0},{2,3},{3,2},{4,5},{5,4},{6,7},{7,6},{8,9},{9,8},{10,11... | collective-permute-start | bytes 3342344 | tf_op jit(solution)/shard_map/ppermute | solution.py:1088
  57.2 9.6 %collective-permute-start.16 = (bf16[1088,128]{1,0:T(8,128)(2,1)S(1)}, bf16[1088,128]{1,0:T(8,128)(2,1)S(1)}, u32[]{:S(2)}, u32[]{:S(2)}) collective-permute-start(bf16[1088,128]{1,0:T(8,128)(2,1)S(1)} %get-tuple-element.64), channel_id=1, source_target_pairs={{0,2},{1,3},{2,0},{3,1},{4,6},{5,7},{6,4},{7,5},{8,10},{9,11},{10,... | collective-permute-start | bytes 835592 | tf_op jit(solution)/shard_map/ppermute | solution.py:1095
  58.8 8.8 %collective-permute-start.17 = (bf16[1088,128]{1,0:T(8,128)(2,1)S(1)}, bf16[1088,128]{1,0:T(8,128)(2,1)S(1)}, u32[]{:S(2)}, u32[]{:S(2)}) collective-permute-start(bf16[1088,128]{1,0:T(8,128)(2,1)S(1)} %get-tuple-element.65), channel_id=1, source_target_pairs={{0,4},{1,5},{2,6},{3,7},{4,0},{5,1},{6,2},{7,3},{8,12},{9,13},{10,... | collective-permute-start | bytes 835592 | tf_op jit(solution)/shard_map/ppermute | solution.py:1095
  59.7 13.5 %collective-permute-start.18 = (bf16[1088,128]{1,0:T(8,128)(2,1)S(1)}, bf16[1088,128]{1,0:T(8,128)(2,1)S(1)}, u32[]{:S(2)}, u32[]{:S(2)}) collective-permute-start(bf16[1088,128]{1,0:T(8,128)(2,1)S(1)} %get-tuple-element.66), channel_id=1, source_target_pairs={{0,6},{1,7},{2,4},{3,5},{4,2},{5,3},{6,0},{7,1},{8,14},{9,15},{10,... | collective-permute-start | bytes 835592 | tf_op jit(solution)/shard_map/ppermute | solution.py:1095
  73.5 9.8 %collective-permute-start.19 = (bf16[272,128]{1,0:T(8,128)(2,1)S(1)}, bf16[272,128]{1,0:T(8,128)(2,1)S(1)}, u32[]{:S(2)}, u32[]{:S(2)}) collective-permute-start(bf16[272,128]{1,0:T(8,128)(2,1)S(1)} %get-tuple-element.68), channel_id=1, source_target_pairs={{0,8},{8,0},{16,24},{24,16},{1,9},{9,1},{17,25},{25,17},{2,10},{10... | collective-permute-start | bytes 208904 | tf_op jit(solution)/shard_map/ppermute | solution.py:1104
  74.9 8.4 %collective-permute-start.20 = (bf16[272,128]{1,0:T(8,128)(2,1)S(1)}, bf16[272,128]{1,0:T(8,128)(2,1)S(1)}, u32[]{:S(2)}, u32[]{:S(2)}) collective-permute-start(bf16[272,128]{1,0:T(8,128)(2,1)S(1)} %get-tuple-element.69), channel_id=1, source_target_pairs={{0,16},{8,24},{16,0},{24,8},{1,17},{9,25},{17,1},{25,9},{2,18},{10... | collective-permute-start | bytes 208904 | tf_op jit(solution)/shard_map/ppermute | solution.py:1104
  77.6 6.9 %collective-permute-start.21 = (bf16[272,128]{1,0:T(8,128)(2,1)S(1)}, bf16[272,128]{1,0:T(8,128)(2,1)S(1)}, u32[]{:S(2)}, u32[]{:S(2)}) collective-permute-start(bf16[272,128]{1,0:T(8,128)(2,1)S(1)} %get-tuple-element.70), channel_id=1, source_target_pairs={{0,24},{8,16},{16,8},{24,0},{1,25},{9,17},{17,9},{25,1},{2,26},{10... | collective-permute-start | bytes 208904 | tf_op jit(solution)/shard_map/ppermute | solution.py:1104
  79.7 10.0 %collective-permute-start.11 = (bf16[64,512]{1,0:T(8,128)(2,1)S(1)}, bf16[64,512]{1,0:T(8,128)(2,1)S(1)}, u32[]{:S(2)}, u32[]{:S(2)}) collective-permute-start(bf16[64,512]{1,0:T(8,128)(2,1)S(1)} %get-tuple-element.55), channel_id=1, source_target_pairs={{0,8},{8,0},{16,24},{24,16},{1,9},{9,1},{17,25},{25,17},{2,10},{10... | collective-permute-start | bytes 196616 | tf_op jit(solution)/shard_map/ppermute | solution.py:279
  80.2 9.5 %collective-permute-start.12 = (bf16[64,512]{1,0:T(8,128)(2,1)S(1)}, bf16[64,512]{1,0:T(8,128)(2,1)S(1)}, u32[]{:S(2)}, u32[]{:S(2)}) collective-permute-start(bf16[64,512]{1,0:T(8,128)(2,1)S(1)} %get-tuple-element.56), channel_id=1, source_target_pairs={{0,24},{8,16},{16,8},{24,0},{1,25},{9,17},{17,9},{25,1},{2,26},{10... | collective-permute-start | bytes 196616 | tf_op jit(solution)/shard_map/ppermute | solution.py:279
  84.5 14.7 %collective-permute-start.24 = (bf16[272,128]{1,0:T(8,128)(2,1)S(1)}, bf16[272,128]{1,0:T(8,128)(2,1)S(1)}, u32[]{:S(2)}, u32[]{:S(2)}) collective-permute-start(bf16[272,128]{1,0:T(8,128)(2,1)S(1)} %sum_parts.1.refs_0_), channel_id=1, source_target_pairs={{0,24},{8,16},{16,8},{24,0},{1,25},{9,17},{17,9},{25,1},{2,26},{10... | collective-permute-start | bytes 208904 | tf_op jit(solution)/shard_map/ppermute | solution.py:1108
  85.6 13.7 %collective-permute-start.23 = (bf16[272,128]{1,0:T(8,128)(2,1)S(1)}, bf16[272,128]{1,0:T(8,128)(2,1)S(1)}, u32[]{:S(2)}, u32[]{:S(2)}) collective-permute-start(bf16[272,128]{1,0:T(8,128)(2,1)S(1)} %sum_parts.1.refs_0_), channel_id=1, source_target_pairs={{0,16},{8,24},{16,0},{24,8},{1,17},{9,25},{17,1},{25,9},{2,18},{10... | collective-permute-start | bytes 208904 | tf_op jit(solution)/shard_map/ppermute | solution.py:1108
  85.9 13.4 %collective-permute-start.22 = (bf16[272,128]{1,0:T(8,128)(2,1)S(1)}, bf16[272,128]{1,0:T(8,128)(2,1)S(1)}, u32[]{:S(2)}, u32[]{:S(2)}) collective-permute-start(bf16[272,128]{1,0:T(8,128)(2,1)S(1)} %sum_parts.1.refs_0_), channel_id=1, source_target_pairs={{0,8},{8,0},{16,24},{24,16},{1,9},{9,1},{17,25},{25,17},{2,10},{10... | collective-permute-start | bytes 208904 | tf_op jit(solution)/shard_map/ppermute | solution.py:1108
  89.9 1.6 %collective-permute-start.13 = (bf16[64,128]{1,0:T(8,128)(2,1)S(1)}, bf16[64,128]{1,0:T(8,128)(2,1)S(1)}, u32[]{:S(2)}, u32[]{:S(2)}) collective-permute-start(bf16[64,128]{1,0:T(8,128)(2,1)S(1)} %get-tuple-element.59.refs_5_), channel_id=1, source_target_pairs={{0,1},{1,0},{2,3},{3,2},{4,5},{5,4},{6,7},{7,6},{8,9},{9,8},{10,11... | collective-permute-start | bytes 49160 | tf_op jit(solution)/shard_map/ppermute | solution.py:279
  90.0 4.3 %collective-permute-start.14 = (bf16[64,128]{1,0:T(8,128)(2,1)S(1)}, bf16[64,128]{1,0:T(8,128)(2,1)S(1)}, u32[]{:S(2)}, u32[]{:S(2)}) collective-permute-start(bf16[64,128]{1,0:T(8,128)(2,1)S(1)} %get-tuple-element.60.refs_6_), channel_id=1, source_target_pairs={{0,7},{1,2},{2,1},{3,4},{4,3},{5,6},{6,5},{7,0},{8,15},{9,10},{10,... | collective-permute-start | bytes 49160 | tf_op jit(solution)/shard_map/ppermute | solution.py:279

commit v7 on v6

--- a/solution.py
+++ b/solution.py
@@ -289,9 +289,15 @@
 
 def beside(row, left, right, x):
     width = row.shape[1]
-    lane = lane_ids(width)
-    return jnp.where(lane == 0, left[:, x + 1 : x + 2], pltpu.roll(row, 1, 1)) + jnp.where(
-        lane == width - 1, right[:, x + 1 : x + 2], pltpu.roll(row, width - 1, 1)
+    lane = lane_ids(LANES)
+    before = pltpu.roll(row, 1, 1)
+    after = pltpu.roll(row, width - 1, 1)
+    first = jnp.where(lane == 0, pltpu.roll(left, (LANES - 1 - x) % LANES, 1), before[:, :LANES])
+    final = jnp.where(
+        lane == LANES - 1, pltpu.roll(right, LANES - 2 - x, 1), after[:, width - LANES :]
+    )
+    return jnp.concatenate([first, before[:, LANES:]], axis=1) + jnp.concatenate(
+        [after[:, : width - LANES], final], axis=1
     )
 
 

time: 101 us -> 97.1 us (0.961)
  Pallas kernels: 39 us -> 35.3 us
    pallas_call x1, Pallas kernels: 5.79 us -> 3.92 us  [forward(): pl.pallas_call(with_flags(functools.partial(forward_body, levels, width_x...]
    pallas_call x1, Pallas kernels: 4.99 us -> 3.15 us  [adjoint(): pl.pallas_call(with_flags(functools.partial(adjoint_body, levels, width_x...]
  transfers between devices with their start and end apart: 25 -> 25, of which waited for: 11 -> 11; matrix products, arithmetic and copies ran while one was open for 0% -> 0% of each run, Pallas kernels for 26% -> 23%
where the time goes in v7:
time: 97.1 us; the launch traced here: 96.9 us
  Pallas kernels  35.3 us (36%)
  starting transfers between devices  30 us (31%)
  waiting for transfers between devices  28.8 us (30%)
  local copies, waits for them, and re-layouts  1.97 us (2%)
    pallas_call x2, Pallas kernels, network(): pl.pallas_call(body, grid=(blocks,), out_shape=[jax.ShapeDtypeStruct((cel...  18.8 us
    ppermute x3, waiting for transfers between devices, local_program(): lax.ppermute(both_grads[c], 'sub', partners(subs, 2 * c))  12.5 us
    ppermute x4, starting transfers between devices, trade_sides(): lax.ppermute(other, axis, beyond(size))  9.85 us
    ppermute x3, waiting for transfers between devices, local_program(): lax.ppermute(weights, 'sub', partners(subs, 2 * c))  8.3 us
    ppermute x4, waiting for transfers between devices, trade_sides(): lax.ppermute(other, axis, beyond(size))  5.58 us
    ppermute x3, starting transfers between devices, local_program(): lax.ppermute(weights, 'sub', partners(subs, 2 * c))  4.63 us
    ppermute x3, starting transfers between devices, local_program(): lax.ppermute(piece, 'tile', partners(tiles, d))  4.45 us
    ppermute x3, starting transfers between devices, local_program(): lax.ppermute(shares[d], 'tile', partners(tiles, d))  4.45 us
  transfers between devices with their start and end apart: 25, of which 11 were waited for; matrix products, arithmetic and copies ran while one was open for 0% of the time, Pallas kernels for 23%

profile of v7, /device:TPU:0, one launch (start us, length us, event | category | flops | bytes accessed | tf_op | source)
XLA Modules:
  0.0 96.9 jit_solution(7516742891231332003)
XLA Ops:
  0.6 0.0 copy-start.5
  0.7 1.9 %pack_weights.1.refs_0_ = bf16[1088,128]{1,0:T(8,128)(2,1)} custom-call(bf16[64,192]{1,0:T(8,128)(2,1)} %bitcast.51, bf16[3,192,192]{2,1,0:T(8,128)(2,1)} %bitcast.50, bf16[64,192]{1,0:T(8,128)(2,1)} %bitcast.52, f32[4,192]{1,0:T(4,128)} %bitcast.54, f32[1,64]{1,0:T(1,128)} %refs_4_.1), custom_call_target="tpu_custom_call" | custom-call | bytes 3000000 | tf_op jit(solution)/shard_map/pack_weights/pallas_call | solution.py:536
  2.6 4.0 %collective-permute-start.2 = (bf16[1088,128]{1,0:T(8,128)(2,1)}, bf16[1088,128]{1,0:T(8,128)(2,1)S(1)}, u32[]{:S(2)}, u32[]{:S(2)}) collective-permute-start(bf16[1088,128]{1,0:T(8,128)(2,1)} %pack_weights.1.refs_0_), channel_id=1, source_target_pairs={{0,6},{1,7},{2,4},{3,5},{4,2},{5,3},{6,0},{7,1},{8,14},{9,15},{10,... | collective-permute-start | bytes 835592 | tf_op jit(solution)/shard_map/ppermute | solution.py:1082
  6.6 0.5 collective-permute-start.1
  7.1 0.1 collective-permute-start
  7.3 1.2 %copy-done = f32[64,16,256]{2,1,0:T(8,128)S(1)} copy-done((f32[64,16,256]{2,1,0:T(8,128)S(1)}, f32[64,16,256]{2,1,0:T(8,128)}, u32[]{:S(2)}) %copy-start) | copy-done | bytes 1048600
  8.5 0.7 copy-done.4
  9.2 0.2 pack_rows.1
  9.4 2.0 %collective-permute-start.3 = (bf16[80,512]{1,0:T(8,128)(2,1)S(1)}, bf16[80,512]{1,0:T(8,128)(2,1)S(1)}, u32[]{:S(2)}, u32[]{:S(2)}) collective-permute-start(bf16[80,512]{1,0:T(8,128)(2,1)S(1)} %get-tuple-element.41), channel_id=1, source_target_pairs={{0,8},{8,0},{16,24},{24,16},{1,9},{9,1},{17,25},{25,17},{2,10},{10... | collective-permute-start | bytes 245768 | tf_op jit(solution)/shard_map/ppermute | solution.py:279
  11.4 0.0 collective-permute-start.7
  11.4 3.0 %collective-permute-done.2.refs_3_ = bf16[1088,128]{1,0:T(8,128)(2,1)S(1)} collective-permute-done((bf16[1088,128]{1,0:T(8,128)(2,1)}, bf16[1088,128]{1,0:T(8,128)(2,1)S(1)}, u32[]{:S(2)}, u32[]{:S(2)}) %collective-permute-start.2) | collective-permute-done | bytes 278560 | tf_op jit(solution)/shard_map/ppermute | solution.py:1082
  14.4 5.1 %collective-permute-done.1.refs_2_ = bf16[1088,128]{1,0:T(8,128)(2,1)S(1)} collective-permute-done((bf16[1088,128]{1,0:T(8,128)(2,1)}, bf16[1088,128]{1,0:T(8,128)(2,1)S(1)}, u32[]{:S(2)}, u32[]{:S(2)}) %collective-permute-start.1) | collective-permute-done | bytes 278560 | tf_op jit(solution)/shard_map/ppermute | solution.py:1082
  19.4 0.0 collective-permute-start.9
  19.5 0.3 collective-permute-done.refs_1_
  19.7 0.2 collective-permute-start.8
  20.0 0.0 collective-permute-done.3.refs_0_.refs_3_
  20.0 3.8 %collective-permute-start.4 = (bf16[80,512]{1,0:T(8,128)(2,1)S(1)}, bf16[80,512]{1,0:T(8,128)(2,1)S(1)}, u32[]{:S(2)}, u32[]{:S(2)}) collective-permute-start(bf16[80,512]{1,0:T(8,128)(2,1)S(1)} %get-tuple-element.42), channel_id=1, source_target_pairs={{0,24},{8,16},{16,8},{24,0},{1,25},{9,17},{17,9},{25,1},{2,26},{10... | collective-permute-start | bytes 245768 | tf_op jit(solution)/shard_map/ppermute | solution.py:279
  23.8 1.1 %pack_columns.1 = (bf16[80,128]{1,0:T(8,128)(2,1)S(1)}, bf16[80,128]{1,0:T(8,128)(2,1)S(1)}) custom-call(f32[2048,128]{1,0:T(8,128)S(1)} %bitcast.38, f32[32,128]{1,0:T(8,128)S(1)} %bitcast.46), custom_call_target="tpu_custom_call" | custom-call | bytes 6000000 | tf_op jit(solution)/shard_map/pack_columns/pallas_call | solution.py:197
  24.8 1.7 %collective-permute-done.4.refs_1_.refs_4_ = bf16[80,512]{1,0:T(8,128)(2,1)S(1)} collective-permute-done((bf16[80,512]{1,0:T(8,128)(2,1)S(1)}, bf16[80,512]{1,0:T(8,128)(2,1)S(1)}, u32[]{:S(2)}, u32[]{:S(2)}) %collective-permute-start.4) | collective-permute-done | bytes 81952 | tf_op jit(solution)/shard_map/ppermute | solution.py:279
  26.6 0.2 add_corners.2
  26.7 0.1 collective-permute-start.5
  26.8 1.2 %collective-permute-done.5.refs_7_ = bf16[80,128]{1,0:T(8,128)(2,1)S(1)} collective-permute-done((bf16[80,128]{1,0:T(8,128)(2,1)S(1)}, bf16[80,128]{1,0:T(8,128)(2,1)S(1)}, u32[]{:S(2)}, u32[]{:S(2)}) %collective-permute-start.5) | collective-permute-done | bytes 20512 | tf_op jit(solution)/shard_map/ppermute | solution.py:279
  28.0 1.5 %collective-permute-start.6 = (bf16[80,128]{1,0:T(8,128)(2,1)S(1)}, bf16[80,128]{1,0:T(8,128)(2,1)S(1)}, u32[]{:S(2)}, u32[]{:S(2)}) collective-permute-start(bf16[80,128]{1,0:T(8,128)(2,1)S(1)} %get-tuple-element.46.refs_6_), channel_id=1, source_target_pairs={{0,7},{1,2},{2,1},{3,4},{4,3},{5,6},{6,5},{7,0},{8,15},{9,10},{10,... | collective-permute-start | bytes 61448 | tf_op jit(solution)/shard_map/ppermute | solution.py:279
  29.5 1.5 %slot_cells.1 = s32[32,128]{1,0:T(8,128)S(1)} custom-call(s32[32]{0:T(128)S(1)} %bitcast.48, s32[44,128]{1,0:T(8,128)S(1)} %pad_bitcast_fusion.refs_1_), custom_call_target="tpu_custom_call" | custom-call | bytes 6000000 | tf_op jit(solution)/shard_map/slot_cells/pallas_call | solution.py:444
  31.0 1.1 %collective-permute-done.6.refs_8_ = bf16[80,128]{1,0:T(8,128)(2,1)S(1)} collective-permute-done((bf16[80,128]{1,0:T(8,128)(2,1)S(1)}, bf16[80,128]{1,0:T(8,128)(2,1)S(1)}, u32[]{:S(2)}, u32[]{:S(2)}) %collective-permute-start.6) | collective-permute-done | bytes 20512 | tf_op jit(solution)/shard_map/ppermute | solution.py:279
  32.1 3.9 %forward.1 = (f32[4096,128]{1,0:T(8,128)S(1)}, f32[8,5120]{1,0:T(8,128)S(1)}, f32[48,128]{1,0:T(8,128)S(1)}) custom-call(f32[2048,128]{1,0:T(8,128)S(1)} %bitcast.39, f32[2048,128]{1,0:T(8,128)S(1)} %bitcast.40, f32[32,128]{1,0:T(8,128)S(1)} %bitcast.47, bf16[80,512]{1,0:T(8,128)(2,1)S(1)} %collective-permute-done.3.refs_0_.refs_3_, ...), custom_call_target="tpu_custom_call" | custom-call | bytes 24000000 | tf_op jit(solution)/shard_map/forward/pallas_call | solution.py:381
  36.0 0.0 copy-start.2
  36.1 0.0 collective-permute-done.7.refs_0_
  36.1 0.0 collective-permute-done.9.refs_2_
  36.1 0.0 collective-permute-done.8.refs_1_
  36.1 9.4 %network.2 = (f32[4096,128]{1,0:T(8,128)S(1)}, bf16[4,1088,128]{2,1,0:T(8,128)(2,1)S(1)}, f32[512,128]{1,0:T(8,128)S(1)}, f32[512,128]{1,0:T(8,128)S(1)}) custom-call(s32[8,1,512]{2,1,0:T(1,128)S(1)} %bitcast.41, s32[8,1,512]{2,1,0:T(1,128)S(1)} %bitcast.42, bf16[1088,128]{1,0:T(8,128)(2,1)S(1)} %collective-permute-done.7.refs_0_, ...), custom_call_target="tpu_custom_call" | custom-call | bytes 36000000 | tf_op jit(solution)/shard_map/network/pallas_call | solution.py:792
  45.5 0.1 collective-permute-start.15
  45.6 9.5 %network.3 = (f32[4096,128]{1,0:T(8,128)S(1)}, bf16[4,1088,128]{2,1,0:T(8,128)(2,1)S(1)}) custom-call(s32[8,1,512]{2,1,0:T(1,128)S(1)} %bitcast.43, s32[8,1,512]{2,1,0:T(1,128)S(1)} %bitcast.44, bf16[1088,128]{1,0:T(8,128)(2,1)S(1)} %copy-done.2, bf16[1088,128]{1,0:T(8,128)(2,1)S(1)} %collective-permute-done.refs_1_, ...), custom_call_target="tpu_custom_call", output_to_operand_aliasing={{0}: (7, {})} | custom-call | bytes 36000000 | tf_op jit(solution)/shard_map/network/pallas_call | solution.py:792
  55.0 0.0 collective-permute-done.15.other
  55.1 0.3 add_pair.1
  55.3 1.7 %collective-permute-start.16 = (bf16[1088,128]{1,0:T(8,128)(2,1)S(1)}, bf16[1088,128]{1,0:T(8,128)(2,1)S(1)}, u32[]{:S(2)}, u32[]{:S(2)}) collective-permute-start(bf16[1088,128]{1,0:T(8,128)(2,1)S(1)} %get-tuple-element.64), channel_id=1, source_target_pairs={{0,2},{1,3},{2,0},{3,1},{4,6},{5,7},{6,4},{7,5},{8,10},{9,11},{10,... | collective-permute-start | bytes 835592 | tf_op jit(solution)/shard_map/ppermute | solution.py:1101
  57.0 0.8 collective-permute-start.17
  57.8 1.1 %collective-permute-start.18 = (bf16[1088,128]{1,0:T(8,128)(2,1)S(1)}, bf16[1088,128]{1,0:T(8,128)(2,1)S(1)}, u32[]{:S(2)}, u32[]{:S(2)}) collective-permute-start(bf16[1088,128]{1,0:T(8,128)(2,1)S(1)} %get-tuple-element.66), channel_id=1, source_target_pairs={{0,6},{1,7},{2,4},{3,5},{4,2},{5,3},{6,0},{7,1},{8,14},{9,15},{10,... | collective-permute-start | bytes 835592 | tf_op jit(solution)/shard_map/ppermute | solution.py:1101
  58.9 6.0 %collective-permute-done.16.refs_1_ = bf16[1088,128]{1,0:T(8,128)(2,1)S(1)} collective-permute-done((bf16[1088,128]{1,0:T(8,128)(2,1)S(1)}, bf16[1088,128]{1,0:T(8,128)(2,1)S(1)}, u32[]{:S(2)}, u32[]{:S(2)}) %collective-permute-start.16) | collective-permute-done | bytes 278560 | tf_op jit(solution)/shard_map/ppermute | solution.py:1101
  64.9 0.9 collective-permute-done.17.refs_2_
  65.8 5.5 %collective-permute-done.18.refs_3_ = bf16[1088,128]{1,0:T(8,128)(2,1)S(1)} collective-permute-done((bf16[1088,128]{1,0:T(8,128)(2,1)S(1)}, bf16[1088,128]{1,0:T(8,128)(2,1)S(1)}, u32[]{:S(2)}, u32[]{:S(2)}) %collective-permute-start.18) | collective-permute-done | bytes 278560 | tf_op jit(solution)/shard_map/ppermute | solution.py:1101
  71.3 0.3 sum_and_share.1
  71.6 1.4 %collective-permute-start.19 = (bf16[272,128]{1,0:T(8,128)(2,1)S(1)}, bf16[272,128]{1,0:T(8,128)(2,1)S(1)}, u32[]{:S(2)}, u32[]{:S(2)}) collective-permute-start(bf16[272,128]{1,0:T(8,128)(2,1)S(1)} %get-tuple-element.68), channel_id=1, source_target_pairs={{0,8},{8,0},{16,24},{24,16},{1,9},{9,1},{17,25},{25,17},{2,10},{10... | collective-permute-start | bytes 208904 | tf_op jit(solution)/shard_map/ppermute | solution.py:1110
  73.0 2.6 %collective-permute-start.20 = (bf16[272,128]{1,0:T(8,128)(2,1)S(1)}, bf16[272,128]{1,0:T(8,128)(2,1)S(1)}, u32[]{:S(2)}, u32[]{:S(2)}) collective-permute-start(bf16[272,128]{1,0:T(8,128)(2,1)S(1)} %get-tuple-element.69), channel_id=1, source_target_pairs={{0,16},{8,24},{16,0},{24,8},{1,17},{9,25},{17,1},{25,9},{2,18},{10... | collective-permute-start | bytes 208904 | tf_op jit(solution)/shard_map/ppermute | solution.py:1110
  75.7 0.4 collective-permute-start.21
  76.1 1.7 %collect.1 = (f32[64,4096]{1,0:T(8,128)S(1)}, bf16[64,512]{1,0:T(8,128)(2,1)S(1)}, bf16[64,512]{1,0:T(8,128)(2,1)S(1)}) custom-call(f32[4096,128]{1,0:T(8,128)S(1)} %get-tuple-element.51.refs_0_), custom_call_target="tpu_custom_call" | custom-call | bytes 9000000 | tf_op jit(solution)/shard_map/collect/pallas_call | solution.py:972
  77.8 0.5 collective-permute-start.11
  78.4 3.1 %collective-permute-start.12 = (bf16[64,512]{1,0:T(8,128)(2,1)S(1)}, bf16[64,512]{1,0:T(8,128)(2,1)S(1)}, u32[]{:S(2)}, u32[]{:S(2)}) collective-permute-start(bf16[64,512]{1,0:T(8,128)(2,1)S(1)} %get-tuple-element.56), channel_id=1, source_target_pairs={{0,24},{8,16},{16,8},{24,0},{1,25},{9,17},{17,9},{25,1},{2,26},{10... | collective-permute-start | bytes 196616 | tf_op jit(solution)/shard_map/ppermute | solution.py:279
  81.4 0.0 collective-permute-done.19.refs_1_
  81.4 0.0 collective-permute-done.20.refs_2_
  81.4 1.2 %collective-permute-done.21.refs_3_ = bf16[272,128]{1,0:T(8,128)(2,1)S(1)} collective-permute-done((bf16[272,128]{1,0:T(8,128)(2,1)S(1)}, bf16[272,128]{1,0:T(8,128)(2,1)S(1)}, u32[]{:S(2)}, u32[]{:S(2)}) %collective-permute-start.21) | collective-permute-done | bytes 69664 | tf_op jit(solution)/shard_map/ppermute | solution.py:1110
  82.7 1.0 %collective-permute-start.24 = (bf16[272,128]{1,0:T(8,128)(2,1)S(1)}, bf16[272,128]{1,0:T(8,128)(2,1)S(1)}, u32[]{:S(2)}, u32[]{:S(2)}) collective-permute-start(bf16[272,128]{1,0:T(8,128)(2,1)S(1)} %sum_parts.1.refs_0_), channel_id=1, source_target_pairs={{0,24},{8,16},{16,8},{24,0},{1,25},{9,17},{17,9},{25,1},{2,26},{10... | collective-permute-start | bytes 208904 | tf_op jit(solution)/shard_map/ppermute | solution.py:1114
  83.7 0.3 collective-permute-start.23
  84.1 3.1 %collective-permute-start.22 = (bf16[272,128]{1,0:T(8,128)(2,1)S(1)}, bf16[272,128]{1,0:T(8,128)(2,1)S(1)}, u32[]{:S(2)}, u32[]{:S(2)}) collective-permute-start(bf16[272,128]{1,0:T(8,128)(2,1)S(1)} %sum_parts.1.refs_0_), channel_id=1, source_target_pairs={{0,8},{8,0},{16,24},{24,16},{1,9},{9,1},{17,25},{25,17},{2,10},{10... | collective-permute-start | bytes 208904 | tf_op jit(solution)/shard_map/ppermute | solution.py:1114
  87.1 0.7 pack_back.1
  87.9 0.0 collective-permute-done.11.refs_0_.refs_3_
  87.9 0.2 add_corners.3
  88.1 0.1 collective-permute-start.13
  88.2 1.5 %collective-permute-start.14 = (bf16[64,128]{1,0:T(8,128)(2,1)S(1)}, bf16[64,128]{1,0:T(8,128)(2,1)S(1)}, u32[]{:S(2)}, u32[]{:S(2)}) collective-permute-start(bf16[64,128]{1,0:T(8,128)(2,1)S(1)} %get-tuple-element.60.refs_6_), channel_id=1, source_target_pairs={{0,7},{1,2},{2,1},{3,4},{4,3},{5,6},{6,5},{7,0},{8,15},{9,10},{10,... | collective-permute-start | bytes 49160 | tf_op jit(solution)/shard_map/ppermute | solution.py:279
  89.7 0.0 collective-permute-done.13.refs_7_
  89.7 2.7 %collective-permute-done.14.refs_8_ = bf16[64,128]{1,0:T(8,128)(2,1)S(1)} collective-permute-done((bf16[64,128]{1,0:T(8,128)(2,1)S(1)}, bf16[64,128]{1,0:T(8,128)(2,1)S(1)}, u32[]{:S(2)}, u32[]{:S(2)}) %collective-permute-start.14) | collective-permute-done | bytes 16416 | tf_op jit(solution)/shard_map/ppermute | solution.py:279
  92.4 3.1 %adjoint.1 = f32[2048,128]{1,0:T(8,128)} custom-call(f32[64,4096]{1,0:T(8,128)S(1)} %get-tuple-element.52.refs_0_, f32[8,5120]{1,0:T(8,128)S(1)} %get-tuple-element.53.refs_1_, f32[48,128]{1,0:T(8,128)S(1)} %get-tuple-element.54.refs_2_, bf16[64,512]{1,0:T(8,128)(2,1)S(1)} %collective-permute-done.11.refs_0_.refs_3_, ...), custom_call_target="tpu_custom_call" | custom-call | bytes 18000000 | tf_op jit(solution)/shard_map/adjoint/pallas_call | solution.py:1053
  95.6 0.0 collective-permute-done.23.refs_2_
  95.6 1.3 %make_steps.1 = (f32[64,192]{1,0:T(8,128)}, f32[3,192,192]{2,1,0:T(8,128)}, f32[64,192]{1,0:T(8,128)}, f32[4,192]{1,0:T(4,128)}, f32[1,64]{1,0:T(1,128)}) custom-call(bf16[272,128]{1,0:T(8,128)(2,1)S(1)} %sum_parts.1.refs_0_, bf16[272,128]{1,0:T(8,128)(2,1)S(1)} %collective-permute-done.22.refs_1_, bf16[272,128]{1,0:T(8,128)(2,1)S(1)} %collective-permute-done.23.refs_2_, ...), custom_call_target="tpu_custom_call" | custom-call | bytes 6000000 | tf_op jit(solution)/shard_map/make_steps/pallas_call | solution.py:929
  (19 shorter events, 0.1 us)
Async XLA Ops:
  0.6 31.5 %copy-start.5 = (f32[16,256]{1,0:T(8,128)S(1)}, f32[16,256]{1,0:T(8,128)}, u32[]{:S(2)}) copy-start(f32[16,256]{1,0:T(8,128)} %param.12) | copy-start | bytes 49156
  0.6 28.8 %copy-start.7 = (s32[1,4096]{1,0:T(1,128)S(1)}, s32[1,4096]{1,0:T(1,128)}, u32[]{:S(2)}) copy-start(s32[1,4096]{1,0:T(1,128)} %param.13) | copy-start | bytes 49156
  0.7 28.8 %copy-start.6 = (s32[1,32]{1,0:T(1,128)S(1)}, s32[1,32]{1,0:T(1,128)}, u32[]{:S(2)}) copy-start(s32[1,32]{1,0:T(1,128)} %param.14) | copy-start | bytes 388
  2.6 11.7 %collective-permute-start.2 = (bf16[1088,128]{1,0:T(8,128)(2,1)}, bf16[1088,128]{1,0:T(8,128)(2,1)S(1)}, u32[]{:S(2)}, u32[]{:S(2)}) collective-permute-start(bf16[1088,128]{1,0:T(8,128)(2,1)} %pack_weights.1.refs_0_), channel_id=1, source_target_pairs={{0,6},{1,7},{2,4},{3,5},{4,2},{5,3},{6,0},{7,1},{8,14},{9,15},{10,... | collective-permute-start | bytes 835592 | tf_op jit(solution)/shard_map/ppermute | solution.py:1082
  6.6 12.8 %collective-permute-start.1 = (bf16[1088,128]{1,0:T(8,128)(2,1)}, bf16[1088,128]{1,0:T(8,128)(2,1)S(1)}, u32[]{:S(2)}, u32[]{:S(2)}) collective-permute-start(bf16[1088,128]{1,0:T(8,128)(2,1)} %pack_weights.1.refs_0_), channel_id=1, source_target_pairs={{0,4},{1,5},{2,6},{3,7},{4,0},{5,1},{6,2},{7,3},{8,12},{9,13},{10,... | collective-permute-start | bytes 835592 | tf_op jit(solution)/shard_map/ppermute | solution.py:1082
  7.1 12.6 %collective-permute-start = (bf16[1088,128]{1,0:T(8,128)(2,1)}, bf16[1088,128]{1,0:T(8,128)(2,1)S(1)}, u32[]{:S(2)}, u32[]{:S(2)}) collective-permute-start(bf16[1088,128]{1,0:T(8,128)(2,1)} %pack_weights.1.refs_0_), channel_id=1, source_target_pairs={{0,2},{1,3},{2,0},{3,1},{4,6},{5,7},{6,4},{7,5},{8,10},{9,11},{10,... | collective-permute-start | bytes 835592 | tf_op jit(solution)/shard_map/ppermute | solution.py:1082
  7.2 1.2 %copy-start = (f32[64,16,256]{2,1,0:T(8,128)S(1)}, f32[64,16,256]{2,1,0:T(8,128)}, u32[]{:S(2)}) copy-start(f32[64,16,256]{2,1,0:T(8,128)} %param.10) | copy-start | bytes 3145732
  8.5 0.7 copy-start.4
  9.2 22.9 %copy-start.1 = (f32[64,16,256]{2,1,0:T(8,128)S(1)}, f32[64,16,256]{2,1,0:T(8,128)}, u32[]{:S(2)}) copy-start(f32[64,16,256]{2,1,0:T(8,128)} %param.10) | copy-start | bytes 3145732
  9.2 22.9 %copy-start.3 = (f32[64,16,256]{2,1,0:T(8,128)S(1)}, f32[64,16,256]{2,1,0:T(8,128)}, u32[]{:S(2)}) copy-start(f32[64,16,256]{2,1,0:T(8,128)} %param.11) | copy-start | bytes 3145732
  9.4 10.6 %collective-permute-start.3 = (bf16[80,512]{1,0:T(8,128)(2,1)S(1)}, bf16[80,512]{1,0:T(8,128)(2,1)S(1)}, u32[]{:S(2)}, u32[]{:S(2)}) collective-permute-start(bf16[80,512]{1,0:T(8,128)(2,1)S(1)} %get-tuple-element.41), channel_id=1, source_target_pairs={{0,8},{8,0},{16,24},{24,16},{1,9},{9,1},{17,25},{25,17},{2,10},{10... | collective-permute-start | bytes 245768 | tf_op jit(solution)/shard_map/ppermute | solution.py:279
  11.4 24.6 %collective-permute-start.7 = (bf16[1088,128]{1,0:T(8,128)(2,1)}, bf16[1088,128]{1,0:T(8,128)(2,1)S(1)}, u32[]{:S(2)}, u32[]{:S(2)}) collective-permute-start(bf16[1088,128]{1,0:T(8,128)(2,1)} %pack_weights.1.refs_0_), channel_id=1, source_target_pairs={{0,1},{1,0},{2,3},{3,2},{4,5},{5,4},{6,7},{7,6},{8,9},{9,8},{10,11... | collective-permute-start | bytes 835592 | tf_op jit(solution)/shard_map/ppermute | solution.py:1089
  14.4 21.7 %collective-permute-start.10 = (bf16[1088,128]{1,0:T(8,128)(2,1)S(1)}, bf16[1088,128]{1,0:T(8,128)(2,1)S(1)}, u32[]{:S(2)}, u32[]{:S(2)}) collective-permute-start(bf16[1088,128]{1,0:T(8,128)(2,1)S(1)} %collective-permute-done.2.refs_3_), channel_id=1, source_target_pairs={{0,1},{1,0},{2,3},{3,2},{4,5},{5,4},{6,7},{7,6},{8,9},{9,8},{10,11... | collective-permute-start | bytes 835592 | tf_op jit(solution)/shard_map/ppermute | solution.py:1089
  19.4 16.6 %collective-permute-start.9 = (bf16[1088,128]{1,0:T(8,128)(2,1)S(1)}, bf16[1088,128]{1,0:T(8,128)(2,1)S(1)}, u32[]{:S(2)}, u32[]{:S(2)}) collective-permute-start(bf16[1088,128]{1,0:T(8,128)(2,1)S(1)} %collective-permute-done.1.refs_2_), channel_id=1, source_target_pairs={{0,1},{1,0},{2,3},{3,2},{4,5},{5,4},{6,7},{7,6},{8,9},{9,8},{10,11... | collective-permute-start | bytes 835592 | tf_op jit(solution)/shard_map/ppermute | solution.py:1089
  19.7 16.4 %collective-permute-start.8 = (bf16[1088,128]{1,0:T(8,128)(2,1)S(1)}, bf16[1088,128]{1,0:T(8,128)(2,1)S(1)}, u32[]{:S(2)}, u32[]{:S(2)}) collective-permute-start(bf16[1088,128]{1,0:T(8,128)(2,1)S(1)} %collective-permute-done.refs_1_), channel_id=1, source_target_pairs={{0,1},{1,0},{2,3},{3,2},{4,5},{5,4},{6,7},{7,6},{8,9},{9,8},{10,11... | collective-permute-start | bytes 835592 | tf_op jit(solution)/shard_map/ppermute | solution.py:1089
  20.0 6.6 %collective-permute-start.4 = (bf16[80,512]{1,0:T(8,128)(2,1)S(1)}, bf16[80,512]{1,0:T(8,128)(2,1)S(1)}, u32[]{:S(2)}, u32[]{:S(2)}) collective-permute-start(bf16[80,512]{1,0:T(8,128)(2,1)S(1)} %get-tuple-element.42), channel_id=1, source_target_pairs={{0,24},{8,16},{16,8},{24,0},{1,25},{9,17},{17,9},{25,1},{2,26},{10... | collective-permute-start | bytes 245768 | tf_op jit(solution)/shard_map/ppermute | solution.py:279
  26.7 1.3 %collective-permute-start.5 = (bf16[80,128]{1,0:T(8,128)(2,1)S(1)}, bf16[80,128]{1,0:T(8,128)(2,1)S(1)}, u32[]{:S(2)}, u32[]{:S(2)}) collective-permute-start(bf16[80,128]{1,0:T(8,128)(2,1)S(1)} %get-tuple-element.45.refs_5_), channel_id=1, source_target_pairs={{0,1},{1,0},{2,3},{3,2},{4,5},{5,4},{6,7},{7,6},{8,9},{9,8},{10,11... | collective-permute-start | bytes 61448 | tf_op jit(solution)/shard_map/ppermute | solution.py:279
  28.0 4.1 %collective-permute-start.6 = (bf16[80,128]{1,0:T(8,128)(2,1)S(1)}, bf16[80,128]{1,0:T(8,128)(2,1)S(1)}, u32[]{:S(2)}, u32[]{:S(2)}) collective-permute-start(bf16[80,128]{1,0:T(8,128)(2,1)S(1)} %get-tuple-element.46.refs_6_), channel_id=1, source_target_pairs={{0,7},{1,2},{2,1},{3,4},{4,3},{5,6},{6,5},{7,0},{8,15},{9,10},{10,... | collective-permute-start | bytes 61448 | tf_op jit(solution)/shard_map/ppermute | solution.py:279
  36.0 9.5 %copy-start.2 = (bf16[1088,128]{1,0:T(8,128)(2,1)S(1)}, bf16[1088,128]{1,0:T(8,128)(2,1)}, u32[]{:S(2)}) copy-start(bf16[1088,128]{1,0:T(8,128)(2,1)} %pack_weights.1.refs_0_) | copy-start | bytes 835588
  45.5 9.6 %collective-permute-start.15 = (bf16[4,1088,128]{2,1,0:T(8,128)(2,1)S(1)}, bf16[4,1088,128]{2,1,0:T(8,128)(2,1)S(1)}, u32[]{:S(2)}, u32[]{:S(2)}) collective-permute-start(bf16[4,1088,128]{2,1,0:T(8,128)(2,1)S(1)} %get-tuple-element.62), channel_id=1, source_target_pairs={{0,1},{1,0},{2,3},{3,2},{4,5},{5,4},{6,7},{7,6},{8,9},{9,8},{10,11... | collective-permute-start | bytes 3342344 | tf_op jit(solution)/shard_map/ppermute | solution.py:1094
  55.3 9.6 %collective-permute-start.16 = (bf16[1088,128]{1,0:T(8,128)(2,1)S(1)}, bf16[1088,128]{1,0:T(8,128)(2,1)S(1)}, u32[]{:S(2)}, u32[]{:S(2)}) collective-permute-start(bf16[1088,128]{1,0:T(8,128)(2,1)S(1)} %get-tuple-element.64), channel_id=1, source_target_pairs={{0,2},{1,3},{2,0},{3,1},{4,6},{5,7},{6,4},{7,5},{8,10},{9,11},{10,... | collective-permute-start | bytes 835592 | tf_op jit(solution)/shard_map/ppermute | solution.py:1101
  57.0 8.8 %collective-permute-start.17 = (bf16[1088,128]{1,0:T(8,128)(2,1)S(1)}, bf16[1088,128]{1,0:T(8,128)(2,1)S(1)}, u32[]{:S(2)}, u32[]{:S(2)}) collective-permute-start(bf16[1088,128]{1,0:T(8,128)(2,1)S(1)} %get-tuple-element.65), channel_id=1, source_target_pairs={{0,4},{1,5},{2,6},{3,7},{4,0},{5,1},{6,2},{7,3},{8,12},{9,13},{10,... | collective-permute-start | bytes 835592 | tf_op jit(solution)/shard_map/ppermute | solution.py:1101
  57.8 13.5 %collective-permute-start.18 = (bf16[1088,128]{1,0:T(8,128)(2,1)S(1)}, bf16[1088,128]{1,0:T(8,128)(2,1)S(1)}, u32[]{:S(2)}, u32[]{:S(2)}) collective-permute-start(bf16[1088,128]{1,0:T(8,128)(2,1)S(1)} %get-tuple-element.66), channel_id=1, source_target_pairs={{0,6},{1,7},{2,4},{3,5},{4,2},{5,3},{6,0},{7,1},{8,14},{9,15},{10,... | collective-permute-start | bytes 835592 | tf_op jit(solution)/shard_map/ppermute | solution.py:1101
  71.6 9.8 %collective-permute-start.19 = (bf16[272,128]{1,0:T(8,128)(2,1)S(1)}, bf16[272,128]{1,0:T(8,128)(2,1)S(1)}, u32[]{:S(2)}, u32[]{:S(2)}) collective-permute-start(bf16[272,128]{1,0:T(8,128)(2,1)S(1)} %get-tuple-element.68), channel_id=1, source_target_pairs={{0,8},{8,0},{16,24},{24,16},{1,9},{9,1},{17,25},{25,17},{2,10},{10... | collective-permute-start | bytes 208904 | tf_op jit(solution)/shard_map/ppermute | solution.py:1110
  73.0 8.4 %collective-permute-start.20 = (bf16[272,128]{1,0:T(8,128)(2,1)S(1)}, bf16[272,128]{1,0:T(8,128)(2,1)S(1)}, u32[]{:S(2)}, u32[]{:S(2)}) collective-permute-start(bf16[272,128]{1,0:T(8,128)(2,1)S(1)} %get-tuple-element.69), channel_id=1, source_target_pairs={{0,16},{8,24},{16,0},{24,8},{1,17},{9,25},{17,1},{25,9},{2,18},{10... | collective-permute-start | bytes 208904 | tf_op jit(solution)/shard_map/ppermute | solution.py:1110
  75.7 6.9 %collective-permute-start.21 = (bf16[272,128]{1,0:T(8,128)(2,1)S(1)}, bf16[272,128]{1,0:T(8,128)(2,1)S(1)}, u32[]{:S(2)}, u32[]{:S(2)}) collective-permute-start(bf16[272,128]{1,0:T(8,128)(2,1)S(1)} %get-tuple-element.70), channel_id=1, source_target_pairs={{0,24},{8,16},{16,8},{24,0},{1,25},{9,17},{17,9},{25,1},{2,26},{10... | collective-permute-start | bytes 208904 | tf_op jit(solution)/shard_map/ppermute | solution.py:1110
  77.8 10.0 %collective-permute-start.11 = (bf16[64,512]{1,0:T(8,128)(2,1)S(1)}, bf16[64,512]{1,0:T(8,128)(2,1)S(1)}, u32[]{:S(2)}, u32[]{:S(2)}) collective-permute-start(bf16[64,512]{1,0:T(8,128)(2,1)S(1)} %get-tuple-element.55), channel_id=1, source_target_pairs={{0,8},{8,0},{16,24},{24,16},{1,9},{9,1},{17,25},{25,17},{2,10},{10... | collective-permute-start | bytes 196616 | tf_op jit(solution)/shard_map/ppermute | solution.py:279
  78.4 9.5 %collective-permute-start.12 = (bf16[64,512]{1,0:T(8,128)(2,1)S(1)}, bf16[64,512]{1,0:T(8,128)(2,1)S(1)}, u32[]{:S(2)}, u32[]{:S(2)}) collective-permute-start(bf16[64,512]{1,0:T(8,128)(2,1)S(1)} %get-tuple-element.56), channel_id=1, source_target_pairs={{0,24},{8,16},{16,8},{24,0},{1,25},{9,17},{17,9},{25,1},{2,26},{10... | collective-permute-start | bytes 196616 | tf_op jit(solution)/shard_map/ppermute | solution.py:279
  82.7 12.9 %collective-permute-start.24 = (bf16[272,128]{1,0:T(8,128)(2,1)S(1)}, bf16[272,128]{1,0:T(8,128)(2,1)S(1)}, u32[]{:S(2)}, u32[]{:S(2)}) collective-permute-start(bf16[272,128]{1,0:T(8,128)(2,1)S(1)} %sum_parts.1.refs_0_), channel_id=1, source_target_pairs={{0,24},{8,16},{16,8},{24,0},{1,25},{9,17},{17,9},{25,1},{2,26},{10... | collective-permute-start | bytes 208904 | tf_op jit(solution)/shard_map/ppermute | solution.py:1114
  83.7 11.8 %collective-permute-start.23 = (bf16[272,128]{1,0:T(8,128)(2,1)S(1)}, bf16[272,128]{1,0:T(8,128)(2,1)S(1)}, u32[]{:S(2)}, u32[]{:S(2)}) collective-permute-start(bf16[272,128]{1,0:T(8,128)(2,1)S(1)} %sum_parts.1.refs_0_), channel_id=1, source_target_pairs={{0,16},{8,24},{16,0},{24,8},{1,17},{9,25},{17,1},{25,9},{2,18},{10... | collective-permute-start | bytes 208904 | tf_op jit(solution)/shard_map/ppermute | solution.py:1114
  84.1 11.5 %collective-permute-start.22 = (bf16[272,128]{1,0:T(8,128)(2,1)S(1)}, bf16[272,128]{1,0:T(8,128)(2,1)S(1)}, u32[]{:S(2)}, u32[]{:S(2)}) collective-permute-start(bf16[272,128]{1,0:T(8,128)(2,1)S(1)} %sum_parts.1.refs_0_), channel_id=1, source_target_pairs={{0,8},{8,0},{16,24},{24,16},{1,9},{9,1},{17,25},{25,17},{2,10},{10... | collective-permute-start | bytes 208904 | tf_op jit(solution)/shard_map/ppermute | solution.py:1114
  88.1 1.6 %collective-permute-start.13 = (bf16[64,128]{1,0:T(8,128)(2,1)S(1)}, bf16[64,128]{1,0:T(8,128)(2,1)S(1)}, u32[]{:S(2)}, u32[]{:S(2)}) collective-permute-start(bf16[64,128]{1,0:T(8,128)(2,1)S(1)} %get-tuple-element.59.refs_5_), channel_id=1, source_target_pairs={{0,1},{1,0},{2,3},{3,2},{4,5},{5,4},{6,7},{7,6},{8,9},{9,8},{10,11... | collective-permute-start | bytes 49160 | tf_op jit(solution)/shard_map/ppermute | solution.py:279
  88.2 4.3 %collective-permute-start.14 = (bf16[64,128]{1,0:T(8,128)(2,1)S(1)}, bf16[64,128]{1,0:T(8,128)(2,1)S(1)}, u32[]{:S(2)}, u32[]{:S(2)}) collective-permute-start(bf16[64,128]{1,0:T(8,128)(2,1)S(1)} %get-tuple-element.60.refs_6_), channel_id=1, source_target_pairs={{0,7},{1,2},{2,1},{3,4},{4,3},{5,6},{6,5},{7,0},{8,15},{9,10},{10,... | collective-permute-start | bytes 49160 | tf_op jit(solution)/shard_map/ppermute | solution.py:279
